TPU v7x, 32 devices: a whole 2x2x4 slice. The times are simulated.
32 devices in a mesh: dp: 8 (over z, y), mp: 4 (over x, core).
Axes of the slice: x: 2, y: 2, z: 4, core: 2. Of those that a mesh axis runs over, the one named last changes fastest.
Arguments:
- pixels: float32 [8, 48, 16, 384], P('dp'), may hold values from -6 to 6
- dataset_id: int32 [8], P('dp'), may hold values from 0 to 5
- variable_mask: int32 [6, 48], replicated, may hold values from 0 to 1, as said below
- lead_hours: int32 [8], P('dp'), may hold values from 6 to 168
- token_counts: int32 [8], P('dp'), may hold values from 128 to 2048
- dataset_weight: int32 [6], replicated, may hold values from 1 to 4
- patch_weight: bfloat16 [48, 16, 1024], replicated, may hold values from -1.5 to 1.5
- variable_embed: float32 [48, 1024], replicated, may hold values from -4 to 4
- position_embed: float32 [384, 1024], replicated, may hold values from -4 to 4
- pool_query: float32 [1024], replicated, may hold values from -6 to 6
- pool_query_weight: bfloat16 [1024, 1024], P(None, 'mp'), may hold values from -0.1875 to 0.1875
- pool_key_weight: bfloat16 [1024, 1024], P(None, 'mp'), may hold values from -0.1875 to 0.1875
- pool_value_weight: bfloat16 [1024, 1024], P(None, 'mp'), may hold values from -0.1875 to 0.1875
- pool_value_bias: float32 [1024], P('mp'), may hold values from -2 to 2
- pool_output_weight: bfloat16 [1024, 1024], P('mp'), may hold values from -0.75 to 0.75
- pool_output_bias: float32 [1024], replicated, may hold values from -2 to 2
- lead_weight: float32 [1024], replicated, may hold values from -0.6 to 0.6
- lead_bias: float32 [1024], replicated, may hold values from -2 to 2
- norm_gain: float32 [2, 2, 1024], replicated, may hold values from 0.5 to 1.5
- norm_bias: float32 [2, 2, 1024], replicated, may hold values from -1.2 to 1.2
- attention_weight: bfloat16 [2, 3, 1024, 1024], P(None, None, None, 'mp'), may hold values from -0.1875 to 0.1875
- attention_bias: float32 [2, 2, 1024], P(None, None, 'mp'), may hold values from -2 to 2
- output_weight: bfloat16 [2, 1024, 1024], P(None, 'mp'), may hold values from -0.75 to 0.75
- output_bias: float32 [2, 1024], replicated, may hold values from -1.2 to 1.2
- up_weight: bfloat16 [2, 1024, 4096], P(None, None, 'mp'), may hold values from -0.1875 to 0.1875
- up_bias: float32 [2, 4096], P(None, 'mp'), may hold values from -2 to 2
- down_weight: bfloat16 [2, 4096, 1024], P(None, 'mp'), may hold values from -0.1875 to 0.1875
- down_bias: float32 [2, 1024], replicated, may hold values from -1.2 to 1.2
- cotangent: float32 [8, 384, 1024], P('dp'), may hold values from -6 to 6
Outputs:
- layer_out: float32 [8, 384, 1024], P('dp')
- pixel_grad: float32 [8, 48, 16, 384], P('dp')
- grad_patch_weight: float32 [48, 16, 1024], P(None, None, ('dp', 'mp'))
- grad_variable_embed: float32 [48, 1024], P(None, ('dp', 'mp'))
- grad_position_embed: float32 [384, 1024], P(None, 'dp')
- grad_pool_query: float32 [1024], P(('dp', 'mp'))
- grad_pool_query_weight: float32 [1024, 1024], P('dp', 'mp')
- grad_pool_key_weight: float32 [1024, 1024], P('dp', 'mp')
- grad_pool_value_weight: float32 [1024, 1024], P('dp', 'mp')
- grad_pool_value_bias: float32 [1024], P(('mp', 'dp'))
- grad_pool_output_weight: float32 [1024, 1024], P('mp', 'dp')
- grad_pool_output_bias: float32 [1024], P('dp')
- grad_lead_weight: float32 [1024], P('dp')
- grad_lead_bias: float32 [1024], P('dp')
- grad_norm_gain: float32 [2, 2, 1024], P(None, None, 'dp')
- grad_norm_bias: float32 [2, 2, 1024], P(None, None, 'dp')
- grad_attention_weight: float32 [2, 3, 1024, 1024], P(None, None, 'dp', 'mp')
- grad_attention_bias: float32 [2, 2, 1024], P(None, None, ('mp', 'dp'))
- grad_output_weight: float32 [2, 1024, 1024], P(None, 'mp', 'dp')
- grad_output_bias: float32 [2, 1024], P(None, 'dp')
- grad_up_weight: float32 [2, 1024, 4096], P(None, 'dp', 'mp')
- grad_up_bias: float32 [2, 4096], P(None, ('mp', 'dp'))
- grad_down_weight: float32 [2, 4096, 1024], P(None, 'mp', 'dp')
- grad_down_bias: float32 [2, 1024], P(None, 'dp')
Inputs may be any that keep to these rules, and one draw needn't show every extreme that they name: `variable_mask`: each dataset's row has at least one 1.
All inputs are finite; a program needn't handle non-finite values.
Results may differ from a plain program's by a relative error of at most 0.035.
Values sent between devices are 32-bit elements; how exact they have to be, the bound alone decides.
No kernel may reach another device: no remote copies, remote signals or barrier semaphores. Data moves between devices by JAX's collectives and lax.ppermute only.
A program may use at most 192 MiB of HBM per device.

v0:
```python
import math

import jax
import jax.numpy as jnp
from jax import lax
from jax.sharding import PartitionSpec as P

HEAD_DIM = 64


HIGHEST = lax.Precision.HIGHEST


def norm_layer(inputs, gain_vec, bias_vec):
    row_mean = jnp.mean(inputs, axis=-1, keepdims=True)
    centred = inputs - row_mean
    spread = jnp.mean(centred * centred, axis=-1, keepdims=True)
    return centred * lax.rsqrt(spread + 1e-05) * gain_vec + bias_vec


def gelu_exact(pre_act):
    return jax.nn.gelu(pre_act, approximate=False)


def softmax_last(scores):
    row_max = jnp.max(scores, axis=-1, keepdims=True)
    exponent = jnp.exp(scores - row_max)
    return exponent / jnp.sum(exponent, axis=-1, keepdims=True)


def matmul(left, right):
    return jnp.dot(left, right, preferred_element_type=jnp.float32)


def per_device(
    pixels,
    dataset_id,
    variable_mask,
    lead_hours,
    token_counts,
    dataset_weight,
    patch_weight,
    variable_embed,
    position_embed,
    pool_query,
    pool_query_weight,
    pool_key_weight,
    pool_value_weight,
    pool_value_bias,
    pool_output_weight,
    pool_output_bias,
    lead_weight,
    lead_bias,
    norm_gain,
    norm_bias,
    attention_weight,
    attention_bias,
    output_weight,
    output_bias,
    up_weight,
    up_bias,
    down_weight,
    down_bias,
    cotangent,
):
    var_count = pixels.shape[1]
    row_count = pixels.shape[3]
    model_width = patch_weight.shape[2]
    local_width = pool_query_weight.shape[1]
    head_count = local_width // HEAD_DIM
    layer_count = attention_weight.shape[0]
    block_vars = 8
    block_count = var_count // block_vars
    root_dim = math.sqrt(HEAD_DIM)
    pixel_low = pixels[0].astype(jnp.bfloat16)
    dataset_pick = jnp.arange(variable_mask.shape[0], dtype=jnp.int32) == dataset_id[0]
    mask_row = jnp.sum(jnp.where(dataset_pick[:, None], variable_mask, 0), axis=0)
    item_weight = jnp.sum(jnp.where(dataset_pick, dataset_weight, 0)).astype(jnp.float32)
    own_count = token_counts[0].astype(jnp.float32)
    count_total = lax.psum(own_count, "dp")
    item_scale = item_weight * own_count / count_total

    def embed_block(block_index):
        first_var = block_index * block_vars
        pixel_block = lax.dynamic_slice_in_dim(pixel_low, first_var, block_vars, 0)
        weight_block = lax.dynamic_slice_in_dim(patch_weight, first_var, block_vars, 0)
        embed_rows = lax.dynamic_slice_in_dim(variable_embed, first_var, block_vars, 0)
        embedded = jnp.einsum(
            "vkp,vkd->vpd", pixel_block, weight_block, preferred_element_type=jnp.float32
        )
        return (pixel_block, weight_block, (embedded + embed_rows[:, None, :]).astype(jnp.bfloat16))

    def project_block(block_index):
        embed_flat = embed_block(block_index)[2].reshape(block_vars * row_count, model_width)
        key_part = matmul(embed_flat, pool_key_weight).astype(jnp.bfloat16)
        value_part = (matmul(embed_flat, pool_value_weight) + pool_value_bias).astype(jnp.bfloat16)
        return (
            key_part.reshape(block_vars, row_count, local_width),
            value_part.reshape(block_vars, row_count, local_width),
        )

    key_rows, value_rows = lax.map(project_block, jnp.arange(block_count, dtype=jnp.int32))
    key_heads = key_rows.reshape(var_count, row_count, head_count, HEAD_DIM)
    value_heads = value_rows.reshape(var_count, row_count, head_count, HEAD_DIM)
    query_low = pool_query.astype(jnp.bfloat16)
    query_vec = matmul(query_low[None, :], pool_query_weight)[0].astype(jnp.bfloat16)
    query_heads = query_vec.reshape(head_count, HEAD_DIM)
    pool_scores = (
        jnp.einsum("vphd,hd->phv", key_heads, query_heads, preferred_element_type=jnp.float32)
        / root_dim
    )
    pool_scores = jnp.where(mask_row[None, None, :] > 0, pool_scores, -1000000000.0)
    pool_probs = softmax_last(pool_scores)
    probs_low = pool_probs.astype(jnp.bfloat16)
    pooled = jnp.einsum("phv,vphd->phd", probs_low, value_heads, preferred_element_type=jnp.float32)
    pooled = pooled.reshape(row_count, local_width).astype(jnp.bfloat16)
    hidden = lax.psum(matmul(pooled, pool_output_weight), "mp") + pool_output_bias
    lead_scale = lead_hours[0].astype(jnp.float32) / 24.0
    hidden = hidden + position_embed + lead_scale * lead_weight + lead_bias
    kept_state = []
    for layer_num in range(layer_count):
        layer_input = hidden
        normed = norm_layer(hidden, norm_gain[layer_num, 0], norm_bias[layer_num, 0]).astype(
            jnp.bfloat16
        )
        queries = (
            matmul(normed, attention_weight[layer_num, 0]) + attention_bias[layer_num, 0]
        ).astype(jnp.bfloat16)
        keys_new = matmul(normed, attention_weight[layer_num, 1]).astype(jnp.bfloat16)
        values_new = (
            matmul(normed, attention_weight[layer_num, 2]) + attention_bias[layer_num, 1]
        ).astype(jnp.bfloat16)
        query_three = queries.reshape(row_count, head_count, HEAD_DIM)
        key_three = keys_new.reshape(row_count, head_count, HEAD_DIM)
        value_three = values_new.reshape(row_count, head_count, HEAD_DIM)
        scores = (
            jnp.einsum("phd,khd->hpk", query_three, key_three, preferred_element_type=jnp.float32)
            / root_dim
        )
        row_max = jnp.max(scores, axis=-1, keepdims=True)
        exponent = jnp.exp(scores - row_max)
        row_sum = jnp.sum(exponent, axis=-1, keepdims=True)
        attend_low = (exponent / row_sum).astype(jnp.bfloat16)
        log_total = row_max + jnp.log(row_sum)
        mixed_heads = jnp.einsum(
            "hpk,khd->phd", attend_low, value_three, preferred_element_type=jnp.float32
        )
        mixed_heads = mixed_heads.reshape(row_count, local_width).astype(jnp.bfloat16)
        hidden = (
            hidden
            + lax.psum(matmul(mixed_heads, output_weight[layer_num]), "mp")
            + output_bias[layer_num]
        )
        middle = hidden
        normed_two = norm_layer(hidden, norm_gain[layer_num, 1], norm_bias[layer_num, 1]).astype(
            jnp.bfloat16
        )
        pre_act = matmul(normed_two, up_weight[layer_num]) + up_bias[layer_num]
        activation = gelu_exact(pre_act).astype(jnp.bfloat16)
        hidden = (
            hidden
            + lax.psum(matmul(activation, down_weight[layer_num]), "mp")
            + down_bias[layer_num]
        )
        kept_state.append(
            (
                layer_input,
                normed,
                queries,
                keys_new,
                values_new,
                log_total,
                mixed_heads,
                middle,
                normed_two,
                pre_act,
                activation,
            )
        )
    grad_hidden = cotangent[0]
    layer_results = []
    for layer_num in reversed(range(layer_count)):
        (
            layer_input,
            normed,
            queries,
            keys_new,
            values_new,
            log_total,
            mixed_heads,
            middle,
            normed_two,
            pre_act,
            activation,
        ) = kept_state[layer_num]
        down_low = grad_hidden.astype(jnp.bfloat16)
        down_bias_grad = jnp.sum(grad_hidden, axis=0) * item_scale
        down_grad = matmul(activation.T, down_low) * item_scale
        grad_activation = matmul(down_low, down_weight[layer_num].T)
        grad_pre = jax.vjp(gelu_exact, pre_act)[1](grad_activation)[0]
        up_bias_grad = jnp.sum(grad_pre, axis=0) * item_scale
        pre_low = grad_pre.astype(jnp.bfloat16)
        up_grad = matmul(normed_two.T, pre_low) * item_scale
        normed_grad_two = lax.psum(matmul(pre_low, up_weight[layer_num].T), "mp")
        norm_pull_two = jax.vjp(
            norm_layer, middle, norm_gain[layer_num, 1], norm_bias[layer_num, 1]
        )[1]
        grad_middle, gain_two, bias_two = norm_pull_two(normed_grad_two)
        grad_hidden = grad_hidden + grad_middle
        out_low = grad_hidden.astype(jnp.bfloat16)
        out_bias_grad = jnp.sum(grad_hidden, axis=0) * item_scale
        out_weight_grad = matmul(mixed_heads.T, out_low) * item_scale
        grad_mixed = matmul(out_low, output_weight[layer_num].T).astype(jnp.bfloat16)
        grad_mixed = grad_mixed.reshape(row_count, head_count, HEAD_DIM)
        query_three = queries.reshape(row_count, head_count, HEAD_DIM)
        key_three = keys_new.reshape(row_count, head_count, HEAD_DIM)
        value_three = values_new.reshape(row_count, head_count, HEAD_DIM)
        scores = (
            jnp.einsum("phd,khd->hpk", query_three, key_three, preferred_element_type=jnp.float32)
            / root_dim
        )
        attend = jnp.exp(scores - log_total)
        attend_low = attend.astype(jnp.bfloat16)
        grad_attend = jnp.einsum(
            "phd,khd->hpk", grad_mixed, value_three, preferred_element_type=jnp.float32
        )
        grad_values = jnp.einsum(
            "hpk,phd->khd", attend_low, grad_mixed, preferred_element_type=jnp.float32
        )
        grad_values = grad_values.reshape(row_count, local_width)
        grad_scores = attend * (grad_attend - jnp.sum(attend * grad_attend, axis=-1, keepdims=True))
        score_low = grad_scores.astype(jnp.bfloat16)
        grad_queries = (
            jnp.einsum("hpk,khd->phd", score_low, key_three, preferred_element_type=jnp.float32)
            / root_dim
        )
        grad_keys = (
            jnp.einsum("hpk,phd->khd", score_low, query_three, preferred_element_type=jnp.float32)
            / root_dim
        )
        grad_queries = grad_queries.reshape(row_count, local_width)
        grad_keys = grad_keys.reshape(row_count, local_width)
        qv_grad = (
            jnp.stack([jnp.sum(grad_queries, axis=0), jnp.sum(grad_values, axis=0)]) * item_scale
        )
        grad_inputs = jnp.concatenate([grad_queries, grad_keys, grad_values], axis=1).astype(
            jnp.bfloat16
        )
        weight_grad_all = matmul(normed.T, grad_inputs)
        attention_grad = (
            weight_grad_all.reshape(model_width, 3, local_width).transpose(1, 0, 2) * item_scale
        )
        stacked_weight = jnp.transpose(attention_weight[layer_num], (0, 2, 1)).reshape(
            3 * local_width, model_width
        )
        normed_grad_one = lax.psum(matmul(grad_inputs, stacked_weight), "mp")
        norm_pull_one = jax.vjp(
            norm_layer, layer_input, norm_gain[layer_num, 0], norm_bias[layer_num, 0]
        )[1]
        grad_input, gain_one, bias_one = norm_pull_one(normed_grad_one)
        grad_hidden = grad_hidden + grad_input
        gain_grad = jnp.stack([gain_one, gain_two]) * item_scale
        bias_grad = jnp.stack([bias_one, bias_two]) * item_scale
        layer_entry = (
            gain_grad,
            bias_grad,
            attention_grad,
            qv_grad,
            out_weight_grad,
            out_bias_grad,
            up_grad,
            up_bias_grad,
            down_grad,
            down_bias_grad,
        )
        layer_results.append(layer_entry)
    ordered = layer_results[::-1]
    stacked = [jnp.stack([layer_entry[member] for layer_entry in ordered]) for member in range(10)]
    (
        gain_all,
        bias_all,
        attention_all,
        qv_all,
        out_weight_all,
        out_bias_all,
        up_all,
        up_bias_all,
        down_all,
        down_bias_all,
    ) = stacked
    column_sum = jnp.sum(grad_hidden, axis=0)
    position_grad = grad_hidden * item_scale
    column_grad = column_sum * item_scale
    lead_weight_grad = lead_scale * column_sum * item_scale
    pool_low_grad = grad_hidden.astype(jnp.bfloat16)
    pool_out_grad = matmul(pooled.T, pool_low_grad) * item_scale
    grad_pooled = matmul(pool_low_grad, pool_output_weight.T).astype(jnp.bfloat16)
    grad_pooled = grad_pooled.reshape(row_count, head_count, HEAD_DIM)
    grad_probs = jnp.einsum(
        "phd,vphd->phv", grad_pooled, value_heads, preferred_element_type=jnp.float32
    )
    grad_pool_scores = pool_probs * (
        grad_probs - jnp.sum(pool_probs * grad_probs, axis=-1, keepdims=True)
    )
    query_float = query_heads.astype(jnp.float32)
    pooled_float = grad_pooled.astype(jnp.float32)

    def pool_block(running, block_index):
        key_weight_acc, value_weight_acc, query_acc, value_bias_acc = running
        pixel_block, weight_block, embed_low = embed_block(block_index)
        first_var = block_index * block_vars
        score_block = lax.dynamic_slice_in_dim(grad_pool_scores, first_var, block_vars, 2)
        prob_block = lax.dynamic_slice_in_dim(probs_low, first_var, block_vars, 2)
        key_block = lax.dynamic_slice_in_dim(key_heads, first_var, block_vars, 0).astype(
            jnp.float32
        )
        query_acc = (
            query_acc
            + jnp.einsum("phv,vphd->hd", score_block, key_block, precision=HIGHEST) / root_dim
        )
        score_turned = jnp.transpose(score_block, (2, 0, 1))[..., None]
        key_grad_low = (score_turned * query_float[None, None] / root_dim).astype(jnp.bfloat16)
        key_grad_low = key_grad_low.reshape(block_vars * row_count, local_width)
        prob_turned = jnp.transpose(prob_block, (2, 0, 1))[..., None].astype(jnp.float32)
        value_grad = (prob_turned * pooled_float[None]).reshape(block_vars, row_count, local_width)
        value_bias_acc = value_bias_acc + jnp.sum(value_grad, axis=(0, 1))
        value_grad_low = value_grad.astype(jnp.bfloat16).reshape(
            block_vars * row_count, local_width
        )
        embed_flat = embed_low.reshape(block_vars * row_count, model_width)
        key_weight_acc = key_weight_acc + matmul(embed_flat.T, key_grad_low)
        value_weight_acc = value_weight_acc + matmul(embed_flat.T, value_grad_low)
        grad_embed = matmul(key_grad_low, pool_key_weight.T) + matmul(
            value_grad_low, pool_value_weight.T
        )
        grad_embed = grad_embed.reshape(block_vars, row_count, model_width)
        patch_grad = jnp.einsum(
            "vkp,vpd->vkd", pixel_block.astype(jnp.float32), grad_embed, precision=HIGHEST
        )
        variable_grad = jnp.sum(grad_embed, axis=1)
        pixel_part = jnp.einsum(
            "vpd,vkd->vkp", grad_embed, weight_block.astype(jnp.float32), precision=HIGHEST
        )
        return (
            (key_weight_acc, value_weight_acc, query_acc, value_bias_acc),
            (patch_grad, variable_grad, pixel_part),
        )

    start_state = (
        jnp.zeros((model_width, local_width), jnp.float32),
        jnp.zeros((model_width, local_width), jnp.float32),
        jnp.zeros((head_count, HEAD_DIM), jnp.float32),
        jnp.zeros((local_width,), jnp.float32),
    )
    final_state, block_outputs = lax.scan(
        pool_block, start_state, jnp.arange(block_count, dtype=jnp.int32)
    )
    key_weight_sum, value_weight_sum, query_sum, value_bias_sum = final_state
    patch_all = block_outputs[0].reshape(var_count, pixels.shape[2], model_width)
    variable_all = block_outputs[1].reshape(var_count, model_width)
    pixel_all = block_outputs[2].reshape(var_count, pixels.shape[2], row_count)
    pixel_grad = lax.psum(pixel_all, "mp")
    query_grad_low = query_sum.reshape(local_width).astype(jnp.bfloat16)
    query_weight_grad = matmul(query_low[:, None], query_grad_low[None, :]) * item_scale
    query_part = matmul(pool_query_weight, query_grad_low[:, None])[:, 0]
    key_weight_grad = key_weight_sum * item_scale
    value_weight_grad = value_weight_sum * item_scale
    pool_bias_grad = value_bias_sum * item_scale
    patch_sum, variable_sum, pool_query_sum = (
        lax.psum_scatter(patch_all * item_scale, ("dp", "mp"), scatter_dimension=2, tiled=True),
        lax.psum_scatter(variable_all * item_scale, ("dp", "mp"), scatter_dimension=1, tiled=True),
        lax.psum_scatter(query_part * item_scale, ("dp", "mp"), scatter_dimension=0, tiled=True),
    )
    (
        gain_all,
        bias_all,
        attention_all,
        qv_all,
        out_weight_all,
        out_bias_all,
        up_all,
        up_bias_all,
        down_all,
        down_bias_all,
        position_sum,
        query_weight_sum,
        key_weight_all,
        value_weight_all,
        pool_bias_sum,
        pool_out_sum,
        column_total,
        lead_weight_sum,
    ) = (
        lax.psum_scatter(gain_all, "dp", scatter_dimension=2, tiled=True),
        lax.psum_scatter(bias_all, "dp", scatter_dimension=2, tiled=True),
        lax.psum_scatter(attention_all, "dp", scatter_dimension=2, tiled=True),
        lax.psum_scatter(qv_all, "dp", scatter_dimension=2, tiled=True),
        lax.psum_scatter(out_weight_all, "dp", scatter_dimension=2, tiled=True),
        lax.psum_scatter(out_bias_all, "dp", scatter_dimension=1, tiled=True),
        lax.psum_scatter(up_all, "dp", scatter_dimension=1, tiled=True),
        lax.psum_scatter(up_bias_all, "dp", scatter_dimension=1, tiled=True),
        lax.psum_scatter(down_all, "dp", scatter_dimension=2, tiled=True),
        lax.psum_scatter(down_bias_all, "dp", scatter_dimension=1, tiled=True),
        lax.psum_scatter(position_grad, "dp", scatter_dimension=1, tiled=True),
        lax.psum_scatter(query_weight_grad, "dp", scatter_dimension=0, tiled=True),
        lax.psum_scatter(key_weight_grad, "dp", scatter_dimension=0, tiled=True),
        lax.psum_scatter(value_weight_grad, "dp", scatter_dimension=0, tiled=True),
        lax.psum_scatter(pool_bias_grad, "dp", scatter_dimension=0, tiled=True),
        lax.psum_scatter(pool_out_grad, "dp", scatter_dimension=1, tiled=True),
        lax.psum_scatter(column_grad, "dp", scatter_dimension=0, tiled=True),
        lax.psum_scatter(lead_weight_grad, "dp", scatter_dimension=0, tiled=True),
    )
    merged = [
        patch_sum,
        variable_sum,
        position_sum,
        pool_query_sum,
        query_weight_sum,
        key_weight_all,
        value_weight_all,
        pool_bias_sum,
        pool_out_sum,
        column_total,
        lead_weight_sum,
        column_total,
        gain_all,
        bias_all,
        attention_all,
        qv_all,
        out_weight_all,
        out_bias_all,
        up_all,
        up_bias_all,
        down_all,
        down_bias_all,
    ]
    return tuple([hidden[None], pixel_grad[None]] + merged)


def solution(mesh):
    return jax.shard_map(
        per_device,
        mesh=mesh,
        in_specs=(
            P("dp", None, None, None),
            P("dp"),
            P(),
            P("dp"),
            P("dp"),
            P(),
            P(),
            P(),
            P(),
            P(),
            P(None, "mp"),
            P(None, "mp"),
            P(None, "mp"),
            P("mp"),
            P("mp", None),
            P(),
            P(),
            P(),
            P(),
            P(),
            P(None, None, None, "mp"),
            P(None, None, "mp"),
            P(None, "mp", None),
            P(),
            P(None, None, "mp"),
            P(None, "mp"),
            P(None, "mp", None),
            P(),
            P("dp", None, None),
        ),
        out_specs=(
            P("dp", None, None),
            P("dp", None, None, None),
            P(None, None, ("dp", "mp")),
            P(None, ("dp", "mp")),
            P(None, "dp"),
            P(("dp", "mp")),
            P("dp", "mp"),
            P("dp", "mp"),
            P("dp", "mp"),
            P(("mp", "dp")),
            P("mp", "dp"),
            P("dp"),
            P("dp"),
            P("dp"),
            P(None, None, "dp"),
            P(None, None, "dp"),
            P(None, None, "dp", "mp"),
            P(None, None, ("mp", "dp")),
            P(None, "mp", "dp"),
            P(None, "dp"),
            P(None, "dp", "mp"),
            P(None, ("mp", "dp")),
            P(None, "mp", "dp"),
            P(None, "dp"),
        ),
        check_vma=False,
    )
```

profile of v0, /device:TPU:0, one launch (start us, length us, event | category | flops | bytes accessed | tf_op | source)
XLA Modules:
  0.0 2214.1 jit_solution(10733894737056458230)
XLA Ops:
  8.8 137.3 %while.36 = (s32[]{:T(128)}, bf16[6,8,384,256]{2,3,1,0:T(8,128)(2,1)}, bf16[6,8,384,256]{2,3,1,0:T(8,128)(2,1)}, s32[6]{0:T(128)S(1)}, bf16[48,16,384]{2,1,0:T(8...) while((s32[]{:T(128)}, ...), condition=%wide.region_2.3_spmd, body=%wide.region_1.2_spmd.sunk | while | flops 3330539520 | bytes 61278944 | solution.py:102
  162.6 43.3 %all-reduce.16.cloned.1.call-done = f32[384,1024]{1,0:T(8,128)} async-done(((f32[384,1024]{1,0:T(8,128)}), f32[384,1024]{1,0:T(8,128)}) %all-reduce.16.cloned.1.call-update) | async-done | bytes 1572880 | tf_op jit(solution)/shard_map/psum | solution.py:117
  216.4 42.4 %all-reduce.18.cloned.1.call-done = f32[384,1024]{1,0:T(8,128)} async-done(((f32[384,1024]{1,0:T(8,128)}), f32[384,1024]{1,0:T(8,128)}) %all-reduce.18.cloned.1.call-update) | async-done | bytes 1572880 | tf_op jit(solution)/shard_map/psum | solution.py:151
  272.2 41.8 %all-reduce.20.cloned.1.call-done = f32[384,1024]{1,0:T(8,128)} async-done(((f32[384,1024]{1,0:T(8,128)}), f32[384,1024]{1,0:T(8,128)}) %all-reduce.20.cloned.1.call-update) | async-done | bytes 1572880 | tf_op jit(solution)/shard_map/psum | solution.py:162
  324.4 43.0 %all-reduce.22.cloned.1.call-done = f32[384,1024]{1,0:T(8,128)} async-done(((f32[384,1024]{1,0:T(8,128)}), f32[384,1024]{1,0:T(8,128)}) %all-reduce.22.cloned.1.call-update) | async-done | bytes 1572880 | tf_op jit(solution)/shard_map/psum | solution.py:151
  387.7 36.4 %all-reduce.24.cloned.1.call-done = f32[384,1024]{1,0:T(8,128)} async-done(((f32[384,1024]{1,0:T(8,128)}), f32[384,1024]{1,0:T(8,128)}) %all-reduce.24.cloned.1.call-update) | async-done | bytes 1572880 | tf_op jit(solution)/shard_map/psum | solution.py:204
  438.1 43.0 %all-reduce.26.cloned.1.call-done = f32[384,1024]{1,0:T(8,128)} async-done(((f32[384,1024]{1,0:T(8,128)}), f32[384,1024]{1,0:T(8,128)}) %all-reduce.26.cloned.1.call-update) | async-done | bytes 1572880 | tf_op jit(solution)/shard_map/psum | solution.py:256
  493.7 22.8 %psum.87 = f32[]{:T(128)} all-reduce(f32[]{:T(128)} %bitcast.84), channel_id=1, replica_groups=mesh['dp'=8,'mp'=4] {'dp'}, use_global_device_ids=true, to_apply=%region_43.44 | all-reduce | flops 1 | bytes 8 | tf_op jit(solution)/shard_map/psum | solution.py:80
  522.8 13.2 all-reduce.28.cloned.1.call-done
  557.4 33.3 %all-reduce.30.cloned.1.call-done = f32[384,1024]{1,0:T(8,128)} async-done(((f32[384,1024]{1,0:T(8,128)}), f32[384,1024]{1,0:T(8,128)}) %all-reduce.30.cloned.1.call-update) | async-done | bytes 1572880 | tf_op jit(solution)/shard_map/psum | solution.py:256
  601.6 7.3 multiply_reduce_fusion.1
  609.0 419.2 %while.37 = (s32[]{:T(128)}, f32[1024,256]{1,0:T(8,128)}, f32[1024,256]{1,0:T(8,128)}, f32[4,64]{1,0:T(4,128)S(1)}, f32[256]{0:T(256)S(1)}, /*index=5*/f32[6,8,1...) while((s32[]{:T(128)}, f32[1024,256]{1,0:T(8,128)}, ...), condition=%wide.wide.region_40.41_spmd.clone, body=%wide.wide.region_37.40_spmd.clone.sunk | while | flops 7783584768 | bytes 232611056 | solution.py:355
  620.2 7.5 fusion.320
  636.5 8.4 convolution_add_fusion.12
  651.0 7.5 fusion.322
  688.2 7.5 fusion.320
  704.6 8.5 convolution_add_fusion.12
  719.0 7.5 fusion.322
  740.9 6.5 convolution_add_fusion.11
  756.6 7.5 fusion.320
  772.9 8.4 convolution_add_fusion.12
  787.4 7.5 fusion.322
  809.2 6.5 convolution_add_fusion.11
  824.9 7.5 fusion.320
  841.2 8.5 convolution_add_fusion.12
  855.7 7.5 fusion.322
  877.6 6.5 convolution_add_fusion.11
  893.3 7.5 fusion.320
  909.6 8.4 convolution_add_fusion.12
  924.1 7.5 fusion.322
  946.0 6.5 convolution_add_fusion.11
  961.7 7.5 fusion.320
  978.0 8.4 convolution_add_fusion.12
  992.4 7.5 fusion.322
  1014.2 6.5 convolution_add_fusion.11
  1034.2 8.3 copy.135
  1101.8 22.1 all-reduce.4
  1125.4 36.9 %all-reduce = f32[1024]{0:T(1024)S(1)} all-reduce(f32[1024]{0:T(1024)S(1)} %broadcast_multiply_fusion.11), channel_id=5, replica_groups=mesh['dp'=8,'mp'=4] {'dp','mp'}, use_global_device_ids=true, to_apply=%region_47.48.clone | all-reduce | flops 1024 | bytes 8192
  1170.8 137.8 %reduce-scatter.32.cloned.1.call-done = f32[48,16,32]{0,1,2:T(8,128)} async-done(((f32[48,16,1024]{0,1,2:T(8,128)}), f32[48,16,32]{0,1,2:T(8,128)}) %reduce-scatter.32.cloned.1.call-update) | async-done | bytes 98320 | tf_op jit(solution)/shard_map/reduce_scatter | solution.py:370
  1310.4 130.9 %reduce-scatter.52.cloned.1.call-done = f32[32,48]{1,0:T(8,128)} async-done(((f32[1024,48]{1,0:T(8,128)}), f32[32,48]{1,0:T(8,128)}) %reduce-scatter.52.cloned.1.call-update) | async-done | bytes 6160
  1441.3 64.1 %reduce-scatter.42.cloned.1.call-done = f32[256,128]{1,0:T(8,128)} async-done(((f32[256,1024]{1,0:T(8,128)}), f32[256,128]{1,0:T(8,128)}) %reduce-scatter.42.cloned.1.call-update) | async-done | bytes 131088 | tf_op jit(solution)/shard_map/reduce_scatter | solution.py:409
  1505.4 66.2 %reduce-scatter.38.cloned.1.call-done = f32[128,256]{1,0:T(8,128)} async-done(((f32[1024,256]{1,0:T(8,128)}), f32[128,256]{1,0:T(8,128)}) %reduce-scatter.38.cloned.1.call-update) | async-done | bytes 131088 | tf_op jit(solution)/shard_map/reduce_scatter | solution.py:406
  1571.6 66.8 %reduce-scatter.40.cloned.1.call-done = f32[128,256]{1,0:T(8,128)} async-done(((f32[1024,256]{1,0:T(8,128)}), f32[128,256]{1,0:T(8,128)}) %reduce-scatter.40.cloned.1.call-update) | async-done | bytes 131088 | tf_op jit(solution)/shard_map/reduce_scatter | solution.py:407
  1638.4 68.6 %reduce-scatter.34.cloned.1.call-done = f32[384,128]{1,0:T(8,128)} async-done(((f32[384,1024]{1,0:T(8,128)}), f32[384,128]{1,0:T(8,128)}) %reduce-scatter.34.cloned.1.call-update) | async-done | bytes 196624 | tf_op jit(solution)/shard_map/reduce_scatter | solution.py:404
  1707.0 71.6 %reduce-scatter.46.cloned.1.call-done = f32[2,256,128]{2,1,0:T(8,128)} async-done(((f32[2,256,1024]{2,1,0:T(8,128)}), f32[2,256,128]{2,1,0:T(8,128)}) %reduce-scatter.46.cloned.1.call-update) | async-done | bytes 262160 | tf_op jit(solution)/shard_map/reduce_scatter | solution.py:398
  1778.6 121.9 %reduce-scatter.44.cloned.1.call-done = f32[2,3,128,256]{3,2,1,0:T(8,128)} async-done(((f32[2,3,1024,256]{3,2,1,0:T(8,128)}), f32[2,3,128,256]{3,2,1,0:T(8,128)}) %reduce-scatter.44.cloned.1.call-update) | async-done | bytes 786448 | tf_op jit(solution)/shard_map/reduce_scatter | solution.py:396
  1900.5 153.2 %reduce-scatter.50.cloned.1.call-done = f32[2,1024,128]{2,1,0:T(8,128)} async-done(((f32[2,1024,1024]{2,1,0:T(8,128)}), f32[2,1024,128]{2,1,0:T(8,128)}) %reduce-scatter.50.cloned.1.call-update) | async-done | bytes 1048592 | tf_op jit(solution)/shard_map/reduce_scatter | solution.py:402
  2053.7 152.1 %reduce-scatter.48.cloned.1.call-done = f32[2,128,1024]{2,1,0:T(8,128)} async-done(((f32[2,1024,1024]{2,1,0:T(8,128)}), f32[2,128,1024]{2,1,0:T(8,128)}) %reduce-scatter.48.cloned.1.call-update) | async-done | bytes 1048592 | tf_op jit(solution)/shard_map/reduce_scatter | solution.py:400
  (878 shorter events, 574.8 us)
Async XLA Ops:
  7.2 151.4 %copy-start = (bf16[256,1024]{1,0:T(8,128)(2,1)S(1)}, bf16[256,1024]{1,0:T(8,128)(2,1)}, u32[]{:S(2)}) copy-start(bf16[256,1024]{1,0:T(8,128)(2,1)} %param.47) | copy-start | bytes 1572868
  7.2 198.7 %all-reduce.16.cloned.1.call-start = ((), (), s32[]{:S(2)}) async-start(), calls=%async_computation.17 | async-start | bytes 3145728 | tf_op jit(solution)/shard_map/psum | solution.py:117
  8.7 137.4 %copy-start.123 = (f32[1024]{0:T(1024)S(1)}, f32[1024]{0:T(1024)}, u32[]{:S(2)}) copy-start(f32[1024]{0:T(1024)} %param.42) | copy-start | bytes 12292
  8.7 140.0 %copy-start.122 = (s32[6,48]{1,0:T(8,128)S(1)}, s32[6,48]{1,0:T(8,128)}, u32[]{:S(2)}) copy-start(s32[6,48]{1,0:T(8,128)} %param.35) | copy-start | bytes 3460
  158.6 47.3 %copy-start.68 = (f32[384,1024]{1,0:T(8,128)S(1)}, f32[384,1024]{1,0:T(8,128)}, u32[]{:S(2)}) copy-start(f32[384,1024]{1,0:T(8,128)} %param.41) | copy-start | bytes 4718596
  158.6 47.3 %copy-start.120 = (f32[1024]{0:T(1024)S(1)}, f32[1024]{0:T(1024)}, u32[]{:S(2)}) copy-start(f32[1024]{0:T(1024)} %param.50) | copy-start | bytes 12292
  158.6 47.3 %copy-start.121 = (f32[1024]{0:T(1024)S(1)}, f32[1024]{0:T(1024)}, u32[]{:S(2)}) copy-start(f32[1024]{0:T(1024)} %param.48) | copy-start | bytes 12292
  160.2 98.5 %all-reduce.18.cloned.1.call-start = ((), (), s32[]{:S(2)}) async-start(), calls=%async_computation.18 | async-start | bytes 3145728 | tf_op jit(solution)/shard_map/psum | solution.py:151
  162.0 265.4 %copy-start.91 = (f32[1,1,1024]{2,1,0:T(1,128)}, f32[1,1,1024]{2,1,0:T(1,128)S(1)}, u32[]{:S(2)}) copy-start(f32[1,1,1024]{2,1,0:T(1,128)S(1)} %get-tuple-element.543) | copy-start | bytes 12292
  162.0 376.7 %copy-start.89 = (f32[1,1,1024]{2,1,0:T(1,128)}, f32[1,1,1024]{2,1,0:T(1,128)S(1)}, u32[]{:S(2)}) copy-start(f32[1,1,1024]{2,1,0:T(1,128)S(1)} %get-tuple-element.544) | copy-start | bytes 12292
  162.6 98.8 %copy-start.128 = (f32[1,1,1024]{2,1,0:T(1,128)}, f32[1,1,1024]{2,1,0:T(1,128)S(1)}, u32[]{:S(2)}) copy-start(f32[1,1,1024]{2,1,0:T(1,128)S(1)} %get-tuple-element.548) | copy-start | bytes 12292
  215.7 98.3 %all-reduce.20.cloned.1.call-start = ((), (), s32[]{:S(2)}) async-start(), calls=%async_computation.19 | async-start | bytes 3145728 | tf_op jit(solution)/shard_map/psum | solution.py:162
  261.0 277.7 %copy-start.93 = (f32[384]{0:T(512)}, f32[384]{0:T(512)S(1)}, u32[]{:S(2)}) copy-start(f32[384]{0:T(512)S(1)} %broadcast_multiply_fusion.15) | copy-start | bytes 4612
  270.9 96.6 %all-reduce.22.cloned.1.call-start = ((), (), s32[]{:S(2)}) async-start(), calls=%async_computation.20 | async-start | bytes 3145728 | tf_op jit(solution)/shard_map/psum | solution.py:151
  324.4 99.8 %all-reduce.24.cloned.1.call-start = ((), (), s32[]{:S(2)}) async-start(), calls=%async_computation.21 | async-start | bytes 3145728 | tf_op jit(solution)/shard_map/psum | solution.py:204
  369.8 57.7 %copy-start.95 = (f32[384]{0:T(512)}, f32[384]{0:T(512)S(1)}, u32[]{:S(2)}) copy-start(f32[384]{0:T(512)S(1)} %broadcast_multiply_fusion.13) | copy-start | bytes 4612
  381.1 100.0 %all-reduce.26.cloned.1.call-start = ((), (), s32[]{:S(2)}) async-start(), calls=%async_computation.22 | async-start | bytes 3145728 | tf_op jit(solution)/shard_map/psum | solution.py:256
  387.7 39.7 %copy-start.107 = (f32[384]{0:T(512)S(1)}, f32[384]{0:T(512)}, u32[]{:S(2)}) copy-start(f32[384]{0:T(512)} %copy-done.106) | copy-start | bytes 4612
  438.0 98.0 %all-reduce.28.cloned.1.call-start = ((), (), s32[]{:S(2)}) async-start(), calls=%async_computation.23 | async-start | bytes 3145728 | tf_op jit(solution)/shard_map/psum | solution.py:204
  492.9 23.5 %copy-start.134 = (bf16[256]{0:T(256)(128)(2,1)S(1)}, bf16[256]{0:T(256)(128)(2,1)}, u32[]{:S(2)}) copy-start(bf16[256]{0:T(256)(128)(2,1)} %copy-done.133) | copy-start | bytes 1540
  492.9 23.6 %copy-start.142 = (s32[6]{0:T(128)S(1)}, s32[6]{0:T(128)}, u32[]{:S(2)}) copy-start(s32[6]{0:T(128)} %param.38) | copy-start | bytes 76
  493.0 97.8 %all-reduce.30.cloned.1.call-start = ((), (), s32[]{:S(2)}) async-start(), calls=%async_computation.24 | async-start | bytes 3145728 | tf_op jit(solution)/shard_map/psum | solution.py:256
  519.3 16.7 copy-start.104
  547.7 548.1 %reduce-scatter.62.cloned.1.call-start = ((), (), s32[]{:S(2)}) async-start(), calls=%async_computation.40 | async-start | bytes 589824
  553.8 36.9 %copy-start.7 = (f32[384,1024]{1,0:T(8,128)S(1)}, f32[384,1024]{1,0:T(8,128)}, u32[]{:S(2)}) copy-start(f32[384,1024]{1,0:T(8,128)} %copy-done.6) | copy-start | bytes 4718596
  553.8 543.5 %reduce-scatter.64.cloned.1.call-start = ((), (), s32[]{:S(2)}) async-start(), calls=%async_computation.41 | async-start | bytes 589824
  555.0 543.8 %reduce-scatter.58.cloned.1.call-start = ((), (), s32[]{:S(2)}) async-start(), calls=%async_computation.38 | async-start | bytes 147456
  556.3 544.0 %reduce-scatter.60.cloned.1.call-start = ((), (), s32[]{:S(2)}) async-start(), calls=%async_computation.39 | async-start | bytes 589824
  557.4 35.5 %copy-start.100 = (f32[384]{0:T(512)S(1)}, f32[384]{0:T(512)}, u32[]{:S(2)}) copy-start(f32[384]{0:T(512)} %copy-done.99) | copy-start | bytes 4612
  557.4 605.5 %reduce-scatter.56.cloned.1.call-start = ((), (), s32[]{:S(2)}) async-start(), calls=%async_computation.37 | async-start | bytes 589824
  598.9 565.7 %reduce-scatter.54.cloned.1.call-start = ((), (), s32[]{:S(2)}) async-start(), calls=%async_computation.36 | async-start | bytes 589824
  601.0 565.2 %all-reduce.32.cloned.1.call-start = ((), (), s32[]{:S(2)}) async-start(), calls=%async_computation.42 | async-start | bytes 5505024 | tf_op jit(solution)/shard_map/psum | solution.py:162
  1028.2 140.9 %reduce-scatter.36.cloned.1.call-start = ((), (), s32[]{:S(2)}) async-start(), calls=%async_computation.27 | async-start | bytes 1179648 | tf_op jit(solution)/shard_map/reduce_scatter | solution.py:405
  1030.0 278.6 %reduce-scatter.32.cloned.1.call-start = ((), (), s32[]{:S(2)}) async-start(), calls=%async_computation.25 | async-start | bytes 8650752 | tf_op jit(solution)/shard_map/reduce_scatter | solution.py:370
  1042.5 398.8 %reduce-scatter.52.cloned.1.call-start = ((), (), s32[]{:S(2)}) async-start(), calls=%async_computation.35 | async-start | bytes 540672
  1044.4 461.0 %reduce-scatter.42.cloned.1.call-start = ((), (), s32[]{:S(2)}) async-start(), calls=%async_computation.30 | async-start | bytes 1179648 | tf_op jit(solution)/shard_map/reduce_scatter | solution.py:409
  1045.9 525.6 %reduce-scatter.38.cloned.1.call-start = ((), (), s32[]{:S(2)}) async-start(), calls=%async_computation.28 | async-start | bytes 1179648 | tf_op jit(solution)/shard_map/reduce_scatter | solution.py:406
  1047.1 591.3 %reduce-scatter.40.cloned.1.call-start = ((), (), s32[]{:S(2)}) async-start(), calls=%async_computation.29 | async-start | bytes 1179648 | tf_op jit(solution)/shard_map/reduce_scatter | solution.py:407
  1049.4 657.7 %reduce-scatter.34.cloned.1.call-start = ((), (), s32[]{:S(2)}) async-start(), calls=%async_computation.26 | async-start | bytes 1769472 | tf_op jit(solution)/shard_map/reduce_scatter | solution.py:404
  1050.8 727.8 %reduce-scatter.46.cloned.1.call-start = ((), (), s32[]{:S(2)}) async-start(), calls=%async_computation.32 | async-start | bytes 2359296 | tf_op jit(solution)/shard_map/reduce_scatter | solution.py:398
  1055.5 845.0 %reduce-scatter.44.cloned.1.call-start = ((), (), s32[]{:S(2)}) async-start(), calls=%async_computation.31 | async-start | bytes 7077888 | tf_op jit(solution)/shard_map/reduce_scatter | solution.py:396
  1075.8 977.9 %reduce-scatter.50.cloned.1.call-start = ((), (), s32[]{:S(2)}) async-start(), calls=%async_computation.34 | async-start | bytes 9437184 | tf_op jit(solution)/shard_map/reduce_scatter | solution.py:402
  1084.5 1121.3 %reduce-scatter.48.cloned.1.call-start = ((), (), s32[]{:S(2)}) async-start(), calls=%async_computation.33 | async-start | bytes 9437184 | tf_op jit(solution)/shard_map/reduce_scatter | solution.py:400
  1093.3 31.9 %copy-start.53 = (bf16[1024,256]{1,0:T(8,128)(2,1)S(1)}, bf16[1024,256]{1,0:T(8,128)(2,1)}, u32[]{:S(2)}) copy-start(bf16[1024,256]{1,0:T(8,128)(2,1)} %param.43) | copy-start | bytes 1572868
  1093.3 72.9 %copy-start.115 = (f32[1,1024]{1,0:T(1,128)S(1)}, f32[1,1024]{1,0:T(1,128)}, u32[]{:S(2)}) copy-start(f32[1,1024]{1,0:T(1,128)} %get-tuple-element.551) | copy-start | bytes 12292
  1124.0 1081.8 %copy-start.146 = (f32[128]{0:T(128)}, f32[128]{0:T(128)S(1)}, u32[]{:S(2)}) copy-start(f32[128]{0:T(128)S(1)} %dynamic-slice.4) | copy-start | bytes 1540
  1166.2 1040.2 %copy-start.69 = (f32[1,48,16,384]{3,2,1,0:T(8,128)S(1)}, f32[1,48,16,384]{3,2,1,0:T(8,128)}, u32[]{:S(2)}) copy-start(f32[1,48,16,384]{3,2,1,0:T(8,128)} %get-tuple-element.1023) | copy-start | bytes 3538948
  1166.2 1041.2 %copy-start.1 = (bf16[256,1024]{1,0:T(8,128)(2,1)S(1)}, bf16[256,1024]{1,0:T(8,128)(2,1)}, u32[]{:S(2)}) copy-start(bf16[256,1024]{1,0:T(8,128)(2,1)} %param.47) | copy-start | bytes 1572868
  (183 other events, 569.0 us)
Sparse Core Ops, SparseCore 0:
  160.3 45.5 all-reduce.15
  215.8 42.8 all-reduce.17
  271.0 42.9 all-reduce.19
  324.5 42.8 all-reduce.21
  381.2 42.8 all-reduce.23
  438.1 42.8 all-reduce.25
  493.1 42.9 all-reduce.27
  547.8 42.8 all-reduce.29
  594.1 61.9 reduce-scatter.61
  659.7 60.9 reduce-scatter.63
  724.5 59.7 reduce-scatter.57
  787.6 60.9 reduce-scatter.59
  852.3 60.8 reduce-scatter.55
  916.4 60.8 reduce-scatter.53
  1028.3 62.3 all-reduce.31
  1094.4 64.0 reduce-scatter.35
  1160.6 148.0 reduce-scatter.31
  1311.3 129.8 reduce-scatter.51
  1445.6 59.7 reduce-scatter.41
  1509.2 62.3 reduce-scatter.37
  1576.0 62.3 reduce-scatter.39
  1642.4 64.5 reduce-scatter.33
  1711.6 66.9 reduce-scatter.45
  1783.1 117.3 reduce-scatter.43
  1905.2 148.5 reduce-scatter.49
  2057.8 148.0 reduce-scatter.47
where the time goes:
time: 2230 us; the launch traced here: 2210 us
  waiting for transfers between devices  1330 us (60%)
  matrix products  425 us (19%)
  local copies, waits for them, and re-layouts  220 us (10%)
  other arithmetic  115 us (5%)
  blocking collectives  81.7 us (4%)
    dot_general x69, matrix products, matmul(): return jnp.dot(left, right, preferred_element_type=jnp.float32)  263 us
    reduce_scatter x1, waiting for transfers between devices, per_device(): lax.psum_scatter(down_all, 'dp', scatter_dimension=2, tiled=True)  153 us
    reduce_scatter x1, waiting for transfers between devices, per_device(): lax.psum_scatter(up_all, 'dp', scatter_dimension=1, tiled=True)  152 us
    reduce_scatter x1, waiting for transfers between devices, per_device(): lax.psum_scatter(patch_all * item_scale, ('dp', 'mp'), scatter_dimension=...  138 us
    unnamed x33, waiting for transfers between devices  131 us
    reduce_scatter x1, waiting for transfers between devices, per_device(): lax.psum_scatter(attention_all, 'dp', scatter_dimension=2, tiled=True)  122 us
    psum x2, waiting for transfers between devices, per_device(): lax.psum(matmul(mixed_heads, output_weight[layer_num]), 'mp')  85.4 us
    psum x2, waiting for transfers between devices, per_device(): normed_grad_one = lax.psum(matmul(grad_inputs, stacked_weight), 'mp')  76.3 us
  transfers between devices with their start and end apart: 26, of which 18 were waited for; matrix products, arithmetic and copies ran while one was open for 23% of the time, Pallas kernels for 0%

commit v1 on v0

v1 whole, which is shorter than its diff:
```python
import math

import jax
import jax.numpy as jnp
from jax import lax
from jax.sharding import PartitionSpec as P

HEAD_DIM = 64
ROOT_DIM = math.sqrt(HEAD_DIM)
BF = jnp.bfloat16
F32 = jnp.float32


def matmul(left, right):
    return jnp.dot(left, right, preferred_element_type=F32)


def matmul_tn(left, right):
    return lax.dot_general(left, right, (((0,), (0,)), ((), ())), preferred_element_type=F32)


def matmul_nt(left, right):
    return lax.dot_general(left, right, (((1,), (1,)), ((), ())), preferred_element_type=F32)


def two_part(tensor):
    high = tensor.astype(BF)
    return high, (tensor - high.astype(F32)).astype(BF)


def gelu_exact(pre_act):
    return jax.nn.gelu(pre_act, approximate=False)


def bit_count(size):
    bits = size.bit_length() - 1
    assert 1 << bits == size
    return bits


def exchange(tensor, axis, size, bit):
    return lax.ppermute(tensor, axis, [(i, i ^ (1 << bit)) for i in range(size)])


def pick(tensor, index, axis):
    return lax.dynamic_index_in_dim(tensor, index, axis, keepdims=False)


class Links:
    def __init__(self, dp, mp):
        self.dp, self.mp = dp, mp
        self.dp_index = lax.axis_index("dp")
        self.mp_index = lax.axis_index("mp")

    def dp_bit(self, bit):
        return (self.dp_index >> bit) & 1

    def mp_bit(self, bit):
        return (self.mp_index >> bit) & 1

    def sum_rows(self, partial):
        half = partial.shape[0] // 2
        total = partial[:half] + exchange(partial[half:], "mp", self.mp, 0)
        for bit in range(1, bit_count(self.mp)):
            total = total + exchange(total, "mp", self.mp, bit)
        return total

    def other_rows(self, own):
        return exchange(own, "mp", self.mp, 0)

    def both_rows(self, own):
        return jnp.concatenate([own, self.other_rows(own)], axis=0)

    def split_rows(self, tensor):
        half = tensor.shape[0] // 2
        core = self.mp_bit(0)
        own = lax.dynamic_slice_in_dim(tensor, core * half, half, 0)
        other = lax.dynamic_slice_in_dim(tensor, (1 - core) * half, half, 0)
        return own, other

    def global_rows(self, own, other):
        core = self.mp_bit(0)
        return jnp.concatenate(
            [jnp.where(core == 0, own, other), jnp.where(core == 0, other, own)], axis=0
        )

    def finish_scatter(self, shards, first_bit):
        for bit in range(first_bit, bit_count(self.dp)):
            count = shards.shape[0] // 2
            pairs = shards.reshape((count, 2) + shards.shape[1:])
            own = self.dp_bit(bit)
            got = exchange(pick(pairs, 1 - own, 1), "dp", self.dp, bit)
            shards = pick(pairs, own, 1) + got
        return shards[0]

    def scatter_sum(self, shards):
        return self.finish_scatter(shards, 0)

    def scatter_product(self, left, right, scale):
        width = left.shape[1]
        parts = left.reshape(left.shape[0], self.dp // 2, 2, width // self.dp)
        own = self.dp_bit(0)
        keep_left = jnp.where(own == 0, parts[:, :, 0], parts[:, :, 1])
        send_left = jnp.where(own == 0, parts[:, :, 1], parts[:, :, 0])
        flat = (left.shape[0], width // 2)
        send = matmul_tn(send_left.reshape(flat), right) * scale
        got = exchange(send, "dp", self.dp, 0)
        total = matmul_tn(keep_left.reshape(flat), right) * scale + got
        return self.finish_scatter(
            total.reshape(self.dp // 2, width // self.dp, right.shape[1]), 1
        )


def norm_parts(rows):
    row_mean = jnp.mean(rows, axis=-1, keepdims=True)
    centred = rows - row_mean
    spread = jnp.mean(centred * centred, axis=-1, keepdims=True)
    inverse = lax.rsqrt(spread + 1e-05)
    return centred * inverse, inverse


def norm_back(grad, gain, unit, inverse):
    scaled = grad * gain
    first = jnp.mean(scaled, axis=-1, keepdims=True)
    second = jnp.mean(scaled * unit, axis=-1, keepdims=True)
    return inverse * (scaled - first - unit * second)


def make_per_device(dp, mp):
    def per_device(
        pixels,
        dataset_id,
        variable_mask,
        lead_hours,
        token_counts,
        dataset_weight,
        patch_weight,
        variable_embed,
        position_embed,
        pool_query,
        pool_query_weight,
        pool_key_weight,
        pool_value_weight,
        pool_value_bias,
        pool_output_weight,
        pool_output_bias,
        lead_weight,
        lead_bias,
        norm_gain,
        norm_bias,
        attention_weight,
        attention_bias,
        output_weight,
        output_bias,
        up_weight,
        up_bias,
        down_weight,
        down_bias,
        cotangent,
    ):
        links = Links(dp, mp)
        var_count, pix_count, row_count = pixels.shape[1:]
        flat_count = var_count * pix_count
        model_width = patch_weight.shape[2]
        local_width = pool_query_weight.shape[1]
        head_count = local_width // HEAD_DIM
        layer_count = attention_weight.shape[0]
        shard = model_width // dp

        def heads_first(tensor):
            return tensor.reshape(row_count, head_count, HEAD_DIM).transpose(1, 0, 2)

        def heads_last(tensor):
            return tensor.transpose(1, 0, 2).reshape(row_count, local_width)

        dataset_pick = jnp.arange(variable_mask.shape[0], dtype=jnp.int32) == dataset_id[0]
        mask_row = jnp.sum(jnp.where(dataset_pick[:, None], variable_mask, 0), axis=0)
        item_weight = jnp.sum(jnp.where(dataset_pick, dataset_weight, 0)).astype(F32)
        own_count = token_counts[0].astype(F32)
        count_total = jnp.full((8, 128), own_count, F32)
        for bit in range(bit_count(dp)):
            count_total = count_total + exchange(count_total, "dp", dp, bit)
        item_scale = item_weight * own_count / count_total[0, 0]
        lead_scale = lead_hours[0].astype(F32) / 24.0

        pix_rows = pixels[0].reshape(flat_count, row_count).T
        pix_own, pix_other = links.split_rows(pix_rows)
        pix_low = jnp.concatenate([pix_own, pix_other], axis=0).astype(BF)
        pix_value = pix_low.astype(F32)
        embed_high, embed_rest = two_part(variable_embed)
        embed_all = jnp.concatenate(
            [patch_weight.reshape(flat_count, model_width), embed_high, embed_rest], axis=0
        )
        query_low = pool_query.astype(BF)
        query_vec = matmul(query_low[None, :], pool_query_weight)[0].astype(BF)
        head_of = jnp.arange(local_width, dtype=jnp.int32) // HEAD_DIM
        head_pick = head_of[:, None] == jnp.arange(head_count, dtype=jnp.int32)[None, :]
        query_heads = jnp.where(head_pick, query_vec[:, None], 0).astype(BF)
        key_query = matmul(pool_key_weight, query_heads) / ROOT_DIM
        key_high, key_rest = two_part(key_query)
        projected = matmul(
            embed_all, jnp.concatenate([pool_value_weight, key_high, key_rest], axis=1)
        )
        tail = projected[flat_count : flat_count + var_count] + projected[flat_count + var_count :]
        score_flat = (
            projected[:flat_count, local_width : local_width + head_count]
            + projected[:flat_count, local_width + head_count :]
        )
        score_var = tail[:, local_width : local_width + head_count] + tail[:, local_width + head_count :]
        value_flat = projected[:flat_count, :local_width].astype(BF)
        value_var = (tail[:, :local_width] + pool_value_bias).astype(BF)
        value_flat = value_flat.reshape(flat_count, head_count, HEAD_DIM).transpose(1, 0, 2)
        value_var = value_var.reshape(var_count, head_count, HEAD_DIM).transpose(1, 0, 2)

        var_of = jnp.arange(flat_count, dtype=jnp.int32) // pix_count
        segment = (
            var_of[None, :] == jnp.arange(var_count, dtype=jnp.int32)[:, None]
        )
        segment_low = segment.astype(BF)
        score_block = jnp.where(segment.T[None], score_flat.T[:, :, None], 0.0)
        block_high, block_rest = two_part(score_block)
        block_both = jnp.concatenate([block_high, block_rest], axis=2)
        pool_scores = jnp.einsum(
            "rk,hkv->hrv", pix_low, block_both, preferred_element_type=F32
        )
        pool_scores = (
            pool_scores[:, :, :var_count] + pool_scores[:, :, var_count:] + score_var.T[:, None, :]
        )
        pool_scores = jnp.where(mask_row[None, None, :] > 0, pool_scores, -1000000000.0)
        pool_top = jnp.max(pool_scores, axis=-1, keepdims=True)
        pool_exp = jnp.exp(pool_scores - pool_top)
        pool_probs = pool_exp / jnp.sum(pool_exp, axis=-1, keepdims=True)
        probs_low = pool_probs.astype(BF)
        probs_wide = jnp.einsum("hrv,vk->hrk", probs_low, segment_low, preferred_element_type=F32)
        mixed_pixels = (probs_wide * pix_value[None]).astype(BF)
        pooled = jnp.einsum(
            "hrk,hkd->hrd", mixed_pixels, value_flat, preferred_element_type=F32
        ) + jnp.einsum("hrv,hvd->hrd", probs_low, value_var, preferred_element_type=F32)
        pooled = heads_last(pooled).astype(BF)

        hidden = links.sum_rows(matmul(pooled, pool_output_weight)) + pool_output_bias
        position_own = links.split_rows(position_embed)[0]
        hidden = hidden + position_own + lead_scale * lead_weight + lead_bias

        kept = []
        for layer in range(layer_count):
            unit_one, inverse_one = norm_parts(hidden)
            normed = links.both_rows(unit_one) * norm_gain[layer, 0] + norm_bias[layer, 0]
            normed = normed.astype(BF)
            queries = (
                matmul(normed, attention_weight[layer, 0]) + attention_bias[layer, 0]
            ).astype(BF)
            keys_new = matmul(normed, attention_weight[layer, 1]).astype(BF)
            values_new = (
                matmul(normed, attention_weight[layer, 2]) + attention_bias[layer, 1]
            ).astype(BF)
            query_three = heads_first(queries)
            key_three = heads_first(keys_new)
            value_three = heads_first(values_new)
            scores = (
                jnp.einsum("hpd,hkd->hpk", query_three, key_three, preferred_element_type=F32)
                / ROOT_DIM
            )
            row_max = jnp.max(scores, axis=-1, keepdims=True)
            exponent = jnp.exp(scores - row_max)
            attend = exponent / jnp.sum(exponent, axis=-1, keepdims=True)
            attend_low = attend.astype(BF)
            mixed = heads_last(
                jnp.einsum("hpk,hkd->hpd", attend_low, value_three, preferred_element_type=F32)
            ).astype(BF)
            hidden = (
                hidden
                + links.sum_rows(matmul(mixed, output_weight[layer]))
                + output_bias[layer]
            )
            unit_two, inverse_two = norm_parts(hidden)
            normed_two = links.both_rows(unit_two) * norm_gain[layer, 1] + norm_bias[layer, 1]
            normed_two = normed_two.astype(BF)
            pre_act = matmul(normed_two, up_weight[layer]) + up_bias[layer]
            activation = gelu_exact(pre_act).astype(BF)
            hidden = (
                hidden
                + links.sum_rows(matmul(activation, down_weight[layer]))
                + down_bias[layer]
            )
            kept.append(
                (
                    unit_one,
                    inverse_one,
                    normed,
                    query_three,
                    key_three,
                    value_three,
                    attend,
                    attend_low,
                    mixed,
                    unit_two,
                    inverse_two,
                    normed_two,
                    pre_act,
                    activation,
                )
            )
        layer_out = links.global_rows(hidden, links.other_rows(hidden))

        grad_own, grad_other = links.split_rows(cotangent[0])
        row_sums = {}
        local_sums = {}
        weight_grads = [None] * layer_count
        for layer in reversed(range(layer_count)):
            (
                unit_one,
                inverse_one,
                normed,
                query_three,
                key_three,
                value_three,
                attend,
                attend_low,
                mixed,
                unit_two,
                inverse_two,
                normed_two,
                pre_act,
                activation,
            ) = kept[layer]
            down_low = jnp.concatenate([grad_own, grad_other], axis=0).astype(BF)
            row_sums["down_bias", layer] = jnp.sum(grad_own, axis=0)
            grad_activation = matmul_nt(down_low, down_weight[layer])
            grad_pre = jax.vjp(gelu_exact, pre_act)[1](grad_activation)[0]
            local_sums["up_bias", layer] = jnp.sum(grad_pre, axis=0)
            pre_low = grad_pre.astype(BF)
            grad_two = links.sum_rows(matmul_nt(pre_low, up_weight[layer]))
            down_grad = links.scatter_product(down_low, activation, item_scale)
            up_grad = links.scatter_product(normed_two, pre_low, item_scale)
            row_sums["gain", layer, 1] = jnp.sum(grad_two * unit_two, axis=0)
            row_sums["bias", layer, 1] = jnp.sum(grad_two, axis=0)
            change = norm_back(grad_two, norm_gain[layer, 1], unit_two, inverse_two)
            grad_own = grad_own + change
            grad_other = grad_other + links.other_rows(change)
            out_low = jnp.concatenate([grad_own, grad_other], axis=0).astype(BF)
            row_sums["out_bias", layer] = jnp.sum(grad_own, axis=0)
            grad_mixed = heads_first(matmul_nt(out_low, output_weight[layer]).astype(BF))
            grad_attend = jnp.einsum(
                "hpd,hkd->hpk", grad_mixed, value_three, preferred_element_type=F32
            )
            grad_values = heads_last(
                jnp.einsum("hpk,hpd->hkd", attend_low, grad_mixed, preferred_element_type=F32)
            )
            grad_scores = attend * (
                grad_attend - jnp.sum(attend * grad_attend, axis=-1, keepdims=True)
            )
            score_low = grad_scores.astype(BF)
            grad_queries = heads_last(
                jnp.einsum("hpk,hkd->hpd", score_low, key_three, preferred_element_type=F32)
                / ROOT_DIM
            )
            grad_keys = heads_last(
                jnp.einsum("hpk,hpd->hkd", score_low, query_three, preferred_element_type=F32)
                / ROOT_DIM
            )
            local_sums["qv", layer, 0] = jnp.sum(grad_queries, axis=0)
            local_sums["qv", layer, 1] = jnp.sum(grad_values, axis=0)
            grad_three = [part.astype(BF) for part in (grad_queries, grad_keys, grad_values)]
            partial = matmul_nt(grad_three[0], attention_weight[layer, 0])
            partial = partial + matmul_nt(grad_three[1], attention_weight[layer, 1])
            partial = partial + matmul_nt(grad_three[2], attention_weight[layer, 2])
            grad_one = links.sum_rows(partial)
            out_grad = links.scatter_product(out_low, mixed, item_scale)
            qkv_grad = links.scatter_product(
                normed, jnp.concatenate(grad_three, axis=1), item_scale
            )
            row_sums["gain", layer, 0] = jnp.sum(grad_one * unit_one, axis=0)
            row_sums["bias", layer, 0] = jnp.sum(grad_one, axis=0)
            change = norm_back(grad_one, norm_gain[layer, 0], unit_one, inverse_one)
            grad_own = grad_own + change
            grad_other = grad_other + links.other_rows(change)
            weight_grads[layer] = (down_grad, up_grad, out_grad, qkv_grad)

        column_sum = jnp.sum(grad_own, axis=0)
        row_sums["column"] = column_sum
        row_sums["lead"] = lead_scale * column_sum
        pool_grad_low = jnp.concatenate([grad_own, grad_other], axis=0).astype(BF)
        grad_pooled = heads_first(matmul_nt(pool_grad_low, pool_output_weight).astype(BF))
        pull_flat = jnp.einsum("hrd,hkd->hrk", grad_pooled, value_flat, preferred_element_type=F32)
        pull_high, pull_rest = two_part(pull_flat * pix_value[None])
        grad_probs = (
            jnp.einsum("hrk,vk->hrv", pull_high, segment_low, preferred_element_type=F32)
            + jnp.einsum("hrk,vk->hrv", pull_rest, segment_low, preferred_element_type=F32)
            + jnp.einsum("hrd,hvd->hrv", grad_pooled, value_var, preferred_element_type=F32)
        )
        grad_pool_scores = pool_probs * (
            grad_probs - jnp.sum(pool_probs * grad_probs, axis=-1, keepdims=True)
        )
        score_high, score_rest = two_part(grad_pool_scores)
        pixel_part = jnp.einsum(
            "hrv,hkv->rk", score_high, block_high, preferred_element_type=F32
        ) + jnp.sum(probs_wide * pull_flat, axis=0)

        turned = jnp.einsum(
            "rk,hrv->hkv", pix_low, score_high, preferred_element_type=F32
        ) + jnp.einsum("rk,hrv->hkv", pix_low, score_rest, preferred_element_type=F32)
        key_flat = jnp.sum(jnp.where(segment.T[None], turned, 0.0), axis=2).T * item_scale
        key_var = jnp.sum(grad_pool_scores, axis=1).T * item_scale
        value_grad_flat = jnp.einsum(
            "hrk,hrd->khd", mixed_pixels, grad_pooled, preferred_element_type=F32
        ).reshape(flat_count, local_width)
        value_grad_var = jnp.einsum(
            "hrv,hrd->vhd", probs_low, grad_pooled, preferred_element_type=F32
        ).reshape(var_count, local_width)
        local_sums["pool_bias"] = jnp.sum(value_grad_var, axis=0)
        value_grad_flat = (value_grad_flat * item_scale).astype(BF)
        value_grad_var = (value_grad_var * item_scale).astype(BF)

        key_grad = jnp.concatenate([key_flat, key_var, key_var], axis=0)
        key_grad_high, key_grad_rest = two_part(key_grad)
        summed_key = matmul_tn(
            embed_all, jnp.concatenate([key_grad_high, key_grad_rest], axis=1)
        )
        summed_key = summed_key[:, :head_count] + summed_key[:, head_count:]
        summed_high, summed_rest = two_part(summed_key)
        query_grad = matmul_tn(
            jnp.concatenate([summed_high, summed_rest], axis=1), pool_key_weight
        )
        query_grad = query_grad[:head_count] + query_grad[head_count:]
        query_grad = jnp.sum(jnp.where(head_pick.T, query_grad, 0.0), axis=0) / ROOT_DIM
        query_part = jnp.sum(pool_query_weight.astype(F32) * query_grad[None, :], axis=1)

        flat_all = flat_count + var_count
        grad_rows = jnp.concatenate([value_grad_flat, value_grad_var], axis=0)
        key_rows_high, key_rows_rest = two_part(jnp.concatenate([key_flat, key_var], axis=0))
        right_side = jnp.concatenate([grad_rows, key_rows_high, key_rows_rest, key_rows_high], axis=1)
        left_side = jnp.concatenate([pool_value_weight, key_high, key_high, key_rest], axis=1)
        sub = shard // mp
        sides = left_side.reshape(dp, mp // 2, 2, sub, left_side.shape[1])
        parts = query_part.reshape(dp, mp // 2, 2, sub)
        core = links.mp_bit(0)

        def embed_side(which):
            side = pick(sides, which, 2).transpose(1, 0, 2, 3)
            part = pick(parts, which, 2).transpose(1, 0, 2)
            block = matmul_nt(side.reshape(model_width // 2, left_side.shape[1]), right_side)
            block = jnp.concatenate([block, part.reshape(model_width // 2, 1)], axis=1)
            return block.reshape(mp // 2, dp, sub, flat_all + 1)

        embed_grad = embed_side(core) + exchange(embed_side(1 - core), "mp", mp, 0)
        for bit in range(1, bit_count(mp)):
            own = links.mp_bit(bit)
            count = embed_grad.shape[0] // 2
            pairs = embed_grad.reshape((count, 2) + embed_grad.shape[1:])
            embed_grad = pick(pairs, own, 1) + exchange(pick(pairs, 1 - own, 1), "mp", mp, bit)
        embed_grad = links.scatter_sum(embed_grad[0])

        pool_out_grad = links.scatter_product(pool_grad_low, pooled, item_scale)
        value_weight_grad = links.scatter_product(
            embed_all,
            jnp.concatenate([value_grad_flat, value_grad_var, value_grad_var], axis=0),
            jnp.float32(1.0),
        )
        position = (grad_own * item_scale).reshape(row_count // 2, dp, shard).transpose(1, 0, 2)
        position = links.scatter_sum(position)
        position = links.global_rows(position, links.other_rows(position))

        pixel_own = links.sum_rows(pixel_part)
        pixel_grad = links.global_rows(pixel_own, links.other_rows(pixel_own))
        pixel_grad = pixel_grad.T.reshape(1, var_count, pix_count, row_count)

        names = []
        for layer in range(layer_count):
            names += [("gain", layer, 0), ("gain", layer, 1), ("bias", layer, 0), ("bias", layer, 1)]
        for layer in range(layer_count):
            names += [("out_bias", layer), ("down_bias", layer)]
        names += ["column", "lead"]
        own_sums = jnp.stack([row_sums[name] for name in names]) * item_scale
        full_sums = own_sums + exchange(own_sums, "mp", mp, 0)
        local = jnp.stack([local_sums["up_bias", layer] for layer in range(layer_count)]) * item_scale
        thin = [local_sums["qv", layer, which] for layer in range(layer_count) for which in range(2)]
        thin = jnp.stack(thin + [local_sums["pool_bias"]]) * item_scale
        packed = jnp.concatenate(
            [
                full_sums.reshape(len(names), dp, shard).transpose(1, 0, 2).reshape(dp, -1),
                summed_key.reshape(dp, -1),
                local.reshape(layer_count, dp, -1).transpose(1, 0, 2).reshape(dp, -1),
                thin.reshape(2 * layer_count + 1, dp, -1).transpose(1, 0, 2).reshape(dp, -1),
                jnp.broadcast_to(query_grad[None, :], (dp, local_width)),
            ],
            axis=1,
        )
        packed = links.scatter_sum(packed[:, None, :])[0]
        offset = 0

        def take(*shape):
            nonlocal offset
            size = math.prod(shape)
            piece = packed[offset : offset + size].reshape(shape)
            offset += size
            return piece

        gains = take(layer_count, 2, shard)
        biases = []
        gain_list = []
        offset = 0
        norm_all = take(layer_count, 2, 2, shard)
        gain_list = norm_all[:, 0]
        biases = norm_all[:, 1]
        dense_bias = take(layer_count, 2, shard)
        column_total = take(shard)
        lead_total = take(shard)
        key_shard = take(shard, head_count)
        up_bias_total = take(layer_count, local.shape[1] // dp)
        thin_total = take(2 * layer_count + 1, local_width // dp)
        query_total = take(local_width)

        query_rows = lax.dynamic_slice_in_dim(query_low, links.dp_index * shard, shard, 0)
        query_weight_grad = query_rows.astype(F32)[:, None] * query_total[None, :]
        key_weight_grad = (
            jnp.repeat(key_shard, HEAD_DIM, axis=1) * query_vec.astype(F32)[None, :] / ROOT_DIM
        )
        embed_turned = embed_grad.T
        hidden_width = weight_grads[0][0].shape[1]
        return (
            layer_out[None],
            pixel_grad,
            embed_turned[:flat_count].reshape(var_count, pix_count, sub),
            embed_turned[flat_count:flat_all],
            position,
            embed_turned[flat_all],
            query_weight_grad,
            key_weight_grad,
            value_weight_grad,
            thin_total[-1],
            pool_out_grad.T,
            column_total,
            lead_total,
            column_total,
            gain_list,
            biases,
            jnp.stack(
                [
                    grads[3].reshape(shard, 3, local_width).transpose(1, 0, 2)
                    for grads in weight_grads
                ]
            ),
            thin_total[:-1].reshape(layer_count, 2, local_width // dp),
            jnp.stack([grads[2].T for grads in weight_grads]),
            dense_bias[:, 0],
            jnp.stack([grads[1] for grads in weight_grads]),
            up_bias_total,
            jnp.stack([grads[0].T for grads in weight_grads]),
            dense_bias[:, 1],
        )

    return per_device


def solution(mesh):
    return jax.shard_map(
        make_per_device(mesh.shape["dp"], mesh.shape["mp"]),
        mesh=mesh,
        in_specs=(
            P("dp", None, None, None),
            P("dp"),
            P(),
            P("dp"),
            P("dp"),
            P(),
            P(),
            P(),
            P(),
            P(),
            P(None, "mp"),
            P(None, "mp"),
            P(None, "mp"),
            P("mp"),
            P("mp", None),
            P(),
            P(),
            P(),
            P(),
            P(),
            P(None, None, None, "mp"),
            P(None, None, "mp"),
            P(None, "mp", None),
            P(),
            P(None, None, "mp"),
            P(None, "mp"),
            P(None, "mp", None),
            P(),
            P("dp", None, None),
        ),
        out_specs=(
            P("dp", None, None),
            P("dp", None, None, None),
            P(None, None, ("dp", "mp")),
            P(None, ("dp", "mp")),
            P(None, "dp"),
            P(("dp", "mp")),
            P("dp", "mp"),
            P("dp", "mp"),
            P("dp", "mp"),
            P(("mp", "dp")),
            P("mp", "dp"),
            P("dp"),
            P("dp"),
            P("dp"),
            P(None, None, "dp"),
            P(None, None, "dp"),
            P(None, None, "dp", "mp"),
            P(None, None, ("mp", "dp")),
            P(None, "mp", "dp"),
            P(None, "dp"),
            P(None, "dp", "mp"),
            P(None, ("mp", "dp")),
            P(None, "mp", "dp"),
            P(None, "dp"),
        ),
        check_vma=False,
    )
```

time: 2230 us -> 837 us (0.38)
  waiting for transfers between devices: 1330 us -> 343 us
  matrix products: 425 us -> 133 us
  blocking collectives: 81.7 us -> 0 us
  starting transfers between devices: 2.63 us -> 74.9 us
  local copies, waits for them, and re-layouts: 220 us -> 162 us
    reduce_scatter x10 -> x0, waiting for transfers between devices: 902 us -> none  [the longest x1 153 us: per_device(): lax.psum_scatter(down_all, 'dp', scatter_dimension=2, tiled=True)]
    ppermute x0 -> x76, waiting for transfers between devices: none -> 343 us  [exchange(): return lax.ppermute(tensor, axis, [(i, i ^ 1 << bit) for i in range(size)])]
    dot_general x112 -> x76, matrix products: 425 us -> 127 us  [the longest x22 40.9 us: matmul_tn(): lax.dot_general(left, right, (((0,), (0,)), ((), ())), preferred_element_...]
    psum x9 -> x0, waiting for transfers between devices: 296 us -> none  [the longest x2 85.4 us: per_device(): lax.psum(matmul(mixed_heads, output_weight[layer_num]), 'mp')]
    unnamed x33 -> x0, waiting for transfers between devices: 131 us -> none
    concatenate x0 -> x49, local copies, waits for them, and re-layouts: none -> 83.2 us  [the longest x16 37.5 us: both_rows(): return jnp.concatenate([own, self.other_rows(own)], axis=0)]
    ppermute x0 -> x76, starting transfers between devices: none -> 74.9 us  [exchange(): return lax.ppermute(tensor, axis, [(i, i ^ 1 << bit) for i in range(size)])]
    unnamed x2 -> x0, blocking collectives: 59 us -> none
  transfers between devices with their start and end apart: 26 -> 76, of which waited for: 18 -> 34; matrix products, arithmetic and copies ran while one was open for 23% -> 40% of each run, Pallas kernels for 0% -> 0%
where the time goes in v1:
time: 837 us; the launch traced here: 824 us
  waiting for transfers between devices  343 us (41%)
  local copies, waits for them, and re-layouts  162 us (19%)
  matrix products  133 us (16%)
  other arithmetic  105 us (13%)
  starting transfers between devices  74.9 us (9%)
    ppermute x76, waiting for transfers between devices, exchange(): return lax.ppermute(tensor, axis, [(i, i ^ 1 << bit) for i in range(size)])  343 us
    ppermute x76, starting transfers between devices, exchange(): return lax.ppermute(tensor, axis, [(i, i ^ 1 << bit) for i in range(size)])  74.9 us
    dot_general x22, matrix products, matmul_tn(): lax.dot_general(left, right, (((0,), (0,)), ((), ())), preferred_element_...  40.9 us
    concatenate x16, local copies, waits for them, and re-layouts, both_rows(): return jnp.concatenate([own, self.other_rows(own)], axis=0)  37.5 us
    dot_general x16, matrix products, matmul(): return jnp.dot(left, right, preferred_element_type=F32)  27 us
    dynamic_slice x26, local copies, waits for them, and re-layouts, pick(): return lax.dynamic_index_in_dim(tensor, index, axis, keepdims=False)  26.6 us
    dot_general x15, matrix products, matmul_nt(): lax.dot_general(left, right, (((1,), (1,)), ((), ())), preferred_element_...  24.6 us
    unnamed x423, local copies, waits for them, and re-layouts  20.9 us
  transfers between devices with their start and end apart: 76, of which 34 were waited for; matrix products, arithmetic and copies ran while one was open for 40% of the time, Pallas kernels for 0%

profile of v1, /device:TPU:0, one launch (start us, length us, event | category | flops | bytes accessed | tf_op | source)
XLA Modules:
  0.0 824.2 jit_solution(8756062066559721024)
XLA Ops:
  14.2 4.1 fusion.196
  18.6 3.2 fusion.183
  26.4 2.9 collective-permute-start.1
  30.0 17.2 %collective-permute-done.1 = f32[192,1024]{1,0:T(8,128)S(1)} collective-permute-done((f32[192,1024]{1,0:T(8,128)S(1)}, f32[192,1024]{1,0:T(8,128)S(1)}, u32[]{:S(2)}, u32[]{:S(2)}) %collective-permute-start.1) | collective-permute-done | bytes 786464 | tf_op jit(solution)/shard_map/ppermute | solution.py:42
  63.0 17.2 %collective-permute-done.4 = f32[192,1024]{1,0:T(8,128)S(1)} collective-permute-done((f32[192,1024]{1,0:T(8,128)S(1)}, f32[192,1024]{1,0:T(8,128)S(1)}, u32[]{:S(2)}, u32[]{:S(2)}) %collective-permute-start.4) | collective-permute-done | bytes 786464 | tf_op jit(solution)/shard_map/ppermute | solution.py:42
  83.3 6.1 multiply_convert_fusion.6
  95.4 17.2 %collective-permute-done.7 = f32[192,1024]{1,0:T(8,128)S(1)} collective-permute-done((f32[192,1024]{1,0:T(8,128)S(1)}, f32[192,1024]{1,0:T(8,128)S(1)}, u32[]{:S(2)}, u32[]{:S(2)}) %collective-permute-start.7) | collective-permute-done | bytes 786464 | tf_op jit(solution)/shard_map/ppermute | solution.py:42
  118.6 3.8 concatenate.223
  133.8 5.0 copy.186
  146.4 3.2 fusion.309
  172.3 2.7 concatenate.232
  183.1 2.7 concatenate.245
  188.0 2.7 concatenate.246
  196.2 2.7 concatenate.235
  201.1 2.7 concatenate.236
  206.0 3.1 fusion.49
  209.1 2.7 concatenate.248
  214.0 6.4 multiply_convert_fusion.5
  227.9 2.7 concatenate.249
  233.0 2.9 fusion.8
  247.7 12.8 %collective-permute-done.16 = f32[192,1024]{1,0:T(8,128)S(1)} collective-permute-done((f32[192,1024]{1,0:T(8,128)S(1)}, f32[192,1024]{1,0:T(8,128)S(1)}, u32[]{:S(2)}, u32[]{:S(2)}) %collective-permute-start.16) | collective-permute-done | bytes 786464 | tf_op jit(solution)/shard_map/ppermute | solution.py:42
  267.4 9.1 %collective-permute-done.13 = f32[192,1024]{1,0:T(8,128)} collective-permute-done((f32[192,1024]{1,0:T(8,128)}, f32[192,1024]{1,0:T(8,128)}, u32[]{:S(2)}, u32[]{:S(2)}) %collective-permute-start.13) | collective-permute-done | bytes 786464 | tf_op jit(solution)/shard_map/ppermute | solution.py:42
  287.0 33.5 %collective-permute-done.67 = f32[512,1024]{1,0:T(8,128)} collective-permute-done((f32[512,1024]{1,0:T(8,128)}, f32[512,1024]{1,0:T(8,128)}, u32[]{:S(2)}, u32[]{:S(2)}) %collective-permute-start.67) | collective-permute-done | bytes 2097184 | tf_op jit(solution)/shard_map/ppermute | solution.py:42
  355.6 5.7 collective-permute-done.61
  379.8 8.7 %collective-permute-done.19 = f32[192,1024]{1,0:T(8,128)S(1)} collective-permute-done((f32[192,1024]{1,0:T(8,128)S(1)}, f32[192,1024]{1,0:T(8,128)S(1)}, u32[]{:S(2)}, u32[]{:S(2)}) %collective-permute-start.19) | collective-permute-done | bytes 786464 | tf_op jit(solution)/shard_map/ppermute | solution.py:42
  391.3 32.4 %collective-permute-done.63 = f32[1,128,256]{1,2,0:T(8,128)S(1)} collective-permute-done((f32[1,128,256]{1,2,0:T(8,128)S(1)}, f32[1,128,256]{1,2,0:T(8,128)S(1)}, u32[]{:S(2)}, u32[]{:S(2)}) %collective-permute-start.63) | collective-permute-done | bytes 131104 | tf_op jit(solution)/shard_map/ppermute | solution.py:42
  436.0 2.9 fusion.285
  439.6 4.0 fusion.313
  447.6 2.9 fusion.18
  457.3 3.2 collective-permute-start.57
  468.8 9.0 %collective-permute-done.57 = f32[1,128,768]{1,2,0:T(8,128)S(1)} collective-permute-done((f32[1,128,768]{1,2,0:T(8,128)}, f32[1,128,768]{1,2,0:T(8,128)S(1)}, u32[]{:S(2)}, u32[]{:S(2)}) %collective-permute-start.57) | collective-permute-done | bytes 393248 | tf_op jit(solution)/shard_map/ppermute | solution.py:42
  485.9 17.7 %collective-permute-done.70 = f32[512,1024]{1,0:T(8,128)} collective-permute-done((f32[512,1024]{1,0:T(8,128)}, f32[512,1024]{1,0:T(8,128)}, u32[]{:S(2)}, u32[]{:S(2)}) %collective-permute-start.70) | collective-permute-done | bytes 2097184 | tf_op jit(solution)/shard_map/ppermute | solution.py:42
  510.8 36.3 %collective-permute-done.64 = f32[512,1024]{1,0:T(8,128)} collective-permute-done((f32[512,1024]{1,0:T(8,128)}, f32[512,1024]{1,0:T(8,128)}, u32[]{:S(2)}, u32[]{:S(2)}) %collective-permute-start.64) | collective-permute-done | bytes 2097184 | tf_op jit(solution)/shard_map/ppermute | solution.py:42
  582.2 3.5 collective-permute-done.58
  593.9 2.8 collective-permute-start.72
  604.7 40.2 %collective-permute-done.60 = f32[1,128,256]{1,2,0:T(8,128)S(1)} collective-permute-done((f32[1,128,256]{1,2,0:T(8,128)S(1)}, f32[1,128,256]{1,2,0:T(8,128)S(1)}, u32[]{:S(2)}, u32[]{:S(2)}) %collective-permute-start.60) | collective-permute-done | bytes 131104 | tf_op jit(solution)/shard_map/ppermute | solution.py:42
  660.7 10.5 %collective-permute-done.38 = f32[4,192,128]{2,1,0:T(8,128)S(1)} collective-permute-done((f32[4,192,128]{2,1,0:T(8,128)S(1)}, f32[4,192,128]{2,1,0:T(8,128)S(1)}, u32[]{:S(2)}, u32[]{:S(2)}) %collective-permute-start.38) | collective-permute-done | bytes 393248 | tf_op jit(solution)/shard_map/ppermute | solution.py:42
  673.2 7.1 collective-permute-done.39
  682.4 5.1 collective-permute-done.40
  690.6 3.5 multiply_reduce_fusion
  702.4 3.8 multiply_convert_fusion.7
  723.3 3.1 fusion.181
  732.3 7.7 collective-permute-done.43
  741.2 2.8 collective-permute-start.44
  777.7 14.1 %collective-permute-done.34 = f32[1,8,32,817]{3,2,1,0:T(8,128)S(1)} collective-permute-done((f32[1,8,32,817]{3,2,1,0:T(8,128)S(1)}, f32[1,8,32,817]{3,2,1,0:T(8,128)S(1)}, u32[]{:S(2)}, u32[]{:S(2)}) %collective-permute-start.34) | collective-permute-done | bytes 836640 | tf_op jit(solution)/shard_map/ppermute | solution.py:42
  793.2 10.4 %collective-permute-done.28 = f32[192,768]{1,0:T(8,128)S(1)} collective-permute-done((f32[192,768]{1,0:T(8,128)S(1)}, f32[192,768]{1,0:T(8,128)S(1)}, u32[]{:S(2)}, u32[]{:S(2)}) %collective-permute-start.28) | collective-permute-done | bytes 589856 | tf_op jit(solution)/shard_map/ppermute | solution.py:42
  806.4 6.2 collective-permute-done.36
  815.8 5.0 collective-permute-done.37
  (922 shorter events, 401.4 us)
Async XLA Ops:
  26.4 20.8 %collective-permute-start.1 = (f32[192,1024]{1,0:T(8,128)S(1)}, f32[192,1024]{1,0:T(8,128)S(1)}, u32[]{:S(2)}, u32[]{:S(2)}) collective-permute-start(f32[192,1024]{1,0:T(8,128)S(1)} %slice_add_fusion.8), channel_id=1, source_target_pairs={{0,2},{1,3},{2,0},{3,1},{4,6},{5,7},{6,4},{7,5},{8,10},{9,11},{10,... | collective-permute-start | bytes 2359304 | tf_op jit(solution)/shard_map/ppermute | solution.py:42
  60.6 19.6 %collective-permute-start.4 = (f32[192,1024]{1,0:T(8,128)S(1)}, f32[192,1024]{1,0:T(8,128)S(1)}, u32[]{:S(2)}, u32[]{:S(2)}) collective-permute-start(f32[192,1024]{1,0:T(8,128)S(1)} %slice_add_fusion.7), channel_id=1, source_target_pairs={{0,2},{1,3},{2,0},{3,1},{4,6},{5,7},{6,4},{7,5},{8,10},{9,11},{10,... | collective-permute-start | bytes 2359304 | tf_op jit(solution)/shard_map/ppermute | solution.py:42
  93.0 19.7 %collective-permute-start.7 = (f32[192,1024]{1,0:T(8,128)S(1)}, f32[192,1024]{1,0:T(8,128)S(1)}, u32[]{:S(2)}, u32[]{:S(2)}) collective-permute-start(f32[192,1024]{1,0:T(8,128)S(1)} %slice_add_fusion.6), channel_id=1, source_target_pairs={{0,2},{1,3},{2,0},{3,1},{4,6},{5,7},{6,4},{7,5},{8,10},{9,11},{10,... | collective-permute-start | bytes 2359304 | tf_op jit(solution)/shard_map/ppermute | solution.py:42
  114.9 26.4 %collective-permute-start.8 = (f32[192,1024]{1,0:T(8,128)}, f32[192,1024]{1,0:T(8,128)}, u32[]{:S(2)}, u32[]{:S(2)}) collective-permute-start(f32[192,1024]{1,0:T(8,128)} %subtract_multiply_fusion.5), channel_id=1, source_target_pairs={{0,1},{1,0},{2,3},{3,2},{4,5},{5,4},{6,7},{7,6},{8,9},{9,8},{10,11... | collective-permute-start | bytes 2359304 | tf_op jit(solution)/shard_map/ppermute | solution.py:42
  116.1 43.9 %collective-permute-start.30 = (f32[8,128]{1,0:T(8,128)}, f32[8,128]{1,0:T(8,128)S(1)}, u32[]{:S(2)}, u32[]{:S(2)}) collective-permute-start(f32[8,128]{1,0:T(8,128)} %broadcast_in_dim.92), channel_id=1, source_target_pairs={{0,4},{4,0},{8,12},{12,8},{16,20},{20,16},{24,28},{28,24},{1,5},{5... | collective-permute-start | bytes 12296 | tf_op jit(solution)/shard_map/ppermute | solution.py:42
  158.5 20.7 %collective-permute-start.10 = (f32[192,1024]{1,0:T(8,128)}, f32[192,1024]{1,0:T(8,128)}, u32[]{:S(2)}, u32[]{:S(2)}) collective-permute-start(f32[192,1024]{1,0:T(8,128)} %slice_add_fusion.5), channel_id=1, source_target_pairs={{0,2},{1,3},{2,0},{3,1},{4,6},{5,7},{6,4},{7,5},{8,10},{9,11},{10,... | collective-permute-start | bytes 2359304 | tf_op jit(solution)/shard_map/ppermute | solution.py:42
  182.1 31.8 %collective-permute-start.11 = (f32[192,1024]{1,0:T(8,128)}, f32[192,1024]{1,0:T(8,128)}, u32[]{:S(2)}, u32[]{:S(2)}) collective-permute-start(f32[192,1024]{1,0:T(8,128)} %subtract_multiply_fusion.4), channel_id=1, source_target_pairs={{0,1},{1,0},{2,3},{3,2},{4,5},{5,4},{6,7},{7,6},{8,9},{9,8},{10,11... | collective-permute-start | bytes 2359304 | tf_op jit(solution)/shard_map/ppermute | solution.py:42
  227.4 51.7 %collective-permute-start.73 = (f32[512,1024]{1,0:T(8,128)}, f32[512,1024]{1,0:T(8,128)}, u32[]{:S(2)}, u32[]{:S(2)}) collective-permute-start(f32[512,1024]{1,0:T(8,128)} %convolution_multiply_fusion), channel_id=1, source_target_pairs={{0,4},{4,0},{8,12},{12,8},{16,20},{20,16},{24,28},{28,24},{1,5},{5... | collective-permute-start | bytes 6291464 | tf_op jit(solution)/shard_map/ppermute | solution.py:42
  240.0 20.5 %collective-permute-start.16 = (f32[192,1024]{1,0:T(8,128)S(1)}, f32[192,1024]{1,0:T(8,128)S(1)}, u32[]{:S(2)}, u32[]{:S(2)}) collective-permute-start(f32[192,1024]{1,0:T(8,128)S(1)} %slice_add_fusion.3), channel_id=1, source_target_pairs={{0,2},{1,3},{2,0},{3,1},{4,6},{5,7},{6,4},{7,5},{8,10},{9,11},{10,... | collective-permute-start | bytes 2359304 | tf_op jit(solution)/shard_map/ppermute | solution.py:42
  243.0 77.5 %collective-permute-start.67 = (f32[512,1024]{1,0:T(8,128)}, f32[512,1024]{1,0:T(8,128)}, u32[]{:S(2)}, u32[]{:S(2)}) collective-permute-start(f32[512,1024]{1,0:T(8,128)} %convolution_multiply_fusion.2), channel_id=1, source_target_pairs={{0,4},{4,0},{8,12},{12,8},{16,20},{20,16},{24,28},{28,24},{1,5},{5... | collective-permute-start | bytes 6291464 | tf_op jit(solution)/shard_map/ppermute | solution.py:42
  246.5 30.1 %collective-permute-start.13 = (f32[192,1024]{1,0:T(8,128)}, f32[192,1024]{1,0:T(8,128)}, u32[]{:S(2)}, u32[]{:S(2)}) collective-permute-start(f32[192,1024]{1,0:T(8,128)} %slice_add_fusion.4), channel_id=1, source_target_pairs={{0,2},{1,3},{2,0},{3,1},{4,6},{5,7},{6,4},{7,5},{8,10},{9,11},{10,... | collective-permute-start | bytes 2359304 | tf_op jit(solution)/shard_map/ppermute | solution.py:42
  263.3 62.5 %collective-permute-start.17 = (f32[192,1024]{1,0:T(8,128)}, f32[192,1024]{1,0:T(8,128)}, u32[]{:S(2)}, u32[]{:S(2)}) collective-permute-start(f32[192,1024]{1,0:T(8,128)} %get-tuple-element.118), channel_id=1, source_target_pairs={{0,1},{1,0},{2,3},{3,2},{4,5},{5,4},{6,7},{7,6},{8,9},{9,8},{10,11... | collective-permute-start | bytes 2359304 | tf_op jit(solution)/shard_map/ppermute | solution.py:42
  279.1 72.1 %collective-permute-start.14 = (f32[192,1024]{1,0:T(8,128)}, f32[192,1024]{1,0:T(8,128)}, u32[]{:S(2)}, u32[]{:S(2)}) collective-permute-start(f32[192,1024]{1,0:T(8,128)} %add_add_fusion.2), channel_id=1, source_target_pairs={{0,1},{1,0},{2,3},{3,2},{4,5},{5,4},{6,7},{7,6},{8,9},{9,8},{10,11... | collective-permute-start | bytes 2359304 | tf_op jit(solution)/shard_map/ppermute | solution.py:42
  283.9 82.9 %collective-permute-start.74 = (f32[2,128,1024]{1,2,0:T(8,128)}, f32[2,128,1024]{1,2,0:T(8,128)}, u32[]{:S(2)}, u32[]{:S(2)}) collective-permute-start(f32[2,128,1024]{1,2,0:T(8,128)} %bitcast.631), channel_id=1, source_target_pairs={{0,8},{4,12},{8,0},{12,4},{16,24},{20,28},{24,16},{28,20},{1,9},{5... | collective-permute-start | bytes 3145736 | tf_op jit(solution)/shard_map/ppermute | solution.py:42
  324.2 49.3 %collective-permute-start.68 = (f32[2,128,1024]{2,1,0:T(8,128)}, f32[2,128,1024]{2,1,0:T(8,128)}, u32[]{:S(2)}, u32[]{:S(2)}) collective-permute-start(f32[2,128,1024]{2,1,0:T(8,128)} %dynamic-slice_bitcast_fusion), channel_id=1, source_target_pairs={{0,8},{4,12},{8,0},{12,4},{16,24},{20,28},{24,16},{28,20},{1,9},{5... | collective-permute-start | bytes 3145736 | tf_op jit(solution)/shard_map/ppermute | solution.py:42
  340.1 28.2 %collective-permute-start.18 = (f32[192,1024]{1,0:T(8,128)}, f32[192,1024]{1,0:T(8,128)}, u32[]{:S(2)}, u32[]{:S(2)}) collective-permute-start(f32[192,1024]{1,0:T(8,128)} %slice.483), channel_id=1, source_target_pairs={{0,1},{1,0},{2,3},{3,2},{4,5},{5,4},{6,7},{7,6},{8,9},{9,8},{10,11... | collective-permute-start | bytes 2359304 | tf_op jit(solution)/shard_map/ppermute | solution.py:42
  351.2 76.5 %collective-permute-start.55 = (f32[512,768]{1,0:T(8,128)}, f32[512,768]{1,0:T(8,128)}, u32[]{:S(2)}, u32[]{:S(2)}) collective-permute-start(f32[512,768]{1,0:T(8,128)} %convolution_multiply_fusion.4), channel_id=1, source_target_pairs={{0,4},{4,0},{8,12},{12,8},{16,20},{20,16},{24,28},{28,24},{1,5},{5... | collective-permute-start | bytes 4718600 | tf_op jit(solution)/shard_map/ppermute | solution.py:42
  369.9 18.6 %collective-permute-start.19 = (f32[192,1024]{1,0:T(8,128)S(1)}, f32[192,1024]{1,0:T(8,128)S(1)}, u32[]{:S(2)}, u32[]{:S(2)}) collective-permute-start(f32[192,1024]{1,0:T(8,128)S(1)} %slice_add_fusion.2), channel_id=1, source_target_pairs={{0,2},{1,3},{2,0},{3,1},{4,6},{5,7},{6,4},{7,5},{8,10},{9,11},{10,... | collective-permute-start | bytes 2359304 | tf_op jit(solution)/shard_map/ppermute | solution.py:42
  370.8 52.9 %collective-permute-start.75 = (f32[1,128,1024]{1,2,0:T(8,128)S(1)}, f32[1,128,1024]{1,2,0:T(8,128)S(1)}, u32[]{:S(2)}, u32[]{:S(2)}) collective-permute-start(f32[1,128,1024]{1,2,0:T(8,128)S(1)} %constant_dynamic-slice_fusion), channel_id=1, source_target_pairs={{0,16},{4,20},{8,24},{12,28},{16,0},{20,4},{24,8},{28,12},{1,17},{... | collective-permute-start | bytes 1572872 | tf_op jit(solution)/shard_map/ppermute | solution.py:42
  375.8 90.4 %collective-permute-start.69 = (f32[1,128,1024]{2,1,0:T(8,128)}, f32[1,128,1024]{2,1,0:T(8,128)}, u32[]{:S(2)}, u32[]{:S(2)}) collective-permute-start(f32[1,128,1024]{2,1,0:T(8,128)} %constant_dynamic-slice_fusion.6), channel_id=1, source_target_pairs={{0,16},{4,20},{8,24},{12,28},{16,0},{20,4},{24,8},{28,12},{1,17},{... | collective-permute-start | bytes 1572872 | tf_op jit(solution)/shard_map/ppermute | solution.py:42
  377.1 46.6 %collective-permute-start.63 = (f32[1,128,256]{1,2,0:T(8,128)S(1)}, f32[1,128,256]{1,2,0:T(8,128)S(1)}, u32[]{:S(2)}, u32[]{:S(2)}) collective-permute-start(f32[1,128,256]{1,2,0:T(8,128)S(1)} %constant_dynamic-slice_fusion.8), channel_id=1, source_target_pairs={{0,16},{4,20},{8,24},{12,28},{16,0},{20,4},{24,8},{28,12},{1,17},{... | collective-permute-start | bytes 393224 | tf_op jit(solution)/shard_map/ppermute | solution.py:42
  391.3 44.7 %collective-permute-start.20 = (f32[192,1024]{1,0:T(8,128)}, f32[192,1024]{1,0:T(8,128)}, u32[]{:S(2)}, u32[]{:S(2)}) collective-permute-start(f32[192,1024]{1,0:T(8,128)} %get-tuple-element.121), channel_id=1, source_target_pairs={{0,1},{1,0},{2,3},{3,2},{4,5},{5,4},{6,7},{7,6},{8,9},{9,8},{10,11... | collective-permute-start | bytes 2359304 | tf_op jit(solution)/shard_map/ppermute | solution.py:42
  433.6 21.6 %collective-permute-start.56 = (f32[2,128,768]{1,2,0:T(8,128)}, f32[2,128,768]{1,2,0:T(8,128)}, u32[]{:S(2)}, u32[]{:S(2)}) collective-permute-start(f32[2,128,768]{1,2,0:T(8,128)} %bitcast.645), channel_id=1, source_target_pairs={{0,8},{4,12},{8,0},{12,4},{16,24},{20,28},{24,16},{28,20},{1,9},{5... | collective-permute-start | bytes 2359304 | tf_op jit(solution)/shard_map/ppermute | solution.py:42
  454.8 48.9 %collective-permute-start.70 = (f32[512,1024]{1,0:T(8,128)}, f32[512,1024]{1,0:T(8,128)}, u32[]{:S(2)}, u32[]{:S(2)}) collective-permute-start(f32[512,1024]{1,0:T(8,128)} %convolution_multiply_fusion.1), channel_id=1, source_target_pairs={{0,4},{4,0},{8,12},{12,8},{16,20},{20,16},{24,28},{28,24},{1,5},{5... | collective-permute-start | bytes 6291464 | tf_op jit(solution)/shard_map/ppermute | solution.py:42
  457.3 20.4 %collective-permute-start.57 = (f32[1,128,768]{1,2,0:T(8,128)}, f32[1,128,768]{1,2,0:T(8,128)S(1)}, u32[]{:S(2)}, u32[]{:S(2)}) collective-permute-start(f32[1,128,768]{1,2,0:T(8,128)} %constant_dynamic-slice_fusion.14), channel_id=1, source_target_pairs={{0,16},{4,20},{8,24},{12,28},{16,0},{20,4},{24,8},{28,12},{1,17},{... | collective-permute-start | bytes 1179656 | tf_op jit(solution)/shard_map/ppermute | solution.py:42
  461.5 18.8 %collective-permute-start.22 = (f32[192,1024]{1,0:T(8,128)}, f32[192,1024]{1,0:T(8,128)}, u32[]{:S(2)}, u32[]{:S(2)}) collective-permute-start(f32[192,1024]{1,0:T(8,128)} %slice_add_fusion.1), channel_id=1, source_target_pairs={{0,2},{1,3},{2,0},{3,1},{4,6},{5,7},{6,4},{7,5},{8,10},{9,11},{10,... | collective-permute-start | bytes 2359304 | tf_op jit(solution)/shard_map/ppermute | solution.py:42
  464.7 82.5 %collective-permute-start.64 = (f32[512,1024]{1,0:T(8,128)}, f32[512,1024]{1,0:T(8,128)}, u32[]{:S(2)}, u32[]{:S(2)}) collective-permute-start(f32[512,1024]{1,0:T(8,128)} %convolution_multiply_fusion.3), channel_id=1, source_target_pairs={{0,4},{4,0},{8,12},{12,8},{16,20},{20,16},{24,28},{28,24},{1,5},{5... | collective-permute-start | bytes 6291464 | tf_op jit(solution)/shard_map/ppermute | solution.py:42
  484.3 68.7 %collective-permute-start.23 = (f32[192,1024]{1,0:T(8,128)}, f32[192,1024]{1,0:T(8,128)}, u32[]{:S(2)}, u32[]{:S(2)}) collective-permute-start(f32[192,1024]{1,0:T(8,128)} %get-tuple-element.131), channel_id=1, source_target_pairs={{0,1},{1,0},{2,3},{3,2},{4,5},{5,4},{6,7},{7,6},{8,9},{9,8},{10,11... | collective-permute-start | bytes 2359304 | tf_op jit(solution)/shard_map/ppermute | solution.py:42
  507.5 84.6 %collective-permute-start.71 = (f32[2,128,1024]{1,2,0:T(8,128)}, f32[2,128,1024]{1,2,0:T(8,128)}, u32[]{:S(2)}, u32[]{:S(2)}) collective-permute-start(f32[2,128,1024]{1,2,0:T(8,128)} %bitcast.632), channel_id=1, source_target_pairs={{0,8},{4,12},{8,0},{12,4},{16,24},{20,28},{24,16},{28,20},{1,9},{5... | collective-permute-start | bytes 3145736 | tf_op jit(solution)/shard_map/ppermute | solution.py:42
  550.9 45.8 %collective-permute-start.65 = (f32[2,128,1024]{2,1,0:T(8,128)}, f32[2,128,1024]{2,1,0:T(8,128)}, u32[]{:S(2)}, u32[]{:S(2)}) collective-permute-start(f32[2,128,1024]{2,1,0:T(8,128)} %dynamic-slice_bitcast_fusion.1), channel_id=1, source_target_pairs={{0,8},{4,12},{8,0},{12,4},{16,24},{20,28},{24,16},{28,20},{1,9},{5... | collective-permute-start | bytes 3145736 | tf_op jit(solution)/shard_map/ppermute | solution.py:42
  574.3 78.3 %collective-permute-start.52 = (f32[512,768]{1,0:T(8,128)}, f32[512,768]{1,0:T(8,128)}, u32[]{:S(2)}, u32[]{:S(2)}) collective-permute-start(f32[512,768]{1,0:T(8,128)} %convolution_multiply_fusion.5), channel_id=1, source_target_pairs={{0,4},{4,0},{8,12},{12,8},{16,20},{20,16},{24,28},{28,24},{1,5},{5... | collective-permute-start | bytes 4718600 | tf_op jit(solution)/shard_map/ppermute | solution.py:42
  580.9 21.3 %collective-permute-start.24 = (f32[192,1024]{1,0:T(8,128)}, f32[192,1024]{1,0:T(8,128)}, u32[]{:S(2)}, u32[]{:S(2)}) collective-permute-start(f32[192,1024]{1,0:T(8,128)} %slice.487), channel_id=1, source_target_pairs={{0,1},{1,0},{2,3},{3,2},{4,5},{5,4},{6,7},{7,6},{8,9},{9,8},{10,11... | collective-permute-start | bytes 2359304 | tf_op jit(solution)/shard_map/ppermute | solution.py:42
  593.9 51.7 %collective-permute-start.72 = (f32[1,128,1024]{1,2,0:T(8,128)S(1)}, f32[1,128,1024]{1,2,0:T(8,128)S(1)}, u32[]{:S(2)}, u32[]{:S(2)}) collective-permute-start(f32[1,128,1024]{1,2,0:T(8,128)S(1)} %constant_dynamic-slice_fusion.3), channel_id=1, source_target_pairs={{0,16},{4,20},{8,24},{12,28},{16,0},{20,4},{24,8},{28,12},{1,17},{... | collective-permute-start | bytes 1572872 | tf_op jit(solution)/shard_map/ppermute | solution.py:42
  598.1 47.5 %collective-permute-start.66 = (f32[1,128,1024]{2,1,0:T(8,128)S(1)}, f32[1,128,1024]{2,1,0:T(8,128)S(1)}, u32[]{:S(2)}, u32[]{:S(2)}) collective-permute-start(f32[1,128,1024]{2,1,0:T(8,128)S(1)} %constant_dynamic-slice_fusion.7), channel_id=1, source_target_pairs={{0,16},{4,20},{8,24},{12,28},{16,0},{20,4},{24,8},{28,12},{1,17},{... | collective-permute-start | bytes 1572872 | tf_op jit(solution)/shard_map/ppermute | solution.py:42
  600.8 44.1 %collective-permute-start.60 = (f32[1,128,256]{1,2,0:T(8,128)S(1)}, f32[1,128,256]{1,2,0:T(8,128)S(1)}, u32[]{:S(2)}, u32[]{:S(2)}) collective-permute-start(f32[1,128,256]{1,2,0:T(8,128)S(1)} %constant_dynamic-slice_fusion.11), channel_id=1, source_target_pairs={{0,16},{4,20},{8,24},{12,28},{16,0},{20,4},{24,8},{28,12},{1,17},{... | collective-permute-start | bytes 393224 | tf_op jit(solution)/shard_map/ppermute | solution.py:42
  603.4 45.3 %collective-permute-start.25 = (f32[192,1024]{1,0:T(8,128)S(1)}, f32[192,1024]{1,0:T(8,128)S(1)}, u32[]{:S(2)}, u32[]{:S(2)}) collective-permute-start(f32[192,1024]{1,0:T(8,128)S(1)} %slice_add_fusion), channel_id=1, source_target_pairs={{0,2},{1,3},{2,0},{3,1},{4,6},{5,7},{6,4},{7,5},{8,10},{9,11},{10,... | collective-permute-start | bytes 2359304 | tf_op jit(solution)/shard_map/ppermute | solution.py:42
  651.1 37.1 %collective-permute-start.26 = (f32[192,1024]{1,0:T(8,128)}, f32[192,1024]{1,0:T(8,128)}, u32[]{:S(2)}, u32[]{:S(2)}) collective-permute-start(f32[192,1024]{1,0:T(8,128)} %get-tuple-element.122), channel_id=1, source_target_pairs={{0,1},{1,0},{2,3},{3,2},{4,5},{5,4},{6,7},{7,6},{8,9},{9,8},{10,11... | collective-permute-start | bytes 2359304 | tf_op jit(solution)/shard_map/ppermute | solution.py:42
  656.0 50.3 %collective-permute-start.53 = (f32[2,128,768]{1,2,0:T(8,128)}, f32[2,128,768]{1,2,0:T(8,128)}, u32[]{:S(2)}, u32[]{:S(2)}) collective-permute-start(f32[2,128,768]{1,2,0:T(8,128)} %bitcast.644), channel_id=1, source_target_pairs={{0,8},{4,12},{8,0},{12,4},{16,24},{20,28},{24,16},{28,20},{1,9},{5... | collective-permute-start | bytes 2359304 | tf_op jit(solution)/shard_map/ppermute | solution.py:42
  688.2 53.0 %collective-permute-start.41 = (f32[192,128]{1,0:T(8,128)}, f32[192,128]{1,0:T(8,128)}, u32[]{:S(2)}, u32[]{:S(2)}) collective-permute-start(f32[192,128]{1,0:T(8,128)} %add_bitcast_fusion.7), channel_id=1, source_target_pairs={{0,1},{1,0},{2,3},{3,2},{4,5},{5,4},{6,7},{7,6},{8,9},{9,8},{10,11... | collective-permute-start | bytes 294920 | tf_op jit(solution)/shard_map/ppermute | solution.py:42
  709.2 46.6 %collective-permute-start.54 = (f32[1,128,768]{1,2,0:T(8,128)}, f32[1,128,768]{1,2,0:T(8,128)}, u32[]{:S(2)}, u32[]{:S(2)}) collective-permute-start(f32[1,128,768]{1,2,0:T(8,128)} %constant_dynamic-slice_fusion.17), channel_id=1, source_target_pairs={{0,16},{4,20},{8,24},{12,28},{16,0},{20,4},{24,8},{28,12},{1,17},{... | collective-permute-start | bytes 1179656 | tf_op jit(solution)/shard_map/ppermute | solution.py:42
  713.2 45.0 %collective-permute-start.49 = (f32[512,256]{1,0:T(8,128)}, f32[512,256]{1,0:T(8,128)}, u32[]{:S(2)}, u32[]{:S(2)}) collective-permute-start(f32[512,256]{1,0:T(8,128)} %convolution_multiply_fusion.10), channel_id=1, source_target_pairs={{0,4},{4,0},{8,12},{12,8},{16,20},{20,16},{24,28},{28,24},{1,5},{5... | collective-permute-start | bytes 1572872 | tf_op jit(solution)/shard_map/ppermute | solution.py:42
  716.3 46.8 %collective-permute-start.46 = (f32[512,256]{1,0:T(8,128)}, f32[512,256]{1,0:T(8,128)}, u32[]{:S(2)}, u32[]{:S(2)}) collective-permute-start(f32[512,256]{1,0:T(8,128)} %fusion.192), channel_id=1, source_target_pairs={{0,4},{4,0},{8,12},{12,8},{16,20},{20,16},{24,28},{28,24},{1,5},{5... | collective-permute-start | bytes 1572872 | tf_op jit(solution)/shard_map/ppermute | solution.py:42
  740.1 25.9 %collective-permute-start.33 = (f32[2,8,32,817]{3,2,1,0:T(8,128)}, f32[2,8,32,817]{3,2,1,0:T(8,128)}, u32[]{:S(2)}, u32[]{:S(2)}) collective-permute-start(f32[2,8,32,817]{3,2,1,0:T(8,128)} %pad_maximum_fusion), channel_id=1, source_target_pairs={{0,1},{1,0},{2,3},{3,2},{4,5},{5,4},{6,7},{7,6},{8,9},{9,8},{10,11... | collective-permute-start | bytes 5019656 | tf_op jit(solution)/shard_map/ppermute | solution.py:42
  750.6 19.2 %collective-permute-start.27 = (f32[192,768]{1,0:T(8,128)}, f32[192,768]{1,0:T(8,128)}, u32[]{:S(2)}, u32[]{:S(2)}) collective-permute-start(f32[192,768]{1,0:T(8,128)} %slice.489), channel_id=1, source_target_pairs={{0,1},{1,0},{2,3},{3,2},{4,5},{5,4},{6,7},{7,6},{8,9},{9,8},{10,11... | collective-permute-start | bytes 1769480 | tf_op jit(solution)/shard_map/ppermute | solution.py:42
  768.5 23.3 %collective-permute-start.34 = (f32[1,8,32,817]{3,2,1,0:T(8,128)S(1)}, f32[1,8,32,817]{3,2,1,0:T(8,128)S(1)}, u32[]{:S(2)}, u32[]{:S(2)}) collective-permute-start(f32[1,8,32,817]{3,2,1,0:T(8,128)S(1)} %constant_dynamic-slice_fusion.30), channel_id=1, source_target_pairs={{0,2},{1,3},{2,0},{3,1},{4,6},{5,7},{6,4},{7,5},{8,10},{9,11},{10,... | collective-permute-start | bytes 2509832 | tf_op jit(solution)/shard_map/ppermute | solution.py:42
  770.9 32.7 %collective-permute-start.28 = (f32[192,768]{1,0:T(8,128)S(1)}, f32[192,768]{1,0:T(8,128)S(1)}, u32[]{:S(2)}, u32[]{:S(2)}) collective-permute-start(f32[192,768]{1,0:T(8,128)S(1)} %slice_add_fusion.9), channel_id=1, source_target_pairs={{0,2},{1,3},{2,0},{3,1},{4,6},{5,7},{6,4},{7,5},{8,10},{9,11},{10,... | collective-permute-start | bytes 1769480 | tf_op jit(solution)/shard_map/ppermute | solution.py:42
  772.8 19.7 %collective-permute-start.51 = (f32[1,128,256]{1,2,0:T(8,128)S(1)}, f32[1,128,256]{1,2,0:T(8,128)S(1)}, u32[]{:S(2)}, u32[]{:S(2)}) collective-permute-start(f32[1,128,256]{1,2,0:T(8,128)S(1)} %constant_dynamic-slice_fusion.20), channel_id=1, source_target_pairs={{0,16},{4,20},{8,24},{12,28},{16,0},{20,4},{24,8},{28,12},{1,17},{... | collective-permute-start | bytes 393224 | tf_op jit(solution)/shard_map/ppermute | solution.py:42
  776.0 27.8 %collective-permute-start.48 = (f32[1,128,256]{2,1,0:T(8,128)S(1)}, f32[1,128,256]{2,1,0:T(8,128)S(1)}, u32[]{:S(2)}, u32[]{:S(2)}) collective-permute-start(f32[1,128,256]{2,1,0:T(8,128)S(1)} %constant_dynamic-slice_fusion.23), channel_id=1, source_target_pairs={{0,16},{4,20},{8,24},{12,28},{16,0},{20,4},{24,8},{28,12},{1,17},{... | collective-permute-start | bytes 393224 | tf_op jit(solution)/shard_map/ppermute | solution.py:42
  (235 other events, 1620.3 us)

commit v2 on v1

--- a/solution.py
+++ b/solution.py
@@ -3,9 +3,42 @@
 import jax
 import jax.numpy as jnp
 from jax import lax
+from jax.experimental import pallas as pl
+from jax.experimental.pallas import tpu as pltpu
 from jax.sharding import PartitionSpec as P
 
 HEAD_DIM = 64
+Z_FIRST = {("down", 0)}
+PLAN = {
+    ("pre", 0): [("down", 0), ("up", 0)],
+    ("wait_two", 0): [],
+    ("mid", 0): [("out", 0)],
+    ("wait_one", 0): [("down", 0), ("qkv", 0)],
+    ("end", 0): [("up", 0), ("out", 0)],
+    ("pre", 1): [("down", 1)],
+    ("wait_two", 1): [("down", 0), ("qkv", 0), ("up", 0), ("out", 0)],
+    ("mid", 1): [("up", 1), ("out", 1)],
+    ("wait_one", 1): [("qkv", 0), ("down", 1), ("qkv", 1), ("out", 1)],
+    ("end", 1): [("down", 0), ("up", 0), ("out", 0)],
+    "pool": [("qkv", 0), ("up", 1), ("pool_out"), ("pool_value")],
+}
+DRAIN = [
+    ("down", 1),
+    ("qkv", 1),
+    ("out", 1),
+    ("up", 1),
+    ("down", 1),
+    "pool_out",
+    "pool_value",
+    ("qkv", 1),
+    ("out", 1),
+    ("up", 1),
+    "pool_out",
+    "pool_value",
+    ("qkv", 1),
+    "pool_out",
+    "pool_value",
+]
 ROOT_DIM = math.sqrt(HEAD_DIM)
 BF = jnp.bfloat16
 F32 = jnp.float32
@@ -44,6 +77,155 @@
 
 def pick(tensor, index, axis):
     return lax.dynamic_index_in_dim(tensor, index, axis, keepdims=False)
+
+
+def after(value, *earlier):
+    return lax.optimization_barrier((value,) + earlier)[0]
+
+
+def spread(index, bits):
+    return sum(((index >> place) & 1) << bit for place, bit in enumerate(bits))
+
+
+def gradient_blocks(left, right, scale, columns, shard, got=None, got_index=None):
+    count = columns.shape[0]
+    rows, width = right.shape
+    has_got = got is not None
+
+    def kernel(columns_ref, index_ref, scale_ref, left_ref, right_ref, *refs):
+        block = (
+            lax.dot_general(
+                left_ref[...], right_ref[...], (((0,), (0,)), ((), ())), preferred_element_type=F32
+            )
+            * scale_ref[0, 0]
+        )
+        if has_got:
+            block = block + refs[0][0]
+        refs[-1][0] = block
+
+    in_specs = [
+        pl.BlockSpec(memory_space=pltpu.SMEM),
+        pl.BlockSpec((rows, shard), lambda j, columns_ref, index_ref: (0, columns_ref[j])),
+        pl.BlockSpec((rows, width), lambda j, columns_ref, index_ref: (0, 0)),
+    ]
+    operands = [scale, left, right]
+    if has_got:
+        in_specs.append(
+            pl.BlockSpec((1, shard, width), lambda j, columns_ref, index_ref: (index_ref[j], 0, 0))
+        )
+        operands.append(got)
+    return pl.pallas_call(
+        kernel,
+        out_shape=jax.ShapeDtypeStruct((count, shard, width), F32),
+        grid_spec=pltpu.PrefetchScalarGridSpec(
+            num_scalar_prefetch=2,
+            grid=(count,),
+            in_specs=in_specs,
+            out_specs=pl.BlockSpec(
+                (1, shard, width), lambda j, columns_ref, index_ref: (j, 0, 0)
+            ),
+        ),
+        cost_estimate=pl.CostEstimate(
+            flops=2 * count * shard * rows * width,
+            bytes_accessed=4 * count * shard * width * (2 if has_got else 1) + 2 * rows * width,
+            transcendentals=0,
+        ),
+        name="gradient_blocks",
+    )(columns, columns if got_index is None else got_index, *operands)
+
+
+def add_blocks(first, first_index, second, second_index):
+    count = first_index.shape[0]
+    rows, width = first.shape[1:]
+
+    def kernel(first_index_ref, second_index_ref, first_ref, second_ref, out_ref):
+        out_ref[...] = first_ref[...] + second_ref[...]
+
+    block = (1, rows, width)
+    return pl.pallas_call(
+        kernel,
+        out_shape=jax.ShapeDtypeStruct((count, rows, width), F32),
+        grid_spec=pltpu.PrefetchScalarGridSpec(
+            num_scalar_prefetch=2,
+            grid=(count,),
+            in_specs=[
+                pl.BlockSpec(block, lambda j, one, two: (one[j], 0, 0)),
+                pl.BlockSpec(block, lambda j, one, two: (two[j], 0, 0)),
+            ],
+            out_specs=pl.BlockSpec(block, lambda j, one, two: (j, 0, 0)),
+        ),
+        cost_estimate=pl.CostEstimate(
+            flops=count * rows * width, bytes_accessed=12 * count * rows * width, transcendentals=0
+        ),
+        name="add_blocks",
+    )(first_index, second_index, first, second)
+
+
+def norm_rows(own, other, gain, bias):
+    half, width = own.shape
+
+    def kernel(own_ref, other_ref, gain_ref, bias_ref, out_ref):
+        out_ref[:half] = (own_ref[...] * gain_ref[...] + bias_ref[...]).astype(BF)
+        out_ref[half:] = (other_ref[...] * gain_ref[...] + bias_ref[...]).astype(BF)
+
+    return pl.pallas_call(
+        kernel,
+        out_shape=jax.ShapeDtypeStruct((2 * half, width), BF),
+        cost_estimate=pl.CostEstimate(
+            flops=4 * half * width, bytes_accessed=12 * half * width, transcendentals=0
+        ),
+        name="norm_rows",
+    )(own, other, gain[None], bias[None])
+
+
+def merge_rows(own, other, change):
+    half, width = own.shape
+
+    def kernel(own_ref, other_ref, change_ref, other_out, low_out):
+        low_out[:half] = own_ref[...].astype(BF)
+        total = other_ref[...] + change_ref[...]
+        other_out[...] = total
+        low_out[half:] = total.astype(BF)
+
+    return pl.pallas_call(
+        kernel,
+        out_shape=(
+            jax.ShapeDtypeStruct((half, width), F32),
+            jax.ShapeDtypeStruct((2 * half, width), BF),
+        ),
+        cost_estimate=pl.CostEstimate(
+            flops=2 * half * width, bytes_accessed=20 * half * width, transcendentals=0
+        ),
+        name="merge_rows",
+    )(own, other, change)
+
+
+def norm_back(mine, got, unit, inverse, gain, grad):
+    half, width = mine.shape
+
+    def kernel(mine_ref, got_ref, unit_ref, inverse_ref, gain_ref, grad_ref, change_out, grad_out, sums_out):
+        pull = mine_ref[...] + got_ref[...]
+        unit_rows = unit_ref[...]
+        scaled = pull * gain_ref[...]
+        first = jnp.mean(scaled, axis=-1, keepdims=True)
+        second = jnp.mean(scaled * unit_rows, axis=-1, keepdims=True)
+        change = inverse_ref[...] * (scaled - first - unit_rows * second)
+        change_out[...] = change
+        total = grad_ref[...] + change
+        grad_out[...] = total
+        sums_out[0:1] = jnp.sum(pull * unit_rows, axis=0, keepdims=True)
+        sums_out[1:2] = jnp.sum(pull, axis=0, keepdims=True)
+        sums_out[2:3] = jnp.sum(total, axis=0, keepdims=True)
+
+    rows = jax.ShapeDtypeStruct((half, width), F32)
+    return pl.pallas_call(
+        kernel,
+        out_shape=(rows, rows, jax.ShapeDtypeStruct((3, width), F32)),
+        cost_estimate=pl.CostEstimate(
+            flops=14 * half * width, bytes_accessed=24 * half * width, transcendentals=0
+        ),
+        name="norm_back",
+    )(mine, got, unit, inverse, gain[None], grad)
 
 
 class Links:
@@ -58,18 +240,20 @@
     def mp_bit(self, bit):
         return (self.mp_index >> bit) & 1
 
+    def begin_sum(self, partial):
+        half = partial.shape[0] // 2
+        mine = partial[:half] + exchange(partial[half:], "mp", self.mp, 0)
+        last = bit_count(self.mp) - 1
+        for bit in range(1, last):
+            mine = mine + exchange(mine, "mp", self.mp, bit)
+        return mine, exchange(mine, "mp", self.mp, last)
+
     def sum_rows(self, partial):
-        half = partial.shape[0] // 2
-        total = partial[:half] + exchange(partial[half:], "mp", self.mp, 0)
-        for bit in range(1, bit_count(self.mp)):
-            total = total + exchange(total, "mp", self.mp, bit)
-        return total
+        mine, got = self.begin_sum(partial)
+        return mine + got
 
     def other_rows(self, own):
         return exchange(own, "mp", self.mp, 0)
-
-    def both_rows(self, own):
-        return jnp.concatenate([own, self.other_rows(own)], axis=0)
 
     def split_rows(self, tensor):
         half = tensor.shape[0] // 2
@@ -84,8 +268,8 @@
             [jnp.where(core == 0, own, other), jnp.where(core == 0, other, own)], axis=0
         )
 
-    def finish_scatter(self, shards, first_bit):
-        for bit in range(first_bit, bit_count(self.dp)):
+    def scatter_sum(self, shards):
+        for bit in range(bit_count(self.dp)):
             count = shards.shape[0] // 2
             pairs = shards.reshape((count, 2) + shards.shape[1:])
             own = self.dp_bit(bit)
@@ -93,22 +277,71 @@
             shards = pick(pairs, own, 1) + got
         return shards[0]
 
-    def scatter_sum(self, shards):
-        return self.finish_scatter(shards, 0)
-
-    def scatter_product(self, left, right, scale):
-        width = left.shape[1]
-        parts = left.reshape(left.shape[0], self.dp // 2, 2, width // self.dp)
-        own = self.dp_bit(0)
-        keep_left = jnp.where(own == 0, parts[:, :, 0], parts[:, :, 1])
-        send_left = jnp.where(own == 0, parts[:, :, 1], parts[:, :, 0])
-        flat = (left.shape[0], width // 2)
-        send = matmul_tn(send_left.reshape(flat), right) * scale
-        got = exchange(send, "dp", self.dp, 0)
-        total = matmul_tn(keep_left.reshape(flat), right) * scale + got
-        return self.finish_scatter(
-            total.reshape(self.dp // 2, width // self.dp, right.shape[1]), 1
-        )
+
+class Merge:
+    def __init__(self, links, left, right, scale, order):
+        self.links, self.left, self.right, self.scale = links, left, right, scale
+        self.order = list(order)
+        self.shard = left.shape[1] // links.dp
+        self.step = 0
+        self.got = None
+        self.keep = None
+
+    def entries(self, fixed, left_bits):
+        count = 1 << len(left_bits)
+        return jnp.array([spread(j, left_bits) for j in range(count)], jnp.int32) + fixed
+
+    def advance(self, *earlier):
+        links = self.links
+        done = self.order[: self.step]
+        bits = sorted(self.order[self.step - 1 :] if self.step else self.order)
+        fixed = sum((links.dp_bit(bit) << bit for bit in done), jnp.int32(0))
+        if self.step == 0:
+            bit = self.order[0]
+            rest = sorted(b for b in self.order if b != bit)
+            left = after(self.left, *earlier) if earlier else self.left
+            send = self.blocks(left, self.entries((1 - links.dp_bit(bit)) << bit, rest))
+        elif self.step < len(self.order):
+            bit = self.order[self.step]
+            before = sorted(self.order[self.step :])
+            place = before.index(bit)
+            rest = [b for b in before if b != bit]
+            slots = [before.index(b) for b in rest]
+            other = self.entries((1 - links.dp_bit(bit)) << place, slots)
+            same = self.entries(links.dp_bit(bit) << place, slots)
+            got = after(self.got, *earlier) if earlier else self.got
+            if self.step == 1:
+                first = self.order[0]
+                base = links.dp_bit(first) << first
+                flip = (1 - links.dp_bit(bit)) << bit
+                send = self.blocks(self.left, self.entries(base + flip, rest), got, other)
+                hold = links.dp_bit(bit) << bit
+                self.keep = self.blocks(
+                    self.left, self.entries(base + hold, rest), after(got, send), same
+                )
+            else:
+                send = add_blocks(self.keep, other, got, other)
+                self.keep = add_blocks(self.keep, same, after(got, send), same)
+        else:
+            got = after(self.got, *earlier) if earlier else self.got
+            self.step += 1
+            self.result = self.keep[0] + got[0]
+            return self.result
+        self.got = exchange(send, "dp", links.dp, self.order[self.step])
+        self.step += 1
+        return send
+
+    def blocks(self, left, columns, got=None, got_index=None):
+        if self.shard % 128 == 0:
+            return gradient_blocks(
+                left, self.right, self.scale, columns, self.shard, got, got_index
+            )
+        rows = left.reshape(left.shape[0], -1, self.shard)[:, columns]
+        block = (
+            jnp.einsum("rcs,rn->csn", rows, self.right, preferred_element_type=F32)
+            * self.scale[0, 0]
+        )
+        return block if got is None else block + got[got_index]
 
 
 def norm_parts(rows):
@@ -117,13 +350,6 @@
     spread = jnp.mean(centred * centred, axis=-1, keepdims=True)
     inverse = lax.rsqrt(spread + 1e-05)
     return centred * inverse, inverse
-
-
-def norm_back(grad, gain, unit, inverse):
-    scaled = grad * gain
-    first = jnp.mean(scaled, axis=-1, keepdims=True)
-    second = jnp.mean(scaled * unit, axis=-1, keepdims=True)
-    return inverse * (scaled - first - unit * second)
 
 
 def make_per_device(dp, mp):
@@ -177,10 +403,6 @@
         mask_row = jnp.sum(jnp.where(dataset_pick[:, None], variable_mask, 0), axis=0)
         item_weight = jnp.sum(jnp.where(dataset_pick, dataset_weight, 0)).astype(F32)
         own_count = token_counts[0].astype(F32)
-        count_total = jnp.full((8, 128), own_count, F32)
-        for bit in range(bit_count(dp)):
-            count_total = count_total + exchange(count_total, "dp", dp, bit)
-        item_scale = item_weight * own_count / count_total[0, 0]
         lead_scale = lead_hours[0].astype(F32) / 24.0
 
         pix_rows = pixels[0].reshape(flat_count, row_count).T
@@ -238,15 +460,24 @@
         ) + jnp.einsum("hrv,hvd->hrd", probs_low, value_var, preferred_element_type=F32)
         pooled = heads_last(pooled).astype(BF)
 
-        hidden = links.sum_rows(matmul(pooled, pool_output_weight)) + pool_output_bias
+        mine, got = links.begin_sum(matmul(pooled, pool_output_weight))
+        count_total = after(jnp.full((8, 128), own_count, F32), mine)
+        for bit in range(bit_count(dp)):
+            count_total = count_total + exchange(count_total, "dp", dp, bit)
+        item_scale = item_weight * own_count / count_total[0, 0]
+        scale_cell = item_scale.reshape(1, 1)
         position_own = links.split_rows(position_embed)[0]
-        hidden = hidden + position_own + lead_scale * lead_weight + lead_bias
+        offset_rows = pool_output_bias + position_own + lead_scale * lead_weight + lead_bias
+        mine, scale_cell = lax.optimization_barrier((mine, scale_cell))
+        hidden = mine + got + offset_rows
 
         kept = []
         for layer in range(layer_count):
+            last = layer == layer_count - 1
             unit_one, inverse_one = norm_parts(hidden)
-            normed = links.both_rows(unit_one) * norm_gain[layer, 0] + norm_bias[layer, 0]
-            normed = normed.astype(BF)
+            normed = norm_rows(
+                unit_one, links.other_rows(unit_one), norm_gain[layer, 0], norm_bias[layer, 0]
+            )
             queries = (
                 matmul(normed, attention_weight[layer, 0]) + attention_bias[layer, 0]
             ).astype(BF)
@@ -268,21 +499,25 @@
             mixed = heads_last(
                 jnp.einsum("hpk,hkd->hpd", attend_low, value_three, preferred_element_type=F32)
             ).astype(BF)
-            hidden = (
-                hidden
-                + links.sum_rows(matmul(mixed, output_weight[layer]))
-                + output_bias[layer]
-            )
+            mine, got = links.begin_sum(matmul(mixed, output_weight[layer]))
+            if layer == 0:
+                grad_own, grad_other = links.split_rows(after(cotangent[0], mine))
+                ones = jnp.ones((model_width,), F32)
+                down_low = norm_rows(grad_own, grad_other, ones, jnp.zeros_like(ones))
+                mine, down_low = lax.optimization_barrier((mine, down_low))
+            hidden = hidden + (mine + got) + output_bias[layer]
             unit_two, inverse_two = norm_parts(hidden)
-            normed_two = links.both_rows(unit_two) * norm_gain[layer, 1] + norm_bias[layer, 1]
-            normed_two = normed_two.astype(BF)
+            normed_two = norm_rows(
+                unit_two, links.other_rows(unit_two), norm_gain[layer, 1], norm_bias[layer, 1]
+            )
             pre_act = matmul(normed_two, up_weight[layer]) + up_bias[layer]
             activation = gelu_exact(pre_act).astype(BF)
-            hidden = (
-                hidden
-                + links.sum_rows(matmul(activation, down_weight[layer]))
-                + down_bias[layer]
-            )
+            if not last:
+                mine, got = links.begin_sum(matmul(activation, down_weight[layer]))
+                if layer == 0:
+                    top_grad = matmul_nt(after(down_low, mine), down_weight[layer_count - 1])
+                    mine, top_grad = lax.optimization_barrier((mine, top_grad))
+                hidden = hidden + (mine + got) + down_bias[layer]
             kept.append(
                 (
                     unit_one,
@@ -301,13 +536,28 @@
                     activation,
                 )
             )
-        layer_out = links.global_rows(hidden, links.other_rows(hidden))
-
-        grad_own, grad_other = links.split_rows(cotangent[0])
+        last_partial = matmul(activation, down_weight[layer_count - 1])
+
         row_sums = {}
         local_sums = {}
-        weight_grads = [None] * layer_count
+        merges = {}
+        top = layer_count - 1
+        row_sums["down_bias", top] = jnp.sum(grad_own, axis=0)
+
+        def add_merge(name, left, right):
+            order = list(range(bit_count(dp)))
+            if name in Z_FIRST:
+                order = order[1:] + order[:1]
+            merges[name] = Merge(links, left, right, scale_cell, order)
+
+        def advance(spot, critical):
+            for name in PLAN.get(spot, ()):
+                if name in merges:
+                    critical = after(critical, merges[name].advance(critical))
+            return critical
+
         for layer in reversed(range(layer_count)):
+            depth = top - layer
             (
                 unit_one,
                 inverse_one,
@@ -324,22 +574,24 @@
                 pre_act,
                 activation,
             ) = kept[layer]
-            down_low = jnp.concatenate([grad_own, grad_other], axis=0).astype(BF)
-            row_sums["down_bias", layer] = jnp.sum(grad_own, axis=0)
-            grad_activation = matmul_nt(down_low, down_weight[layer])
+            grad_activation = top_grad if layer == top else matmul_nt(down_low, down_weight[layer])
             grad_pre = jax.vjp(gelu_exact, pre_act)[1](grad_activation)[0]
             local_sums["up_bias", layer] = jnp.sum(grad_pre, axis=0)
             pre_low = grad_pre.astype(BF)
-            grad_two = links.sum_rows(matmul_nt(pre_low, up_weight[layer]))
-            down_grad = links.scatter_product(down_low, activation, item_scale)
-            up_grad = links.scatter_product(normed_two, pre_low, item_scale)
-            row_sums["gain", layer, 1] = jnp.sum(grad_two * unit_two, axis=0)
-            row_sums["bias", layer, 1] = jnp.sum(grad_two, axis=0)
-            change = norm_back(grad_two, norm_gain[layer, 1], unit_two, inverse_two)
-            grad_own = grad_own + change
-            grad_other = grad_other + links.other_rows(change)
-            out_low = jnp.concatenate([grad_own, grad_other], axis=0).astype(BF)
-            row_sums["out_bias", layer] = jnp.sum(grad_own, axis=0)
+            add_merge(("down", depth), down_low, activation)
+            add_merge(("up", depth), normed_two, pre_low)
+            pre_low = advance(("pre", depth), pre_low)
+            mine, got = links.begin_sum(matmul_nt(pre_low, up_weight[layer]))
+            mine = advance(("wait_two", depth), mine)
+            change, grad_own, sums = norm_back(
+                mine, got, unit_two, inverse_two, norm_gain[layer, 1], grad_own
+            )
+            row_sums["gain", layer, 1] = sums[0]
+            row_sums["bias", layer, 1] = sums[1]
+            row_sums["out_bias", layer] = sums[2]
+            grad_other, out_low = merge_rows(grad_own, grad_other, links.other_rows(change))
+            add_merge(("out", depth), out_low, mixed)
+            out_low = advance(("mid", depth), out_low)
             grad_mixed = heads_first(matmul_nt(out_low, output_weight[layer]).astype(BF))
             grad_attend = jnp.einsum(
                 "hpd,hkd->hpk", grad_mixed, value_three, preferred_element_type=F32
@@ -365,22 +617,22 @@
             partial = matmul_nt(grad_three[0], attention_weight[layer, 0])
             partial = partial + matmul_nt(grad_three[1], attention_weight[layer, 1])
             partial = partial + matmul_nt(grad_three[2], attention_weight[layer, 2])
-            grad_one = links.sum_rows(partial)
-            out_grad = links.scatter_product(out_low, mixed, item_scale)
-            qkv_grad = links.scatter_product(
-                normed, jnp.concatenate(grad_three, axis=1), item_scale
-            )
-            row_sums["gain", layer, 0] = jnp.sum(grad_one * unit_one, axis=0)
-            row_sums["bias", layer, 0] = jnp.sum(grad_one, axis=0)
-            change = norm_back(grad_one, norm_gain[layer, 0], unit_one, inverse_one)
-            grad_own = grad_own + change
-            grad_other = grad_other + links.other_rows(change)
-            weight_grads[layer] = (down_grad, up_grad, out_grad, qkv_grad)
-
-        column_sum = jnp.sum(grad_own, axis=0)
-        row_sums["column"] = column_sum
-        row_sums["lead"] = lead_scale * column_sum
-        pool_grad_low = jnp.concatenate([grad_own, grad_other], axis=0).astype(BF)
+            mine, got = links.begin_sum(partial)
+            add_merge(("qkv", depth), normed, jnp.concatenate(grad_three, axis=1))
+            mine = advance(("wait_one", depth), mine)
+            change, grad_own, sums = norm_back(
+                mine, got, unit_one, inverse_one, norm_gain[layer, 0], grad_own
+            )
+            row_sums["gain", layer, 0] = sums[0]
+            row_sums["bias", layer, 0] = sums[1]
+            if layer:
+                row_sums["down_bias", layer - 1] = sums[2]
+            grad_other, down_low = merge_rows(grad_own, grad_other, links.other_rows(change))
+            down_low = advance(("end", depth), down_low)
+
+        row_sums["column"] = sums[2]
+        row_sums["lead"] = lead_scale * sums[2]
+        pool_grad_low = down_low
         grad_pooled = heads_first(matmul_nt(pool_grad_low, pool_output_weight).astype(BF))
         pull_flat = jnp.einsum("hrd,hkd->hrk", grad_pooled, value_flat, preferred_element_type=F32)
         pull_high, pull_rest = two_part(pull_flat * pix_value[None])
@@ -451,12 +703,26 @@
             embed_grad = pick(pairs, own, 1) + exchange(pick(pairs, 1 - own, 1), "mp", mp, bit)
         embed_grad = links.scatter_sum(embed_grad[0])
 
-        pool_out_grad = links.scatter_product(pool_grad_low, pooled, item_scale)
-        value_weight_grad = links.scatter_product(
+        add_merge("pool_out", pool_grad_low, pooled)
+        merges["pool_value"] = Merge(
+            links,
             embed_all,
             jnp.concatenate([value_grad_flat, value_grad_var, value_grad_var], axis=0),
-            jnp.float32(1.0),
-        )
+            jnp.ones((1, 1), F32),
+            list(range(bit_count(dp))),
+        )
+        marker = value_grad_flat
+        marker = advance("pool", marker)
+        for name in DRAIN:
+            marker = after(marker, merges[name].advance(marker))
+        weight_grads = {}
+        for name, merge in merges.items():
+            while merge.step <= bit_count(dp):
+                result = merge.advance()
+            weight_grads[name] = merge.result
+        last_mine, last_got = links.begin_sum(last_partial)
+        hidden = hidden + (last_mine + last_got) + down_bias[top]
+        layer_out = links.global_rows(hidden, links.other_rows(hidden))
         position = (grad_own * item_scale).reshape(row_count // 2, dp, shard).transpose(1, 0, 2)
         position = links.scatter_sum(position)
         position = links.global_rows(position, links.other_rows(position))
@@ -517,7 +783,6 @@
             jnp.repeat(key_shard, HEAD_DIM, axis=1) * query_vec.astype(F32)[None, :] / ROOT_DIM
         )
         embed_turned = embed_grad.T
-        hidden_width = weight_grads[0][0].shape[1]
         return (
             layer_out[None],
             pixel_grad,
@@ -527,9 +792,9 @@
             embed_turned[flat_all],
             query_weight_grad,
             key_weight_grad,
-            value_weight_grad,
+            weight_grads["pool_value"],
             thin_total[-1],
-            pool_out_grad.T,
+            weight_grads["pool_out"].T,
             column_total,
             lead_total,
             column_total,
@@ -537,16 +802,24 @@
             biases,
             jnp.stack(
                 [
-                    grads[3].reshape(shard, 3, local_width).transpose(1, 0, 2)
-                    for grads in weight_grads
+                    weight_grads["qkv", top - layer]
+                    .reshape(shard, 3, local_width)
+                    .transpose(1, 0, 2)
+                    for layer in range(layer_count)
                 ]
             ),
             thin_total[:-1].reshape(layer_count, 2, local_width // dp),
-            jnp.stack([grads[2].T for grads in weight_grads]),
+            jnp.stack(
+                [weight_grads["out", top - layer].T for layer in range(layer_count)]
+            ),
             dense_bias[:, 0],
-            jnp.stack([grads[1] for grads in weight_grads]),
+            jnp.stack(
+                [weight_grads["up", top - layer] for layer in range(layer_count)]
+            ),
             up_bias_total,
-            jnp.stack([grads[0].T for grads in weight_grads]),
+            jnp.stack(
+                [weight_grads["down", top - layer].T for layer in range(layer_count)]
+            ),
             dense_bias[:, 1],
         )
 

time: 837 us -> 828 us (0.989)
  Pallas kernels: 0 us -> 189 us
  local copies, waits for them, and re-layouts: 162 us -> 83.7 us
  waiting for transfers between devices: 343 us -> 269 us
  matrix products: 133 us -> 103 us
  other arithmetic: 105 us -> 90.1 us
    pallas_call x0 -> x63, Pallas kernels: none -> 189 us  [the longest x30 114 us: gradient_blocks(): pl.pallas_call(kernel, out_shape=jax.ShapeDtypeStruct((count, shard, widt...]
    concatenate x42 -> x0, local copies, waits for them, and re-layouts: 79.7 us -> none  [the longest x16 37.5 us: both_rows(): return jnp.concatenate([own, self.other_rows(own)], axis=0)]
    ppermute x76, waiting for transfers between devices: 343 us -> 269 us  [exchange(): return lax.ppermute(tensor, axis, [(i, i ^ 1 << bit) for i in range(size)])]
    dot_general x22 -> x2, matrix products: 40.9 us -> 1.56 us  [matmul_tn(): lax.dot_general(left, right, (((0,), (0,)), ((), ())), preferred_element_...]
    dynamic_slice x26 -> x5, local copies, waits for them, and re-layouts: 26.6 us -> 3.1 us  [pick(): return lax.dynamic_index_in_dim(tensor, index, axis, keepdims=False)]
    convert_element_type x0 -> x10, local copies, waits for them, and re-layouts: none -> 16.6 us  [the longest x6 10.4 us: per_device(): part.astype(BF)]
    select_n x10 -> x0, other arithmetic: 14.1 us -> none  [scatter_product(): keep_left = jnp.where(own == 0, parts[:, :, 0], parts[:, :, 1])]
    unnamed x423 -> x302, local copies, waits for them, and re-layouts: 20.9 us -> 30 us
  transfers between devices with their start and end apart: 76 -> 76, of which waited for: 34 -> 33; matrix products, arithmetic and copies ran while one was open for 40% -> 19% of each run, Pallas kernels for 0% -> 19%
where the time goes in v2:
time: 828 us; the launch traced here: 814 us
  waiting for transfers between devices  269 us (32%)
  Pallas kernels  189 us (23%)
  matrix products  103 us (12%)
  other arithmetic  90.1 us (11%)
  local copies, waits for them, and re-layouts  83.7 us (10%)
  starting transfers between devices  73.3 us (9%)
    ppermute x76, waiting for transfers between devices, exchange(): return lax.ppermute(tensor, axis, [(i, i ^ 1 << bit) for i in range(size)])  269 us
    pallas_call x30, Pallas kernels, gradient_blocks(): pl.pallas_call(kernel, out_shape=jax.ShapeDtypeStruct((count, shard, widt...  114 us
    ppermute x76, starting transfers between devices, exchange(): return lax.ppermute(tensor, axis, [(i, i ^ 1 << bit) for i in range(size)])  73.3 us
    pallas_call x20, Pallas kernels, add_blocks(): pl.pallas_call(kernel, out_shape=jax.ShapeDtypeStruct((count, rows, width...  37.2 us
    dot_general x16, matrix products, matmul(): return jnp.dot(left, right, preferred_element_type=F32)  32.6 us
    unnamed x302, local copies, waits for them, and re-layouts  30 us
    dot_general x15, matrix products, matmul_nt(): lax.dot_general(left, right, (((1,), (1,)), ((), ())), preferred_element_...  24.6 us
  transfers between devices with their start and end apart: 76, of which 33 were waited for; matrix products, arithmetic and copies ran while one was open for 19% of the time, Pallas kernels for 19%

profile of v2, /device:TPU:0, one launch (start us, length us, event | category | flops | bytes accessed | tf_op | source)
XLA Modules:
  0.0 814.5 jit_solution(6891592460817685334)
XLA Ops:
  21.3 4.2 fusion.145
  27.2 4.1 fusion.135
  54.8 4.5 collective-permute-done.4
  92.8 12.7 %collective-permute-done.7 = f32[192,1024]{1,0:T(8,128)} collective-permute-done((f32[192,1024]{1,0:T(8,128)}, f32[192,1024]{1,0:T(8,128)}, u32[]{:S(2)}, u32[]{:S(2)}) %collective-permute-start.7) | collective-permute-done | bytes 786464 | tf_op jit(solution)/shard_map/ppermute | solution.py:75
  114.8 7.9 multiply_convert_fusion.6
  130.3 15.6 %collective-permute-done.10 = f32[192,1024]{1,0:T(8,128)S(1)} collective-permute-done((f32[192,1024]{1,0:T(8,128)S(1)}, f32[192,1024]{1,0:T(8,128)S(1)}, u32[]{:S(2)}, u32[]{:S(2)}) %collective-permute-start.10) | collective-permute-done | bytes 786464 | tf_op jit(solution)/shard_map/ppermute | solution.py:75
  171.2 17.8 %collective-permute-done.13 = f32[192,1024]{1,0:T(8,128)S(1)} collective-permute-done((f32[192,1024]{1,0:T(8,128)S(1)}, f32[192,1024]{1,0:T(8,128)S(1)}, u32[]{:S(2)}, u32[]{:S(2)}) %collective-permute-start.13) | collective-permute-done | bytes 786464 | tf_op jit(solution)/shard_map/ppermute | solution.py:75
  199.1 5.0 fusion.214
  205.4 5.1 gradient_blocks.30
  210.5 5.1 gradient_blocks.31
  224.4 17.4 %collective-permute-done.19.got_ref = f32[192,1024]{1,0:T(8,128)} collective-permute-done((f32[192,1024]{1,0:T(8,128)}, f32[192,1024]{1,0:T(8,128)}, u32[]{:S(2)}, u32[]{:S(2)}) %collective-permute-start.19) | collective-permute-done | bytes 786464 | tf_op jit(solution)/shard_map/ppermute | solution.py:75
  241.7 3.5 norm_back.4
  251.8 4.4 gradient_blocks.32
  279.1 16.3 %collective-permute-done.22.refs_0_ = f32[4,128,1024]{2,1,0:T(8,128)} collective-permute-done((f32[4,128,1024]{2,1,0:T(8,128)}, f32[4,128,1024]{2,1,0:T(8,128)}, u32[]{:S(2)}, u32[]{:S(2)}) %collective-permute-start.22) | collective-permute-done | bytes 2097184 | tf_op jit(solution)/shard_map/ppermute | solution.py:75
  295.5 3.5 gradient_blocks.33
  299.0 4.9 gradient_blocks.34
  303.9 3.6 norm_back.5
  314.3 3.5 gradient_blocks.35
  317.9 7.0 collective-permute-done.26.refs_0_
  327.8 5.1 fusion.223
  332.9 5.3 gradient_blocks.37
  358.3 38.3 %collective-permute-done.28.second_ref = f32[2,128,1024]{2,1,0:T(8,128)} collective-permute-done((f32[2,128,1024]{2,1,0:T(8,128)}, f32[2,128,1024]{2,1,0:T(8,128)}, u32[]{:S(2)}, u32[]{:S(2)}) %collective-permute-start.28) | collective-permute-done | bytes 1048608 | tf_op jit(solution)/shard_map/ppermute | solution.py:75
  398.6 3.5 gradient_blocks.38.first_ref
  405.0 3.5 gradient_blocks.40.first_ref
  410.6 3.4 gradient_blocks.39
  417.7 3.5 norm_back.6
  432.6 5.1 gradient_blocks.42
  437.6 4.4 gradient_blocks.43
  467.4 3.4 gradient_blocks.44.first_ref
  479.9 3.5 gradient_blocks.45
  483.4 4.9 gradient_blocks.46
  514.4 3.5 gradient_blocks.59.first_ref
  519.6 3.5 norm_back.7
  531.0 30.1 %collective-permute-done.50 = f32[4,192,128]{2,1,0:T(8,128)} collective-permute-done((f32[4,192,128]{2,1,0:T(8,128)}, f32[4,192,128]{2,1,0:T(8,128)}, u32[]{:S(2)}, u32[]{:S(2)}) %collective-permute-start.50) | collective-permute-done | bytes 393248 | tf_op jit(solution)/shard_map/ppermute | solution.py:75
  562.7 5.4 collective-permute-done.51
  578.8 3.6 gradient_blocks.48
  582.4 3.5 gradient_blocks.58.first_ref
  585.9 6.3 collective-permute-done.52
  598.9 4.4 multiply_reduce_fusion
  608.4 17.5 %collective-permute-done.41 = f32[1,128,256]{2,1,0:T(8,128)} collective-permute-done((f32[1,128,256]{2,1,0:T(8,128)}, f32[1,128,256]{2,1,0:T(8,128)}, u32[]{:S(2)}, u32[]{:S(2)}) %collective-permute-start.41) | collective-permute-done | bytes 131104 | tf_op jit(solution)/shard_map/ppermute | solution.py:75
  626.4 10.8 %collective-permute-done.75 = f32[1,128,1024]{2,1,0:T(8,128)} collective-permute-done((f32[1,128,1024]{2,1,0:T(8,128)}, f32[1,128,1024]{2,1,0:T(8,128)}, u32[]{:S(2)}, u32[]{:S(2)}) %collective-permute-start.75) | collective-permute-done | bytes 524320 | tf_op jit(solution)/shard_map/ppermute | solution.py:75
  651.7 3.8 multiply_convert_fusion.7
  655.5 3.4 gradient_blocks.55
  659.0 4.7 gradient_blocks.49
  683.8 4.7 gradient_blocks.50
  750.4 31.5 %collective-permute-done.61 = f32[1,128,256]{2,1,0:T(8,128)S(1)} collective-permute-done((f32[1,128,256]{2,1,0:T(8,128)S(1)}, f32[1,128,256]{2,1,0:T(8,128)S(1)}, u32[]{:S(2)}, u32[]{:S(2)}) %collective-permute-start.61) | collective-permute-done | bytes 131104 | tf_op jit(solution)/shard_map/ppermute | solution.py:75
  793.2 3.7 collective-permute-done.47
  799.2 4.8 collective-permute-done.48
  (749 shorter events, 432.6 us)
Async XLA Ops:
  38.3 21.0 %collective-permute-start.4 = (f32[192,1024]{1,0:T(8,128)}, f32[192,1024]{1,0:T(8,128)}, u32[]{:S(2)}, u32[]{:S(2)}) collective-permute-start(f32[192,1024]{1,0:T(8,128)} %slice_add_fusion.8), channel_id=1, source_target_pairs={{0,2},{1,3},{2,0},{3,1},{4,6},{5,7},{6,4},{7,5},{8,10},{9,11},{10,... | collective-permute-start | bytes 2359304 | tf_op jit(solution)/shard_map/ppermute | solution.py:75
  85.6 19.9 %collective-permute-start.7 = (f32[192,1024]{1,0:T(8,128)}, f32[192,1024]{1,0:T(8,128)}, u32[]{:S(2)}, u32[]{:S(2)}) collective-permute-start(f32[192,1024]{1,0:T(8,128)} %slice_add_fusion.7), channel_id=1, source_target_pairs={{0,2},{1,3},{2,0},{3,1},{4,6},{5,7},{6,4},{7,5},{8,10},{9,11},{10,... | collective-permute-start | bytes 2359304 | tf_op jit(solution)/shard_map/ppermute | solution.py:75
  126.3 19.7 %collective-permute-start.10 = (f32[192,1024]{1,0:T(8,128)S(1)}, f32[192,1024]{1,0:T(8,128)S(1)}, u32[]{:S(2)}, u32[]{:S(2)}) collective-permute-start(f32[192,1024]{1,0:T(8,128)S(1)} %slice_add_fusion.6), channel_id=1, source_target_pairs={{0,2},{1,3},{2,0},{3,1},{4,6},{5,7},{6,4},{7,5},{8,10},{9,11},{10,... | collective-permute-start | bytes 2359304 | tf_op jit(solution)/shard_map/ppermute | solution.py:75
  169.4 19.6 %collective-permute-start.13 = (f32[192,1024]{1,0:T(8,128)S(1)}, f32[192,1024]{1,0:T(8,128)S(1)}, u32[]{:S(2)}, u32[]{:S(2)}) collective-permute-start(f32[192,1024]{1,0:T(8,128)S(1)} %slice_add_fusion.5), channel_id=1, source_target_pairs={{0,2},{1,3},{2,0},{3,1},{4,6},{5,7},{6,4},{7,5},{8,10},{9,11},{10,... | collective-permute-start | bytes 2359304 | tf_op jit(solution)/shard_map/ppermute | solution.py:75
  221.8 19.9 %collective-permute-start.19 = (f32[192,1024]{1,0:T(8,128)}, f32[192,1024]{1,0:T(8,128)}, u32[]{:S(2)}, u32[]{:S(2)}) collective-permute-start(f32[192,1024]{1,0:T(8,128)} %slice_add_fusion.3.mine_ref), channel_id=1, source_target_pairs={{0,2},{1,3},{2,0},{3,1},{4,6},{5,7},{6,4},{7,5},{8,10},{9,11},{10,... | collective-permute-start | bytes 2359304 | tf_op jit(solution)/shard_map/ppermute | solution.py:75
  247.0 48.4 %collective-permute-start.22 = (f32[4,128,1024]{2,1,0:T(8,128)}, f32[4,128,1024]{2,1,0:T(8,128)}, u32[]{:S(2)}, u32[]{:S(2)}) collective-permute-start(f32[4,128,1024]{2,1,0:T(8,128)} %gradient_blocks.30), channel_id=1, source_target_pairs={{0,8},{4,12},{8,0},{12,4},{16,24},{20,28},{24,16},{28,20},{1,9},{5... | collective-permute-start | bytes 6291464 | tf_op jit(solution)/shard_map/ppermute | solution.py:75
  265.6 48.8 %collective-permute-start.25 = (f32[4,128,1024]{2,1,0:T(8,128)}, f32[4,128,1024]{2,1,0:T(8,128)}, u32[]{:S(2)}, u32[]{:S(2)}) collective-permute-start(f32[4,128,1024]{2,1,0:T(8,128)} %gradient_blocks.31), channel_id=1, source_target_pairs={{0,4},{4,0},{8,12},{12,8},{16,20},{20,16},{24,28},{28,24},{1,5},{5... | collective-permute-start | bytes 6291464 | tf_op jit(solution)/shard_map/ppermute | solution.py:75
  268.6 35.2 %collective-permute-start.23 = (f32[192,1024]{1,0:T(8,128)}, f32[192,1024]{1,0:T(8,128)}, u32[]{:S(2)}, u32[]{:S(2)}) collective-permute-start(f32[192,1024]{1,0:T(8,128)} %slice_add_fusion.2.mine_ref), channel_id=1, source_target_pairs={{0,2},{1,3},{2,0},{3,1},{4,6},{5,7},{6,4},{7,5},{8,10},{9,11},{10,... | collective-permute-start | bytes 2359304 | tf_op jit(solution)/shard_map/ppermute | solution.py:75
  307.4 17.5 %collective-permute-start.26 = (f32[4,128,256]{2,1,0:T(8,128)}, f32[4,128,256]{2,1,0:T(8,128)}, u32[]{:S(2)}, u32[]{:S(2)}) collective-permute-start(f32[4,128,256]{2,1,0:T(8,128)} %gradient_blocks.32), channel_id=1, source_target_pairs={{0,4},{4,0},{8,12},{12,8},{16,20},{20,16},{24,28},{28,24},{1,5},{5... | collective-permute-start | bytes 1572872 | tf_op jit(solution)/shard_map/ppermute | solution.py:75
  342.6 68.0 %collective-permute-start.29 = (f32[4,128,768]{2,1,0:T(8,128)}, f32[4,128,768]{2,1,0:T(8,128)}, u32[]{:S(2)}, u32[]{:S(2)}) collective-permute-start(f32[4,128,768]{2,1,0:T(8,128)} %gradient_blocks.34), channel_id=1, source_target_pairs={{0,4},{4,0},{8,12},{12,8},{16,20},{20,16},{24,28},{28,24},{1,5},{5... | collective-permute-start | bytes 4718600 | tf_op jit(solution)/shard_map/ppermute | solution.py:75
  347.2 49.4 %collective-permute-start.28 = (f32[2,128,1024]{2,1,0:T(8,128)}, f32[2,128,1024]{2,1,0:T(8,128)}, u32[]{:S(2)}, u32[]{:S(2)}) collective-permute-start(f32[2,128,1024]{2,1,0:T(8,128)} %gradient_blocks.33), channel_id=1, source_target_pairs={{0,16},{4,20},{8,24},{12,28},{16,0},{20,4},{24,8},{28,12},{1,17},{... | collective-permute-start | bytes 3145736 | tf_op jit(solution)/shard_map/ppermute | solution.py:75
  349.8 64.1 %collective-permute-start.30 = (f32[2,128,1024]{2,1,0:T(8,128)}, f32[2,128,1024]{2,1,0:T(8,128)}, u32[]{:S(2)}, u32[]{:S(2)}) collective-permute-start(f32[2,128,1024]{2,1,0:T(8,128)} %gradient_blocks.35), channel_id=1, source_target_pairs={{0,8},{4,12},{8,0},{12,4},{16,24},{20,28},{24,16},{28,20},{1,9},{5... | collective-permute-start | bytes 3145736 | tf_op jit(solution)/shard_map/ppermute | solution.py:75
  353.1 64.6 %collective-permute-start.32 = (f32[192,1024]{1,0:T(8,128)}, f32[192,1024]{1,0:T(8,128)}, u32[]{:S(2)}, u32[]{:S(2)}) collective-permute-start(f32[192,1024]{1,0:T(8,128)} %slice_add_fusion.1.mine_ref), channel_id=1, source_target_pairs={{0,2},{1,3},{2,0},{3,1},{4,6},{5,7},{6,4},{7,5},{8,10},{9,11},{10,... | collective-permute-start | bytes 2359304 | tf_op jit(solution)/shard_map/ppermute | solution.py:75
  357.2 68.7 %collective-permute-start.16 = (f32[192,1024]{1,0:T(8,128)}, f32[192,1024]{1,0:T(8,128)}, u32[]{:S(2)}, u32[]{:S(2)}) collective-permute-start(f32[192,1024]{1,0:T(8,128)} %slice_add_fusion.4), channel_id=1, source_target_pairs={{0,2},{1,3},{2,0},{3,1},{4,6},{5,7},{6,4},{7,5},{8,10},{9,11},{10,... | collective-permute-start | bytes 2359304 | tf_op jit(solution)/shard_map/ppermute | solution.py:75
  396.6 19.4 %collective-permute-start.31 = (f32[2,128,256]{2,1,0:T(8,128)}, f32[2,128,256]{2,1,0:T(8,128)}, u32[]{:S(2)}, u32[]{:S(2)}) collective-permute-start(f32[2,128,256]{2,1,0:T(8,128)} %gradient_blocks.36), channel_id=1, source_target_pairs={{0,8},{4,12},{8,0},{12,4},{16,24},{20,28},{24,16},{28,20},{1,9},{5... | collective-permute-start | bytes 786440 | tf_op jit(solution)/shard_map/ppermute | solution.py:75
  428.7 29.3 %collective-permute-start.17 = (f32[192,1024]{1,0:T(8,128)}, f32[192,1024]{1,0:T(8,128)}, u32[]{:S(2)}, u32[]{:S(2)}) collective-permute-start(f32[192,1024]{1,0:T(8,128)} %add_add_fusion.2), channel_id=1, source_target_pairs={{0,1},{1,0},{2,3},{3,2},{4,5},{5,4},{6,7},{7,6},{8,9},{9,8},{10,11... | collective-permute-start | bytes 2359304 | tf_op jit(solution)/shard_map/ppermute | solution.py:75
  429.2 50.7 %collective-permute-start.36 = (f32[4,128,1024]{2,1,0:T(8,128)}, f32[4,128,1024]{2,1,0:T(8,128)}, u32[]{:S(2)}, u32[]{:S(2)}) collective-permute-start(f32[4,128,1024]{2,1,0:T(8,128)} %gradient_blocks.37), channel_id=1, source_target_pairs={{0,4},{4,0},{8,12},{12,8},{16,20},{20,16},{24,28},{28,24},{1,5},{5... | collective-permute-start | bytes 6291464 | tf_op jit(solution)/shard_map/ppermute | solution.py:75
  456.0 22.0 %collective-permute-start.35 = (f32[2,128,768]{2,1,0:T(8,128)}, f32[2,128,768]{2,1,0:T(8,128)}, u32[]{:S(2)}, u32[]{:S(2)}) collective-permute-start(f32[2,128,768]{2,1,0:T(8,128)} %gradient_blocks.39), channel_id=1, source_target_pairs={{0,8},{4,12},{8,0},{12,4},{16,24},{20,28},{24,16},{28,20},{1,9},{5... | collective-permute-start | bytes 2359304 | tf_op jit(solution)/shard_map/ppermute | solution.py:75
  459.5 28.8 %collective-permute-start.37 = (f32[4,128,256]{2,1,0:T(8,128)}, f32[4,128,256]{2,1,0:T(8,128)}, u32[]{:S(2)}, u32[]{:S(2)}) collective-permute-start(f32[4,128,256]{2,1,0:T(8,128)} %gradient_blocks.43), channel_id=1, source_target_pairs={{0,4},{4,0},{8,12},{12,8},{16,20},{20,16},{24,28},{28,24},{1,5},{5... | collective-permute-start | bytes 1572872 | tf_op jit(solution)/shard_map/ppermute | solution.py:75
  463.2 56.3 %collective-permute-start.38 = (f32[192,1024]{1,0:T(8,128)}, f32[192,1024]{1,0:T(8,128)}, u32[]{:S(2)}, u32[]{:S(2)}) collective-permute-start(f32[192,1024]{1,0:T(8,128)} %slice_add_fusion.mine_ref), channel_id=1, source_target_pairs={{0,2},{1,3},{2,0},{3,1},{4,6},{5,7},{6,4},{7,5},{8,10},{9,11},{10,... | collective-permute-start | bytes 2359304 | tf_op jit(solution)/shard_map/ppermute | solution.py:75
  491.6 12.5 %collective-permute-start.69 = (f32[2,128,256]{2,1,0:T(8,128)}, f32[2,128,256]{2,1,0:T(8,128)}, u32[]{:S(2)}, u32[]{:S(2)}) collective-permute-start(f32[2,128,256]{2,1,0:T(8,128)} %gradient_blocks.47), channel_id=1, source_target_pairs={{0,8},{4,12},{8,0},{12,4},{16,24},{20,28},{24,16},{28,20},{1,9},{5... | collective-permute-start | bytes 786440 | tf_op jit(solution)/shard_map/ppermute | solution.py:75
  494.7 110.7 %collective-permute-start.40 = (f32[1,128,1024]{2,1,0:T(8,128)}, f32[1,128,1024]{2,1,0:T(8,128)}, u32[]{:S(2)}, u32[]{:S(2)}) collective-permute-start(f32[1,128,1024]{2,1,0:T(8,128)} %add_blocks.20), channel_id=1, source_target_pairs={{0,4},{4,0},{8,12},{12,8},{16,20},{20,16},{24,28},{28,24},{1,5},{5... | collective-permute-start | bytes 1572872 | tf_op jit(solution)/shard_map/ppermute | solution.py:75
  504.0 73.1 %collective-permute-start.58 = (f32[4,128,1024]{2,1,0:T(8,128)}, f32[4,128,1024]{2,1,0:T(8,128)}, u32[]{:S(2)}, u32[]{:S(2)}) collective-permute-start(f32[4,128,1024]{2,1,0:T(8,128)} %gradient_blocks.42), channel_id=1, source_target_pairs={{0,4},{4,0},{8,12},{12,8},{16,20},{20,16},{24,28},{28,24},{1,5},{5... | collective-permute-start | bytes 6291464 | tf_op jit(solution)/shard_map/ppermute | solution.py:75
  507.2 12.4 %collective-permute-start.70 = (f32[1,128,256]{2,1,0:T(8,128)}, f32[1,128,256]{2,1,0:T(8,128)}, u32[]{:S(2)}, u32[]{:S(2)}) collective-permute-start(f32[1,128,256]{2,1,0:T(8,128)} %add_blocks.33), channel_id=1, source_target_pairs={{0,16},{4,20},{8,24},{12,28},{16,0},{20,4},{24,8},{28,12},{1,17},{... | collective-permute-start | bytes 393224 | tf_op jit(solution)/shard_map/ppermute | solution.py:75
  510.6 61.1 %collective-permute-start.74 = (f32[2,128,1024]{2,1,0:T(8,128)}, f32[2,128,1024]{2,1,0:T(8,128)}, u32[]{:S(2)}, u32[]{:S(2)}) collective-permute-start(f32[2,128,1024]{2,1,0:T(8,128)} %gradient_blocks.45), channel_id=1, source_target_pairs={{0,8},{4,12},{8,0},{12,4},{16,24},{20,28},{24,16},{28,20},{1,9},{5... | collective-permute-start | bytes 3145736 | tf_op jit(solution)/shard_map/ppermute | solution.py:75
  526.7 34.4 %collective-permute-start.50 = (f32[4,192,128]{2,1,0:T(8,128)}, f32[4,192,128]{2,1,0:T(8,128)}, u32[]{:S(2)}, u32[]{:S(2)}) collective-permute-start(f32[4,192,128]{2,1,0:T(8,128)} %bitcast.438), channel_id=1, source_target_pairs={{0,4},{4,0},{8,12},{12,8},{16,20},{20,16},{24,28},{28,24},{1,5},{5... | collective-permute-start | bytes 1179656 | tf_op jit(solution)/shard_map/ppermute | solution.py:75
  528.8 65.5 %collective-permute-start.39 = (f32[192,1024]{1,0:T(8,128)}, f32[192,1024]{1,0:T(8,128)}, u32[]{:S(2)}, u32[]{:S(2)}) collective-permute-start(f32[192,1024]{1,0:T(8,128)} %get-tuple-element.183), channel_id=1, source_target_pairs={{0,1},{1,0},{2,3},{3,2},{4,5},{5,4},{6,7},{7,6},{8,9},{9,8},{10,11... | collective-permute-start | bytes 2359304 | tf_op jit(solution)/shard_map/ppermute | solution.py:75
  569.4 22.8 %collective-permute-start.52 = (f32[1,192,128]{2,1,0:T(8,128)}, f32[1,192,128]{2,1,0:T(8,128)}, u32[]{:S(2)}, u32[]{:S(2)}) collective-permute-start(f32[1,192,128]{2,1,0:T(8,128)} %constant_dynamic-slice_fusion.1), channel_id=1, source_target_pairs={{0,16},{4,20},{8,24},{12,28},{16,0},{20,4},{24,8},{28,12},{1,17},{... | collective-permute-start | bytes 294920 | tf_op jit(solution)/shard_map/ppermute | solution.py:75
  571.7 73.5 %collective-permute-start.73 = (f32[1,128,1024]{2,1,0:T(8,128)}, f32[1,128,1024]{2,1,0:T(8,128)}, u32[]{:S(2)}, u32[]{:S(2)}) collective-permute-start(f32[1,128,1024]{2,1,0:T(8,128)} %add_blocks.21), channel_id=1, source_target_pairs={{0,16},{4,20},{8,24},{12,28},{16,0},{20,4},{24,8},{28,12},{1,17},{... | collective-permute-start | bytes 1572872 | tf_op jit(solution)/shard_map/ppermute | solution.py:75
  577.1 48.8 %collective-permute-start.41 = (f32[1,128,256]{2,1,0:T(8,128)}, f32[1,128,256]{2,1,0:T(8,128)}, u32[]{:S(2)}, u32[]{:S(2)}) collective-permute-start(f32[1,128,256]{2,1,0:T(8,128)} %add_blocks.22), channel_id=1, source_target_pairs={{0,16},{4,20},{8,24},{12,28},{16,0},{20,4},{24,8},{28,12},{1,17},{... | collective-permute-start | bytes 393224 | tf_op jit(solution)/shard_map/ppermute | solution.py:75
  592.2 63.3 %collective-permute-start.65 = (f32[4,128,768]{2,1,0:T(8,128)}, f32[4,128,768]{2,1,0:T(8,128)}, u32[]{:S(2)}, u32[]{:S(2)}) collective-permute-start(f32[4,128,768]{2,1,0:T(8,128)} %gradient_blocks.46), channel_id=1, source_target_pairs={{0,4},{4,0},{8,12},{12,8},{16,20},{20,16},{24,28},{28,24},{1,5},{5... | collective-permute-start | bytes 4718600 | tf_op jit(solution)/shard_map/ppermute | solution.py:75
  594.3 43.0 %collective-permute-start.75 = (f32[1,128,1024]{2,1,0:T(8,128)}, f32[1,128,1024]{2,1,0:T(8,128)}, u32[]{:S(2)}, u32[]{:S(2)}) collective-permute-start(f32[1,128,1024]{2,1,0:T(8,128)} %add_blocks.38), channel_id=1, source_target_pairs={{0,16},{4,20},{8,24},{12,28},{16,0},{20,4},{24,8},{28,12},{1,17},{... | collective-permute-start | bytes 1572872 | tf_op jit(solution)/shard_map/ppermute | solution.py:75
  605.4 83.1 %collective-permute-start.68 = (f32[1,128,768]{2,1,0:T(8,128)}, f32[1,128,768]{2,1,0:T(8,128)}, u32[]{:S(2)}, u32[]{:S(2)}) collective-permute-start(f32[1,128,768]{2,1,0:T(8,128)} %add_blocks.23), channel_id=1, source_target_pairs={{0,16},{4,20},{8,24},{12,28},{16,0},{20,4},{24,8},{28,12},{1,17},{... | collective-permute-start | bytes 1179656 | tf_op jit(solution)/shard_map/ppermute | solution.py:75
  625.9 106.2 %collective-permute-start.71 = (f32[2,128,1024]{2,1,0:T(8,128)}, f32[2,128,1024]{2,1,0:T(8,128)}, u32[]{:S(2)}, u32[]{:S(2)}) collective-permute-start(f32[2,128,1024]{2,1,0:T(8,128)} %gradient_blocks.48), channel_id=1, source_target_pairs={{0,8},{4,12},{8,0},{12,4},{16,24},{20,28},{24,16},{28,20},{1,9},{5... | collective-permute-start | bytes 3145736 | tf_op jit(solution)/shard_map/ppermute | solution.py:75
  637.2 39.5 %collective-permute-start.53 = (f32[192,128]{1,0:T(8,128)}, f32[192,128]{1,0:T(8,128)}, u32[]{:S(2)}, u32[]{:S(2)}) collective-permute-start(f32[192,128]{1,0:T(8,128)} %add_bitcast_fusion.7), channel_id=1, source_target_pairs={{0,1},{1,0},{2,3},{3,2},{4,5},{5,4},{6,7},{7,6},{8,9},{9,8},{10,11... | collective-permute-start | bytes 294920 | tf_op jit(solution)/shard_map/ppermute | solution.py:75
  659.0 75.7 %collective-permute-start.66 = (f32[2,128,768]{2,1,0:T(8,128)}, f32[2,128,768]{2,1,0:T(8,128)}, u32[]{:S(2)}, u32[]{:S(2)}) collective-permute-start(f32[2,128,768]{2,1,0:T(8,128)} %gradient_blocks.55), channel_id=1, source_target_pairs={{0,8},{4,12},{8,0},{12,4},{16,24},{20,28},{24,16},{28,20},{1,9},{5... | collective-permute-start | bytes 2359304 | tf_op jit(solution)/shard_map/ppermute | solution.py:75
  663.7 40.1 %collective-permute-start.62 = (f32[4,128,256]{2,1,0:T(8,128)}, f32[4,128,256]{2,1,0:T(8,128)}, u32[]{:S(2)}, u32[]{:S(2)}) collective-permute-start(f32[4,128,256]{2,1,0:T(8,128)} %gradient_blocks.49), channel_id=1, source_target_pairs={{0,4},{4,0},{8,12},{12,8},{16,20},{20,16},{24,28},{28,24},{1,5},{5... | collective-permute-start | bytes 1572872 | tf_op jit(solution)/shard_map/ppermute | solution.py:75
  681.1 15.7 %collective-permute-start.56 = (f32[2,1,2976]{2,1,0:T(1,128)S(1)}, f32[2,1,2976]{2,1,0:T(1,128)S(1)}, u32[]{:S(2)}, u32[]{:S(2)}) collective-permute-start(f32[2,1,2976]{2,1,0:T(1,128)S(1)} %dynamic-slice_bitcast_fusion.4), channel_id=1, source_target_pairs={{0,8},{4,12},{8,0},{12,4},{16,24},{20,28},{24,16},{28,20},{1,9},{5... | collective-permute-start | bytes 71432 | tf_op jit(solution)/shard_map/ppermute | solution.py:75
  688.5 23.9 %collective-permute-start.59 = (f32[4,128,256]{2,1,0:T(8,128)}, f32[4,128,256]{2,1,0:T(8,128)S(1)}, u32[]{:S(2)}, u32[]{:S(2)}) collective-permute-start(f32[4,128,256]{2,1,0:T(8,128)} %gradient_blocks.50), channel_id=1, source_target_pairs={{0,4},{4,0},{8,12},{12,8},{16,20},{20,16},{24,28},{28,24},{1,5},{5... | collective-permute-start | bytes 1572872 | tf_op jit(solution)/shard_map/ppermute | solution.py:75
  703.8 24.4 %collective-permute-start.42 = (f32[192,768]{1,0:T(8,128)}, f32[192,768]{1,0:T(8,128)}, u32[]{:S(2)}, u32[]{:S(2)}) collective-permute-start(f32[192,768]{1,0:T(8,128)} %slice.438), channel_id=1, source_target_pairs={{0,1},{1,0},{2,3},{3,2},{4,5},{5,4},{6,7},{7,6},{8,9},{9,8},{10,11... | collective-permute-start | bytes 1769480 | tf_op jit(solution)/shard_map/ppermute | solution.py:75
  707.2 15.8 %collective-permute-start.63 = (f32[2,128,256]{2,1,0:T(8,128)}, f32[2,128,256]{2,1,0:T(8,128)S(1)}, u32[]{:S(2)}, u32[]{:S(2)}) collective-permute-start(f32[2,128,256]{2,1,0:T(8,128)} %gradient_blocks.53), channel_id=1, source_target_pairs={{0,8},{4,12},{8,0},{12,4},{16,24},{20,28},{24,16},{28,20},{1,9},{5... | collective-permute-start | bytes 786440 | tf_op jit(solution)/shard_map/ppermute | solution.py:75
  712.3 70.2 %collective-permute-start.46 = (f32[1,8,32,817]{3,2,1,0:T(8,128)}, f32[1,8,32,817]{3,2,1,0:T(8,128)}, u32[]{:S(2)}, u32[]{:S(2)}) collective-permute-start(f32[1,8,32,817]{3,2,1,0:T(8,128)} %constant_dynamic-slice_fusion.5), channel_id=1, source_target_pairs={{0,2},{1,3},{2,0},{3,1},{4,6},{5,7},{6,4},{7,5},{8,10},{9,11},{10,... | collective-permute-start | bytes 2509832 | tf_op jit(solution)/shard_map/ppermute | solution.py:75
  723.0 16.8 %collective-permute-start.60 = (f32[2,128,256]{2,1,0:T(8,128)S(1)}, f32[2,128,256]{2,1,0:T(8,128)S(1)}, u32[]{:S(2)}, u32[]{:S(2)}) collective-permute-start(f32[2,128,256]{2,1,0:T(8,128)S(1)} %copy-done.85), channel_id=1, source_target_pairs={{0,8},{4,12},{8,0},{12,4},{16,24},{20,28},{24,16},{28,20},{1,9},{5... | collective-permute-start | bytes 786440 | tf_op jit(solution)/shard_map/ppermute | solution.py:75
  728.2 20.2 %collective-permute-start.64 = (f32[1,128,256]{2,1,0:T(8,128)}, f32[1,128,256]{2,1,0:T(8,128)S(1)}, u32[]{:S(2)}, u32[]{:S(2)}) collective-permute-start(f32[1,128,256]{2,1,0:T(8,128)} %add_blocks.28), channel_id=1, source_target_pairs={{0,16},{4,20},{8,24},{12,28},{16,0},{20,4},{24,8},{28,12},{1,17},{... | collective-permute-start | bytes 393224 | tf_op jit(solution)/shard_map/ppermute | solution.py:75
  732.1 53.8 %collective-permute-start.43 = (f32[192,768]{1,0:T(8,128)}, f32[192,768]{1,0:T(8,128)}, u32[]{:S(2)}, u32[]{:S(2)}) collective-permute-start(f32[192,768]{1,0:T(8,128)} %slice_add_fusion.9), channel_id=1, source_target_pairs={{0,2},{1,3},{2,0},{3,1},{4,6},{5,7},{6,4},{7,5},{8,10},{9,11},{10,... | collective-permute-start | bytes 1769480 | tf_op jit(solution)/shard_map/ppermute | solution.py:75
  734.7 56.1 %collective-permute-start.72 = (f32[1,128,1024]{2,1,0:T(8,128)}, f32[1,128,1024]{2,1,0:T(8,128)}, u32[]{:S(2)}, u32[]{:S(2)}) collective-permute-start(f32[1,128,1024]{2,1,0:T(8,128)} %add_blocks.35), channel_id=1, source_target_pairs={{0,16},{4,20},{8,24},{12,28},{16,0},{20,4},{24,8},{28,12},{1,17},{... | collective-permute-start | bytes 1572872 | tf_op jit(solution)/shard_map/ppermute | solution.py:75
  739.8 47.5 %collective-permute-start.67 = (f32[1,128,768]{2,1,0:T(8,128)}, f32[1,128,768]{2,1,0:T(8,128)}, u32[]{:S(2)}, u32[]{:S(2)}) collective-permute-start(f32[1,128,768]{2,1,0:T(8,128)} %add_blocks.30), channel_id=1, source_target_pairs={{0,16},{4,20},{8,24},{12,28},{16,0},{20,4},{24,8},{28,12},{1,17},{... | collective-permute-start | bytes 1179656 | tf_op jit(solution)/shard_map/ppermute | solution.py:75
  748.5 33.5 %collective-permute-start.61 = (f32[1,128,256]{2,1,0:T(8,128)S(1)}, f32[1,128,256]{2,1,0:T(8,128)S(1)}, u32[]{:S(2)}, u32[]{:S(2)}) collective-permute-start(f32[1,128,256]{2,1,0:T(8,128)S(1)} %copy-done.93), channel_id=1, source_target_pairs={{0,16},{4,20},{8,24},{12,28},{16,0},{20,4},{24,8},{28,12},{1,17},{... | collective-permute-start | bytes 393224 | tf_op jit(solution)/shard_map/ppermute | solution.py:75
  (173 other events, 1588.8 us)

commit v3 on v1

--- a/solution.py
+++ b/solution.py
@@ -3,9 +3,23 @@
 import jax
 import jax.numpy as jnp
 from jax import lax
+from jax.experimental import pallas as pl
+from jax.experimental.pallas import tpu as pltpu
 from jax.sharding import PartitionSpec as P
 
 HEAD_DIM = 64
+PLAN = {
+    ("pre", 0): [("down", 0), ("up", 0)],
+    ("wait_one", 0): [("att", 0), ("down", 0), ("up", 0)],
+    ("wait_two", 1): [("down", 1)],
+    ("mid", 1): [("up", 0), ("att", 0)],
+    ("wait_one", 1): [("up", 1), ("down", 0), ("att", 0)],
+    ("end", 1): [("down", 1), ("att", 1)],
+    "scores": [("up", 1), ("down", 1)],
+    "values": ["tail"],
+}
+DRAIN = [("att", 1), ("up", 1), "position", "vectors", "embed", "tail", ("att", 1),
+         "position", "vectors", "embed", "tail", "position", "vectors", "embed"]
 ROOT_DIM = math.sqrt(HEAD_DIM)
 BF = jnp.bfloat16
 F32 = jnp.float32
@@ -44,6 +58,393 @@
 
 def pick(tensor, index, axis):
     return lax.dynamic_index_in_dim(tensor, index, axis, keepdims=False)
+
+
+def after(value, *earlier):
+    return lax.optimization_barrier((value,) + earlier)[0]
+
+
+def vmem_limit(size):
+    return pltpu.CompilerParams(vmem_limit_bytes=int(size * 1.25) + (2 << 20))
+
+
+LONG = pl.CostEstimate(flops=10**12, bytes_accessed=8, transcendentals=0)
+
+
+def step_cell(cell):
+    def kernel(cell_ref, out_ref):
+        out_ref[...] = cell_ref[...]
+
+    return pl.pallas_call(
+        kernel,
+        out_shape=jax.ShapeDtypeStruct(cell.shape, F32),
+        cost_estimate=LONG,
+        compiler_params=vmem_limit(0),
+        name="step_cell",
+    )(cell)
+
+
+class Clock:
+    def __init__(self, cell):
+        self.cell = cell
+
+    def both(self, *values):
+        *values, self.cell = lax.optimization_barrier((*values, self.cell))
+        return values
+
+    def one(self, value):
+        return self.both(value)[0]
+
+    def hold(self):
+        self.cell = step_cell(self.cell)
+
+
+def ordered_columns(source, target, shards_ref, count, shard):
+    for place in range(count):
+        column = pl.multiple_of(shards_ref[place] * shard, shard)
+        target[:, place * shard : (place + 1) * shard] = source[:, pl.ds(column, shard)]
+
+
+def take_columns(rows, shards, shard):
+    pieces = rows.reshape(rows.shape[0], -1, shard)[:, shards]
+    return pieces.reshape(rows.shape)
+
+
+def norm_rows(own, other, gain, bias, shards):
+    half, width = own.shape
+    count = shards.shape[0]
+    shard = width // count
+    if shard % 128:
+        rows = jnp.concatenate([own, other], axis=0) * gain + bias
+        return take_columns(rows.astype(BF), shards, shard)
+
+    def kernel(shards_ref, own_ref, other_ref, gain_ref, bias_ref, out_ref, low_ref):
+        low_ref[:half] = (own_ref[...] * gain_ref[...] + bias_ref[...]).astype(BF)
+        low_ref[half:] = (other_ref[...] * gain_ref[...] + bias_ref[...]).astype(BF)
+        ordered_columns(low_ref, out_ref, shards_ref, count, shard)
+
+    return pl.pallas_call(
+        kernel,
+        out_shape=jax.ShapeDtypeStruct((2 * half, width), BF),
+        in_specs=[pl.BlockSpec(memory_space=pltpu.SMEM)] + [pl.BlockSpec()] * 4,
+        scratch_shapes=[pltpu.VMEM((2 * half, width), BF)],
+        cost_estimate=pl.CostEstimate(
+            flops=4 * half * width, bytes_accessed=12 * half * width, transcendentals=0
+        ),
+        compiler_params=vmem_limit(16 * half * width),
+        name="norm_rows",
+    )(shards, own, other, gain[None], bias[None])
+
+
+def merge_rows(own, other, change, shards):
+    half, width = own.shape
+    count = shards.shape[0]
+    shard = width // count
+    if shard % 128:
+        total = other + change
+        low = jnp.concatenate([own, total], axis=0).astype(BF)
+        return total, low, take_columns(low, shards, shard)
+
+    def kernel(shards_ref, own_ref, other_ref, change_ref, other_out, low_out, ordered_out):
+        low_out[:half] = own_ref[...].astype(BF)
+        total = other_ref[...] + change_ref[...]
+        other_out[...] = total
+        low_out[half:] = total.astype(BF)
+        ordered_columns(low_out, ordered_out, shards_ref, count, shard)
+
+    return pl.pallas_call(
+        kernel,
+        out_shape=(
+            jax.ShapeDtypeStruct((half, width), F32),
+            jax.ShapeDtypeStruct((2 * half, width), BF),
+            jax.ShapeDtypeStruct((2 * half, width), BF),
+        ),
+        in_specs=[pl.BlockSpec(memory_space=pltpu.SMEM)] + [pl.BlockSpec()] * 3,
+        cost_estimate=LONG,
+        compiler_params=vmem_limit(26 * half * width),
+        name="merge_rows",
+    )(shards, own, other, change)
+
+
+def norm_back(mine, got, unit, inverse, gain, grad):
+    half, width = mine.shape
+
+    def kernel(mine_ref, got_ref, unit_ref, inverse_ref, gain_ref, grad_ref, change_out, grad_out, sums_out):
+        pull = mine_ref[...] + got_ref[...]
+        unit_rows = unit_ref[...]
+        scaled = pull * gain_ref[...]
+        first = jnp.mean(scaled, axis=-1, keepdims=True)
+        second = jnp.mean(scaled * unit_rows, axis=-1, keepdims=True)
+        change = inverse_ref[:, :1] * (scaled - first - unit_rows * second)
+        change_out[...] = change
+        total = grad_ref[...] + change
+        grad_out[...] = total
+        sums_out[0:1] = jnp.sum(pull * unit_rows, axis=0, keepdims=True)
+        sums_out[1:2] = jnp.sum(pull, axis=0, keepdims=True)
+        sums_out[2:3] = jnp.sum(total, axis=0, keepdims=True)
+
+    rows = jax.ShapeDtypeStruct((half, width), F32)
+    return pl.pallas_call(
+        kernel,
+        out_shape=(rows, rows, jax.ShapeDtypeStruct((3, width), F32)),
+        cost_estimate=LONG,
+        compiler_params=vmem_limit(30 * half * width),
+        name="norm_back",
+    )(mine, got, unit, inverse, gain[None], grad)
+
+
+def product_rows(pairs, scale, start, first, second, got=None):
+    widths = [right.shape[1] for _, right in pairs]
+    total = sum(widths)
+    has_got = got is not None
+    count = first + second
+
+    def kernel(scale_ref, *refs):
+        ins = refs[: 2 * len(pairs)]
+        outs = refs[2 * len(pairs) + has_got :]
+        step = pl.program_id(0)
+
+        def fill(out_ref):
+            column = 0
+            for i, width in enumerate(widths):
+                block = (
+                    lax.dot_general(
+                        ins[2 * i][...],
+                        ins[2 * i + 1][...],
+                        (((0,), (0,)), ((), ())),
+                        preferred_element_type=F32,
+                    )
+                    * scale_ref[0:1, 0:1]
+                )
+                if has_got:
+                    block = block + refs[2 * len(pairs)][:, column : column + width]
+                out_ref[:, column : column + width] = block
+                column += width
+
+        if second:
+            pl.when(step < first)(lambda: fill(outs[0]))
+            pl.when(step >= first)(lambda: fill(outs[1]))
+        else:
+            fill(outs[0])
+
+    in_specs = [pl.BlockSpec(scale.shape, lambda j: (0, 0))]
+    operands = [scale]
+    traffic = 0
+    for left, right in pairs:
+        rows = left.shape[0]
+        in_specs.append(pl.BlockSpec((rows, 128), lambda j: (0, start + j)))
+        in_specs.append(pl.BlockSpec(right.shape, lambda j: (0, 0)))
+        operands += [left, right]
+        traffic += 2 * 2 * rows * (128 + right.shape[1])
+    if has_got:
+        in_specs.append(pl.BlockSpec((128, total), lambda j: (j, 0)))
+        operands.append(got)
+    out_shape = [jax.ShapeDtypeStruct((first * 128, total), F32)]
+    out_specs = [pl.BlockSpec((128, total), lambda j: (jnp.minimum(j, first - 1), 0))]
+    if second:
+        out_shape.append(jax.ShapeDtypeStruct((second * 128, total), F32))
+        out_specs.append(pl.BlockSpec((128, total), lambda j: (jnp.maximum(j - first, 0), 0)))
+    return pl.pallas_call(
+        kernel,
+        out_shape=out_shape,
+        grid=(count,),
+        in_specs=in_specs,
+        out_specs=out_specs,
+        cost_estimate=LONG,
+        compiler_params=vmem_limit(traffic + 2 * 4 * 128 * total * 3),
+        name="product_rows",
+    )(*operands)
+
+
+def add_split(keep, got):
+    rows, width = keep.shape
+    half = rows // 2
+    size = min(64, half)
+    count = half // size
+
+    def kernel(keep_ref, got_ref, first_out, second_out):
+        total = keep_ref[...] + got_ref[...]
+
+        @pl.when(pl.program_id(0) < count)
+        def _():
+            first_out[...] = total
+
+        @pl.when(pl.program_id(0) >= count)
+        def _():
+            second_out[...] = total
+
+    block = (size, width)
+    return pl.pallas_call(
+        kernel,
+        out_shape=[jax.ShapeDtypeStruct((half, width), F32)] * 2,
+        grid=(2 * count,),
+        in_specs=[pl.BlockSpec(block, lambda j: (j, 0))] * 2,
+        out_specs=[
+            pl.BlockSpec(block, lambda j: (jnp.minimum(j, count - 1), 0)),
+            pl.BlockSpec(block, lambda j: (jnp.maximum(j - count, 0), 0)),
+        ],
+        cost_estimate=LONG,
+        compiler_params=vmem_limit(32 * size * width),
+        name="add_split",
+    )(keep, got)
+
+
+def attend_forward(unit_own, unit_other, gain, bias, weights, biases, out_weight):
+    half, model_width = unit_own.shape
+    rows = 2 * half
+    local_width = weights.shape[2]
+    head_count = local_width // HEAD_DIM
+
+    def kernel(own_ref, other_ref, gain_ref, bias_ref, weight_ref, biases_ref, out_weight_ref,
+               qkv_out, mixed_out, total_out, own_out, send_out, normed_ref):
+        normed_ref[:half] = (own_ref[...] * gain_ref[...] + bias_ref[...]).astype(BF)
+        normed_ref[half:] = (other_ref[...] * gain_ref[...] + bias_ref[...]).astype(BF)
+        normed = normed_ref[...]
+        qkv_out[:, :local_width] = (matmul(normed, weight_ref[0]) + biases_ref[0:1]).astype(BF)
+        qkv_out[:, local_width : 2 * local_width] = matmul(normed, weight_ref[1]).astype(BF)
+        qkv_out[:, 2 * local_width :] = (matmul(normed, weight_ref[2]) + biases_ref[1:2]).astype(BF)
+        for head in range(head_count):
+            one = slice(head * HEAD_DIM, (head + 1) * HEAD_DIM)
+            query = qkv_out[:, one]
+            key = qkv_out[:, local_width + head * HEAD_DIM : local_width + (head + 1) * HEAD_DIM]
+            value = qkv_out[:, 2 * local_width + head * HEAD_DIM : 2 * local_width + (head + 1) * HEAD_DIM]
+            scores = matmul_nt(query, key) / ROOT_DIM
+            top = jnp.max(scores, axis=-1, keepdims=True)
+            exponent = jnp.exp(scores - top)
+            row_sum = jnp.sum(exponent, axis=-1, keepdims=True)
+            attend = (exponent / row_sum).astype(BF)
+            mixed_out[:, one] = matmul(attend, value).astype(BF)
+            total_out[:, head : head + 1] = top + jnp.log(row_sum)
+        send_out[...] = matmul(mixed_out[half:], out_weight_ref[...])
+        own_out[...] = matmul(mixed_out[:half], out_weight_ref[...])
+
+    piece = jax.ShapeDtypeStruct((half, model_width), F32)
+    return pl.pallas_call(
+        kernel,
+        out_shape=(
+            jax.ShapeDtypeStruct((rows, 3 * local_width), BF),
+            jax.ShapeDtypeStruct((rows, local_width), BF),
+            jax.ShapeDtypeStruct((rows, 128), F32),
+            piece,
+            piece,
+        ),
+        scratch_shapes=[pltpu.VMEM((rows, model_width), BF)],
+        cost_estimate=pl.CostEstimate(
+            flops=2 * rows * local_width * (4 * model_width + 2 * rows),
+            bytes_accessed=8 * rows * model_width + 8 * local_width * model_width,
+            transcendentals=rows * rows * head_count,
+        ),
+        compiler_params=vmem_limit(22 * rows * model_width),
+        name="attend_forward",
+    )(unit_own, unit_other, gain[None], bias[None], weights, biases, out_weight)
+
+
+def attend_back(low, qkv, totals, weights, out_weight):
+    rows, model_width = low.shape
+    half = rows // 2
+    local_width = weights.shape[2]
+    head_count = local_width // HEAD_DIM
+
+    def kernel(low_ref, qkv_ref, total_ref, weight_ref, out_weight_ref,
+               grads_out, sums_out, own_out, send_out, mix_ref):
+        mix_ref[...] = matmul_nt(low_ref[...], out_weight_ref[...]).astype(BF)
+        for head in range(head_count):
+            one = slice(head * HEAD_DIM, (head + 1) * HEAD_DIM)
+            two = slice(local_width + head * HEAD_DIM, local_width + (head + 1) * HEAD_DIM)
+            three = slice(2 * local_width + head * HEAD_DIM, 2 * local_width + (head + 1) * HEAD_DIM)
+            query, key, value = qkv_ref[:, one], qkv_ref[:, two], qkv_ref[:, three]
+            mix = mix_ref[:, one]
+            attend = jnp.exp(matmul_nt(query, key) / ROOT_DIM - total_ref[:, head : head + 1])
+            grad_attend = matmul_nt(mix, value)
+            grad_value = matmul_tn(attend.astype(BF), mix)
+            weighted = attend * grad_attend
+            grad_scores = weighted - attend * jnp.sum(weighted, axis=-1, keepdims=True)
+            grad_low = grad_scores.astype(BF)
+            grad_query = matmul(grad_low, key) / ROOT_DIM
+            grad_key = matmul_tn(grad_low, query) / ROOT_DIM
+            grads_out[:, one] = grad_query.astype(BF)
+            grads_out[:, two] = grad_key.astype(BF)
+            grads_out[:, three] = grad_value.astype(BF)
+            sums_out[0:1, one] = jnp.sum(grad_query, axis=0, keepdims=True)
+            sums_out[1:2, one] = jnp.sum(grad_value, axis=0, keepdims=True)
+
+        def pull(part):
+            total = matmul_nt(grads_out[part, :local_width], weight_ref[0])
+            total = total + matmul_nt(grads_out[part, local_width : 2 * local_width], weight_ref[1])
+            return total + matmul_nt(grads_out[part, 2 * local_width :], weight_ref[2])
+
+        send_out[...] = pull(slice(half, rows))
+        own_out[...] = pull(slice(0, half))
+
+    piece = jax.ShapeDtypeStruct((half, model_width), F32)
+    return pl.pallas_call(
+        kernel,
+        out_shape=(
+            jax.ShapeDtypeStruct((rows, 3 * local_width), BF),
+            jax.ShapeDtypeStruct((2, local_width), F32),
+            piece,
+            piece,
+        ),
+        scratch_shapes=[pltpu.VMEM((rows, local_width), BF)],
+        cost_estimate=LONG,
+        compiler_params=vmem_limit(24 * rows * model_width),
+        name="attend_back",
+    )(low, qkv, totals, weights, out_weight)
+
+
+def finish_layers(kind, pieces, layer_count, shard, local_width):
+    width = pieces[0].shape[1]
+    shapes = {
+        "down": [(layer_count, width, shard)],
+        "up": [(layer_count, shard, width)],
+        "att": [
+            (layer_count, local_width, shard),
+            (layer_count, 3, shard, local_width),
+        ],
+    }[kind]
+
+    def store(values, outs):
+        for layer, value in enumerate(values):
+            if kind == "down":
+                outs[0][layer] = value.T
+            elif kind == "up":
+                outs[0][layer] = value
+            else:
+                outs[0][layer] = value[:, :local_width].T
+                for which in range(3):
+                    begin = (1 + which) * local_width
+                    outs[1][layer, which] = value[:, begin : begin + local_width]
+
+    if shard % 128:
+        values = [pieces[2 * i] + pieces[2 * i + 1] for i in range(layer_count)]
+        if kind == "down":
+            return [jnp.stack([value.T for value in values])]
+        if kind == "up":
+            return [jnp.stack(values)]
+        rest = [
+            value[:, local_width:].reshape(shard, 3, local_width).transpose(1, 0, 2)
+            for value in values
+        ]
+        return [jnp.stack([value[:, :local_width].T for value in values]), jnp.stack(rest)]
+
+    def kernel(*refs):
+        ins = refs[: 2 * layer_count]
+        store(
+            [ins[2 * i][...] + ins[2 * i + 1][...] for i in range(layer_count)],
+            refs[2 * layer_count :],
+        )
+
+    return pl.pallas_call(
+        kernel,
+        out_shape=[jax.ShapeDtypeStruct(shape, F32) for shape in shapes],
+        cost_estimate=pl.CostEstimate(
+            flops=layer_count * shard * width,
+            bytes_accessed=12 * layer_count * shard * width,
+            transcendentals=0,
+        ),
+        compiler_params=vmem_limit(20 * layer_count * shard * width),
+        name="finish_layers",
+    )(*pieces)
 
 
 class Links:
@@ -58,18 +459,35 @@
     def mp_bit(self, bit):
         return (self.mp_index >> bit) & 1
 
+    def ordered_sum(self, clock, own, send):
+        send = clock.one(send)
+        got = exchange(send, "mp", self.mp, 0)
+        clock.hold()
+        mine = clock.one(own() + clock.one(got))
+        last = bit_count(self.mp) - 1
+        for bit in range(1, last):
+            mine = clock.one(mine + exchange(mine, "mp", self.mp, bit))
+        return mine, exchange(mine, "mp", self.mp, last)
+
+    def begin_sum(self, own, send):
+        mine = own + exchange(send, "mp", self.mp, 0)
+        last = bit_count(self.mp) - 1
+        for bit in range(1, last):
+            mine = mine + exchange(mine, "mp", self.mp, bit)
+        return mine, exchange(mine, "mp", self.mp, last)
+
+    def begin_product(self, left, right, product=matmul):
+        half = left.shape[0] // 2
+        send = product(left[half:], right)
+        return self.begin_sum(product(left[:half], right), send)
+
     def sum_rows(self, partial):
         half = partial.shape[0] // 2
-        total = partial[:half] + exchange(partial[half:], "mp", self.mp, 0)
-        for bit in range(1, bit_count(self.mp)):
-            total = total + exchange(total, "mp", self.mp, bit)
-        return total
+        mine, got = self.begin_sum(partial[:half], partial[half:])
+        return mine + got
 
     def other_rows(self, own):
         return exchange(own, "mp", self.mp, 0)
-
-    def both_rows(self, own):
-        return jnp.concatenate([own, self.other_rows(own)], axis=0)
 
     def split_rows(self, tensor):
         half = tensor.shape[0] // 2
@@ -84,31 +502,69 @@
             [jnp.where(core == 0, own, other), jnp.where(core == 0, other, own)], axis=0
         )
 
-    def finish_scatter(self, shards, first_bit):
-        for bit in range(first_bit, bit_count(self.dp)):
-            count = shards.shape[0] // 2
-            pairs = shards.reshape((count, 2) + shards.shape[1:])
-            own = self.dp_bit(bit)
-            got = exchange(pick(pairs, 1 - own, 1), "dp", self.dp, bit)
-            shards = pick(pairs, own, 1) + got
-        return shards[0]
-
-    def scatter_sum(self, shards):
-        return self.finish_scatter(shards, 0)
-
-    def scatter_product(self, left, right, scale):
-        width = left.shape[1]
-        parts = left.reshape(left.shape[0], self.dp // 2, 2, width // self.dp)
-        own = self.dp_bit(0)
-        keep_left = jnp.where(own == 0, parts[:, :, 0], parts[:, :, 1])
-        send_left = jnp.where(own == 0, parts[:, :, 1], parts[:, :, 0])
-        flat = (left.shape[0], width // 2)
-        send = matmul_tn(send_left.reshape(flat), right) * scale
-        got = exchange(send, "dp", self.dp, 0)
-        total = matmul_tn(keep_left.reshape(flat), right) * scale + got
-        return self.finish_scatter(
-            total.reshape(self.dp // 2, width // self.dp, right.shape[1]), 1
-        )
+    def order(self, bits):
+        masks = []
+        for place in range(self.dp):
+            mask = 0
+            for i, bit in enumerate(bits):
+                if not (place >> (len(bits) - 1 - i)) & 1:
+                    mask |= 1 << bit
+            masks.append(mask)
+        return jnp.array(masks, jnp.int32) ^ self.dp_index
+
+
+class Merge:
+    def __init__(self, links, pairs, bits):
+        self.links, self.pairs, self.bits = links, pairs, bits
+        self.blocks = pairs[0][0].shape[1] // 128
+        self.step = 0
+
+    def advance(self, clock):
+        got, pairs = None, self.pairs
+        if self.step:
+            got = clock.one(self.got)
+        else:
+            pairs = [(clock.one(pairs[0][0]), pairs[0][1])] + pairs[1:]
+        if self.step == 0:
+            send = product_rows(pairs, clock.cell, 0, self.blocks // 2, 0)[0]
+        elif self.step == 1:
+            send, self.keep = product_rows(
+                pairs, clock.cell, self.blocks // 2, self.blocks // 4, self.blocks // 4, got
+            )
+        else:
+            send, self.keep = add_split(self.keep, got)
+        send = clock.one(send)
+        self.got = exchange(send, "dp", self.links.dp, self.bits[self.step])
+        self.step += 1
+
+    @property
+    def open(self):
+        return self.step < len(self.bits)
+
+
+class ShardMerge:
+    def __init__(self, links, shards):
+        self.links, self.shards = links, shards
+        self.step = 0
+
+    def split(self, total):
+        pairs = total.reshape((total.shape[0] // 2, 2) + total.shape[1:])
+        own = self.links.dp_bit(self.step)
+        self.keep = pick(pairs, own, 1)
+        return pick(pairs, 1 - own, 1)
+
+    def advance(self, clock):
+        total = self.shards
+        if self.step:
+            total = self.keep + clock.one(self.got)
+        send = clock.one(self.split(clock.one(total)))
+        self.got = exchange(send, "dp", self.links.dp, self.step)
+        clock.hold()
+        self.step += 1
+
+    @property
+    def open(self):
+        return self.step < bit_count(self.links.dp)
 
 
 def norm_parts(rows):
@@ -116,14 +572,7 @@
     centred = rows - row_mean
     spread = jnp.mean(centred * centred, axis=-1, keepdims=True)
     inverse = lax.rsqrt(spread + 1e-05)
-    return centred * inverse, inverse
-
-
-def norm_back(grad, gain, unit, inverse):
-    scaled = grad * gain
-    first = jnp.mean(scaled, axis=-1, keepdims=True)
-    second = jnp.mean(scaled * unit, axis=-1, keepdims=True)
-    return inverse * (scaled - first - unit * second)
+    return centred * inverse, jnp.broadcast_to(inverse, (rows.shape[0], 128))
 
 
 def make_per_device(dp, mp):
@@ -177,10 +626,6 @@
         mask_row = jnp.sum(jnp.where(dataset_pick[:, None], variable_mask, 0), axis=0)
         item_weight = jnp.sum(jnp.where(dataset_pick, dataset_weight, 0)).astype(F32)
         own_count = token_counts[0].astype(F32)
-        count_total = jnp.full((8, 128), own_count, F32)
-        for bit in range(bit_count(dp)):
-            count_total = count_total + exchange(count_total, "dp", dp, bit)
-        item_scale = item_weight * own_count / count_total[0, 0]
         lead_scale = lead_hours[0].astype(F32) / 24.0
 
         pix_rows = pixels[0].reshape(flat_count, row_count).T
@@ -191,6 +636,7 @@
         embed_all = jnp.concatenate(
             [patch_weight.reshape(flat_count, model_width), embed_high, embed_rest], axis=0
         )
+        embed_left = take_columns(embed_all, links.order(list(range(bit_count(dp)))), shard)
         query_low = pool_query.astype(BF)
         query_vec = matmul(query_low[None, :], pool_query_weight)[0].astype(BF)
         head_of = jnp.arange(local_width, dtype=jnp.int32) // HEAD_DIM
@@ -238,61 +684,72 @@
         ) + jnp.einsum("hrv,hvd->hrd", probs_low, value_var, preferred_element_type=F32)
         pooled = heads_last(pooled).astype(BF)
 
-        hidden = links.sum_rows(matmul(pooled, pool_output_weight)) + pool_output_bias
+        mine, got = links.begin_product(pooled, pool_output_weight)
+        count_total = after(jnp.full((8, 128), own_count, F32), mine)
+        for bit in range(bit_count(dp)):
+            count_total = count_total + exchange(count_total, "dp", dp, bit)
+        scale_cell = item_weight * own_count / count_total
+        item_scale = scale_cell[0, 0]
         position_own = links.split_rows(position_embed)[0]
-        hidden = hidden + position_own + lead_scale * lead_weight + lead_bias
-
+        offset_rows = pool_output_bias + position_own + lead_scale * lead_weight + lead_bias
+        mine, scale_cell = lax.optimization_barrier((mine, scale_cell))
+        hidden = mine + got + offset_rows
+
+        bits = list(range(bit_count(dp)))
+        bits_late = bits[1:] + bits[:1]
+        shards, shards_late = links.order(bits), links.order(bits_late)
+        top = layer_count - 1
         kept = []
         for layer in range(layer_count):
             unit_one, inverse_one = norm_parts(hidden)
-            normed = links.both_rows(unit_one) * norm_gain[layer, 0] + norm_bias[layer, 0]
-            normed = normed.astype(BF)
-            queries = (
-                matmul(normed, attention_weight[layer, 0]) + attention_bias[layer, 0]
-            ).astype(BF)
-            keys_new = matmul(normed, attention_weight[layer, 1]).astype(BF)
-            values_new = (
-                matmul(normed, attention_weight[layer, 2]) + attention_bias[layer, 1]
-            ).astype(BF)
-            query_three = heads_first(queries)
-            key_three = heads_first(keys_new)
-            value_three = heads_first(values_new)
-            scores = (
-                jnp.einsum("hpd,hkd->hpk", query_three, key_three, preferred_element_type=F32)
-                / ROOT_DIM
-            )
-            row_max = jnp.max(scores, axis=-1, keepdims=True)
-            exponent = jnp.exp(scores - row_max)
-            attend = exponent / jnp.sum(exponent, axis=-1, keepdims=True)
-            attend_low = attend.astype(BF)
-            mixed = heads_last(
-                jnp.einsum("hpk,hkd->hpd", attend_low, value_three, preferred_element_type=F32)
-            ).astype(BF)
-            hidden = (
-                hidden
-                + links.sum_rows(matmul(mixed, output_weight[layer]))
-                + output_bias[layer]
-            )
+            unit_other = links.other_rows(unit_one)
+            qkv, mixed, totals, part_own, part_send = attend_forward(
+                unit_one,
+                unit_other,
+                norm_gain[layer, 0],
+                norm_bias[layer, 0],
+                attention_weight[layer],
+                attention_bias[layer],
+                output_weight[layer],
+            )
+            mine, got = links.begin_sum(part_own, part_send)
+            normed = norm_rows(
+                after(unit_one, mine), unit_other, norm_gain[layer, 0], norm_bias[layer, 0], shards
+            )
+            mine, normed = lax.optimization_barrier((mine, normed))
+            if layer == 0:
+                grad_own, grad_other = links.split_rows(after(cotangent[0], mine))
+                grad_other, down_low, down_left = merge_rows(
+                    grad_own, grad_other, jnp.zeros_like(grad_other), shards_late
+                )
+                mine, down_low = lax.optimization_barrier((mine, down_low))
+            hidden = hidden + (mine + got) + output_bias[layer]
             unit_two, inverse_two = norm_parts(hidden)
-            normed_two = links.both_rows(unit_two) * norm_gain[layer, 1] + norm_bias[layer, 1]
-            normed_two = normed_two.astype(BF)
+            unit_other = links.other_rows(unit_two)
+            normed_two = jnp.concatenate([unit_two, unit_other], axis=0)
+            normed_two = (normed_two * norm_gain[layer, 1] + norm_bias[layer, 1]).astype(BF)
             pre_act = matmul(normed_two, up_weight[layer]) + up_bias[layer]
             activation = gelu_exact(pre_act).astype(BF)
-            hidden = (
-                hidden
-                + links.sum_rows(matmul(activation, down_weight[layer]))
-                + down_bias[layer]
-            )
+            marker = activation
+            if layer < top:
+                mine, got = links.begin_product(activation, down_weight[layer])
+                marker = mine
+            normed_two = norm_rows(
+                after(unit_two, marker), unit_other, norm_gain[layer, 1], norm_bias[layer, 1], shards
+            )
+            if layer < top:
+                if layer == 0:
+                    top_grad = matmul_nt(after(down_low, mine), down_weight[top])
+                    mine, top_grad = lax.optimization_barrier((mine, top_grad))
+                mine, normed_two = lax.optimization_barrier((mine, normed_two))
+                hidden = hidden + (mine + got) + down_bias[layer]
             kept.append(
                 (
                     unit_one,
                     inverse_one,
                     normed,
-                    query_three,
-                    key_three,
-                    value_three,
-                    attend,
-                    attend_low,
+                    qkv,
+                    totals,
                     mixed,
                     unit_two,
                     inverse_two,
@@ -301,22 +758,28 @@
                     activation,
                 )
             )
-        layer_out = links.global_rows(hidden, links.other_rows(hidden))
-
-        grad_own, grad_other = links.split_rows(cotangent[0])
+
+        activation_top = kept[top][-1]
         row_sums = {}
         local_sums = {}
-        weight_grads = [None] * layer_count
+        merges = {}
+        row_sums["down_bias", top] = jnp.sum(grad_own, axis=0)
+
+        clock = Clock(scale_cell)
+
+        def advance(spot):
+            for name in PLAN.get(spot, ()):
+                if name in merges and merges[name].open:
+                    merges[name].advance(clock)
+
         for layer in reversed(range(layer_count)):
+            depth = top - layer
             (
                 unit_one,
                 inverse_one,
                 normed,
-                query_three,
-                key_three,
-                value_three,
-                attend,
-                attend_low,
+                qkv,
+                totals,
                 mixed,
                 unit_two,
                 inverse_two,
@@ -324,63 +787,78 @@
                 pre_act,
                 activation,
             ) = kept[layer]
-            down_low = jnp.concatenate([grad_own, grad_other], axis=0).astype(BF)
-            row_sums["down_bias", layer] = jnp.sum(grad_own, axis=0)
-            grad_activation = matmul_nt(down_low, down_weight[layer])
+            merges["down", depth] = Merge(
+                links, [(down_left, activation)], bits if depth else bits_late
+            )
+            grad_activation = top_grad if layer == top else matmul_nt(down_low, down_weight[layer])
             grad_pre = jax.vjp(gelu_exact, pre_act)[1](grad_activation)[0]
             local_sums["up_bias", layer] = jnp.sum(grad_pre, axis=0)
-            pre_low = grad_pre.astype(BF)
-            grad_two = links.sum_rows(matmul_nt(pre_low, up_weight[layer]))
-            down_grad = links.scatter_product(down_low, activation, item_scale)
-            up_grad = links.scatter_product(normed_two, pre_low, item_scale)
-            row_sums["gain", layer, 1] = jnp.sum(grad_two * unit_two, axis=0)
-            row_sums["bias", layer, 1] = jnp.sum(grad_two, axis=0)
-            change = norm_back(grad_two, norm_gain[layer, 1], unit_two, inverse_two)
-            grad_own = grad_own + change
-            grad_other = grad_other + links.other_rows(change)
-            out_low = jnp.concatenate([grad_own, grad_other], axis=0).astype(BF)
-            row_sums["out_bias", layer] = jnp.sum(grad_own, axis=0)
-            grad_mixed = heads_first(matmul_nt(out_low, output_weight[layer]).astype(BF))
-            grad_attend = jnp.einsum(
-                "hpd,hkd->hpk", grad_mixed, value_three, preferred_element_type=F32
-            )
-            grad_values = heads_last(
-                jnp.einsum("hpk,hpd->hkd", attend_low, grad_mixed, preferred_element_type=F32)
-            )
-            grad_scores = attend * (
-                grad_attend - jnp.sum(attend * grad_attend, axis=-1, keepdims=True)
-            )
-            score_low = grad_scores.astype(BF)
-            grad_queries = heads_last(
-                jnp.einsum("hpk,hkd->hpd", score_low, key_three, preferred_element_type=F32)
-                / ROOT_DIM
-            )
-            grad_keys = heads_last(
-                jnp.einsum("hpk,hpd->hkd", score_low, query_three, preferred_element_type=F32)
-                / ROOT_DIM
-            )
-            local_sums["qv", layer, 0] = jnp.sum(grad_queries, axis=0)
-            local_sums["qv", layer, 1] = jnp.sum(grad_values, axis=0)
-            grad_three = [part.astype(BF) for part in (grad_queries, grad_keys, grad_values)]
-            partial = matmul_nt(grad_three[0], attention_weight[layer, 0])
-            partial = partial + matmul_nt(grad_three[1], attention_weight[layer, 1])
-            partial = partial + matmul_nt(grad_three[2], attention_weight[layer, 2])
-            grad_one = links.sum_rows(partial)
-            out_grad = links.scatter_product(out_low, mixed, item_scale)
-            qkv_grad = links.scatter_product(
-                normed, jnp.concatenate(grad_three, axis=1), item_scale
-            )
-            row_sums["gain", layer, 0] = jnp.sum(grad_one * unit_one, axis=0)
-            row_sums["bias", layer, 0] = jnp.sum(grad_one, axis=0)
-            change = norm_back(grad_one, norm_gain[layer, 0], unit_one, inverse_one)
-            grad_own = grad_own + change
-            grad_other = grad_other + links.other_rows(change)
-            weight_grads[layer] = (down_grad, up_grad, out_grad, qkv_grad)
-
-        column_sum = jnp.sum(grad_own, axis=0)
-        row_sums["column"] = column_sum
-        row_sums["lead"] = lead_scale * column_sum
-        pool_grad_low = jnp.concatenate([grad_own, grad_other], axis=0).astype(BF)
+            pre_low = clock.one(grad_pre.astype(BF))
+            merges["up", depth] = Merge(links, [(normed_two, pre_low)], bits)
+            advance(("pre", depth))
+            pre_low = clock.one(pre_low)
+            half = row_count // 2
+            mine, got = links.ordered_sum(
+                clock,
+                lambda: matmul_nt(pre_low[:half], up_weight[layer]),
+                matmul_nt(pre_low[half:], up_weight[layer]),
+            )
+            if not PLAN.get(("wait_two", depth)):
+                clock.hold()
+            advance(("wait_two", depth))
+            mine, got = clock.both(mine, got)
+            change, grad_own, sums = norm_back(
+                mine, got, unit_two, inverse_two, norm_gain[layer, 1], grad_own
+            )
+            change, sums = clock.both(change, sums)
+            row_sums["gain", layer, 1] = sums[0]
+            row_sums["bias", layer, 1] = sums[1]
+            row_sums["out_bias", layer] = sums[2]
+            other_change = links.other_rows(change)
+            clock.hold()
+            grad_other, out_low, out_left = merge_rows(
+                grad_own, grad_other, clock.one(other_change), shards
+            )
+            out_low = clock.one(out_low)
+            advance(("mid", depth))
+            grads, qv_sums, part_own, part_send = attend_back(
+                clock.one(out_low), qkv, totals, attention_weight[layer], output_weight[layer]
+            )
+            local_sums["qv", layer] = qv_sums
+            mine, got = links.ordered_sum(clock, lambda: part_own, part_send)
+            if not PLAN.get(("wait_one", depth)):
+                clock.hold()
+            merges["att", depth] = Merge(links, [(out_left, mixed), (normed, grads)], bits)
+            advance(("wait_one", depth))
+            mine, got = clock.both(mine, got)
+            change, grad_own, sums = norm_back(
+                mine, got, unit_one, inverse_one, norm_gain[layer, 0], grad_own
+            )
+            change, sums = clock.both(change, sums)
+            row_sums["gain", layer, 0] = sums[0]
+            row_sums["bias", layer, 0] = sums[1]
+            if layer:
+                row_sums["down_bias", layer - 1] = sums[2]
+            other_change = links.other_rows(change)
+            clock.hold()
+            grad_other, down_low, down_left = merge_rows(
+                grad_own, grad_other, clock.one(other_change), shards
+            )
+            down_low = clock.one(down_low)
+            advance(("end", depth))
+            down_low = clock.one(down_low)
+
+        activation_top = clock.one(activation_top)
+        half = row_count // 2
+        last_mine, last_got = links.ordered_sum(
+            clock,
+            lambda: matmul(activation_top[:half], down_weight[top]),
+            matmul(activation_top[half:], down_weight[top]),
+        )
+        clock.hold()
+        row_sums["column"] = sums[2]
+        row_sums["lead"] = lead_scale * sums[2]
+        pool_grad_low = down_low
         grad_pooled = heads_first(matmul_nt(pool_grad_low, pool_output_weight).astype(BF))
         pull_flat = jnp.einsum("hrd,hkd->hrk", grad_pooled, value_flat, preferred_element_type=F32)
         pull_high, pull_rest = two_part(pull_flat * pix_value[None])
@@ -392,6 +870,9 @@
         grad_pool_scores = pool_probs * (
             grad_probs - jnp.sum(pool_probs * grad_probs, axis=-1, keepdims=True)
         )
+        grad_pool_scores = clock.one(grad_pool_scores)
+        advance("scores")
+        grad_pool_scores = clock.one(grad_pool_scores)
         score_high, score_rest = two_part(grad_pool_scores)
         pixel_part = jnp.einsum(
             "hrv,hkv->rk", score_high, block_high, preferred_element_type=F32
@@ -409,7 +890,16 @@
             "hrv,hrd->vhd", probs_low, grad_pooled, preferred_element_type=F32
         ).reshape(var_count, local_width)
         local_sums["pool_bias"] = jnp.sum(value_grad_var, axis=0)
-        value_grad_flat = (value_grad_flat * item_scale).astype(BF)
+        value_rows_grad = jnp.concatenate(
+            [part.astype(BF) for part in (value_grad_flat, value_grad_var, value_grad_var)], axis=0
+        )
+        merges["tail"] = Merge(
+            links,
+            [(down_left, pooled), (embed_left, value_rows_grad)],
+            bits,
+        )
+        advance("values")
+        value_grad_flat = (clock.one(value_grad_flat) * item_scale).astype(BF)
         value_grad_var = (value_grad_var * item_scale).astype(BF)
 
         key_grad = jnp.concatenate([key_flat, key_var, key_var], axis=0)
@@ -449,18 +939,9 @@
             count = embed_grad.shape[0] // 2
             pairs = embed_grad.reshape((count, 2) + embed_grad.shape[1:])
             embed_grad = pick(pairs, own, 1) + exchange(pick(pairs, 1 - own, 1), "mp", mp, bit)
-        embed_grad = links.scatter_sum(embed_grad[0])
-
-        pool_out_grad = links.scatter_product(pool_grad_low, pooled, item_scale)
-        value_weight_grad = links.scatter_product(
-            embed_all,
-            jnp.concatenate([value_grad_flat, value_grad_var, value_grad_var], axis=0),
-            jnp.float32(1.0),
-        )
+        merges["embed"] = ShardMerge(links, embed_grad[0])
         position = (grad_own * item_scale).reshape(row_count // 2, dp, shard).transpose(1, 0, 2)
-        position = links.scatter_sum(position)
-        position = links.global_rows(position, links.other_rows(position))
-
+        merges["position"] = ShardMerge(links, position)
         pixel_own = links.sum_rows(pixel_part)
         pixel_grad = links.global_rows(pixel_own, links.other_rows(pixel_own))
         pixel_grad = pixel_grad.T.reshape(1, var_count, pix_count, row_count)
@@ -474,8 +955,8 @@
         own_sums = jnp.stack([row_sums[name] for name in names]) * item_scale
         full_sums = own_sums + exchange(own_sums, "mp", mp, 0)
         local = jnp.stack([local_sums["up_bias", layer] for layer in range(layer_count)]) * item_scale
-        thin = [local_sums["qv", layer, which] for layer in range(layer_count) for which in range(2)]
-        thin = jnp.stack(thin + [local_sums["pool_bias"]]) * item_scale
+        thin = [local_sums["qv", layer] for layer in range(layer_count)]
+        thin = jnp.concatenate(thin + [local_sums["pool_bias"][None]], axis=0) * item_scale
         packed = jnp.concatenate(
             [
                 full_sums.reshape(len(names), dp, shard).transpose(1, 0, 2).reshape(dp, -1),
@@ -486,7 +967,36 @@
             ],
             axis=1,
         )
-        packed = links.scatter_sum(packed[:, None, :])[0]
+        merges["vectors"] = ShardMerge(links, packed[:, None, :])
+        for name in DRAIN:
+            if merges[name].open:
+                merges[name].advance(clock)
+        for merge in merges.values():
+            while merge.open:
+                merge.advance(clock)
+        hidden = hidden + (last_mine + last_got) + down_bias[top]
+        layer_out = links.global_rows(hidden, links.other_rows(hidden))
+        finished = {
+            kind: finish_layers(
+                kind,
+                [
+                    part
+                    for layer in range(layer_count)
+                    for part in (merges[kind, top - layer].keep, merges[kind, top - layer].got)
+                ],
+                layer_count,
+                shard,
+                local_width,
+            )
+            for kind in ("down", "up", "att")
+        }
+        tail_total = merges["tail"].keep + merges["tail"].got
+        embed_grad = (merges["embed"].keep + merges["embed"].got)[0]
+        position = (merges["position"].keep + merges["position"].got)[0]
+        position = links.global_rows(position, links.other_rows(position))
+        packed, _ = lax.optimization_barrier(
+            ((merges["vectors"].keep + merges["vectors"].got)[0, 0], clock.cell)
+        )
         offset = 0
 
         def take(*shape):
@@ -517,7 +1027,6 @@
             jnp.repeat(key_shard, HEAD_DIM, axis=1) * query_vec.astype(F32)[None, :] / ROOT_DIM
         )
         embed_turned = embed_grad.T
-        hidden_width = weight_grads[0][0].shape[1]
         return (
             layer_out[None],
             pixel_grad,
@@ -527,26 +1036,21 @@
             embed_turned[flat_all],
             query_weight_grad,
             key_weight_grad,
-            value_weight_grad,
+            tail_total[:, local_width:],
             thin_total[-1],
-            pool_out_grad.T,
+            tail_total[:, :local_width].T,
             column_total,
             lead_total,
             column_total,
             gain_list,
             biases,
-            jnp.stack(
-                [
-                    grads[3].reshape(shard, 3, local_width).transpose(1, 0, 2)
-                    for grads in weight_grads
-                ]
-            ),
+            finished["att"][1],
             thin_total[:-1].reshape(layer_count, 2, local_width // dp),
-            jnp.stack([grads[2].T for grads in weight_grads]),
+            finished["att"][0],
             dense_bias[:, 0],
-            jnp.stack([grads[1] for grads in weight_grads]),
+            finished["up"][0],
             up_bias_total,
-            jnp.stack([grads[0].T for grads in weight_grads]),
+            finished["down"][0],
             dense_bias[:, 1],
         )
 

time: 837 us -> 659 us (0.79)
  Pallas kernels: 0 us -> 119 us
  waiting for transfers between devices: 343 us -> 238 us
  local copies, waits for them, and re-layouts: 162 us -> 84.1 us
  matrix products: 133 us -> 61.4 us
  other arithmetic: 105 us -> 68.6 us
    pallas_call x0 -> x55, Pallas kernels: none -> 119 us  [the longest x14 50.5 us: product_rows(): pl.pallas_call(kernel, out_shape=out_shape, grid=(count,), in_specs=in_sp...]
    ppermute x76 -> x67, waiting for transfers between devices: 343 us -> 238 us  [exchange(): return lax.ppermute(tensor, axis, [(i, i ^ 1 << bit) for i in range(size)])]
    concatenate x36 -> x5, local copies, waits for them, and re-layouts: 67.6 us -> 1.44 us  [per_device(): jnp.concatenate(thin + [local_sums['pool_bias'][None]], axis=0) * item_scale]
    dot_general x22 -> x2, matrix products: 40.9 us -> 0.52 us  [matmul_tn(): lax.dot_general(left, right, (((0,), (0,)), ((), ())), preferred_element_...]
    dynamic_slice x26 -> x5, local copies, waits for them, and re-layouts: 26.6 us -> 2.42 us  [pick(): return lax.dynamic_index_in_dim(tensor, index, axis, keepdims=False)]
    unnamed x423 -> x534, local copies, waits for them, and re-layouts: 20.9 us -> 42.6 us
    another operation x15 -> x0, other arithmetic: 13.8 us -> none
    select_n x10 -> x1, other arithmetic: 14.1 us -> 0.52 us  [take_columns(): pieces = rows.reshape(rows.shape[0], -1, shard)[:, shards]]
  transfers between devices with their start and end apart: 76 -> 67, of which waited for: 34 -> 34; matrix products, arithmetic and copies ran while one was open for 40% -> 20% of each run, Pallas kernels for 0% -> 16%
where the time goes in v3:
time: 659 us; the launch traced here: 647 us
  waiting for transfers between devices  238 us (36%)
  Pallas kernels  119 us (18%)
  local copies, waits for them, and re-layouts  84.1 us (13%)
  starting transfers between devices  69.3 us (11%)
  other arithmetic  68.6 us (10%)
  matrix products  61.4 us (9%)
  between operations  6.73 us (1%)
    ppermute x67, waiting for transfers between devices, exchange(): return lax.ppermute(tensor, axis, [(i, i ^ 1 << bit) for i in range(size)])  238 us
    ppermute x67, starting transfers between devices, exchange(): return lax.ppermute(tensor, axis, [(i, i ^ 1 << bit) for i in range(size)])  69.3 us
    pallas_call x14, Pallas kernels, product_rows(): pl.pallas_call(kernel, out_shape=out_shape, grid=(count,), in_specs=in_sp...  50.5 us
    unnamed x534, local copies, waits for them, and re-layouts  42.6 us
    pallas_call x7, Pallas kernels, add_split(): pl.pallas_call(kernel, out_shape=[jax.ShapeDtypeStruct((half, width), F32...  20.8 us
    dot_general x11, matrix products, matmul(): return jnp.dot(left, right, preferred_element_type=F32)  18.2 us
  transfers between devices with their start and end apart: 67, of which 34 were waited for; matrix products, arithmetic and copies ran while one was open for 20% of the time, Pallas kernels for 16%

profile of v3, /device:TPU:0, one launch (start us, length us, event | category | flops | bytes accessed | tf_op | source)
XLA Modules:
  0.0 647.2 jit_solution(1496775301410291620)
XLA Ops:
  12.8 4.2 fusion.119
  17.2 3.2 fusion.112
  25.0 2.9 collective-permute-start.4
  40.3 5.5 collective-permute-done.4
  51.9 3.9 attend_forward.2
  69.2 13.4 %collective-permute-done.7 = f32[192,1024]{1,0:T(8,128)} collective-permute-done((f32[192,1024]{1,0:T(8,128)}, f32[192,1024]{1,0:T(8,128)}, u32[]{:S(2)}, u32[]{:S(2)}) %collective-permute-start.7) | collective-permute-done | bytes 786464 | tf_op jit(solution)/shard_map/ppermute | solution.py:56
  87.2 6.0 multiply_convert_fusion.4
  103.3 13.1 %collective-permute-done.10 = f32[192,1024]{1,0:T(8,128)S(1)} collective-permute-done((f32[192,1024]{1,0:T(8,128)S(1)}, f32[192,1024]{1,0:T(8,128)S(1)}, u32[]{:S(2)}, u32[]{:S(2)}) %collective-permute-start.10) | collective-permute-done | bytes 786464 | tf_op jit(solution)/shard_map/ppermute | solution.py:56
  120.0 3.1 attend_forward.3
  139.7 7.5 %collective-permute-done.13 = f32[192,1024]{1,0:T(8,128)} collective-permute-done((f32[192,1024]{1,0:T(8,128)}, f32[192,1024]{1,0:T(8,128)}, u32[]{:S(2)}, u32[]{:S(2)}) %collective-permute-start.13) | collective-permute-done | bytes 786464 | tf_op jit(solution)/shard_map/ppermute | solution.py:56
  149.9 3.6 gather_fusion
  162.2 4.4 fusion.183
  186.1 17.8 %collective-permute-done.16.got_ref = f32[192,1024]{1,0:T(8,128)} collective-permute-done((f32[192,1024]{1,0:T(8,128)}, f32[192,1024]{1,0:T(8,128)}, u32[]{:S(2)}, u32[]{:S(2)}) %collective-permute-start.16) | collective-permute-done | bytes 786464 | tf_op jit(solution)/shard_map/ppermute | solution.py:56
  212.9 4.9 attend_back.2
  226.6 4.5 product_rows.17
  233.6 4.6 product_rows.18
  244.0 8.1 %collective-permute-done.19.got_ref = f32[192,1024]{1,0:T(8,128)} collective-permute-done((f32[192,1024]{1,0:T(8,128)}, f32[192,1024]{1,0:T(8,128)}, u32[]{:S(2)}, u32[]{:S(2)}) %collective-permute-start.19) | collective-permute-done | bytes 786464 | tf_op jit(solution)/shard_map/ppermute | solution.py:56
  276.4 14.5 %collective-permute-done.24.got_ref = f32[192,1024]{1,0:T(8,128)} collective-permute-done((f32[192,1024]{1,0:T(8,128)}, f32[192,1024]{1,0:T(8,128)}, u32[]{:S(2)}, u32[]{:S(2)}) %collective-permute-start.24) | collective-permute-done | bytes 786464 | tf_op jit(solution)/shard_map/ppermute | solution.py:56
  298.0 3.9 add_split.7
  302.8 4.7 product_rows.20
  308.5 4.9 attend_back.3
  323.8 3.5 add_split.8
  330.3 20.6 %collective-permute-done.30.got_ref = f32[256,1024]{1,0:T(8,128)} collective-permute-done((f32[256,1024]{1,0:T(8,128)}, f32[256,1024]{1,0:T(8,128)}, u32[]{:S(2)}, u32[]{:S(2)}) %collective-permute-start.30) | collective-permute-done | bytes 1048608 | tf_op jit(solution)/shard_map/ppermute | solution.py:56
  351.0 3.7 add_split.9
  367.4 4.6 product_rows.22
  373.0 2.9 product_rows.23
  376.9 6.5 %multiply_reduce_fusion = (f32[384,768]{1,0:T(8,128)}, f32[4,384,768]{2,1,0:T(8,128)}) fusion(f32[4,384,768]{2,1,0:T(8,128)} %fusion.119, bf16[4,384,64]{1,2,0:T(8,128)(2,1)S(1)} %bitcast.315, bf16[4,768,64]{1,2,0:T(8,128)(2,1)S(1)} %bitcast.312), kind=kOutput, calls=%fused_computation.3 | convolution fusion | flops 153059328 | bytes 11206656 | tf_op jit(solution)/shard_map/hrd,hkd->hrk/dot_general | solution.py:863
  383.4 3.3 fusion.193
  386.8 4.0 fusion.111
  407.4 4.5 product_rows.24
  413.1 9.0 %collective-permute-done.37.got_ref = f32[256,1024]{1,0:T(8,128)} collective-permute-done((f32[256,1024]{1,0:T(8,128)}, f32[256,1024]{1,0:T(8,128)}, u32[]{:S(2)}, u32[]{:S(2)}) %collective-permute-start.37) | collective-permute-done | bytes 1048608 | tf_op jit(solution)/shard_map/ppermute | solution.py:56
  423.6 3.5 add_split.10
  434.4 2.9 product_rows.25
  455.0 4.7 product_rows.26
  469.6 8.4 %collective-permute-done.65.refs_1_ = f32[128,1024]{1,0:T(8,128)} collective-permute-done((f32[128,1024]{1,0:T(8,128)}, f32[128,1024]{1,0:T(8,128)}, u32[]{:S(2)}, u32[]{:S(2)}) %collective-permute-start.65) | collective-permute-done | bytes 524320 | tf_op jit(solution)/shard_map/ppermute | solution.py:56
  498.1 3.4 collective-permute-start.62
  508.4 38.5 %collective-permute-done.63.refs_1_ = f32[128,1024]{1,0:T(8,128)S(1)} collective-permute-done((f32[128,1024]{1,0:T(8,128)S(1)}, f32[128,1024]{1,0:T(8,128)S(1)}, u32[]{:S(2)}, u32[]{:S(2)}) %collective-permute-start.63) | collective-permute-done | bytes 524320 | tf_op jit(solution)/shard_map/ppermute | solution.py:56
  549.1 3.3 collective-permute-start.55
  555.4 16.6 %collective-permute-done.55 = f32[1,192,128]{2,1,0:T(8,128)S(1)} collective-permute-done((f32[1,192,128]{2,1,0:T(8,128)S(1)}, f32[1,192,128]{2,1,0:T(8,128)S(1)}, u32[]{:S(2)}, u32[]{:S(2)}) %collective-permute-start.55) | collective-permute-done | bytes 98336 | tf_op jit(solution)/shard_map/ppermute | solution.py:56
  577.7 3.5 add_split.12
  581.3 3.4 collective-permute-start.61
  584.7 9.3 %collective-permute-done.43 = f32[1,8,32,817]{3,2,1,0:T(8,128)} collective-permute-done((f32[1,8,32,817]{3,2,1,0:T(8,128)}, f32[1,8,32,817]{3,2,1,0:T(8,128)}, u32[]{:S(2)}, u32[]{:S(2)}) %collective-permute-start.43) | collective-permute-done | bytes 836640 | tf_op jit(solution)/shard_map/ppermute | solution.py:56
  598.0 3.3 product_rows.27
  603.0 4.6 collective-permute-done.47
  613.3 6.7 %collective-permute-done.59.got_ref = f32[256,512]{1,0:T(8,128)S(1)} collective-permute-done((f32[256,512]{1,0:T(8,128)S(1)}, f32[256,512]{1,0:T(8,128)S(1)}, u32[]{:S(2)}, u32[]{:S(2)}) %collective-permute-start.59) | collective-permute-done | bytes 524320 | tf_op jit(solution)/shard_map/ppermute | solution.py:56
  620.0 4.8 collective-permute-done.52
  625.8 3.0 collective-permute-start.60
  628.8 10.5 %collective-permute-done.53 = f32[1,32,817]{2,1,0:T(8,128)} collective-permute-done((f32[1,32,817]{2,1,0:T(8,128)}, f32[1,32,817]{2,1,0:T(8,128)}, u32[]{:S(2)}, u32[]{:S(2)}) %collective-permute-start.53) | collective-permute-done | bytes 104608 | tf_op jit(solution)/shard_map/ppermute | solution.py:56
  (892 shorter events, 308.4 us)
Async XLA Ops:
  25.0 20.8 %collective-permute-start.4 = (f32[192,1024]{1,0:T(8,128)S(1)}, f32[192,1024]{1,0:T(8,128)S(1)}, u32[]{:S(2)}, u32[]{:S(2)}) collective-permute-start(f32[192,1024]{1,0:T(8,128)S(1)} %convolution_add_fusion), channel_id=1, source_target_pairs={{0,2},{1,3},{2,0},{3,1},{4,6},{5,7},{6,4},{7,5},{8,10},{9,11},{10,... | collective-permute-start | bytes 2359304 | tf_op jit(solution)/shard_map/ppermute | solution.py:56
  62.7 19.9 %collective-permute-start.7 = (f32[192,1024]{1,0:T(8,128)}, f32[192,1024]{1,0:T(8,128)}, u32[]{:S(2)}, u32[]{:S(2)}) collective-permute-start(f32[192,1024]{1,0:T(8,128)} %add.411), channel_id=1, source_target_pairs={{0,2},{1,3},{2,0},{3,1},{4,6},{5,7},{6,4},{7,5},{8,10},{9,11},{10,... | collective-permute-start | bytes 2359304 | tf_op jit(solution)/shard_map/ppermute | solution.py:56
  96.8 19.6 %collective-permute-start.10 = (f32[192,1024]{1,0:T(8,128)S(1)}, f32[192,1024]{1,0:T(8,128)S(1)}, u32[]{:S(2)}, u32[]{:S(2)}) collective-permute-start(f32[192,1024]{1,0:T(8,128)S(1)} %fusion.64), channel_id=1, source_target_pairs={{0,2},{1,3},{2,0},{3,1},{4,6},{5,7},{6,4},{7,5},{8,10},{9,11},{10,... | collective-permute-start | bytes 2359304 | tf_op jit(solution)/shard_map/ppermute | solution.py:56
  127.3 19.9 %collective-permute-start.13 = (f32[192,1024]{1,0:T(8,128)}, f32[192,1024]{1,0:T(8,128)}, u32[]{:S(2)}, u32[]{:S(2)}) collective-permute-start(f32[192,1024]{1,0:T(8,128)} %add.431), channel_id=1, source_target_pairs={{0,2},{1,3},{2,0},{3,1},{4,6},{5,7},{6,4},{7,5},{8,10},{9,11},{10,... | collective-permute-start | bytes 2359304 | tf_op jit(solution)/shard_map/ppermute | solution.py:56
  149.8 10.1 %collective-permute-start.14 = (f32[192,1024]{1,0:T(8,128)S(1)}, f32[192,1024]{1,0:T(8,128)}, u32[]{:S(2)}, u32[]{:S(2)}) collective-permute-start(f32[192,1024]{1,0:T(8,128)S(1)} %subtract_multiply_fusion.own_ref.unit_ref), channel_id=1, source_target_pairs={{0,1},{1,0},{2,3},{3,2},{4,5},{5,4},{6,7},{7,6},{8,9},{9,8},{10,11... | collective-permute-start | bytes 2359304 | tf_op jit(solution)/shard_map/ppermute | solution.py:56
  178.3 48.3 %collective-permute-start.21 = (f32[512,1024]{1,0:T(8,128)}, f32[512,1024]{1,0:T(8,128)}, u32[]{:S(2)}, u32[]{:S(2)}) collective-permute-start(f32[512,1024]{1,0:T(8,128)} %product_rows.14), channel_id=1, source_target_pairs={{0,8},{4,12},{8,0},{12,4},{16,24},{20,28},{24,16},{28,20},{1,9},{5... | collective-permute-start | bytes 6291464 | tf_op jit(solution)/shard_map/ppermute | solution.py:56
  180.1 52.0 %collective-permute-start.20 = (f32[512,1024]{1,0:T(8,128)}, f32[512,1024]{1,0:T(8,128)}, u32[]{:S(2)}, u32[]{:S(2)}) collective-permute-start(f32[512,1024]{1,0:T(8,128)} %product_rows.15), channel_id=1, source_target_pairs={{0,4},{4,0},{8,12},{12,8},{16,20},{20,16},{24,28},{28,24},{1,5},{5... | collective-permute-start | bytes 6291464 | tf_op jit(solution)/shard_map/ppermute | solution.py:56
  184.6 19.3 %collective-permute-start.16 = (f32[192,1024]{1,0:T(8,128)}, f32[192,1024]{1,0:T(8,128)}, u32[]{:S(2)}, u32[]{:S(2)}) collective-permute-start(f32[192,1024]{1,0:T(8,128)} %add.444.mine_ref), channel_id=1, source_target_pairs={{0,2},{1,3},{2,0},{3,1},{4,6},{5,7},{6,4},{7,5},{8,10},{9,11},{10,... | collective-permute-start | bytes 2359304 | tf_op jit(solution)/shard_map/ppermute | solution.py:56
  232.1 19.9 %collective-permute-start.19 = (f32[192,1024]{1,0:T(8,128)}, f32[192,1024]{1,0:T(8,128)}, u32[]{:S(2)}, u32[]{:S(2)}) collective-permute-start(f32[192,1024]{1,0:T(8,128)} %add.445.mine_ref), channel_id=1, source_target_pairs={{0,2},{1,3},{2,0},{3,1},{4,6},{5,7},{6,4},{7,5},{8,10},{9,11},{10,... | collective-permute-start | bytes 2359304 | tf_op jit(solution)/shard_map/ppermute | solution.py:56
  238.3 59.7 %collective-permute-start.27 = (f32[256,1024]{1,0:T(8,128)}, f32[256,1024]{1,0:T(8,128)}, u32[]{:S(2)}, u32[]{:S(2)}) collective-permute-start(f32[256,1024]{1,0:T(8,128)} %get-tuple-element.431), channel_id=1, source_target_pairs={{0,8},{4,12},{8,0},{12,4},{16,24},{20,28},{24,16},{28,20},{1,9},{5... | collective-permute-start | bytes 3145736 | tf_op jit(solution)/shard_map/ppermute | solution.py:56
  239.9 62.9 %collective-permute-start.26 = (f32[512,1024]{1,0:T(8,128)}, f32[512,1024]{1,0:T(8,128)}, u32[]{:S(2)}, u32[]{:S(2)}) collective-permute-start(f32[512,1024]{1,0:T(8,128)} %product_rows.16), channel_id=1, source_target_pairs={{0,4},{4,0},{8,12},{12,8},{16,20},{20,16},{24,28},{28,24},{1,5},{5... | collective-permute-start | bytes 6291464 | tf_op jit(solution)/shard_map/ppermute | solution.py:56
  241.4 82.4 %collective-permute-start.31 = (f32[256,1024]{1,0:T(8,128)}, f32[256,1024]{1,0:T(8,128)}, u32[]{:S(2)}, u32[]{:S(2)}) collective-permute-start(f32[256,1024]{1,0:T(8,128)} %get-tuple-element.455), channel_id=1, source_target_pairs={{0,16},{4,20},{8,24},{12,28},{16,0},{20,4},{24,8},{28,12},{1,17},{... | collective-permute-start | bytes 3145736 | tf_op jit(solution)/shard_map/ppermute | solution.py:56
  270.8 20.1 %collective-permute-start.24 = (f32[192,1024]{1,0:T(8,128)}, f32[192,1024]{1,0:T(8,128)}, u32[]{:S(2)}, u32[]{:S(2)}) collective-permute-start(f32[192,1024]{1,0:T(8,128)} %add.446.mine_ref), channel_id=1, source_target_pairs={{0,2},{1,3},{2,0},{3,1},{4,6},{5,7},{6,4},{7,5},{8,10},{9,11},{10,... | collective-permute-start | bytes 2359304 | tf_op jit(solution)/shard_map/ppermute | solution.py:56
  275.0 92.3 %collective-permute-start.33 = (f32[512,1024]{1,0:T(8,128)}, f32[512,1024]{1,0:T(8,128)}, u32[]{:S(2)}, u32[]{:S(2)}) collective-permute-start(f32[512,1024]{1,0:T(8,128)} %product_rows.19), channel_id=1, source_target_pairs={{0,4},{4,0},{8,12},{12,8},{16,20},{20,16},{24,28},{28,24},{1,5},{5... | collective-permute-start | bytes 6291464 | tf_op jit(solution)/shard_map/ppermute | solution.py:56
  313.4 5.5 collective-permute-start.28
  314.2 36.7 %collective-permute-start.30 = (f32[256,1024]{1,0:T(8,128)}, f32[256,1024]{1,0:T(8,128)}, u32[]{:S(2)}, u32[]{:S(2)}) collective-permute-start(f32[256,1024]{1,0:T(8,128)} %get-tuple-element.453), channel_id=1, source_target_pairs={{0,8},{4,12},{8,0},{12,4},{16,24},{20,28},{24,16},{28,20},{1,9},{5... | collective-permute-start | bytes 3145736 | tf_op jit(solution)/shard_map/ppermute | solution.py:56
  315.7 192.1 %collective-permute-start.64 = (f32[128,1024]{1,0:T(8,128)}, f32[128,1024]{1,0:T(8,128)}, u32[]{:S(2)}, u32[]{:S(2)}) collective-permute-start(f32[128,1024]{1,0:T(8,128)} %get-tuple-element.593), channel_id=1, source_target_pairs={{0,16},{4,20},{8,24},{12,28},{16,0},{20,4},{24,8},{28,12},{1,17},{... | collective-permute-start | bytes 1572872 | tf_op jit(solution)/shard_map/ppermute | solution.py:56
  327.3 27.3 %collective-permute-start.29 = (f32[192,1024]{1,0:T(8,128)}, f32[192,1024]{1,0:T(8,128)}, u32[]{:S(2)}, u32[]{:S(2)}) collective-permute-start(f32[192,1024]{1,0:T(8,128)} %add.447.mine_ref), channel_id=1, source_target_pairs={{0,2},{1,3},{2,0},{3,1},{4,6},{5,7},{6,4},{7,5},{8,10},{9,11},{10,... | collective-permute-start | bytes 2359304 | tf_op jit(solution)/shard_map/ppermute | solution.py:56
  328.8 77.2 %collective-permute-start.38 = (f32[512,1024]{1,0:T(8,128)}, f32[512,1024]{1,0:T(8,128)}, u32[]{:S(2)}, u32[]{:S(2)}) collective-permute-start(f32[512,1024]{1,0:T(8,128)} %product_rows.21), channel_id=1, source_target_pairs={{0,4},{4,0},{8,12},{12,8},{16,20},{20,16},{24,28},{28,24},{1,5},{5... | collective-permute-start | bytes 6291464 | tf_op jit(solution)/shard_map/ppermute | solution.py:56
  357.6 6.6 %collective-permute-start.32 = (f32[192,1024]{1,0:T(8,128)}, f32[192,1024]{1,0:T(8,128)}, u32[]{:S(2)}, u32[]{:S(2)}) collective-permute-start(f32[192,1024]{1,0:T(8,128)} %get-tuple-element.477), channel_id=1, source_target_pairs={{0,1},{1,0},{2,3},{3,2},{4,5},{5,4},{6,7},{7,6},{8,9},{9,8},{10,11... | collective-permute-start | bytes 2359304 | tf_op jit(solution)/shard_map/ppermute | solution.py:56
  361.5 108.1 %collective-permute-start.66 = (f32[128,1024]{1,0:T(8,128)}, f32[128,1024]{1,0:T(8,128)}, u32[]{:S(2)}, u32[]{:S(2)}) collective-permute-start(f32[128,1024]{1,0:T(8,128)} %get-tuple-element.597), channel_id=1, source_target_pairs={{0,4},{4,0},{8,12},{12,8},{16,20},{20,16},{24,28},{28,24},{1,5},{5... | collective-permute-start | bytes 1572872 | tf_op jit(solution)/shard_map/ppermute | solution.py:56
  395.7 7.5 %collective-permute-start.34 = (f32[192,1024]{1,0:T(8,128)}, f32[192,1024]{1,0:T(8,128)}, u32[]{:S(2)}, u32[]{:S(2)}) collective-permute-start(f32[192,1024]{1,0:T(8,128)} %fusion.11), channel_id=1, source_target_pairs={{0,1},{1,0},{2,3},{3,2},{4,5},{5,4},{6,7},{7,6},{8,9},{9,8},{10,11... | collective-permute-start | bytes 2359304 | tf_op jit(solution)/shard_map/ppermute | solution.py:56
  395.8 26.3 %collective-permute-start.37 = (f32[256,1024]{1,0:T(8,128)}, f32[256,1024]{1,0:T(8,128)}, u32[]{:S(2)}, u32[]{:S(2)}) collective-permute-start(f32[256,1024]{1,0:T(8,128)} %get-tuple-element.508), channel_id=1, source_target_pairs={{0,8},{4,12},{8,0},{12,4},{16,24},{20,28},{24,16},{28,20},{1,9},{5... | collective-permute-start | bytes 3145736 | tf_op jit(solution)/shard_map/ppermute | solution.py:56
  403.2 49.6 %collective-permute-start.46 = (f32[512,1024]{1,0:T(8,128)}, f32[512,1024]{1,0:T(8,128)}, u32[]{:S(2)}, u32[]{:S(2)}) collective-permute-start(f32[512,1024]{1,0:T(8,128)} %product_rows.23), channel_id=1, source_target_pairs={{0,4},{4,0},{8,12},{12,8},{16,20},{20,16},{24,28},{28,24},{1,5},{5... | collective-permute-start | bytes 6291464 | tf_op jit(solution)/shard_map/ppermute | solution.py:56
  411.9 47.7 %collective-permute-start.45 = (f32[256,1024]{1,0:T(8,128)}, f32[256,1024]{1,0:T(8,128)}, u32[]{:S(2)}, u32[]{:S(2)}) collective-permute-start(f32[256,1024]{1,0:T(8,128)} %get-tuple-element.533), channel_id=1, source_target_pairs={{0,8},{4,12},{8,0},{12,4},{16,24},{20,28},{24,16},{28,20},{1,9},{5... | collective-permute-start | bytes 3145736 | tf_op jit(solution)/shard_map/ppermute | solution.py:56
  422.1 44.1 %collective-permute-start.35 = (f32[192,1024]{1,0:T(8,128)}, f32[192,1024]{1,0:T(8,128)}, u32[]{:S(2)}, u32[]{:S(2)}) collective-permute-start(f32[192,1024]{1,0:T(8,128)} %add.448), channel_id=1, source_target_pairs={{0,2},{1,3},{2,0},{3,1},{4,6},{5,7},{6,4},{7,5},{8,10},{9,11},{10,... | collective-permute-start | bytes 2359304 | tf_op jit(solution)/shard_map/ppermute | solution.py:56
  452.7 25.3 %collective-permute-start.65 = (f32[128,1024]{1,0:T(8,128)}, f32[128,1024]{1,0:T(8,128)}, u32[]{:S(2)}, u32[]{:S(2)}) collective-permute-start(f32[128,1024]{1,0:T(8,128)} %get-tuple-element.595), channel_id=1, source_target_pairs={{0,16},{4,20},{8,24},{12,28},{16,0},{20,4},{24,8},{28,12},{1,17},{... | collective-permute-start | bytes 1572872 | tf_op jit(solution)/shard_map/ppermute | solution.py:56
  459.6 89.4 %collective-permute-start.42 = (f32[2,8,32,817]{3,2,1,0:T(8,128)}, f32[2,8,32,817]{3,2,1,0:T(8,128)}, u32[]{:S(2)}, u32[]{:S(2)}) collective-permute-start(f32[2,8,32,817]{3,2,1,0:T(8,128)} %pad_maximum_fusion), channel_id=1, source_target_pairs={{0,1},{1,0},{2,3},{3,2},{4,5},{5,4},{6,7},{7,6},{8,9},{9,8},{10,11... | collective-permute-start | bytes 5019656 | tf_op jit(solution)/shard_map/ppermute | solution.py:56
  466.2 14.3 %collective-permute-start.48 = (f32[4,1,2976]{2,1,0:T(1,128)S(1)}, f32[4,1,2976]{2,1,0:T(1,128)S(1)}, u32[]{:S(2)}, u32[]{:S(2)}) collective-permute-start(f32[4,1,2976]{2,1,0:T(1,128)S(1)} %dynamic-slice_bitcast_fusion.3), channel_id=1, source_target_pairs={{0,4},{4,0},{8,12},{12,8},{16,20},{20,16},{24,28},{28,24},{1,5},{5... | collective-permute-start | bytes 142856 | tf_op jit(solution)/shard_map/ppermute | solution.py:56
  469.6 11.9 %collective-permute-start.39 = (f32[192,768]{1,0:T(8,128)S(1)}, f32[192,768]{1,0:T(8,128)S(1)}, u32[]{:S(2)}, u32[]{:S(2)}) collective-permute-start(f32[192,768]{1,0:T(8,128)S(1)} %copy-done.159), channel_id=1, source_target_pairs={{0,1},{1,0},{2,3},{3,2},{4,5},{5,4},{6,7},{7,6},{8,9},{9,8},{10,11... | collective-permute-start | bytes 1769480 | tf_op jit(solution)/shard_map/ppermute | solution.py:56
  478.1 25.9 %collective-permute-start.36 = (f32[192,1024]{1,0:T(8,128)}, f32[192,1024]{1,0:T(8,128)}, u32[]{:S(2)}, u32[]{:S(2)}) collective-permute-start(f32[192,1024]{1,0:T(8,128)} %add_add_fusion), channel_id=1, source_target_pairs={{0,1},{1,0},{2,3},{3,2},{4,5},{5,4},{6,7},{7,6},{8,9},{9,8},{10,11... | collective-permute-start | bytes 2359304 | tf_op jit(solution)/shard_map/ppermute | solution.py:56
  482.3 15.8 %collective-permute-start.40 = (f32[192,768]{1,0:T(8,128)}, f32[192,768]{1,0:T(8,128)}, u32[]{:S(2)}, u32[]{:S(2)}) collective-permute-start(f32[192,768]{1,0:T(8,128)} %slice_add_fusion), channel_id=1, source_target_pairs={{0,2},{1,3},{2,0},{3,1},{4,6},{5,7},{6,4},{7,5},{8,10},{9,11},{10,... | collective-permute-start | bytes 1769480 | tf_op jit(solution)/shard_map/ppermute | solution.py:56
  490.1 12.7 %collective-permute-start.49 = (f32[4,192,128]{2,1,0:T(8,128)S(1)}, f32[4,192,128]{2,1,0:T(8,128)}, u32[]{:S(2)}, u32[]{:S(2)}) collective-permute-start(f32[4,192,128]{2,1,0:T(8,128)S(1)} %bitcast.342), channel_id=1, source_target_pairs={{0,4},{4,0},{8,12},{12,8},{16,20},{20,16},{24,28},{28,24},{1,5},{5... | collective-permute-start | bytes 1179656 | tf_op jit(solution)/shard_map/ppermute | solution.py:56
  498.1 112.9 %collective-permute-start.62 = (f32[128,1024]{1,0:T(8,128)}, f32[128,1024]{1,0:T(8,128)}, u32[]{:S(2)}, u32[]{:S(2)}) collective-permute-start(f32[128,1024]{1,0:T(8,128)} %get-tuple-element.587), channel_id=1, source_target_pairs={{0,16},{4,20},{8,24},{12,28},{16,0},{20,4},{24,8},{28,12},{1,17},{... | collective-permute-start | bytes 1572872 | tf_op jit(solution)/shard_map/ppermute | solution.py:56
  502.8 44.1 %collective-permute-start.63 = (f32[128,1024]{1,0:T(8,128)S(1)}, f32[128,1024]{1,0:T(8,128)S(1)}, u32[]{:S(2)}, u32[]{:S(2)}) collective-permute-start(f32[128,1024]{1,0:T(8,128)S(1)} %copy-done.47), channel_id=1, source_target_pairs={{0,16},{4,20},{8,24},{12,28},{16,0},{20,4},{24,8},{28,12},{1,17},{... | collective-permute-start | bytes 1572872 | tf_op jit(solution)/shard_map/ppermute | solution.py:56
  504.0 45.0 %collective-permute-start.54 = (f32[2,192,128]{2,1,0:T(8,128)S(1)}, f32[2,192,128]{2,1,0:T(8,128)S(1)}, u32[]{:S(2)}, u32[]{:S(2)}) collective-permute-start(f32[2,192,128]{2,1,0:T(8,128)S(1)} %dynamic-slice_bitcast_fusion.2), channel_id=1, source_target_pairs={{0,8},{4,12},{8,0},{12,4},{16,24},{20,28},{24,16},{28,20},{1,9},{5... | collective-permute-start | bytes 589832 | tf_op jit(solution)/shard_map/ppermute | solution.py:56
  507.8 88.6 %collective-permute-start.51 = (f32[512,512]{1,0:T(8,128)}, f32[512,512]{1,0:T(8,128)}, u32[]{:S(2)}, u32[]{:S(2)}) collective-permute-start(f32[512,512]{1,0:T(8,128)} %product_rows.25), channel_id=1, source_target_pairs={{0,4},{4,0},{8,12},{12,8},{16,20},{20,16},{24,28},{28,24},{1,5},{5... | collective-permute-start | bytes 3145736 | tf_op jit(solution)/shard_map/ppermute | solution.py:56
  546.9 30.8 %collective-permute-start.50 = (f32[256,1024]{1,0:T(8,128)}, f32[256,1024]{1,0:T(8,128)}, u32[]{:S(2)}, u32[]{:S(2)}) collective-permute-start(f32[256,1024]{1,0:T(8,128)} %get-tuple-element.556), channel_id=1, source_target_pairs={{0,8},{4,12},{8,0},{12,4},{16,24},{20,28},{24,16},{28,20},{1,9},{5... | collective-permute-start | bytes 3145736 | tf_op jit(solution)/shard_map/ppermute | solution.py:56
  549.0 24.7 %collective-permute-start.41 = (f32[192,768]{1,0:T(8,128)S(1)}, f32[192,768]{1,0:T(8,128)S(1)}, u32[]{:S(2)}, u32[]{:S(2)}) collective-permute-start(f32[192,768]{1,0:T(8,128)S(1)} %add.458), channel_id=1, source_target_pairs={{0,1},{1,0},{2,3},{3,2},{4,5},{5,4},{6,7},{7,6},{8,9},{9,8},{10,11... | collective-permute-start | bytes 1769480 | tf_op jit(solution)/shard_map/ppermute | solution.py:56
  549.1 22.9 %collective-permute-start.55 = (f32[1,192,128]{2,1,0:T(8,128)S(1)}, f32[1,192,128]{2,1,0:T(8,128)S(1)}, u32[]{:S(2)}, u32[]{:S(2)}) collective-permute-start(f32[1,192,128]{2,1,0:T(8,128)S(1)} %constant_dynamic-slice_fusion.1), channel_id=1, source_target_pairs={{0,16},{4,20},{8,24},{12,28},{16,0},{20,4},{24,8},{28,12},{1,17},{... | collective-permute-start | bytes 294920 | tf_op jit(solution)/shard_map/ppermute | solution.py:56
  572.0 22.0 %collective-permute-start.43 = (f32[1,8,32,817]{3,2,1,0:T(8,128)}, f32[1,8,32,817]{3,2,1,0:T(8,128)}, u32[]{:S(2)}, u32[]{:S(2)}) collective-permute-start(f32[1,8,32,817]{3,2,1,0:T(8,128)} %constant_dynamic-slice_fusion.5), channel_id=1, source_target_pairs={{0,2},{1,3},{2,0},{3,1},{4,6},{5,7},{6,4},{7,5},{8,10},{9,11},{10,... | collective-permute-start | bytes 2509832 | tf_op jit(solution)/shard_map/ppermute | solution.py:56
  573.8 35.5 %collective-permute-start.56 = (f32[192,128]{1,0:T(8,128)}, f32[192,128]{1,0:T(8,128)}, u32[]{:S(2)}, u32[]{:S(2)}) collective-permute-start(f32[192,128]{1,0:T(8,128)} %add_bitcast_fusion.2), channel_id=1, source_target_pairs={{0,1},{1,0},{2,3},{3,2},{4,5},{5,4},{6,7},{7,6},{8,9},{9,8},{10,11... | collective-permute-start | bytes 294920 | tf_op jit(solution)/shard_map/ppermute | solution.py:56
  581.3 29.7 %collective-permute-start.61 = (f32[128,1024]{1,0:T(8,128)}, f32[128,1024]{1,0:T(8,128)}, u32[]{:S(2)}, u32[]{:S(2)}) collective-permute-start(f32[128,1024]{1,0:T(8,128)} %get-tuple-element.585), channel_id=1, source_target_pairs={{0,16},{4,20},{8,24},{12,28},{16,0},{20,4},{24,8},{28,12},{1,17},{... | collective-permute-start | bytes 1572872 | tf_op jit(solution)/shard_map/ppermute | solution.py:56
  596.4 11.2 %collective-permute-start.47 = (f32[4,32,817]{2,1,0:T(8,128)}, f32[4,32,817]{2,1,0:T(8,128)}, u32[]{:S(2)}, u32[]{:S(2)}) collective-permute-start(f32[4,32,817]{2,1,0:T(8,128)} %dynamic-slice_bitcast_fusion), channel_id=1, source_target_pairs={{0,4},{4,0},{8,12},{12,8},{16,20},{20,16},{24,28},{28,24},{1,5},{5... | collective-permute-start | bytes 1254920 | tf_op jit(solution)/shard_map/ppermute | solution.py:56
  601.3 18.8 %collective-permute-start.59 = (f32[256,512]{1,0:T(8,128)S(1)}, f32[256,512]{1,0:T(8,128)S(1)}, u32[]{:S(2)}, u32[]{:S(2)}) collective-permute-start(f32[256,512]{1,0:T(8,128)S(1)} %get-tuple-element.581), channel_id=1, source_target_pairs={{0,8},{4,12},{8,0},{12,4},{16,24},{20,28},{24,16},{28,20},{1,9},{5... | collective-permute-start | bytes 1572872 | tf_op jit(solution)/shard_map/ppermute | solution.py:56
  608.8 16.1 %collective-permute-start.52 = (f32[2,32,817]{2,1,0:T(8,128)S(1)}, f32[2,32,817]{2,1,0:T(8,128)S(1)}, u32[]{:S(2)}, u32[]{:S(2)}) collective-permute-start(f32[2,32,817]{2,1,0:T(8,128)S(1)} %dynamic-slice_bitcast_fusion.1), channel_id=1, source_target_pairs={{0,8},{4,12},{8,0},{12,4},{16,24},{20,28},{24,16},{28,20},{1,9},{5... | collective-permute-start | bytes 627464 | tf_op jit(solution)/shard_map/ppermute | solution.py:56
  625.6 13.7 %collective-permute-start.53 = (f32[1,32,817]{2,1,0:T(8,128)}, f32[1,32,817]{2,1,0:T(8,128)}, u32[]{:S(2)}, u32[]{:S(2)}) collective-permute-start(f32[1,32,817]{2,1,0:T(8,128)} %constant_dynamic-slice_fusion.2), channel_id=1, source_target_pairs={{0,16},{4,20},{8,24},{12,28},{16,0},{20,4},{24,8},{28,12},{1,17},{... | collective-permute-start | bytes 313736 | tf_op jit(solution)/shard_map/ppermute | solution.py:56
  625.8 19.0 %collective-permute-start.60 = (f32[128,512]{1,0:T(8,128)S(1)}, f32[128,512]{1,0:T(8,128)S(1)}, u32[]{:S(2)}, u32[]{:S(2)}) collective-permute-start(f32[128,512]{1,0:T(8,128)S(1)} %get-tuple-element.583), channel_id=1, source_target_pairs={{0,16},{4,20},{8,24},{12,28},{16,0},{20,4},{24,8},{28,12},{1,17},{... | collective-permute-start | bytes 786440 | tf_op jit(solution)/shard_map/ppermute | solution.py:56
  (281 other events, 1451.5 us)

commit v4 on v3

--- a/solution.py
+++ b/solution.py
@@ -14,12 +14,15 @@
     ("wait_two", 1): [("down", 1)],
     ("mid", 1): [("up", 0), ("att", 0)],
     ("wait_one", 1): [("up", 1), ("down", 0), ("att", 0)],
-    ("end", 1): [("down", 1), ("att", 1)],
-    "scores": [("up", 1), ("down", 1)],
-    "values": ["tail"],
+    ("end", 1): [("up", 0), ("down", 1), ("down", 0), ("att", 1)],
+    "values": [("up", 1), ("att", 0), ("down", 1), "tail"],
+    "vectors": [("att", 1), ("down", 1), ("up", 1)],
+    "small": ["small"],
+    "output": ["tail"],
+    "pixels": [("att", 1), ("up", 1)],
+    "rows": ["tail", "small"],
 }
-DRAIN = [("att", 1), ("up", 1), "position", "vectors", "embed", "tail", ("att", 1),
-         "position", "vectors", "embed", "tail", "position", "vectors", "embed"]
+DRAIN = [("att", 1), "small", "tail", "small"]
 ROOT_DIM = math.sqrt(HEAD_DIM)
 BF = jnp.bfloat16
 F32 = jnp.float32
@@ -416,7 +419,7 @@
                     outs[1][layer, which] = value[:, begin : begin + local_width]
 
     if shard % 128:
-        values = [pieces[2 * i] + pieces[2 * i + 1] for i in range(layer_count)]
+        values = pieces
         if kind == "down":
             return [jnp.stack([value.T for value in values])]
         if kind == "up":
@@ -428,11 +431,7 @@
         return [jnp.stack([value[:, :local_width].T for value in values]), jnp.stack(rest)]
 
     def kernel(*refs):
-        ins = refs[: 2 * layer_count]
-        store(
-            [ins[2 * i][...] + ins[2 * i + 1][...] for i in range(layer_count)],
-            refs[2 * layer_count :],
-        )
+        store([ref[...] for ref in refs[:layer_count]], refs[layer_count:])
 
     return pl.pallas_call(
         kernel,
@@ -447,6 +446,144 @@
     )(*pieces)
 
 
+def one_hot_segments(var_count, pix_count):
+    flat = var_count * pix_count
+    rows = lax.broadcasted_iota(jnp.int32, (var_count, flat), 0)
+    columns = lax.broadcasted_iota(jnp.int32, (var_count, flat), 1)
+    inside = (columns >= rows * pix_count) & (columns < (rows + 1) * pix_count)
+    return jnp.where(inside, 1.0, 0.0).astype(BF)
+
+
+def pool_front(core, pixels, patch, embed, query, query_weight, key_weight, value_weight,
+               value_bias, mask, out_weight):
+    var_count = embed.shape[0]
+    flat, rows = pixels.shape
+    pix_count = flat // var_count
+    model_width, local_width = key_weight.shape
+    head_count = local_width // HEAD_DIM
+    half = rows // 2
+
+    def kernel(core_ref, pixels_ref, patch_ref, embed_ref, query_ref, query_weight_ref, key_weight_ref,
+               value_weight_ref, bias_ref, mask_ref, out_weight_ref,
+               low_out, query_out, key_out, score_out, flat_out, var_out, probs_out, pooled_out,
+               own_out, send_out, turned_ref):
+        turned_ref[...] = pixels_ref[...].T
+        mine = pl.multiple_of(core_ref[0] * half, 8)
+        theirs = pl.multiple_of(half - core_ref[0] * half, 8)
+        low_out[:half] = turned_ref[pl.ds(mine, half)].astype(BF)
+        low_out[half:] = turned_ref[pl.ds(theirs, half)].astype(BF)
+        query = matmul(query_ref[...].astype(BF), query_weight_ref[...]).astype(BF)
+        query_out[...] = query.astype(F32)
+        for head in range(head_count):
+            one = slice(head * HEAD_DIM, (head + 1) * HEAD_DIM)
+            key_out[head : head + 1] = matmul_nt(query[:, one], key_weight_ref[:, one]) / ROOT_DIM
+        key_high, key_rest = two_part(key_out[...])
+        embed_high, embed_rest = two_part(embed_ref[...])
+        score_out[...] = matmul_nt(key_high, patch_ref[...]) + matmul_nt(key_rest, patch_ref[...])
+        score_var = (
+            matmul_nt(key_high, embed_high)
+            + matmul_nt(key_rest, embed_high)
+            + matmul_nt(key_high, embed_rest)
+        )
+        flat_out[...] = matmul(patch_ref[...], value_weight_ref[...]).astype(BF)
+        value_var = matmul(embed_high, value_weight_ref[...]) + matmul(embed_rest, value_weight_ref[...])
+        var_out[...] = (value_var + bias_ref[...]).astype(BF)
+        segment = one_hot_segments(var_count, pix_count)
+        for head in range(head_count):
+            one = slice(head * HEAD_DIM, (head + 1) * HEAD_DIM)
+            pix = low_out[...].astype(F32)
+            high, rest = two_part(pix * score_out[head : head + 1])
+            scores = matmul_nt(high, segment) + matmul_nt(rest, segment) + score_var[head : head + 1]
+            scores = jnp.where(mask_ref[...] > 0, scores, -1000000000.0)
+            exponent = jnp.exp(scores - jnp.max(scores, axis=-1, keepdims=True))
+            probs = exponent / jnp.sum(exponent, axis=-1, keepdims=True)
+            probs_out[head] = probs
+            low = probs.astype(BF)
+            mixed = (matmul(low, segment) * pix).astype(BF)
+            pooled_out[:, one] = (matmul(mixed, flat_out[:, one]) + matmul(low, var_out[:, one])).astype(BF)
+        send_out[...] = matmul(pooled_out[half:], out_weight_ref[...])
+        own_out[...] = matmul(pooled_out[:half], out_weight_ref[...])
+
+    piece = jax.ShapeDtypeStruct((half, model_width), F32)
+    return pl.pallas_call(
+        kernel,
+        out_shape=(
+            jax.ShapeDtypeStruct((rows, flat), BF),
+            jax.ShapeDtypeStruct((1, local_width), F32),
+            jax.ShapeDtypeStruct((head_count, model_width), F32),
+            jax.ShapeDtypeStruct((head_count, flat), F32),
+            jax.ShapeDtypeStruct((flat, local_width), BF),
+            jax.ShapeDtypeStruct((var_count, local_width), BF),
+            jax.ShapeDtypeStruct((head_count, rows, var_count), F32),
+            jax.ShapeDtypeStruct((rows, local_width), BF),
+            piece,
+            piece,
+        ),
+        in_specs=[pl.BlockSpec(memory_space=pltpu.SMEM)] + [pl.BlockSpec()] * 10,
+        scratch_shapes=[pltpu.VMEM((rows, flat), F32)],
+        cost_estimate=LONG,
+        compiler_params=vmem_limit(20 << 20),
+        name="pool_front",
+    )(core, pixels, patch, embed, query, query_weight, key_weight, value_weight, value_bias, mask, out_weight)
+
+
+def pool_back(low, out_weight, value_flat, value_var, pix_low, probs, scores):
+    rows, flat = pix_low.shape
+    head_count, _, var_count = probs.shape
+    pix_count = flat // var_count
+    local_width = value_flat.shape[1]
+    half = rows // 2
+
+    def kernel(low_ref, out_weight_ref, flat_ref, var_ref, pix_ref, probs_ref, score_ref,
+               value_out, key_out, key_var_out, own_out, send_out, pooled_ref, pixel_ref):
+        pooled_ref[...] = matmul_nt(low_ref[...], out_weight_ref[...]).astype(BF)
+        segment = one_hot_segments(var_count, pix_count)
+        for head in range(head_count):
+            one = slice(head * HEAD_DIM, (head + 1) * HEAD_DIM)
+            pix = pix_ref[...].astype(F32)
+            pooled = pooled_ref[:, one]
+            pull = matmul_nt(pooled, flat_ref[:, one])
+            high, rest = two_part(pull * pix)
+            grad_probs = (
+                matmul_nt(high, segment) + matmul_nt(rest, segment) + matmul_nt(pooled, var_ref[:, one])
+            )
+            probs_one = probs_ref[head]
+            weighted = probs_one * grad_probs
+            grad_scores = weighted - probs_one * jnp.sum(weighted, axis=-1, keepdims=True)
+            high, rest = two_part(grad_scores)
+            wide = matmul(high, segment) + matmul(rest, segment)
+            key_out[head : head + 1] = jnp.sum(wide * pix, axis=0, keepdims=True)
+            key_var_out[head : head + 1] = jnp.sum(grad_scores, axis=0, keepdims=True)
+            probs_low = probs_one.astype(BF)
+            probs_wide = matmul(probs_low, segment)
+            term = wide * score_ref[head : head + 1] + probs_wide * pull
+            if head:
+                pixel_ref[...] += term
+            else:
+                pixel_ref[...] = term
+            mixed = (probs_wide * pix).astype(BF)
+            value_out[:flat, one] = matmul_tn(mixed, pooled)
+            value_out[flat:, one] = matmul_tn(probs_low, pooled)
+        own_out[...] = pixel_ref[:half]
+        send_out[...] = pixel_ref[half:]
+
+    piece = jax.ShapeDtypeStruct((half, flat), F32)
+    return pl.pallas_call(
+        kernel,
+        out_shape=(
+            jax.ShapeDtypeStruct((flat + var_count, local_width), F32),
+            jax.ShapeDtypeStruct((head_count, flat), F32),
+            jax.ShapeDtypeStruct((head_count, var_count), F32),
+            piece,
+            piece,
+        ),
+        scratch_shapes=[pltpu.VMEM((rows, local_width), BF), pltpu.VMEM((rows, flat), F32)],
+        cost_estimate=LONG,
+        compiler_params=vmem_limit(20 << 20),
+        name="pool_back",
+    )(low, out_weight, value_flat, value_var, pix_low, probs, scores)
+
+
 class Links:
     def __init__(self, dp, mp):
         self.dp, self.mp = dp, mp
@@ -520,6 +657,10 @@
         self.step = 0
 
     def advance(self, clock):
+        if self.step == len(self.bits):
+            self.total = clock.one(self.keep + clock.one(self.got))
+            self.step += 1
+            return
         got, pairs = None, self.pairs
         if self.step:
             got = clock.one(self.got)
@@ -539,7 +680,7 @@
 
     @property
     def open(self):
-        return self.step < len(self.bits)
+        return self.step <= len(self.bits)
 
 
 class ShardMerge:
@@ -554,6 +695,10 @@
         return pick(pairs, 1 - own, 1)
 
     def advance(self, clock):
+        if self.step == bit_count(self.links.dp):
+            self.total = clock.one(self.keep + clock.one(self.got))
+            self.step += 1
+            return
         total = self.shards
         if self.step:
             total = self.keep + clock.one(self.got)
@@ -564,7 +709,7 @@
 
     @property
     def open(self):
-        return self.step < bit_count(self.links.dp)
+        return self.step <= bit_count(self.links.dp)
 
 
 def norm_parts(rows):
@@ -628,63 +773,32 @@
         own_count = token_counts[0].astype(F32)
         lead_scale = lead_hours[0].astype(F32) / 24.0
 
-        pix_rows = pixels[0].reshape(flat_count, row_count).T
-        pix_own, pix_other = links.split_rows(pix_rows)
-        pix_low = jnp.concatenate([pix_own, pix_other], axis=0).astype(BF)
-        pix_value = pix_low.astype(F32)
-        embed_high, embed_rest = two_part(variable_embed)
-        embed_all = jnp.concatenate(
-            [patch_weight.reshape(flat_count, model_width), embed_high, embed_rest], axis=0
+        patch_flat = patch_weight.reshape(flat_count, model_width)
+        (
+            pix_low,
+            query_row,
+            key_rows,
+            score_rows,
+            value_flat,
+            value_var,
+            pool_probs,
+            pooled,
+            part_own,
+            part_send,
+        ) = pool_front(
+            links.mp_bit(0).reshape(1),
+            pixels[0].reshape(flat_count, row_count),
+            patch_flat,
+            variable_embed,
+            pool_query[None],
+            pool_query_weight,
+            pool_key_weight,
+            pool_value_weight,
+            pool_value_bias[None],
+            mask_row[None],
+            pool_output_weight,
         )
-        embed_left = take_columns(embed_all, links.order(list(range(bit_count(dp)))), shard)
-        query_low = pool_query.astype(BF)
-        query_vec = matmul(query_low[None, :], pool_query_weight)[0].astype(BF)
-        head_of = jnp.arange(local_width, dtype=jnp.int32) // HEAD_DIM
-        head_pick = head_of[:, None] == jnp.arange(head_count, dtype=jnp.int32)[None, :]
-        query_heads = jnp.where(head_pick, query_vec[:, None], 0).astype(BF)
-        key_query = matmul(pool_key_weight, query_heads) / ROOT_DIM
-        key_high, key_rest = two_part(key_query)
-        projected = matmul(
-            embed_all, jnp.concatenate([pool_value_weight, key_high, key_rest], axis=1)
-        )
-        tail = projected[flat_count : flat_count + var_count] + projected[flat_count + var_count :]
-        score_flat = (
-            projected[:flat_count, local_width : local_width + head_count]
-            + projected[:flat_count, local_width + head_count :]
-        )
-        score_var = tail[:, local_width : local_width + head_count] + tail[:, local_width + head_count :]
-        value_flat = projected[:flat_count, :local_width].astype(BF)
-        value_var = (tail[:, :local_width] + pool_value_bias).astype(BF)
-        value_flat = value_flat.reshape(flat_count, head_count, HEAD_DIM).transpose(1, 0, 2)
-        value_var = value_var.reshape(var_count, head_count, HEAD_DIM).transpose(1, 0, 2)
-
-        var_of = jnp.arange(flat_count, dtype=jnp.int32) // pix_count
-        segment = (
-            var_of[None, :] == jnp.arange(var_count, dtype=jnp.int32)[:, None]
-        )
-        segment_low = segment.astype(BF)
-        score_block = jnp.where(segment.T[None], score_flat.T[:, :, None], 0.0)
-        block_high, block_rest = two_part(score_block)
-        block_both = jnp.concatenate([block_high, block_rest], axis=2)
-        pool_scores = jnp.einsum(
-            "rk,hkv->hrv", pix_low, block_both, preferred_element_type=F32
-        )
-        pool_scores = (
-            pool_scores[:, :, :var_count] + pool_scores[:, :, var_count:] + score_var.T[:, None, :]
-        )
-        pool_scores = jnp.where(mask_row[None, None, :] > 0, pool_scores, -1000000000.0)
-        pool_top = jnp.max(pool_scores, axis=-1, keepdims=True)
-        pool_exp = jnp.exp(pool_scores - pool_top)
-        pool_probs = pool_exp / jnp.sum(pool_exp, axis=-1, keepdims=True)
-        probs_low = pool_probs.astype(BF)
-        probs_wide = jnp.einsum("hrv,vk->hrk", probs_low, segment_low, preferred_element_type=F32)
-        mixed_pixels = (probs_wide * pix_value[None]).astype(BF)
-        pooled = jnp.einsum(
-            "hrk,hkd->hrd", mixed_pixels, value_flat, preferred_element_type=F32
-        ) + jnp.einsum("hrv,hvd->hrd", probs_low, value_var, preferred_element_type=F32)
-        pooled = heads_last(pooled).astype(BF)
-
-        mine, got = links.begin_product(pooled, pool_output_weight)
+        mine, got = links.begin_sum(part_own, part_send)
         count_total = after(jnp.full((8, 128), own_count, F32), mine)
         for bit in range(bit_count(dp)):
             count_total = count_total + exchange(count_total, "dp", dp, bit)
@@ -740,7 +854,29 @@
             if layer < top:
                 if layer == 0:
                     top_grad = matmul_nt(after(down_low, mine), down_weight[top])
-                    mine, top_grad = lax.optimization_barrier((mine, top_grad))
+                    embed_high, embed_rest = two_part(variable_embed)
+                    embed_all = jnp.concatenate([patch_flat, embed_high, embed_rest], axis=0)
+                    mine, embed_all = lax.optimization_barrier((mine, embed_all))
+                    embed_left = take_columns(embed_all, shards, shard)
+                    key_high, key_rest = two_part(key_rows)
+                    left_side = jnp.concatenate(
+                        [
+                            pool_value_weight,
+                            pool_query_weight,
+                            jnp.concatenate([key_high, key_high, key_rest], axis=0).T,
+                        ],
+                        axis=1,
+                    )
+                    sides = left_side.reshape(dp, mp // 2, 2, shard // mp, left_side.shape[1])
+                    side_own, side_send = [
+                        pick(sides, which, 2)
+                        .transpose(1, 0, 2, 3)
+                        .reshape(model_width // 2, left_side.shape[1])
+                        for which in (links.mp_bit(0), 1 - links.mp_bit(0))
+                    ]
+                    mine, top_grad, embed_left, side_own, side_send = lax.optimization_barrier(
+                        (mine, top_grad, embed_left, side_own, side_send)
+                    )
                 mine, normed_two = lax.optimization_barrier((mine, normed_two))
                 hidden = hidden + (mine + got) + down_bias[layer]
             kept.append(
@@ -765,6 +901,8 @@
         merges = {}
         row_sums["down_bias", top] = jnp.sum(grad_own, axis=0)
 
+        head_of = jnp.arange(local_width, dtype=jnp.int32) // HEAD_DIM
+        head_pick = head_of[:, None] == jnp.arange(head_count, dtype=jnp.int32)[None, :]
         clock = Clock(scale_cell)
 
         def advance(spot):
@@ -848,6 +986,122 @@
             advance(("end", depth))
             down_low = clock.one(down_low)
 
+        row_sums["column"] = sums[2]
+        row_sums["lead"] = lead_scale * sums[2]
+        value_grad, key_grad, key_grad_var, pixel_own, pixel_send = pool_back(
+            clock.one(down_low), pool_output_weight, value_flat, value_var, pix_low, pool_probs, score_rows
+        )
+        value_grad = clock.one(value_grad)
+        embed_all, embed_left = clock.both(embed_all, embed_left)
+        value_low = value_grad.astype(BF)
+        merges["tail"] = Merge(
+            links,
+            [
+                (down_left, pooled),
+                (embed_left, jnp.concatenate([value_low, value_low[flat_count:]], axis=0)),
+            ],
+            bits,
+        )
+        advance("values")
+
+        flat_all = flat_count + var_count
+        item_scale = clock.cell[0, 0]
+        value_scaled = (clock.one(value_grad) * item_scale).astype(BF)
+        key_scaled = jnp.concatenate([key_grad, key_grad_var], axis=1) * item_scale
+        key_high, key_rest = two_part(key_scaled)
+        key_twice = jnp.concatenate([key_high, key_rest], axis=0)
+        summed_key = matmul(
+            jnp.concatenate([key_twice, key_twice[:, flat_count:]], axis=1), embed_all
+        )
+        summed_key = summed_key[:head_count] + summed_key[head_count:]
+        summed_high, summed_rest = two_part(summed_key)
+        query_grad = matmul(
+            jnp.concatenate([summed_high, summed_rest], axis=0), pool_key_weight
+        )
+        query_grad = query_grad[:head_count] + query_grad[head_count:]
+        query_grad = jnp.sum(jnp.where(head_pick.T, query_grad, 0.0), axis=0) / ROOT_DIM
+        query_high, query_rest = two_part(query_grad[None])
+        right_side = jnp.concatenate([key_high, key_rest, key_high], axis=0)
+        sub = shard // mp
+        core = links.mp_bit(0)
+
+        def embed_side(side):
+            block = matmul_nt(side[:, :local_width], value_scaled)
+            block = block + matmul(side[:, 2 * local_width :], right_side)
+            weight = side[:, local_width : 2 * local_width]
+            part = matmul_nt(weight, query_high) + matmul_nt(weight, query_rest)
+            block = jnp.concatenate([block, part], axis=1)
+            return block.reshape(mp // 2, dp, sub, flat_all + 1)
+
+        embed_send = clock.one(embed_side(side_send))
+        embed_got = exchange(embed_send, "mp", mp, 0)
+        clock.hold()
+        embed_grad = embed_side(clock.one(side_own)) + clock.one(embed_got)
+        own = links.mp_bit(1)
+        for bit in range(1, bit_count(mp)):
+            own = links.mp_bit(bit)
+            count = embed_grad.shape[0] // 2
+            pairs = embed_grad.reshape((count, 2) + embed_grad.shape[1:])
+            embed_keep = pick(pairs, own, 1)
+            embed_send = clock.one(pick(pairs, 1 - own, 1))
+            embed_got = exchange(embed_send, "mp", mp, bit)
+            if bit + 1 < bit_count(mp):
+                embed_grad = embed_keep + embed_got
+        clock.hold()
+        advance("embed")
+
+        names = []
+        for layer in range(layer_count):
+            names += [("gain", layer, 0), ("gain", layer, 1), ("bias", layer, 0), ("bias", layer, 1)]
+        for layer in range(layer_count):
+            names += [("out_bias", layer), ("down_bias", layer)]
+        names += ["column", "lead"]
+        own_sums = clock.one(jnp.stack([row_sums[name] for name in names]) * item_scale)
+        other_sums = exchange(own_sums, "mp", mp, 0)
+        clock.hold()
+        full_sums = own_sums + clock.one(other_sums)
+        local = jnp.stack([local_sums["up_bias", layer] for layer in range(layer_count)]) * item_scale
+        thin = [local_sums["qv", layer] for layer in range(layer_count)]
+        pool_bias = jnp.sum(value_grad[flat_count:], axis=0, keepdims=True)
+        thin = jnp.concatenate(thin + [pool_bias], axis=0) * item_scale
+        packed = jnp.concatenate(
+            [
+                full_sums.reshape(len(names), dp, shard).transpose(1, 0, 2).reshape(dp, -1),
+                summed_key.reshape(head_count, dp, shard).transpose(1, 0, 2).reshape(dp, -1),
+                local.reshape(layer_count, dp, -1).transpose(1, 0, 2).reshape(dp, -1),
+                thin.reshape(2 * layer_count + 1, dp, -1).transpose(1, 0, 2).reshape(dp, -1),
+                jnp.broadcast_to(query_grad[None, :], (dp, local_width)),
+            ],
+            axis=1,
+        )
+        packed_size = packed.shape[1]
+        packed_rows = -(-packed_size // 1024) * 8
+        packed = jnp.pad(packed, ((0, 0), (0, packed_rows * 128 - packed_size)))
+        packed = packed.reshape(dp, packed_rows, 128)
+        position = (grad_own * item_scale).reshape(row_count // 2, dp, shard).transpose(1, 0, 2)
+        position, packed = clock.both(position, packed)
+        advance("vectors")
+        embed_grad = (embed_keep + clock.one(embed_got)).reshape(dp, sub, flat_all + 1)
+        lane_blocks = -(-(flat_all + 1) // 128)
+        embed_grad = jnp.pad(
+            embed_grad, ((0, 0), (0, 0), (0, lane_blocks * 128 - flat_all - 1))
+        )
+        if shard == 128:
+            tall = jnp.concatenate(
+                [embed_grad[:, :, i * 128 : (i + 1) * 128] for i in range(lane_blocks)]
+                + [packed, position],
+                axis=1,
+            )
+            merges["small"] = ShardMerge(links, tall)
+        else:
+            merges["small"] = ShardMerge(
+                links,
+                jnp.concatenate(
+                    [part.reshape(dp, 1, -1) for part in (embed_grad, packed, position)], axis=2
+                ),
+            )
+        advance("small")
+
         activation_top = clock.one(activation_top)
         half = row_count // 2
         last_mine, last_got = links.ordered_sum(
@@ -856,147 +1110,48 @@
             matmul(activation_top[half:], down_weight[top]),
         )
         clock.hold()
-        row_sums["column"] = sums[2]
-        row_sums["lead"] = lead_scale * sums[2]
-        pool_grad_low = down_low
-        grad_pooled = heads_first(matmul_nt(pool_grad_low, pool_output_weight).astype(BF))
-        pull_flat = jnp.einsum("hrd,hkd->hrk", grad_pooled, value_flat, preferred_element_type=F32)
-        pull_high, pull_rest = two_part(pull_flat * pix_value[None])
-        grad_probs = (
-            jnp.einsum("hrk,vk->hrv", pull_high, segment_low, preferred_element_type=F32)
-            + jnp.einsum("hrk,vk->hrv", pull_rest, segment_low, preferred_element_type=F32)
-            + jnp.einsum("hrd,hvd->hrv", grad_pooled, value_var, preferred_element_type=F32)
-        )
-        grad_pool_scores = pool_probs * (
-            grad_probs - jnp.sum(pool_probs * grad_probs, axis=-1, keepdims=True)
-        )
-        grad_pool_scores = clock.one(grad_pool_scores)
-        advance("scores")
-        grad_pool_scores = clock.one(grad_pool_scores)
-        score_high, score_rest = two_part(grad_pool_scores)
-        pixel_part = jnp.einsum(
-            "hrv,hkv->rk", score_high, block_high, preferred_element_type=F32
-        ) + jnp.sum(probs_wide * pull_flat, axis=0)
-
-        turned = jnp.einsum(
-            "rk,hrv->hkv", pix_low, score_high, preferred_element_type=F32
-        ) + jnp.einsum("rk,hrv->hkv", pix_low, score_rest, preferred_element_type=F32)
-        key_flat = jnp.sum(jnp.where(segment.T[None], turned, 0.0), axis=2).T * item_scale
-        key_var = jnp.sum(grad_pool_scores, axis=1).T * item_scale
-        value_grad_flat = jnp.einsum(
-            "hrk,hrd->khd", mixed_pixels, grad_pooled, preferred_element_type=F32
-        ).reshape(flat_count, local_width)
-        value_grad_var = jnp.einsum(
-            "hrv,hrd->vhd", probs_low, grad_pooled, preferred_element_type=F32
-        ).reshape(var_count, local_width)
-        local_sums["pool_bias"] = jnp.sum(value_grad_var, axis=0)
-        value_rows_grad = jnp.concatenate(
-            [part.astype(BF) for part in (value_grad_flat, value_grad_var, value_grad_var)], axis=0
-        )
-        merges["tail"] = Merge(
-            links,
-            [(down_left, pooled), (embed_left, value_rows_grad)],
-            bits,
-        )
-        advance("values")
-        value_grad_flat = (clock.one(value_grad_flat) * item_scale).astype(BF)
-        value_grad_var = (value_grad_var * item_scale).astype(BF)
-
-        key_grad = jnp.concatenate([key_flat, key_var, key_var], axis=0)
-        key_grad_high, key_grad_rest = two_part(key_grad)
-        summed_key = matmul_tn(
-            embed_all, jnp.concatenate([key_grad_high, key_grad_rest], axis=1)
-        )
-        summed_key = summed_key[:, :head_count] + summed_key[:, head_count:]
-        summed_high, summed_rest = two_part(summed_key)
-        query_grad = matmul_tn(
-            jnp.concatenate([summed_high, summed_rest], axis=1), pool_key_weight
-        )
-        query_grad = query_grad[:head_count] + query_grad[head_count:]
-        query_grad = jnp.sum(jnp.where(head_pick.T, query_grad, 0.0), axis=0) / ROOT_DIM
-        query_part = jnp.sum(pool_query_weight.astype(F32) * query_grad[None, :], axis=1)
-
-        flat_all = flat_count + var_count
-        grad_rows = jnp.concatenate([value_grad_flat, value_grad_var], axis=0)
-        key_rows_high, key_rows_rest = two_part(jnp.concatenate([key_flat, key_var], axis=0))
-        right_side = jnp.concatenate([grad_rows, key_rows_high, key_rows_rest, key_rows_high], axis=1)
-        left_side = jnp.concatenate([pool_value_weight, key_high, key_high, key_rest], axis=1)
-        sub = shard // mp
-        sides = left_side.reshape(dp, mp // 2, 2, sub, left_side.shape[1])
-        parts = query_part.reshape(dp, mp // 2, 2, sub)
-        core = links.mp_bit(0)
-
-        def embed_side(which):
-            side = pick(sides, which, 2).transpose(1, 0, 2, 3)
-            part = pick(parts, which, 2).transpose(1, 0, 2)
-            block = matmul_nt(side.reshape(model_width // 2, left_side.shape[1]), right_side)
-            block = jnp.concatenate([block, part.reshape(model_width // 2, 1)], axis=1)
-            return block.reshape(mp // 2, dp, sub, flat_all + 1)
-
-        embed_grad = embed_side(core) + exchange(embed_side(1 - core), "mp", mp, 0)
-        for bit in range(1, bit_count(mp)):
-            own = links.mp_bit(bit)
-            count = embed_grad.shape[0] // 2
-            pairs = embed_grad.reshape((count, 2) + embed_grad.shape[1:])
-            embed_grad = pick(pairs, own, 1) + exchange(pick(pairs, 1 - own, 1), "mp", mp, bit)
-        merges["embed"] = ShardMerge(links, embed_grad[0])
-        position = (grad_own * item_scale).reshape(row_count // 2, dp, shard).transpose(1, 0, 2)
-        merges["position"] = ShardMerge(links, position)
-        pixel_own = links.sum_rows(pixel_part)
-        pixel_grad = links.global_rows(pixel_own, links.other_rows(pixel_own))
-        pixel_grad = pixel_grad.T.reshape(1, var_count, pix_count, row_count)
-
-        names = []
-        for layer in range(layer_count):
-            names += [("gain", layer, 0), ("gain", layer, 1), ("bias", layer, 0), ("bias", layer, 1)]
-        for layer in range(layer_count):
-            names += [("out_bias", layer), ("down_bias", layer)]
-        names += ["column", "lead"]
-        own_sums = jnp.stack([row_sums[name] for name in names]) * item_scale
-        full_sums = own_sums + exchange(own_sums, "mp", mp, 0)
-        local = jnp.stack([local_sums["up_bias", layer] for layer in range(layer_count)]) * item_scale
-        thin = [local_sums["qv", layer] for layer in range(layer_count)]
-        thin = jnp.concatenate(thin + [local_sums["pool_bias"][None]], axis=0) * item_scale
-        packed = jnp.concatenate(
-            [
-                full_sums.reshape(len(names), dp, shard).transpose(1, 0, 2).reshape(dp, -1),
-                summed_key.reshape(dp, -1),
-                local.reshape(layer_count, dp, -1).transpose(1, 0, 2).reshape(dp, -1),
-                thin.reshape(2 * layer_count + 1, dp, -1).transpose(1, 0, 2).reshape(dp, -1),
-                jnp.broadcast_to(query_grad[None, :], (dp, local_width)),
-            ],
-            axis=1,
-        )
-        merges["vectors"] = ShardMerge(links, packed[:, None, :])
+        advance("output")
+        pixel_mine, pixel_got = links.ordered_sum(clock, lambda: pixel_own, pixel_send)
+        clock.hold()
+        advance("pixels")
+        last_mine, last_got = clock.both(last_mine, last_got)
+        hidden = clock.one(hidden + (last_mine + last_got) + down_bias[top])
+        hidden_other = links.other_rows(hidden)
+        clock.hold()
+        layer_out = clock.one(links.global_rows(hidden, clock.one(hidden_other)))
+        advance("rows")
+        pixel_mine, pixel_got = clock.both(pixel_mine, pixel_got)
+        pixel_mine = clock.one(pixel_mine + pixel_got)
+        pixel_other = links.other_rows(pixel_mine)
+        clock.hold()
+        pixel_grad = links.global_rows(pixel_mine, clock.one(pixel_other))
+        pixel_grad = clock.one(pixel_grad.T.reshape(1, var_count, pix_count, row_count))
         for name in DRAIN:
             if merges[name].open:
                 merges[name].advance(clock)
         for merge in merges.values():
             while merge.open:
                 merge.advance(clock)
-        hidden = hidden + (last_mine + last_got) + down_bias[top]
-        layer_out = links.global_rows(hidden, links.other_rows(hidden))
-        finished = {
-            kind: finish_layers(
-                kind,
-                [
-                    part
-                    for layer in range(layer_count)
-                    for part in (merges[kind, top - layer].keep, merges[kind, top - layer].got)
-                ],
-                layer_count,
-                shard,
-                local_width,
-            )
-            for kind in ("down", "up", "att")
-        }
-        tail_total = merges["tail"].keep + merges["tail"].got
-        embed_grad = (merges["embed"].keep + merges["embed"].got)[0]
-        position = (merges["position"].keep + merges["position"].got)[0]
+        finished = {}
+        for kind in ("down", "up", "att"):
+            parts = [merges[kind, top - layer].total for layer in range(layer_count)]
+            finished[kind] = finish_layers(kind, parts, layer_count, shard, local_width)
+        tail_total = merges["tail"].total
+        small = merges["small"].total[0]
+        if shard == 128:
+            embed_rows = sub * lane_blocks
+            embed_grad = jnp.concatenate(
+                [small[i * sub : (i + 1) * sub] for i in range(lane_blocks)], axis=1
+            )
+            packed = small[embed_rows : embed_rows + packed_rows].reshape(-1)
+            position = small[embed_rows + packed_rows :]
+        else:
+            size = sub * lane_blocks * 128
+            embed_grad = small[0, :size].reshape(sub, lane_blocks * 128)
+            packed = small[0, size : size + packed_rows * 128]
+            position = small[0, size + packed_rows * 128 :].reshape(row_count // 2, shard)
+        packed, position, _ = lax.optimization_barrier((packed, position, clock.cell))
         position = links.global_rows(position, links.other_rows(position))
-        packed, _ = lax.optimization_barrier(
-            ((merges["vectors"].keep + merges["vectors"].got)[0, 0], clock.cell)
-        )
         offset = 0
 
         def take(*shape):
@@ -1016,15 +1171,16 @@
         dense_bias = take(layer_count, 2, shard)
         column_total = take(shard)
         lead_total = take(shard)
-        key_shard = take(shard, head_count)
+        key_shard = take(head_count, shard)
         up_bias_total = take(layer_count, local.shape[1] // dp)
         thin_total = take(2 * layer_count + 1, local_width // dp)
         query_total = take(local_width)
 
+        query_low = pool_query.astype(BF)
         query_rows = lax.dynamic_slice_in_dim(query_low, links.dp_index * shard, shard, 0)
         query_weight_grad = query_rows.astype(F32)[:, None] * query_total[None, :]
         key_weight_grad = (
-            jnp.repeat(key_shard, HEAD_DIM, axis=1) * query_vec.astype(F32)[None, :] / ROOT_DIM
+            jnp.repeat(key_shard.T, HEAD_DIM, axis=1) * query_row / ROOT_DIM
         )
         embed_turned = embed_grad.T
         return (

time: 659 us -> 602 us (0.914)
  waiting for transfers between devices: 238 us -> 187 us
  matrix products: 61.4 us -> 41.5 us
  local copies, waits for them, and re-layouts: 84.1 us -> 102 us
  Pallas kernels: 119 us -> 133 us
  starting transfers between devices: 69.3 us -> 56.4 us
  other arithmetic: 68.6 us -> 58.9 us
  between operations: 6.73 us -> 15.9 us
    ppermute x67 -> x61, waiting for transfers between devices: 238 us -> 187 us  [exchange(): return lax.ppermute(tensor, axis, [(i, i ^ 1 << bit) for i in range(size)])]
    dot_general x15 -> x0, matrix products: 30.8 us -> none  [the longest x1 6.54 us: per_device(): jnp.einsum('hrd,hkd->hrk', grad_pooled, value_flat, preferred_element_typ...]
    unnamed x534 -> x486, local copies, waits for them, and re-layouts: 42.6 us -> 61 us
    pallas_call x0 -> x2, Pallas kernels: none -> 15 us  [the longest x1 8.37 us: pool_back(): pl.pallas_call(kernel, out_shape=(jax.ShapeDtypeStruct((flat + var_count,...]
    ppermute x67 -> x61, starting transfers between devices: 69.3 us -> 56.4 us  [exchange(): return lax.ppermute(tensor, axis, [(i, i ^ 1 << bit) for i in range(size)])]
    reduce_sum x3 -> x1, other arithmetic: 6.76 us -> 0.02 us  [per_device(): pool_bias = jnp.sum(value_grad[flat_count:], axis=0, keepdims=True)]
    dot_general x9 -> x12, matrix products: 12.4 us -> 18.2 us  [matmul_nt(): lax.dot_general(left, right, (((1,), (1,)), ((), ())), preferred_element_...]
    dot_general x11 -> x10, matrix products: 18.2 us -> 23.3 us  [matmul(): return jnp.dot(left, right, preferred_element_type=F32)]
  transfers between devices with their start and end apart: 67 -> 61, of which waited for: 34 -> 33; matrix products, arithmetic and copies ran while one was open for 20% -> 19% of each run, Pallas kernels for 16% -> 19%
where the time goes in v4:
time: 602 us; the launch traced here: 595 us
  waiting for transfers between devices  187 us (31%)
  Pallas kernels  133 us (22%)
  local copies, waits for them, and re-layouts  102 us (17%)
  other arithmetic  58.9 us (10%)
  starting transfers between devices  56.4 us (9%)
  matrix products  41.5 us (7%)
  between operations  15.9 us (3%)
    ppermute x61, waiting for transfers between devices, exchange(): return lax.ppermute(tensor, axis, [(i, i ^ 1 << bit) for i in range(size)])  187 us
    unnamed x486, local copies, waits for them, and re-layouts  61 us
    ppermute x61, starting transfers between devices, exchange(): return lax.ppermute(tensor, axis, [(i, i ^ 1 << bit) for i in range(size)])  56.4 us
    pallas_call x14, Pallas kernels, product_rows(): pl.pallas_call(kernel, out_shape=out_shape, grid=(count,), in_specs=in_sp...  50 us
    pallas_call x7, Pallas kernels, add_split(): pl.pallas_call(kernel, out_shape=[jax.ShapeDtypeStruct((half, width), F32...  23.4 us
    dot_general x10, matrix products, matmul(): return jnp.dot(left, right, preferred_element_type=F32)  23.3 us
    dot_general x12, matrix products, matmul_nt(): lax.dot_general(left, right, (((1,), (1,)), ((), ())), preferred_element_...  18.2 us
    add x6, other arithmetic, ordered_sum(): mine = clock.one(own() + clock.one(got))  12.9 us
  transfers between devices with their start and end apart: 61, of which 33 were waited for; matrix products, arithmetic and copies ran while one was open for 19% of the time, Pallas kernels for 19%

profile of v4, /device:TPU:0, one launch (start us, length us, event | category | flops | bytes accessed | tf_op | source)
XLA Modules:
  0.0 595.3 jit_solution(1825595254680065127)
XLA Ops:
  11.2 6.6 %pool_front.1 = (bf16[384,768]{1,0:T(8,128)(2,1)S(1)}, f32[1,256]{1,0:T(1,128)S(1)}, f32[4,1024]{1,0:T(4,128)S(1)}, f32[4,768]{1,0:T(4,128)S(1)}, bf16[768,256]{...) custom-call(s32[1]{0:T(128)} %bitcast.core_ref, ...), custom_call_target="tpu_custom_call" | custom-call | flops 999999995904 | bytes 8 | tf_op jit(solution)/shard_map/pool_front/pallas_call | solution.py:508
  20.5 2.9 collective-permute-start.4
  35.2 6.1 %collective-permute-done.4 = f32[192,1024]{1,0:T(8,128)S(1)} collective-permute-done((f32[192,1024]{1,0:T(8,128)S(1)}, f32[192,1024]{1,0:T(8,128)S(1)}, u32[]{:S(2)}, u32[]{:S(2)}) %collective-permute-start.4) | collective-permute-done | bytes 786464 | tf_op jit(solution)/shard_map/ppermute | solution.py:59
  46.5 3.9 attend_forward.2
  66.0 11.7 %collective-permute-done.7 = f32[192,1024]{1,0:T(8,128)} collective-permute-done((f32[192,1024]{1,0:T(8,128)}, f32[192,1024]{1,0:T(8,128)}, u32[]{:S(2)}, u32[]{:S(2)}) %collective-permute-start.7) | collective-permute-done | bytes 786464 | tf_op jit(solution)/shard_map/ppermute | solution.py:59
  83.1 7.7 %multiply_convert_fusion.1 = (bf16[384,1024]{1,0:T(8,128)(2,1)S(1)}, f32[384,1024]{1,0:T(8,128)}, f32[384,1024]{1,0:T(8,128)}) fusion(f32[1024]{0:T(1024)S(1)} %bitcast.284, bf16[2,1024,1024]{2,1,0:T(8,128)(2,1)} %param.55, f32[192,1024]{1,0:T(8,128)} %collective-permute-done.8.other_ref, f32[192,1024]{1,0:T(8,128)S(1)} %subtract_multiply_fusion.2.own_ref.unit_ref, ...), kind=kOutput, calls=%fused_computation.69 | convolution fusion | flops 832831488 | bytes 7614464 | tf_op jit(solution)/shard_map/dot_general | solution.py:32
  100.2 3.5 gather_fusion
  103.7 3.0 copy_bitcast_fusion.refs_2_
  106.7 3.8 fusion.10
  113.1 3.6 collective-permute-done.10
  121.0 3.1 attend_forward.3
  131.1 15.9 %collective-permute-done.13 = f32[192,1024]{1,0:T(8,128)S(1)} collective-permute-done((f32[192,1024]{1,0:T(8,128)S(1)}, f32[192,1024]{1,0:T(8,128)S(1)}, u32[]{:S(2)}, u32[]{:S(2)}) %collective-permute-start.13) | collective-permute-done | bytes 786464 | tf_op jit(solution)/shard_map/ppermute | solution.py:59
  161.3 7.7 %fusion.126 = (f32[1024]{0:T(1024)}, bf16[384,1024]{1,0:T(8,128)(2,1)S(1)}, f32[384,1024]{1,0:T(8,128)S(1)}, f32[384,1024]{1,0:T(8,128)S(1)}) fusion(f32[384,1024]{1,0:T(8,128)} %fusion.10, f32[1024]{0:T(1024)S(1)} %bitcast.283, bf16[2,1024,1024]{2,1,0:T(8,128)(2,1)} %param.55, f32[192,1024]{1,0:T(8,128)} %collective-permute-done.14.other_ref, ...), kind=kOutput, calls=%fused_computation.277 | convolution fusion | flops 835976192 | bytes 9191424 | tf_op jit(solution)/shard_map/dot_general | solution.py:32
  188.4 18.1 %collective-permute-done.16.got_ref = f32[192,1024]{1,0:T(8,128)} collective-permute-done((f32[192,1024]{1,0:T(8,128)}, f32[192,1024]{1,0:T(8,128)}, u32[]{:S(2)}, u32[]{:S(2)}) %collective-permute-start.16) | collective-permute-done | bytes 786464 | tf_op jit(solution)/shard_map/ppermute | solution.py:59
  206.6 3.0 norm_back.4
  215.7 4.9 attend_back.2
  225.6 2.8 product_rows.16
  228.9 4.6 product_rows.17
  236.1 5.0 product_rows.18
  246.8 7.1 %collective-permute-done.19.got_ref = f32[192,1024]{1,0:T(8,128)} collective-permute-done((f32[192,1024]{1,0:T(8,128)}, f32[192,1024]{1,0:T(8,128)}, u32[]{:S(2)}, u32[]{:S(2)}) %collective-permute-start.19) | collective-permute-done | bytes 786464 | tf_op jit(solution)/shard_map/ppermute | solution.py:59
  254.0 2.8 norm_back.5
  274.3 2.8 product_rows.19
  278.6 14.2 %collective-permute-done.24.got_ref = f32[192,1024]{1,0:T(8,128)} collective-permute-done((f32[192,1024]{1,0:T(8,128)}, f32[192,1024]{1,0:T(8,128)}, u32[]{:S(2)}, u32[]{:S(2)}) %collective-permute-start.24) | collective-permute-done | bytes 786464 | tf_op jit(solution)/shard_map/ppermute | solution.py:59
  292.9 2.8 norm_back.6
  300.7 3.7 add_split.7
  304.5 4.7 product_rows.20
  310.2 4.9 attend_back.3
  325.7 3.5 add_split.8
  332.2 20.4 %collective-permute-done.30.got_ref = f32[256,1024]{1,0:T(8,128)} collective-permute-done((f32[256,1024]{1,0:T(8,128)}, f32[256,1024]{1,0:T(8,128)}, u32[]{:S(2)}, u32[]{:S(2)}) %collective-permute-start.30) | collective-permute-done | bytes 1048608 | tf_op jit(solution)/shard_map/ppermute | solution.py:59
  354.3 3.6 add_split.9
  369.7 4.4 product_rows.22
  380.8 8.4 %pool_back.1 = (f32[816,256]{1,0:T(8,128)S(1)}, f32[4,768]{1,0:T(4,128)S(1)}, f32[4,48]{1,0:T(4,128)S(1)}, f32[192,768]{1,0:T(8,128)S(1)}, f32[192,768]{1,0:T(8,128)S(1)}) custom-call(bf16[384,1024]{1,0:T(8,128)(2,1)S(1)} %get-tuple-element.578.low_ref, bf16[256,1024]{1,0:T(8,128)(2,1)S(1)} %copy-done.61, bf16[768,256]{1,0:T(8,128)(2,1)S(1)} %copy-done.130, ...), custom_call_target="tpu_custom_call" | custom-call | flops 999999995904 | bytes 8 | tf_op jit(solution)/shard_map/pool_back/pallas_call | solution.py:571
  394.0 7.6 %collective-permute-done.38.refs_2_ = f32[512,1024]{1,0:T(8,128)} collective-permute-done((f32[512,1024]{1,0:T(8,128)}, f32[512,1024]{1,0:T(8,128)}, u32[]{:S(2)}, u32[]{:S(2)}) %collective-permute-start.38) | collective-permute-done | bytes 2097184 | tf_op jit(solution)/shard_map/ppermute | solution.py:59
  402.7 4.4 product_rows.24
  412.9 4.2 collective-permute-done.36.got_ref
  417.1 3.6 add_split.10
  427.2 2.9 copy.65
  434.7 3.0 pad_maximum_fusion
  468.6 4.5 product_rows.26
  473.2 6.9 %collective-permute-done.42 = f32[128,1024]{1,0:T(8,128)} collective-permute-done((f32[128,1024]{1,0:T(8,128)}, f32[128,1024]{1,0:T(8,128)}, u32[]{:S(2)}, u32[]{:S(2)}) %collective-permute-start.42) | collective-permute-done | bytes 524320 | tf_op jit(solution)/shard_map/ppermute | solution.py:59
  481.2 3.6 add_split.11
  500.9 20.9 %collective-permute-done.48.got_ref = f32[256,1024]{1,0:T(8,128)} collective-permute-done((f32[256,1024]{1,0:T(8,128)}, f32[256,1024]{1,0:T(8,128)}, u32[]{:S(2)}, u32[]{:S(2)}) %collective-permute-start.48) | collective-permute-done | bytes 1048608 | tf_op jit(solution)/shard_map/ppermute | solution.py:59
  521.8 3.5 add_split.12
  529.6 4.2 product_rows.27
  545.2 4.7 collective-permute-done.60
  554.3 6.6 %collective-permute-done.55.got_ref = f32[256,512]{1,0:T(8,128)} collective-permute-done((f32[256,512]{1,0:T(8,128)}, f32[256,512]{1,0:T(8,128)}, u32[]{:S(2)}, u32[]{:S(2)}) %collective-permute-start.55) | collective-permute-done | bytes 524320 | tf_op jit(solution)/shard_map/ppermute | solution.py:59
  563.0 9.1 %collective-permute-done.56 = f32[2,440,128]{2,1,0:T(8,128)} collective-permute-done((f32[2,440,128]{2,1,0:T(8,128)}, f32[2,440,128]{2,1,0:T(8,128)}, u32[]{:S(2)}, u32[]{:S(2)}) %collective-permute-start.56) | collective-permute-done | bytes 450592 | tf_op jit(solution)/shard_map/ppermute | solution.py:59
  573.3 7.1 %collective-permute-done.59 = f32[128,512]{1,0:T(8,128)S(1)} collective-permute-done((f32[128,512]{1,0:T(8,128)S(1)}, f32[128,512]{1,0:T(8,128)S(1)}, u32[]{:S(2)}, u32[]{:S(2)}) %collective-permute-start.59) | collective-permute-done | bytes 262176 | tf_op jit(solution)/shard_map/ppermute | solution.py:59
  (792 shorter events, 281.6 us)
Async XLA Ops:
  20.5 20.8 %collective-permute-start.4 = (f32[192,1024]{1,0:T(8,128)S(1)}, f32[192,1024]{1,0:T(8,128)S(1)}, u32[]{:S(2)}, u32[]{:S(2)}) collective-permute-start(f32[192,1024]{1,0:T(8,128)S(1)} %add.329), channel_id=1, source_target_pairs={{0,2},{1,3},{2,0},{3,1},{4,6},{5,7},{6,4},{7,5},{8,10},{9,11},{10,... | collective-permute-start | bytes 2359304 | tf_op jit(solution)/shard_map/ppermute | solution.py:59
  23.4 3.6 collective-permute-start.1
  27.1 3.6 collective-permute-start.2
  30.7 4.5 collective-permute-start.3
  57.8 19.9 %collective-permute-start.7 = (f32[192,1024]{1,0:T(8,128)}, f32[192,1024]{1,0:T(8,128)}, u32[]{:S(2)}, u32[]{:S(2)}) collective-permute-start(f32[192,1024]{1,0:T(8,128)} %add.343), channel_id=1, source_target_pairs={{0,2},{1,3},{2,0},{3,1},{4,6},{5,7},{6,4},{7,5},{8,10},{9,11},{10,... | collective-permute-start | bytes 2359304 | tf_op jit(solution)/shard_map/ppermute | solution.py:59
  91.4 4.0 collective-permute-start.9
  96.9 19.8 %collective-permute-start.10 = (f32[192,1024]{1,0:T(8,128)}, f32[192,1024]{1,0:T(8,128)}, u32[]{:S(2)}, u32[]{:S(2)}) collective-permute-start(f32[192,1024]{1,0:T(8,128)} %fusion.58), channel_id=1, source_target_pairs={{0,2},{1,3},{2,0},{3,1},{4,6},{5,7},{6,4},{7,5},{8,10},{9,11},{10,... | collective-permute-start | bytes 2359304 | tf_op jit(solution)/shard_map/ppermute | solution.py:59
  127.3 19.6 %collective-permute-start.13 = (f32[192,1024]{1,0:T(8,128)S(1)}, f32[192,1024]{1,0:T(8,128)S(1)}, u32[]{:S(2)}, u32[]{:S(2)}) collective-permute-start(f32[192,1024]{1,0:T(8,128)S(1)} %add.367), channel_id=1, source_target_pairs={{0,2},{1,3},{2,0},{3,1},{4,6},{5,7},{6,4},{7,5},{8,10},{9,11},{10,... | collective-permute-start | bytes 2359304 | tf_op jit(solution)/shard_map/ppermute | solution.py:59
  180.4 4.3 collective-permute-start.15
  180.5 48.3 %collective-permute-start.21 = (f32[512,1024]{1,0:T(8,128)}, f32[512,1024]{1,0:T(8,128)}, u32[]{:S(2)}, u32[]{:S(2)}) collective-permute-start(f32[512,1024]{1,0:T(8,128)} %product_rows.14), channel_id=1, source_target_pairs={{0,8},{4,12},{8,0},{12,4},{16,24},{20,28},{24,16},{28,20},{1,9},{5... | collective-permute-start | bytes 6291464 | tf_op jit(solution)/shard_map/ppermute | solution.py:59
  182.4 52.1 %collective-permute-start.20 = (f32[512,1024]{1,0:T(8,128)}, f32[512,1024]{1,0:T(8,128)}, u32[]{:S(2)}, u32[]{:S(2)}) collective-permute-start(f32[512,1024]{1,0:T(8,128)} %product_rows.15), channel_id=1, source_target_pairs={{0,4},{4,0},{8,12},{12,8},{16,20},{20,16},{24,28},{28,24},{1,5},{5... | collective-permute-start | bytes 6291464 | tf_op jit(solution)/shard_map/ppermute | solution.py:59
  186.9 19.6 %collective-permute-start.16 = (f32[192,1024]{1,0:T(8,128)}, f32[192,1024]{1,0:T(8,128)}, u32[]{:S(2)}, u32[]{:S(2)}) collective-permute-start(f32[192,1024]{1,0:T(8,128)} %add.380.mine_ref), channel_id=1, source_target_pairs={{0,2},{1,3},{2,0},{3,1},{4,6},{5,7},{6,4},{7,5},{8,10},{9,11},{10,... | collective-permute-start | bytes 2359304 | tf_op jit(solution)/shard_map/ppermute | solution.py:59
  234.4 19.5 %collective-permute-start.19 = (f32[192,1024]{1,0:T(8,128)}, f32[192,1024]{1,0:T(8,128)}, u32[]{:S(2)}, u32[]{:S(2)}) collective-permute-start(f32[192,1024]{1,0:T(8,128)} %add.381.mine_ref), channel_id=1, source_target_pairs={{0,2},{1,3},{2,0},{3,1},{4,6},{5,7},{6,4},{7,5},{8,10},{9,11},{10,... | collective-permute-start | bytes 2359304 | tf_op jit(solution)/shard_map/ppermute | solution.py:59
  241.1 59.6 %collective-permute-start.27 = (f32[256,1024]{1,0:T(8,128)}, f32[256,1024]{1,0:T(8,128)}, u32[]{:S(2)}, u32[]{:S(2)}) collective-permute-start(f32[256,1024]{1,0:T(8,128)} %get-tuple-element.503), channel_id=1, source_target_pairs={{0,8},{4,12},{8,0},{12,4},{16,24},{20,28},{24,16},{28,20},{1,9},{5... | collective-permute-start | bytes 3145736 | tf_op jit(solution)/shard_map/ppermute | solution.py:59
  242.7 61.7 %collective-permute-start.26 = (f32[512,1024]{1,0:T(8,128)}, f32[512,1024]{1,0:T(8,128)}, u32[]{:S(2)}, u32[]{:S(2)}) collective-permute-start(f32[512,1024]{1,0:T(8,128)} %product_rows.16), channel_id=1, source_target_pairs={{0,4},{4,0},{8,12},{12,8},{16,20},{20,16},{24,28},{28,24},{1,5},{5... | collective-permute-start | bytes 6291464 | tf_op jit(solution)/shard_map/ppermute | solution.py:59
  244.3 81.4 %collective-permute-start.31 = (f32[256,1024]{1,0:T(8,128)}, f32[256,1024]{1,0:T(8,128)}, u32[]{:S(2)}, u32[]{:S(2)}) collective-permute-start(f32[256,1024]{1,0:T(8,128)} %get-tuple-element.527), channel_id=1, source_target_pairs={{0,16},{4,20},{8,24},{12,28},{16,0},{20,4},{24,8},{28,12},{1,17},{... | collective-permute-start | bytes 3145736 | tf_op jit(solution)/shard_map/ppermute | solution.py:59
  267.0 3.4 collective-permute-start.23
  272.6 20.1 %collective-permute-start.24 = (f32[192,1024]{1,0:T(8,128)}, f32[192,1024]{1,0:T(8,128)}, u32[]{:S(2)}, u32[]{:S(2)}) collective-permute-start(f32[192,1024]{1,0:T(8,128)} %add.382.mine_ref), channel_id=1, source_target_pairs={{0,2},{1,3},{2,0},{3,1},{4,6},{5,7},{6,4},{7,5},{8,10},{9,11},{10,... | collective-permute-start | bytes 2359304 | tf_op jit(solution)/shard_map/ppermute | solution.py:59
  277.1 92.4 %collective-permute-start.34 = (f32[512,1024]{1,0:T(8,128)}, f32[512,1024]{1,0:T(8,128)}, u32[]{:S(2)}, u32[]{:S(2)}) collective-permute-start(f32[512,1024]{1,0:T(8,128)} %product_rows.19), channel_id=1, source_target_pairs={{0,4},{4,0},{8,12},{12,8},{16,20},{20,16},{24,28},{28,24},{1,5},{5... | collective-permute-start | bytes 6291464 | tf_op jit(solution)/shard_map/ppermute | solution.py:59
  315.1 5.8 collective-permute-start.28
  315.9 36.7 %collective-permute-start.30 = (f32[256,1024]{1,0:T(8,128)}, f32[256,1024]{1,0:T(8,128)}, u32[]{:S(2)}, u32[]{:S(2)}) collective-permute-start(f32[256,1024]{1,0:T(8,128)} %get-tuple-element.525), channel_id=1, source_target_pairs={{0,8},{4,12},{8,0},{12,4},{16,24},{20,28},{24,16},{28,20},{1,9},{5... | collective-permute-start | bytes 3145736 | tf_op jit(solution)/shard_map/ppermute | solution.py:59
  317.6 50.7 %collective-permute-start.35 = (f32[128,1024]{1,0:T(8,128)}, f32[128,1024]{1,0:T(8,128)}, u32[]{:S(2)}, u32[]{:S(2)}) collective-permute-start(f32[128,1024]{1,0:T(8,128)} %get-tuple-element.560), channel_id=1, source_target_pairs={{0,16},{4,20},{8,24},{12,28},{16,0},{20,4},{24,8},{28,12},{1,17},{... | collective-permute-start | bytes 1572872 | tf_op jit(solution)/shard_map/ppermute | solution.py:59
  329.2 28.7 %collective-permute-start.29 = (f32[192,1024]{1,0:T(8,128)}, f32[192,1024]{1,0:T(8,128)}, u32[]{:S(2)}, u32[]{:S(2)}) collective-permute-start(f32[192,1024]{1,0:T(8,128)} %add.383.mine_ref), channel_id=1, source_target_pairs={{0,2},{1,3},{2,0},{3,1},{4,6},{5,7},{6,4},{7,5},{8,10},{9,11},{10,... | collective-permute-start | bytes 2359304 | tf_op jit(solution)/shard_map/ppermute | solution.py:59
  330.7 44.4 %collective-permute-start.33 = (f32[128,1024]{1,0:T(8,128)}, f32[128,1024]{1,0:T(8,128)}, u32[]{:S(2)}, u32[]{:S(2)}) collective-permute-start(f32[128,1024]{1,0:T(8,128)} %get-tuple-element.557), channel_id=1, source_target_pairs={{0,4},{4,0},{8,12},{12,8},{16,20},{20,16},{24,28},{28,24},{1,5},{5... | collective-permute-start | bytes 1572872 | tf_op jit(solution)/shard_map/ppermute | solution.py:59
  352.6 48.9 %collective-permute-start.38 = (f32[512,1024]{1,0:T(8,128)}, f32[512,1024]{1,0:T(8,128)}, u32[]{:S(2)}, u32[]{:S(2)}) collective-permute-start(f32[512,1024]{1,0:T(8,128)} %product_rows.21), channel_id=1, source_target_pairs={{0,4},{4,0},{8,12},{12,8},{16,20},{20,16},{24,28},{28,24},{1,5},{5... | collective-permute-start | bytes 6291464 | tf_op jit(solution)/shard_map/ppermute | solution.py:59
  363.5 44.6 %collective-permute-start.37 = (f32[128,1024]{1,0:T(8,128)}, f32[128,1024]{1,0:T(8,128)}, u32[]{:S(2)}, u32[]{:S(2)}) collective-permute-start(f32[128,1024]{1,0:T(8,128)} %get-tuple-element.591), channel_id=1, source_target_pairs={{0,16},{4,20},{8,24},{12,28},{16,0},{20,4},{24,8},{28,12},{1,17},{... | collective-permute-start | bytes 1572872 | tf_op jit(solution)/shard_map/ppermute | solution.py:59
  390.1 26.9 %collective-permute-start.36 = (f32[256,1024]{1,0:T(8,128)}, f32[256,1024]{1,0:T(8,128)}, u32[]{:S(2)}, u32[]{:S(2)}) collective-permute-start(f32[256,1024]{1,0:T(8,128)} %get-tuple-element.589), channel_id=1, source_target_pairs={{0,8},{4,12},{8,0},{12,4},{16,24},{20,28},{24,16},{28,20},{1,9},{5... | collective-permute-start | bytes 3145736 | tf_op jit(solution)/shard_map/ppermute | solution.py:59
  393.4 73.0 %collective-permute-start.43 = (f32[512,1024]{1,0:T(8,128)}, f32[512,1024]{1,0:T(8,128)}, u32[]{:S(2)}, u32[]{:S(2)}) collective-permute-start(f32[512,1024]{1,0:T(8,128)} %copy-done.53), channel_id=1, source_target_pairs={{0,4},{4,0},{8,12},{12,8},{16,20},{20,16},{24,28},{28,24},{1,5},{5... | collective-permute-start | bytes 6291464 | tf_op jit(solution)/shard_map/ppermute | solution.py:59
  393.9 15.4 %collective-permute-start.50 = (f32[192,768]{1,0:T(8,128)}, f32[192,768]{1,0:T(8,128)}, u32[]{:S(2)}, u32[]{:S(2)}) collective-permute-start(f32[192,768]{1,0:T(8,128)} %copy-done.59), channel_id=1, source_target_pairs={{0,1},{1,0},{2,3},{3,2},{4,5},{5,4},{6,7},{7,6},{8,9},{9,8},{10,11... | collective-permute-start | bytes 1769480 | tf_op jit(solution)/shard_map/ppermute | solution.py:59
  409.2 72.0 %collective-permute-start.41 = (f32[256,1024]{1,0:T(8,128)}, f32[256,1024]{1,0:T(8,128)}, u32[]{:S(2)}, u32[]{:S(2)}) collective-permute-start(f32[256,1024]{1,0:T(8,128)} %get-tuple-element.625), channel_id=1, source_target_pairs={{0,8},{4,12},{8,0},{12,4},{16,24},{20,28},{24,16},{28,20},{1,9},{5... | collective-permute-start | bytes 3145736 | tf_op jit(solution)/shard_map/ppermute | solution.py:59
  411.3 38.9 %collective-permute-start.52 = (f32[192,768]{1,0:T(8,128)}, f32[192,768]{1,0:T(8,128)}, u32[]{:S(2)}, u32[]{:S(2)}) collective-permute-start(f32[192,768]{1,0:T(8,128)} %add.401), channel_id=1, source_target_pairs={{0,2},{1,3},{2,0},{3,1},{4,6},{5,7},{6,4},{7,5},{8,10},{9,11},{10,... | collective-permute-start | bytes 1769480 | tf_op jit(solution)/shard_map/ppermute | solution.py:59
  439.2 19.3 %collective-permute-start.39 = (f32[2,8,32,817]{3,2,1,0:T(8,128)}, f32[2,8,32,817]{3,2,1,0:T(8,128)}, u32[]{:S(2)}, u32[]{:S(2)}) collective-permute-start(f32[2,8,32,817]{3,2,1,0:T(8,128)} %pad_maximum_fusion), channel_id=1, source_target_pairs={{0,1},{1,0},{2,3},{3,2},{4,5},{5,4},{6,7},{7,6},{8,9},{9,8},{10,11... | collective-permute-start | bytes 5019656 | tf_op jit(solution)/shard_map/ppermute | solution.py:59
  451.5 5.2 collective-permute-start.53
  453.3 26.8 %collective-permute-start.42 = (f32[128,1024]{1,0:T(8,128)}, f32[128,1024]{1,0:T(8,128)}, u32[]{:S(2)}, u32[]{:S(2)}) collective-permute-start(f32[128,1024]{1,0:T(8,128)} %get-tuple-element.627), channel_id=1, source_target_pairs={{0,16},{4,20},{8,24},{12,28},{16,0},{20,4},{24,8},{28,12},{1,17},{... | collective-permute-start | bytes 1572872 | tf_op jit(solution)/shard_map/ppermute | solution.py:59
  456.7 71.1 %collective-permute-start.49 = (f32[512,512]{1,0:T(8,128)}, f32[512,512]{1,0:T(8,128)}, u32[]{:S(2)}, u32[]{:S(2)}) collective-permute-start(f32[512,512]{1,0:T(8,128)} %product_rows.25), channel_id=1, source_target_pairs={{0,4},{4,0},{8,12},{12,8},{16,20},{20,16},{24,28},{28,24},{1,5},{5... | collective-permute-start | bytes 3145736 | tf_op jit(solution)/shard_map/ppermute | solution.py:59
  463.4 23.6 %collective-permute-start.40 = (f32[1,8,32,817]{3,2,1,0:T(8,128)}, f32[1,8,32,817]{3,2,1,0:T(8,128)}, u32[]{:S(2)}, u32[]{:S(2)}) collective-permute-start(f32[1,8,32,817]{3,2,1,0:T(8,128)} %constant_dynamic-slice_fusion.3), channel_id=1, source_target_pairs={{0,2},{1,3},{2,0},{3,1},{4,6},{5,7},{6,4},{7,5},{8,10},{9,11},{10,... | collective-permute-start | bytes 2509832 | tf_op jit(solution)/shard_map/ppermute | solution.py:59
  484.8 56.8 %collective-permute-start.47 = (f32[128,1024]{1,0:T(8,128)}, f32[128,1024]{1,0:T(8,128)}, u32[]{:S(2)}, u32[]{:S(2)}) collective-permute-start(f32[128,1024]{1,0:T(8,128)} %get-tuple-element.667), channel_id=1, source_target_pairs={{0,16},{4,20},{8,24},{12,28},{16,0},{20,4},{24,8},{28,12},{1,17},{... | collective-permute-start | bytes 1572872 | tf_op jit(solution)/shard_map/ppermute | solution.py:59
  484.8 37.0 %collective-permute-start.48 = (f32[256,1024]{1,0:T(8,128)}, f32[256,1024]{1,0:T(8,128)}, u32[]{:S(2)}, u32[]{:S(2)}) collective-permute-start(f32[256,1024]{1,0:T(8,128)} %get-tuple-element.669), channel_id=1, source_target_pairs={{0,8},{4,12},{8,0},{12,4},{16,24},{20,28},{24,16},{28,20},{1,9},{5... | collective-permute-start | bytes 3145736 | tf_op jit(solution)/shard_map/ppermute | solution.py:59
  497.0 28.6 %collective-permute-start.45 = (f32[192,1024]{1,0:T(8,128)}, f32[192,1024]{1,0:T(8,128)}, u32[]{:S(2)}, u32[]{:S(2)}) collective-permute-start(f32[192,1024]{1,0:T(8,128)} %fusion.6), channel_id=1, source_target_pairs={{0,1},{1,0},{2,3},{3,2},{4,5},{5,4},{6,7},{7,6},{8,9},{9,8},{10,11... | collective-permute-start | bytes 2359304 | tf_op jit(solution)/shard_map/ppermute | solution.py:59
  497.0 55.1 %collective-permute-start.54 = (f32[4,440,128]{2,1,0:T(8,128)}, f32[4,440,128]{2,1,0:T(8,128)}, u32[]{:S(2)}, u32[]{:S(2)}) collective-permute-start(f32[4,440,128]{2,1,0:T(8,128)} %bitcast.233), channel_id=1, source_target_pairs={{0,4},{4,0},{8,12},{12,8},{16,20},{20,16},{24,28},{28,24},{1,5},{5... | collective-permute-start | bytes 2703368 | tf_op jit(solution)/shard_map/ppermute | solution.py:59
  525.2 24.7 %collective-permute-start.60 = (f32[128,1024]{1,0:T(8,128)}, f32[128,1024]{1,0:T(8,128)}, u32[]{:S(2)}, u32[]{:S(2)}) collective-permute-start(f32[128,1024]{1,0:T(8,128)} %get-tuple-element.720), channel_id=1, source_target_pairs={{0,16},{4,20},{8,24},{12,28},{16,0},{20,4},{24,8},{28,12},{1,17},{... | collective-permute-start | bytes 1572872 | tf_op jit(solution)/shard_map/ppermute | solution.py:59
  534.6 26.3 %collective-permute-start.55 = (f32[256,512]{1,0:T(8,128)}, f32[256,512]{1,0:T(8,128)}, u32[]{:S(2)}, u32[]{:S(2)}) collective-permute-start(f32[256,512]{1,0:T(8,128)} %get-tuple-element.703), channel_id=1, source_target_pairs={{0,8},{4,12},{8,0},{12,4},{16,24},{20,28},{24,16},{28,20},{1,9},{5... | collective-permute-start | bytes 1572872 | tf_op jit(solution)/shard_map/ppermute | solution.py:59
  543.7 38.2 %collective-permute-start.46 = (f32[192,1024]{1,0:T(8,128)}, f32[192,1024]{1,0:T(8,128)}, u32[]{:S(2)}, u32[]{:S(2)}) collective-permute-start(f32[192,1024]{1,0:T(8,128)} %add.400), channel_id=1, source_target_pairs={{0,2},{1,3},{2,0},{3,1},{4,6},{5,7},{6,4},{7,5},{8,10},{9,11},{10,... | collective-permute-start | bytes 2359304 | tf_op jit(solution)/shard_map/ppermute | solution.py:59
  554.3 17.7 %collective-permute-start.56 = (f32[2,440,128]{2,1,0:T(8,128)}, f32[2,440,128]{2,1,0:T(8,128)}, u32[]{:S(2)}, u32[]{:S(2)}) collective-permute-start(f32[2,440,128]{2,1,0:T(8,128)} %dynamic-slice_bitcast_fusion), channel_id=1, source_target_pairs={{0,8},{4,12},{8,0},{12,4},{16,24},{20,28},{24,16},{28,20},{1,9},{5... | collective-permute-start | bytes 1351688 | tf_op jit(solution)/shard_map/ppermute | solution.py:59
  562.9 17.5 %collective-permute-start.59 = (f32[128,512]{1,0:T(8,128)S(1)}, f32[128,512]{1,0:T(8,128)S(1)}, u32[]{:S(2)}, u32[]{:S(2)}) collective-permute-start(f32[128,512]{1,0:T(8,128)S(1)} %get-tuple-element.718), channel_id=1, source_target_pairs={{0,16},{4,20},{8,24},{12,28},{16,0},{20,4},{24,8},{28,12},{1,17},{... | collective-permute-start | bytes 786440 | tf_op jit(solution)/shard_map/ppermute | solution.py:59
  573.3 11.6 %collective-permute-start.57 = (f32[1,440,128]{2,1,0:T(8,128)S(1)}, f32[1,440,128]{2,1,0:T(8,128)S(1)}, u32[]{:S(2)}, u32[]{:S(2)}) collective-permute-start(f32[1,440,128]{2,1,0:T(8,128)S(1)} %constant_dynamic-slice_fusion), channel_id=1, source_target_pairs={{0,16},{4,20},{8,24},{12,28},{16,0},{20,4},{24,8},{28,12},{1,17},{... | collective-permute-start | bytes 675848 | tf_op jit(solution)/shard_map/ppermute | solution.py:59
  583.5 9.6 %collective-permute-start.51 = (f32[192,1024]{1,0:T(8,128)S(1)}, f32[192,1024]{1,0:T(8,128)S(1)}, u32[]{:S(2)}, u32[]{:S(2)}) collective-permute-start(f32[192,1024]{1,0:T(8,128)S(1)} %add_add_fusion), channel_id=1, source_target_pairs={{0,1},{1,0},{2,3},{3,2},{4,5},{5,4},{6,7},{7,6},{8,9},{9,8},{10,11... | collective-permute-start | bytes 2359304 | tf_op jit(solution)/shard_map/ppermute | solution.py:59
  588.1 4.3 collective-permute-start.58
  (245 other events, 1152.2 us)

commit v5 on v4

--- a/solution.py
+++ b/solution.py
@@ -9,21 +9,22 @@
 
 HEAD_DIM = 64
 PLAN = {
-    ("pre", 0): [("down", 0), ("up", 0)],
+    ("top", 0): [("down", 0)],
+    ("pre", 0): [("up", 0)],
     ("wait_one", 0): [("att", 0), ("down", 0), ("up", 0)],
-    ("wait_two", 1): [("down", 1)],
-    ("mid", 1): [("up", 0), ("att", 0)],
-    ("wait_one", 1): [("up", 1), ("down", 0), ("att", 0)],
-    ("end", 1): [("up", 0), ("down", 1), ("down", 0), ("att", 1)],
-    "values": [("up", 1), ("att", 0), ("down", 1), "tail"],
-    "vectors": [("att", 1), ("down", 1), ("up", 1)],
+    ("wait_two", 1): [("down", 1), ("up", 0)],
+    ("mid", 1): [("down", 0), ("att", 0)],
+    ("wait_one", 1): [("up", 0), ("up", 1), ("att", 0), ("down", 1)],
+    ("end", 1): [("down", 0), ("att", 1)],
+    "back": [("down", 1), ("att", 0), ("up", 1)],
     "small": ["small"],
-    "output": ["tail"],
-    "pixels": [("att", 1), ("up", 1)],
-    "rows": ["tail", "small"],
+    "values": ["tail", ("down", 1), ("up", 1), ("att", 1)],
+    "pixels": ["small", ("up", 1), "tail", ("att", 1)],
+    "rows": ["small", ("att", 1), "tail", "small", "tail"],
 }
-DRAIN = [("att", 1), "small", "tail", "small"]
+DRAIN = []
 ROOT_DIM = math.sqrt(HEAD_DIM)
+PRODUCT_BLOCKS = 2
 BF = jnp.bfloat16
 F32 = jnp.float32
 
@@ -169,31 +170,222 @@
     )(shards, own, other, change)
 
 
-def norm_back(mine, got, unit, inverse, gain, grad):
+def norm_back(mine, got, unit, inverse, gains, place, grad):
     half, width = mine.shape
+    size = half
 
     def kernel(mine_ref, got_ref, unit_ref, inverse_ref, gain_ref, grad_ref, change_out, grad_out, sums_out):
         pull = mine_ref[...] + got_ref[...]
         unit_rows = unit_ref[...]
-        scaled = pull * gain_ref[...]
+        scaled = pull * gain_ref[place[0], place[1] : place[1] + 1]
         first = jnp.mean(scaled, axis=-1, keepdims=True)
         second = jnp.mean(scaled * unit_rows, axis=-1, keepdims=True)
         change = inverse_ref[:, :1] * (scaled - first - unit_rows * second)
         change_out[...] = change
         total = grad_ref[...] + change
         grad_out[...] = total
-        sums_out[0:1] = jnp.sum(pull * unit_rows, axis=0, keepdims=True)
-        sums_out[1:2] = jnp.sum(pull, axis=0, keepdims=True)
-        sums_out[2:3] = jnp.sum(total, axis=0, keepdims=True)
+
+        @pl.when(pl.program_id(0) == 0)
+        def _():
+            sums_out[...] = jnp.zeros_like(sums_out)
+
+        sums_out[0:1] += jnp.sum(pull * unit_rows, axis=0, keepdims=True)
+        sums_out[1:2] += jnp.sum(pull, axis=0, keepdims=True)
+        sums_out[2:3] += jnp.sum(total, axis=0, keepdims=True)
 
     rows = jax.ShapeDtypeStruct((half, width), F32)
+    block = pl.BlockSpec((size, width), lambda j: (j, 0))
     return pl.pallas_call(
         kernel,
         out_shape=(rows, rows, jax.ShapeDtypeStruct((3, width), F32)),
+        grid=(half // size,),
+        in_specs=[
+            block,
+            block,
+            block,
+            pl.BlockSpec((size, 128), lambda j: (j, 0)),
+            pl.BlockSpec(gains.shape, lambda j: (0, 0, 0)),
+            block,
+        ],
+        out_specs=(block, block, pl.BlockSpec((3, width), lambda j: (0, 0))),
         cost_estimate=LONG,
-        compiler_params=vmem_limit(30 * half * width),
+        compiler_params=vmem_limit(64 * size * width),
         name="norm_back",
-    )(mine, got, unit, inverse, gain[None], grad)
+    )(mine, got, unit, inverse, gains, grad)
+
+
+def feed_forward(unit_own, unit_other, gains, biases, place, up_weight, up_bias, down_weight):
+    half, width = unit_own.shape
+    rows = 2 * half
+    layer, which = place
+    hidden = up_weight.shape[2]
+    size = hidden // 4
+    spread_of = math.sqrt(2.0)
+    peak = 1.0 / math.sqrt(2.0 * math.pi)
+
+    def kernel(own_ref, other_ref, gain_ref, bias_ref, up_ref, up_bias_ref, down_ref,
+               activation_out, slope_out, own_out, send_out, normed_ref):
+        step = pl.program_id(0)
+
+        @pl.when(step == 0)
+        def _():
+            gain = gain_ref[layer, which : which + 1]
+            bias = bias_ref[layer, which : which + 1]
+            normed_ref[:half] = (own_ref[...] * gain + bias).astype(BF)
+            normed_ref[half:] = (other_ref[...] * gain + bias).astype(BF)
+            own_out[...] = jnp.zeros_like(own_out)
+            send_out[...] = jnp.zeros_like(send_out)
+
+        pre = matmul(normed_ref[...], up_ref[0]) + up_bias_ref[layer : layer + 1]
+        below = 0.5 + 0.5 * lax.erf(pre / spread_of)
+        slope_out[...] = below + pre * (jnp.exp(-0.5 * pre * pre) * peak)
+        activation = (pre * below).astype(BF)
+        activation_out[...] = activation
+        send_out[...] += matmul(activation[half:], down_ref[0])
+        own_out[...] += matmul(activation[:half], down_ref[0])
+
+    piece = jax.ShapeDtypeStruct((half, width), F32)
+    whole = pl.BlockSpec((half, width), lambda j: (0, 0))
+    return pl.pallas_call(
+        kernel,
+        out_shape=(
+            jax.ShapeDtypeStruct((rows, hidden), BF),
+            jax.ShapeDtypeStruct((rows, hidden), F32),
+            piece,
+            piece,
+        ),
+        grid=(hidden // size,),
+        in_specs=[
+            whole,
+            whole,
+            pl.BlockSpec(gains.shape, lambda j: (0, 0, 0)),
+            pl.BlockSpec(biases.shape, lambda j: (0, 0, 0)),
+            pl.BlockSpec((1, width, size), lambda j: (layer, 0, j)),
+            pl.BlockSpec((up_bias.shape[0], size), lambda j: (0, j)),
+            pl.BlockSpec((1, size, width), lambda j: (layer, j, 0)),
+        ],
+        out_specs=(
+            pl.BlockSpec((rows, size), lambda j: (0, j)),
+            pl.BlockSpec((rows, size), lambda j: (0, j)),
+            whole,
+            whole,
+        ),
+        scratch_shapes=[pltpu.VMEM((rows, width), BF)],
+        cost_estimate=LONG,
+        compiler_params=vmem_limit(30 * rows * width),
+        name="feed_forward",
+    )(unit_own, unit_other, gains, biases, up_weight, up_bias, down_weight)
+
+
+def feed_back(low, slope, down_weight, up_weight, layer):
+    rows, width = low.shape
+    half = rows // 2
+    hidden = slope.shape[1]
+    size = hidden // 4
+
+    def kernel(low_ref, slope_ref, down_ref, up_ref, pre_out, sums_out, own_out, send_out):
+        @pl.when(pl.program_id(0) == 0)
+        def _():
+            own_out[...] = jnp.zeros_like(own_out)
+            send_out[...] = jnp.zeros_like(send_out)
+
+        grad = matmul_nt(low_ref[...], down_ref[0]) * slope_ref[...]
+        sums_out[...] = jnp.sum(grad, axis=0, keepdims=True)
+        grad_low = grad.astype(BF)
+        pre_out[...] = grad_low
+        send_out[...] += matmul_nt(grad_low[half:], up_ref[0])
+        own_out[...] += matmul_nt(grad_low[:half], up_ref[0])
+
+    piece = jax.ShapeDtypeStruct((half, width), F32)
+    whole = pl.BlockSpec((half, width), lambda j: (0, 0))
+    return pl.pallas_call(
+        kernel,
+        out_shape=(
+            jax.ShapeDtypeStruct((rows, hidden), BF),
+            jax.ShapeDtypeStruct((1, hidden), F32),
+            piece,
+            piece,
+        ),
+        grid=(hidden // size,),
+        in_specs=[
+            pl.BlockSpec((rows, width), lambda j: (0, 0)),
+            pl.BlockSpec((rows, size), lambda j: (0, j)),
+            pl.BlockSpec((1, size, width), lambda j: (layer, j, 0)),
+            pl.BlockSpec((1, width, size), lambda j: (layer, 0, j)),
+        ],
+        out_specs=(
+            pl.BlockSpec((rows, size), lambda j: (0, j)),
+            pl.BlockSpec((1, size), lambda j: (0, j)),
+            whole,
+            whole,
+        ),
+        cost_estimate=LONG,
+        compiler_params=vmem_limit(26 * rows * width),
+        name="feed_back",
+    )(low, slope, down_weight, up_weight)
+
+
+def embed_terms(side_send, side_own, value_grad, key_grad, key_var, cell, patch, embed, key_weight):
+    count, _ = side_send.shape
+    flat_all, local_width = value_grad.shape
+    head_count, flat = key_grad.shape
+    model_width = patch.shape[1]
+    lanes = -(-(flat_all + 1) // 128) * 128
+
+    def kernel(send_ref, own_ref, value_ref, key_ref, var_ref, cell_ref, patch_ref, embed_ref, weight_ref,
+               send_out, own_out, sum_out, query_out, bias_out, value_low_ref):
+        scale = cell_ref[0:1, 0:1]
+        value_low_ref[...] = (value_ref[...] * scale).astype(BF)
+        bias_out[...] = jnp.sum(value_ref[flat:], axis=0, keepdims=True) * scale
+        key_high, key_rest = two_part(key_ref[...] * scale)
+        var_high, var_rest = two_part(var_ref[...] * scale)
+        embed_high, embed_rest = two_part(embed_ref[...])
+        total = matmul(key_high, patch_ref[...]) + matmul(key_rest, patch_ref[...])
+        total = total + matmul(var_high, embed_high) + matmul(var_rest, embed_high)
+        total = total + matmul(var_high, embed_rest)
+        sum_out[...] = total
+        high, rest = two_part(total)
+        query = matmul(high, weight_ref[...]) + matmul(rest, weight_ref[...])
+        head = lax.broadcasted_iota(jnp.int32, (head_count, local_width), 0)
+        column = lax.broadcasted_iota(jnp.int32, (head_count, local_width), 1)
+        inside = (column >= head * HEAD_DIM) & (column < (head + 1) * HEAD_DIM)
+        query = jnp.sum(jnp.where(inside, query, 0.0), axis=0, keepdims=True) / ROOT_DIM
+        query_out[...] = query
+        query_high, query_rest = two_part(query)
+        query_rows = jnp.concatenate(
+            [query_high.astype(F32), query_rest.astype(F32), jnp.zeros((6, local_width), F32)], axis=0
+        ).astype(BF)
+        flat_rows, var_rows = [
+            jnp.concatenate(
+                [part.astype(F32) for part in (first, second, first, jnp.zeros_like(first))], axis=0
+            ).astype(BF)
+            for first, second in ((key_high, key_rest), (var_high, var_rest))
+        ]
+        for side_ref, out_ref in ((send_ref, send_out), (own_ref, own_out)):
+            keys = side_ref[:, 2 * local_width :]
+            values = side_ref[:, :local_width]
+            weight = side_ref[:, local_width : 2 * local_width]
+            out_ref[...] = jnp.zeros_like(out_ref)
+            out_ref[:, :flat] = matmul_nt(values, value_low_ref[:flat]) + matmul(keys, flat_rows)
+            out_ref[:, flat:flat_all] = matmul_nt(values, value_low_ref[flat:]) + matmul(keys, var_rows)
+            part = matmul_nt(weight, query_rows)
+            out_ref[:, flat_all : flat_all + 1] = jnp.sum(part, axis=1, keepdims=True)
+
+    block = jax.ShapeDtypeStruct((count, lanes), F32)
+    return pl.pallas_call(
+        kernel,
+        out_shape=(
+            block,
+            block,
+            jax.ShapeDtypeStruct((head_count, model_width), F32),
+            jax.ShapeDtypeStruct((1, local_width), F32),
+            jax.ShapeDtypeStruct((1, local_width), F32),
+        ),
+        scratch_shapes=[pltpu.VMEM((flat_all, local_width), BF)],
+        cost_estimate=LONG,
+        compiler_params=vmem_limit(14 << 20),
+        name="embed_terms",
+    )(side_send, side_own, value_grad, key_grad, key_var, cell, patch, embed, key_weight)
 
 
 def product_rows(pairs, scale, start, first, second, got=None):
@@ -201,6 +393,8 @@
     total = sum(widths)
     has_got = got is not None
     count = first + second
+    size = 128 * PRODUCT_BLOCKS
+    start, first, second, count = [n // PRODUCT_BLOCKS for n in (start, first, second, count)]
 
     def kernel(scale_ref, *refs):
         ins = refs[: 2 * len(pairs)]
@@ -235,18 +429,18 @@
     traffic = 0
     for left, right in pairs:
         rows = left.shape[0]
-        in_specs.append(pl.BlockSpec((rows, 128), lambda j: (0, start + j)))
+        in_specs.append(pl.BlockSpec((rows, size), lambda j: (0, start + j)))
         in_specs.append(pl.BlockSpec(right.shape, lambda j: (0, 0)))
         operands += [left, right]
-        traffic += 2 * 2 * rows * (128 + right.shape[1])
+        traffic += 2 * 2 * rows * (size + right.shape[1])
     if has_got:
-        in_specs.append(pl.BlockSpec((128, total), lambda j: (j, 0)))
+        in_specs.append(pl.BlockSpec((size, total), lambda j: (j, 0)))
         operands.append(got)
-    out_shape = [jax.ShapeDtypeStruct((first * 128, total), F32)]
-    out_specs = [pl.BlockSpec((128, total), lambda j: (jnp.minimum(j, first - 1), 0))]
+    out_shape = [jax.ShapeDtypeStruct((first * size, total), F32)]
+    out_specs = [pl.BlockSpec((size, total), lambda j: (jnp.minimum(j, first - 1), 0))]
     if second:
-        out_shape.append(jax.ShapeDtypeStruct((second * 128, total), F32))
-        out_specs.append(pl.BlockSpec((128, total), lambda j: (jnp.maximum(j - first, 0), 0)))
+        out_shape.append(jax.ShapeDtypeStruct((second * size, total), F32))
+        out_specs.append(pl.BlockSpec((size, total), lambda j: (jnp.maximum(j - first, 0), 0)))
     return pl.pallas_call(
         kernel,
         out_shape=out_shape,
@@ -254,7 +448,7 @@
         in_specs=in_specs,
         out_specs=out_specs,
         cost_estimate=LONG,
-        compiler_params=vmem_limit(traffic + 2 * 4 * 128 * total * 3),
+        compiler_params=vmem_limit(traffic + 2 * 4 * size * total * 4),
         name="product_rows",
     )(*operands)
 
@@ -262,7 +456,7 @@
 def add_split(keep, got):
     rows, width = keep.shape
     half = rows // 2
-    size = min(64, half)
+    size = min(128, half)
     count = half // size
 
     def kernel(keep_ref, got_ref, first_out, second_out):
@@ -395,7 +589,7 @@
     )(low, qkv, totals, weights, out_weight)
 
 
-def finish_layers(kind, pieces, layer_count, shard, local_width):
+def finish_layers(kind, pieces, cell, layer_count, shard, local_width):
     width = pieces[0].shape[1]
     shapes = {
         "down": [(layer_count, width, shard)],
@@ -431,7 +625,7 @@
         return [jnp.stack([value[:, :local_width].T for value in values]), jnp.stack(rest)]
 
     def kernel(*refs):
-        store([ref[...] for ref in refs[:layer_count]], refs[layer_count:])
+        store([ref[...] for ref in refs[:layer_count]], refs[layer_count + 1 :])
 
     return pl.pallas_call(
         kernel,
@@ -443,7 +637,7 @@
         ),
         compiler_params=vmem_limit(20 * layer_count * shard * width),
         name="finish_layers",
-    )(*pieces)
+    )(*pieces, cell)
 
 
 def one_hot_segments(var_count, pix_count):
@@ -463,20 +657,36 @@
     head_count = local_width // HEAD_DIM
     half = rows // 2
 
-    def kernel(core_ref, pixels_ref, patch_ref, embed_ref, query_ref, query_weight_ref, key_weight_ref,
-               value_weight_ref, bias_ref, mask_ref, out_weight_ref,
-               low_out, query_out, key_out, score_out, flat_out, var_out, probs_out, pooled_out,
-               own_out, send_out, turned_ref):
+    large = (query_weight, key_weight, pixels, patch, embed, value_weight, out_weight)
+
+    def kernel(core_ref, query_ref, bias_ref, mask_ref, *refs):
+        sources, refs = refs[: len(large)], refs[len(large) :]
+        (low_out, query_out, key_out, score_out, flat_out, var_out, probs_out, pooled_out,
+         own_out, send_out, turned_ref) = refs[:11]
+        held, sems = refs[11 : 11 + len(large)], refs[11 + len(large)]
+        copies = [
+            pltpu.make_async_copy(source, target, sems.at[i])
+            for i, (source, target) in enumerate(zip(sources, held))
+        ]
+        for copy in copies:
+            copy.start()
+        (query_weight_ref, key_weight_ref, pixels_ref, patch_ref, embed_ref, value_weight_ref,
+         out_weight_ref) = held
+        copies[0].wait()
+        query = matmul(query_ref[...].astype(BF), query_weight_ref[...]).astype(BF)
+        query_out[...] = query.astype(F32)
+        copies[1].wait()
+        for head in range(head_count):
+            one = slice(head * HEAD_DIM, (head + 1) * HEAD_DIM)
+            key_out[head : head + 1] = matmul_nt(query[:, one], key_weight_ref[:, one]) / ROOT_DIM
+        copies[2].wait()
         turned_ref[...] = pixels_ref[...].T
         mine = pl.multiple_of(core_ref[0] * half, 8)
         theirs = pl.multiple_of(half - core_ref[0] * half, 8)
         low_out[:half] = turned_ref[pl.ds(mine, half)].astype(BF)
         low_out[half:] = turned_ref[pl.ds(theirs, half)].astype(BF)
-        query = matmul(query_ref[...].astype(BF), query_weight_ref[...]).astype(BF)
-        query_out[...] = query.astype(F32)
-        for head in range(head_count):
-            one = slice(head * HEAD_DIM, (head + 1) * HEAD_DIM)
-            key_out[head : head + 1] = matmul_nt(query[:, one], key_weight_ref[:, one]) / ROOT_DIM
+        for copy in copies[3:]:
+            copy.wait()
         key_high, key_rest = two_part(key_out[...])
         embed_high, embed_rest = two_part(embed_ref[...])
         score_out[...] = matmul_nt(key_high, patch_ref[...]) + matmul_nt(key_rest, patch_ref[...])
@@ -519,12 +729,16 @@
             piece,
             piece,
         ),
-        in_specs=[pl.BlockSpec(memory_space=pltpu.SMEM)] + [pl.BlockSpec()] * 10,
-        scratch_shapes=[pltpu.VMEM((rows, flat), F32)],
+        in_specs=[pl.BlockSpec(memory_space=pltpu.SMEM)]
+        + [pl.BlockSpec()] * 3
+        + [pl.BlockSpec(memory_space=pltpu.HBM)] * len(large),
+        scratch_shapes=[pltpu.VMEM((rows, flat), F32)]
+        + [pltpu.VMEM(array.shape, array.dtype) for array in large]
+        + [pltpu.SemaphoreType.DMA((len(large),))],
         cost_estimate=LONG,
-        compiler_params=vmem_limit(20 << 20),
+        compiler_params=vmem_limit(46 << 20),
         name="pool_front",
-    )(core, pixels, patch, embed, query, query_weight, key_weight, value_weight, value_bias, mask, out_weight)
+    )(core, query, value_bias, mask, *large)
 
 
 def pool_back(low, out_weight, value_flat, value_var, pix_low, probs, scores):
@@ -840,20 +1054,25 @@
             hidden = hidden + (mine + got) + output_bias[layer]
             unit_two, inverse_two = norm_parts(hidden)
             unit_other = links.other_rows(unit_two)
-            normed_two = jnp.concatenate([unit_two, unit_other], axis=0)
-            normed_two = (normed_two * norm_gain[layer, 1] + norm_bias[layer, 1]).astype(BF)
-            pre_act = matmul(normed_two, up_weight[layer]) + up_bias[layer]
-            activation = gelu_exact(pre_act).astype(BF)
+            activation, slope, part_own, part_send = feed_forward(
+                unit_two,
+                unit_other,
+                norm_gain,
+                norm_bias,
+                (layer, 1),
+                up_weight,
+                up_bias,
+                down_weight,
+            )
             marker = activation
             if layer < top:
-                mine, got = links.begin_product(activation, down_weight[layer])
+                mine, got = links.begin_sum(part_own, part_send)
                 marker = mine
             normed_two = norm_rows(
                 after(unit_two, marker), unit_other, norm_gain[layer, 1], norm_bias[layer, 1], shards
             )
             if layer < top:
                 if layer == 0:
-                    top_grad = matmul_nt(after(down_low, mine), down_weight[top])
                     embed_high, embed_rest = two_part(variable_embed)
                     embed_all = jnp.concatenate([patch_flat, embed_high, embed_rest], axis=0)
                     mine, embed_all = lax.optimization_barrier((mine, embed_all))
@@ -863,19 +1082,24 @@
                         [
                             pool_value_weight,
                             pool_query_weight,
-                            jnp.concatenate([key_high, key_high, key_rest], axis=0).T,
+                            jnp.concatenate(
+                                [key_high, key_high, key_rest, jnp.zeros_like(key_high)], axis=0
+                            ).T,
                         ],
                         axis=1,
                     )
-                    sides = left_side.reshape(dp, mp // 2, 2, shard // mp, left_side.shape[1])
-                    side_own, side_send = [
-                        pick(sides, which, 2)
-                        .transpose(1, 0, 2, 3)
-                        .reshape(model_width // 2, left_side.shape[1])
-                        for which in (links.mp_bit(0), 1 - links.mp_bit(0))
+                    sides = left_side.reshape(dp, mp, shard // mp, left_side.shape[1])
+                    mp_bits = range(bit_count(mp))
+                    masks = [
+                        sum((1 - ((i >> (len(mp_bits) - 1 - b)) & 1)) << b for b in mp_bits)
+                        for i in range(mp)
                     ]
-                    mine, top_grad, embed_left, side_own, side_send = lax.optimization_barrier(
-                        (mine, top_grad, embed_left, side_own, side_send)
+                    sides = jnp.stack(
+                        [pick(sides, links.mp_index ^ mask, 1) for mask in masks]
+                    ).reshape(2, model_width // 2, left_side.shape[1])
+                    side_send, side_own = sides[0], sides[1]
+                    mine, embed_left, side_own, side_send = lax.optimization_barrier(
+                        (mine, embed_left, side_own, side_send)
                     )
                 mine, normed_two = lax.optimization_barrier((mine, normed_two))
                 hidden = hidden + (mine + got) + down_bias[layer]
@@ -890,12 +1114,12 @@
                     unit_two,
                     inverse_two,
                     normed_two,
-                    pre_act,
+                    slope,
                     activation,
                 )
             )
 
-        activation_top = kept[top][-1]
+        last_own, last_send = part_own, part_send
         row_sums = {}
         local_sums = {}
         merges = {}
@@ -922,31 +1146,38 @@
                 unit_two,
                 inverse_two,
                 normed_two,
-                pre_act,
+                slope,
                 activation,
             ) = kept[layer]
             merges["down", depth] = Merge(
                 links, [(down_left, activation)], bits if depth else bits_late
             )
-            grad_activation = top_grad if layer == top else matmul_nt(down_low, down_weight[layer])
-            grad_pre = jax.vjp(gelu_exact, pre_act)[1](grad_activation)[0]
-            local_sums["up_bias", layer] = jnp.sum(grad_pre, axis=0)
-            pre_low = clock.one(grad_pre.astype(BF))
+            advance(("top", depth))
+            pre_low, up_sums, part_own, part_send = feed_back(
+                clock.one(down_low), slope, down_weight, up_weight, layer
+            )
+            local_sums["up_bias", layer] = up_sums[0]
+            pre_low, part_send = clock.both(pre_low, part_send)
             merges["up", depth] = Merge(links, [(normed_two, pre_low)], bits)
             advance(("pre", depth))
-            pre_low = clock.one(pre_low)
-            half = row_count // 2
-            mine, got = links.ordered_sum(
-                clock,
-                lambda: matmul_nt(pre_low[:half], up_weight[layer]),
-                matmul_nt(pre_low[half:], up_weight[layer]),
-            )
+            mine, got = links.ordered_sum(clock, lambda: part_own, part_send)
             if not PLAN.get(("wait_two", depth)):
                 clock.hold()
             advance(("wait_two", depth))
+            if layer == top:
+                last_send = clock.one(last_send)
+                last_other = exchange(last_send, "mp", mp, 0)
+                clock.hold()
+                last_mine = clock.one(last_own + clock.one(last_other))
             mine, got = clock.both(mine, got)
+            if layer == top:
+                for bit in range(1, bit_count(mp)):
+                    last_mine = clock.one(last_mine)
+                    last_other = exchange(last_mine, "mp", mp, bit)
+                    if bit + 1 < bit_count(mp):
+                        last_mine = last_mine + last_other
             change, grad_own, sums = norm_back(
-                mine, got, unit_two, inverse_two, norm_gain[layer, 1], grad_own
+                mine, got, unit_two, inverse_two, norm_gain, (layer, 1), grad_own
             )
             change, sums = clock.both(change, sums)
             row_sums["gain", layer, 1] = sums[0]
@@ -968,9 +1199,14 @@
                 clock.hold()
             merges["att", depth] = Merge(links, [(out_left, mixed), (normed, grads)], bits)
             advance(("wait_one", depth))
+            if layer == top:
+                hidden = clock.one(hidden + (last_mine + clock.one(last_other)) + down_bias[top])
+                hidden_other = links.other_rows(hidden)
+                clock.hold()
+                layer_out = clock.one(links.global_rows(hidden, clock.one(hidden_other)))
             mine, got = clock.both(mine, got)
             change, grad_own, sums = norm_back(
-                mine, got, unit_one, inverse_one, norm_gain[layer, 0], grad_own
+                mine, got, unit_one, inverse_one, norm_gain, (layer, 0), grad_own
             )
             change, sums = clock.both(change, sums)
             row_sums["gain", layer, 0] = sums[0]
@@ -988,10 +1224,24 @@
 
         row_sums["column"] = sums[2]
         row_sums["lead"] = lead_scale * sums[2]
+        clock.hold()
         value_grad, key_grad, key_grad_var, pixel_own, pixel_send = pool_back(
             clock.one(down_low), pool_output_weight, value_flat, value_var, pix_low, pool_probs, score_rows
         )
-        value_grad = clock.one(value_grad)
+        flat_all = flat_count + var_count
+        item_scale = clock.cell[0, 0]
+        sub = shard // mp
+        embed_send, embed_own, summed_key, query_grad, pool_bias = embed_terms(
+            side_send,
+            side_own,
+            clock.one(value_grad),
+            key_grad,
+            key_grad_var,
+            clock.cell,
+            patch_flat,
+            variable_embed,
+            pool_key_weight,
+        )
         embed_all, embed_left = clock.both(embed_all, embed_left)
         value_low = value_grad.astype(BF)
         merges["tail"] = Merge(
@@ -1002,53 +1252,17 @@
             ],
             bits,
         )
-        advance("values")
-
-        flat_all = flat_count + var_count
-        item_scale = clock.cell[0, 0]
-        value_scaled = (clock.one(value_grad) * item_scale).astype(BF)
-        key_scaled = jnp.concatenate([key_grad, key_grad_var], axis=1) * item_scale
-        key_high, key_rest = two_part(key_scaled)
-        key_twice = jnp.concatenate([key_high, key_rest], axis=0)
-        summed_key = matmul(
-            jnp.concatenate([key_twice, key_twice[:, flat_count:]], axis=1), embed_all
-        )
-        summed_key = summed_key[:head_count] + summed_key[head_count:]
-        summed_high, summed_rest = two_part(summed_key)
-        query_grad = matmul(
-            jnp.concatenate([summed_high, summed_rest], axis=0), pool_key_weight
-        )
-        query_grad = query_grad[:head_count] + query_grad[head_count:]
-        query_grad = jnp.sum(jnp.where(head_pick.T, query_grad, 0.0), axis=0) / ROOT_DIM
-        query_high, query_rest = two_part(query_grad[None])
-        right_side = jnp.concatenate([key_high, key_rest, key_high], axis=0)
-        sub = shard // mp
-        core = links.mp_bit(0)
-
-        def embed_side(side):
-            block = matmul_nt(side[:, :local_width], value_scaled)
-            block = block + matmul(side[:, 2 * local_width :], right_side)
-            weight = side[:, local_width : 2 * local_width]
-            part = matmul_nt(weight, query_high) + matmul_nt(weight, query_rest)
-            block = jnp.concatenate([block, part], axis=1)
-            return block.reshape(mp // 2, dp, sub, flat_all + 1)
-
-        embed_send = clock.one(embed_side(side_send))
+        query_grad = query_grad[0]
+        embed_send = clock.one(embed_send)
         embed_got = exchange(embed_send, "mp", mp, 0)
         clock.hold()
-        embed_grad = embed_side(clock.one(side_own)) + clock.one(embed_got)
-        own = links.mp_bit(1)
+        embed_got = clock.one(embed_got)
         for bit in range(1, bit_count(mp)):
-            own = links.mp_bit(bit)
-            count = embed_grad.shape[0] // 2
-            pairs = embed_grad.reshape((count, 2) + embed_grad.shape[1:])
-            embed_keep = pick(pairs, own, 1)
-            embed_send = clock.one(pick(pairs, 1 - own, 1))
+            embed_send, embed_own = add_split(embed_own, embed_got)
+            embed_send = clock.one(embed_send)
             embed_got = exchange(embed_send, "mp", mp, bit)
-            if bit + 1 < bit_count(mp):
-                embed_grad = embed_keep + embed_got
-        clock.hold()
-        advance("embed")
+        advance("back")
+        lanes = embed_own.shape[1]
 
         names = []
         for layer in range(layer_count):
@@ -1062,8 +1276,7 @@
         full_sums = own_sums + clock.one(other_sums)
         local = jnp.stack([local_sums["up_bias", layer] for layer in range(layer_count)]) * item_scale
         thin = [local_sums["qv", layer] for layer in range(layer_count)]
-        pool_bias = jnp.sum(value_grad[flat_count:], axis=0, keepdims=True)
-        thin = jnp.concatenate(thin + [pool_bias], axis=0) * item_scale
+        thin = jnp.concatenate([jnp.concatenate(thin, axis=0) * item_scale, pool_bias], axis=0)
         packed = jnp.concatenate(
             [
                 full_sums.reshape(len(names), dp, shard).transpose(1, 0, 2).reshape(dp, -1),
@@ -1081,11 +1294,8 @@
         position = (grad_own * item_scale).reshape(row_count // 2, dp, shard).transpose(1, 0, 2)
         position, packed = clock.both(position, packed)
         advance("vectors")
-        embed_grad = (embed_keep + clock.one(embed_got)).reshape(dp, sub, flat_all + 1)
-        lane_blocks = -(-(flat_all + 1) // 128)
-        embed_grad = jnp.pad(
-            embed_grad, ((0, 0), (0, 0), (0, lane_blocks * 128 - flat_all - 1))
-        )
+        embed_grad = (embed_own + clock.one(embed_got)).reshape(dp, sub, lanes)
+        lane_blocks = lanes // 128
         if shard == 128:
             tall = jnp.concatenate(
                 [embed_grad[:, :, i * 128 : (i + 1) * 128] for i in range(lane_blocks)]
@@ -1102,30 +1312,17 @@
             )
         advance("small")
 
-        activation_top = clock.one(activation_top)
-        half = row_count // 2
-        last_mine, last_got = links.ordered_sum(
-            clock,
-            lambda: matmul(activation_top[:half], down_weight[top]),
-            matmul(activation_top[half:], down_weight[top]),
-        )
-        clock.hold()
-        advance("output")
         pixel_mine, pixel_got = links.ordered_sum(clock, lambda: pixel_own, pixel_send)
         clock.hold()
-        advance("pixels")
-        last_mine, last_got = clock.both(last_mine, last_got)
-        hidden = clock.one(hidden + (last_mine + last_got) + down_bias[top])
-        hidden_other = links.other_rows(hidden)
-        clock.hold()
-        layer_out = clock.one(links.global_rows(hidden, clock.one(hidden_other)))
-        advance("rows")
+        advance("values")
         pixel_mine, pixel_got = clock.both(pixel_mine, pixel_got)
         pixel_mine = clock.one(pixel_mine + pixel_got)
         pixel_other = links.other_rows(pixel_mine)
         clock.hold()
+        advance("pixels")
         pixel_grad = links.global_rows(pixel_mine, clock.one(pixel_other))
         pixel_grad = clock.one(pixel_grad.T.reshape(1, var_count, pix_count, row_count))
+        advance("rows")
         for name in DRAIN:
             if merges[name].open:
                 merges[name].advance(clock)
@@ -1135,7 +1332,9 @@
         finished = {}
         for kind in ("down", "up", "att"):
             parts = [merges[kind, top - layer].total for layer in range(layer_count)]
-            finished[kind] = finish_layers(kind, parts, layer_count, shard, local_width)
+            finished[kind] = finish_layers(
+                kind, parts, clock.cell, layer_count, shard, local_width
+            )
         tail_total = merges["tail"].total
         small = merges["small"].total[0]
         if shard == 128:

time: 602 us -> 568 us (0.944)
  matrix products: 41.5 us -> 0 us
  local copies, waits for them, and re-layouts: 102 us -> 80.7 us
  waiting for transfers between devices: 187 us -> 208 us
  Pallas kernels: 133 us -> 150 us
  between operations: 15.9 us -> 5.82 us
  starting transfers between devices: 56.4 us -> 49.7 us
    dot_general x22 -> x0, matrix products: 41.5 us -> none  [the longest x10 23.3 us: matmul(): return jnp.dot(left, right, preferred_element_type=F32)]
    pallas_call x0 -> x5, Pallas kernels: none -> 29.3 us  [the longest x2 14.5 us: feed_forward(): pl.pallas_call(kernel, out_shape=(jax.ShapeDtypeStruct((rows, hidden), BF...]
    ppermute x61, waiting for transfers between devices: 187 us -> 208 us  [exchange(): return lax.ppermute(tensor, axis, [(i, i ^ 1 << bit) for i in range(size)])]
    pallas_call x14, Pallas kernels: 50 us -> 37.7 us  [product_rows(): pl.pallas_call(kernel, out_shape=out_shape, grid=(count,), in_specs=in_sp...]
    unnamed x486 -> x398, local copies, waits for them, and re-layouts: 61 us -> 49 us
    ppermute x61, starting transfers between devices: 56.4 us -> 49.7 us  [exchange(): return lax.ppermute(tensor, axis, [(i, i ^ 1 << bit) for i in range(size)])]
    pallas_call x7 -> x8, Pallas kernels: 23.4 us -> 19.2 us  [add_split(): pl.pallas_call(kernel, out_shape=[jax.ShapeDtypeStruct((half, width), F32...]
    add x6 -> x5, other arithmetic: 12.9 us -> 10.5 us  [ordered_sum(): mine = clock.one(own() + clock.one(got))]
  transfers between devices with their start and end apart: 61 -> 61, of which waited for: 33 -> 38; matrix products, arithmetic and copies ran while one was open for 19% -> 14% of each run, Pallas kernels for 19% -> 19%
where the time goes in v5:
time: 568 us; the launch traced here: 557 us
  waiting for transfers between devices  208 us (37%)
  Pallas kernels  150 us (26%)
  local copies, waits for them, and re-layouts  80.7 us (14%)
  other arithmetic  62.2 us (11%)
  starting transfers between devices  49.7 us (9%)
  between operations  5.82 us (1%)
    ppermute x61, waiting for transfers between devices, exchange(): return lax.ppermute(tensor, axis, [(i, i ^ 1 << bit) for i in range(size)])  208 us
    ppermute x61, starting transfers between devices, exchange(): return lax.ppermute(tensor, axis, [(i, i ^ 1 << bit) for i in range(size)])  49.7 us
    unnamed x398, local copies, waits for them, and re-layouts  49 us
    pallas_call x14, Pallas kernels, product_rows(): pl.pallas_call(kernel, out_shape=out_shape, grid=(count,), in_specs=in_sp...  37.7 us
    pallas_call x8, Pallas kernels, add_split(): pl.pallas_call(kernel, out_shape=[jax.ShapeDtypeStruct((half, width), F32...  19.2 us
    pallas_call x2, Pallas kernels, feed_forward(): pl.pallas_call(kernel, out_shape=(jax.ShapeDtypeStruct((rows, hidden), BF...  14.5 us
    pallas_call x2, Pallas kernels, feed_back(): pl.pallas_call(kernel, out_shape=(jax.ShapeDtypeStruct((rows, hidden), BF...  12.1 us
  transfers between devices with their start and end apart: 61, of which 38 were waited for; matrix products, arithmetic and copies ran while one was open for 14% of the time, Pallas kernels for 19%

profile of v5, /device:TPU:0, one launch (start us, length us, event | category | flops | bytes accessed | tf_op | source)
XLA Modules:
  0.0 556.8 jit_solution(2340890947445397132)
XLA Ops:
  2.6 10.2 %pool_front.1 = (bf16[384,768]{1,0:T(8,128)(2,1)}, f32[1,256]{1,0:T(1,128)}, f32[4,1024]{1,0:T(4,128)}, f32[4,768]{1,0:T(4,128)}, bf16[768,256]{1,0:T(8,128)(2,1...) custom-call(s32[1]{0:T(128)} %bitcast.core_ref, ...), custom_call_target="tpu_custom_call" | custom-call | flops 999999995904 | bytes 8 | tf_op jit(solution)/shard_map/pool_front/pallas_call | solution.py:718
  16.8 2.9 collective-permute-start.4
  26.9 2.6 collective-permute-start.3
  31.4 6.1 %collective-permute-done.4 = f32[192,1024]{1,0:T(8,128)S(1)} collective-permute-done((f32[192,1024]{1,0:T(8,128)S(1)}, f32[192,1024]{1,0:T(8,128)S(1)}, u32[]{:S(2)}, u32[]{:S(2)}) %collective-permute-start.4) | collective-permute-done | bytes 786464 | tf_op jit(solution)/shard_map/ppermute | solution.py:60
  42.8 3.9 attend_forward.2
  62.3 11.8 %collective-permute-done.7 = f32[192,1024]{1,0:T(8,128)} collective-permute-done((f32[192,1024]{1,0:T(8,128)}, f32[192,1024]{1,0:T(8,128)}, u32[]{:S(2)}, u32[]{:S(2)}) %collective-permute-start.7) | collective-permute-done | bytes 786464 | tf_op jit(solution)/shard_map/ppermute | solution.py:60
  83.5 7.2 %feed_forward.2 = (bf16[384,1024]{1,0:T(8,128)(2,1)S(1)}, f32[384,1024]{1,0:T(8,128)S(1)}, f32[192,1024]{1,0:T(8,128)S(1)}, f32[192,1024]{1,0:T(8,128)}) custom-call(f32[192,1024]{1,0:T(8,128)S(1)} %subtract_multiply_fusion.2.own_ref.unit_ref, f32[192,1024]{1,0:T(8,128)} %collective-permute-done.8.other_ref, f32[2,2,1024]{2,1,0:T(2,128)S(1)} %copy-done.47, ...), custom_call_target="tpu_custom_call" | custom-call | flops 999999995904 | bytes 8 | tf_op jit(solution)/shard_map/feed_forward/pallas_call | solution.py:249
  103.9 3.5 gather_fusion
  107.4 3.0 copy_bitcast_fusion.refs_2_
  113.0 7.6 %collective-permute-done.10 = f32[192,1024]{1,0:T(8,128)} collective-permute-done((f32[192,1024]{1,0:T(8,128)}, f32[192,1024]{1,0:T(8,128)}, u32[]{:S(2)}, u32[]{:S(2)}) %collective-permute-start.10) | collective-permute-done | bytes 786464 | tf_op jit(solution)/shard_map/ppermute | solution.py:60
  124.9 3.1 attend_forward.3
  135.0 15.9 %collective-permute-done.13 = f32[192,1024]{1,0:T(8,128)S(1)} collective-permute-done((f32[192,1024]{1,0:T(8,128)S(1)}, f32[192,1024]{1,0:T(8,128)S(1)}, u32[]{:S(2)}, u32[]{:S(2)}) %collective-permute-start.13) | collective-permute-done | bytes 786464 | tf_op jit(solution)/shard_map/ppermute | solution.py:60
  160.0 7.4 %feed_forward.3 = (bf16[384,1024]{1,0:T(8,128)(2,1)S(1)}, f32[384,1024]{1,0:T(8,128)S(1)}, f32[192,1024]{1,0:T(8,128)S(1)}, f32[192,1024]{1,0:T(8,128)}) custom-call(f32[192,1024]{1,0:T(8,128)} %subtract_multiply_fusion.own_ref.unit_ref, f32[192,1024]{1,0:T(8,128)} %collective-permute-done.14.other_ref, f32[2,2,1024]{2,1,0:T(2,128)S(1)} %copy-done.47, ...), custom_call_target="tpu_custom_call" | custom-call | flops 999999995904 | bytes 8 | tf_op jit(solution)/shard_map/feed_forward/pallas_call | solution.py:249
  170.9 6.0 %feed_back.2 = (bf16[384,1024]{1,0:T(8,128)(2,1)S(1)}, f32[1,1024]{1,0:T(1,128)S(1)}, f32[192,1024]{1,0:T(8,128)S(1)}, f32[192,1024]{1,0:T(8,128)}) custom-call(bf16[384,1024]{1,0:T(8,128)(2,1)S(1)} %copy-done.81, f32[384,1024]{1,0:T(8,128)S(1)} %get-tuple-element.453.slope_ref, bf16[2,1024,1024]{2,1,0:T(8,128)(2,1)S(1)} %copy-done.54, ...), custom_call_target="tpu_custom_call" | custom-call | flops 999999995904 | bytes 8 | tf_op jit(solution)/shard_map/feed_back/pallas_call | solution.py:301
  191.7 15.5 %collective-permute-done.17.got_ref = f32[192,1024]{1,0:T(8,128)} collective-permute-done((f32[192,1024]{1,0:T(8,128)}, f32[192,1024]{1,0:T(8,128)}, u32[]{:S(2)}, u32[]{:S(2)}) %collective-permute-start.17) | collective-permute-done | bytes 786464 | tf_op jit(solution)/shard_map/ppermute | solution.py:60
  207.3 3.0 norm_back.4
  214.6 4.9 attend_back.2
  226.5 3.3 collective-permute-done.20.refs_2_
  229.8 3.3 product_rows.17
  233.1 3.3 product_rows.18
  249.1 10.1 %collective-permute-done.24.got_ref = f32[192,1024]{1,0:T(8,128)} collective-permute-done((f32[192,1024]{1,0:T(8,128)}, f32[192,1024]{1,0:T(8,128)}, u32[]{:S(2)}, u32[]{:S(2)}) %collective-permute-start.24) | collective-permute-done | bytes 786464 | tf_op jit(solution)/shard_map/ppermute | solution.py:60
  259.3 2.8 norm_back.5
  267.8 6.0 %feed_back.3 = (bf16[384,1024]{1,0:T(8,128)(2,1)S(1)}, f32[1,1024]{1,0:T(1,128)S(1)}, f32[192,1024]{1,0:T(8,128)S(1)}, f32[192,1024]{1,0:T(8,128)}) custom-call(bf16[384,1024]{1,0:T(8,128)(2,1)S(1)} %get-tuple-element.540.low_ref, f32[384,1024]{1,0:T(8,128)S(1)} %copy-done.73, bf16[2,1024,1024]{2,1,0:T(8,128)(2,1)S(1)} %copy-done.55, ...), custom_call_target="tpu_custom_call" | custom-call | flops 999999995904 | bytes 8 | tf_op jit(solution)/shard_map/feed_back/pallas_call | solution.py:301
  280.7 7.8 %collective-permute-done.28.got_ref = f32[256,1024]{1,0:T(8,128)} collective-permute-done((f32[256,1024]{1,0:T(8,128)}, f32[256,1024]{1,0:T(8,128)}, u32[]{:S(2)}, u32[]{:S(2)}) %collective-permute-start.28) | collective-permute-done | bytes 1048608 | tf_op jit(solution)/shard_map/ppermute | solution.py:60
  293.5 14.2 %collective-permute-done.27.got_ref = f32[192,1024]{1,0:T(8,128)} collective-permute-done((f32[192,1024]{1,0:T(8,128)}, f32[192,1024]{1,0:T(8,128)}, u32[]{:S(2)}, u32[]{:S(2)}) %collective-permute-start.27) | collective-permute-done | bytes 786464 | tf_op jit(solution)/shard_map/ppermute | solution.py:60
  307.8 2.8 norm_back.6
  318.1 3.4 product_rows.20
  321.6 4.9 attend_back.3
  336.5 16.4 %collective-permute-done.35.got_ref = f32[256,1024]{1,0:T(8,128)} collective-permute-done((f32[256,1024]{1,0:T(8,128)}, f32[256,1024]{1,0:T(8,128)}, u32[]{:S(2)}, u32[]{:S(2)}) %collective-permute-start.35) | collective-permute-done | bytes 1048608 | tf_op jit(solution)/shard_map/ppermute | solution.py:60
  355.9 3.3 product_rows.22
  360.4 2.8 collective-permute-start.42
  363.3 2.8 norm_back.7
  376.4 8.9 %pool_back.1 = (f32[816,256]{1,0:T(8,128)S(1)}, f32[4,768]{1,0:T(4,128)S(1)}, f32[4,48]{1,0:T(4,128)S(1)}, f32[192,768]{1,0:T(8,128)S(1)}, f32[192,768]{1,0:T(8,128)}) custom-call(bf16[384,1024]{1,0:T(8,128)(2,1)S(1)} %get-tuple-element.651.low_ref, bf16[256,1024]{1,0:T(8,128)(2,1)S(1)} %copy-done.60, bf16[768,256]{1,0:T(8,128)(2,1)S(1)} %copy-done.119, ...), custom_call_target="tpu_custom_call" | custom-call | flops 999999995904 | bytes 8 | tf_op jit(solution)/shard_map/pool_back/pallas_call | solution.py:785
  385.4 2.7 embed_terms.1
  398.7 3.9 add_split.11
  406.3 3.4 product_rows.24
  413.7 19.2 %collective-permute-done.40 = f32[256,896]{1,0:T(8,128)} collective-permute-done((f32[256,896]{1,0:T(8,128)}, f32[256,896]{1,0:T(8,128)}, u32[]{:S(2)}, u32[]{:S(2)}) %collective-permute-start.40) | collective-permute-done | bytes 917536 | tf_op jit(solution)/shard_map/ppermute | solution.py:60
  451.1 3.3 product_rows.26
  457.8 8.2 %collective-permute-done.46 = f32[192,768]{1,0:T(8,128)} collective-permute-done((f32[192,768]{1,0:T(8,128)}, f32[192,768]{1,0:T(8,128)}, u32[]{:S(2)}, u32[]{:S(2)}) %collective-permute-start.46) | collective-permute-done | bytes 589856 | tf_op jit(solution)/shard_map/ppermute | solution.py:60
  473.0 7.1 %collective-permute-done.53 = f32[128,1024]{1,0:T(8,128)} collective-permute-done((f32[128,1024]{1,0:T(8,128)}, f32[128,1024]{1,0:T(8,128)}, u32[]{:S(2)}, u32[]{:S(2)}) %collective-permute-start.53) | collective-permute-done | bytes 524320 | tf_op jit(solution)/shard_map/ppermute | solution.py:60
  481.3 2.8 collective-permute-done.52.refs_4_
  484.1 2.9 product_rows.27
  487.0 6.7 %collective-permute-done.51.got_ref = f32[256,1024]{1,0:T(8,128)} collective-permute-done((f32[256,1024]{1,0:T(8,128)}, f32[256,1024]{1,0:T(8,128)}, u32[]{:S(2)}, u32[]{:S(2)}) %collective-permute-start.51) | collective-permute-done | bytes 1048608 | tf_op jit(solution)/shard_map/ppermute | solution.py:60
  501.0 2.7 copy.78
  503.6 5.0 collective-permute-done.55
  511.4 9.2 %collective-permute-done.58 = f32[128,1024]{1,0:T(8,128)} collective-permute-done((f32[128,1024]{1,0:T(8,128)}, f32[128,1024]{1,0:T(8,128)}, u32[]{:S(2)}, u32[]{:S(2)}) %collective-permute-start.58) | collective-permute-done | bytes 524320 | tf_op jit(solution)/shard_map/ppermute | solution.py:60
  521.7 6.4 %collective-permute-done.57.got_ref = f32[256,512]{1,0:T(8,128)} collective-permute-done((f32[256,512]{1,0:T(8,128)}, f32[256,512]{1,0:T(8,128)}, u32[]{:S(2)}, u32[]{:S(2)}) %collective-permute-start.57) | collective-permute-done | bytes 524320 | tf_op jit(solution)/shard_map/ppermute | solution.py:60
  537.4 6.9 %collective-permute-done.59 = f32[128,512]{1,0:T(8,128)} collective-permute-done((f32[128,512]{1,0:T(8,128)}, f32[128,512]{1,0:T(8,128)}, u32[]{:S(2)}, u32[]{:S(2)}) %collective-permute-start.59) | collective-permute-done | bytes 262176 | tf_op jit(solution)/shard_map/ppermute | solution.py:60
  (674 shorter events, 250.1 us)
Async XLA Ops:
  12.9 2.6 collective-permute-start
  16.8 20.8 %collective-permute-start.4 = (f32[192,1024]{1,0:T(8,128)S(1)}, f32[192,1024]{1,0:T(8,128)S(1)}, u32[]{:S(2)}, u32[]{:S(2)}) collective-permute-start(f32[192,1024]{1,0:T(8,128)S(1)} %add.256), channel_id=1, source_target_pairs={{0,2},{1,3},{2,0},{3,1},{4,6},{5,7},{6,4},{7,5},{8,10},{9,11},{10,... | collective-permute-start | bytes 2359304 | tf_op jit(solution)/shard_map/ppermute | solution.py:60
  19.7 3.6 collective-permute-start.1
  23.3 3.6 collective-permute-start.2
  26.9 4.5 collective-permute-start.3
  49.0 2.6 collective-permute-start.6
  54.1 19.9 %collective-permute-start.7 = (f32[192,1024]{1,0:T(8,128)}, f32[192,1024]{1,0:T(8,128)}, u32[]{:S(2)}, u32[]{:S(2)}) collective-permute-start(f32[192,1024]{1,0:T(8,128)} %add.270), channel_id=1, source_target_pairs={{0,2},{1,3},{2,0},{3,1},{4,6},{5,7},{6,4},{7,5},{8,10},{9,11},{10,... | collective-permute-start | bytes 2359304 | tf_op jit(solution)/shard_map/ppermute | solution.py:60
  93.6 4.7 collective-permute-start.9
  100.4 20.1 %collective-permute-start.10 = (f32[192,1024]{1,0:T(8,128)}, f32[192,1024]{1,0:T(8,128)}, u32[]{:S(2)}, u32[]{:S(2)}) collective-permute-start(f32[192,1024]{1,0:T(8,128)} %add.278), channel_id=1, source_target_pairs={{0,2},{1,3},{2,0},{3,1},{4,6},{5,7},{6,4},{7,5},{8,10},{9,11},{10,... | collective-permute-start | bytes 2359304 | tf_op jit(solution)/shard_map/ppermute | solution.py:60
  131.2 19.6 %collective-permute-start.13 = (f32[192,1024]{1,0:T(8,128)S(1)}, f32[192,1024]{1,0:T(8,128)S(1)}, u32[]{:S(2)}, u32[]{:S(2)}) collective-permute-start(f32[192,1024]{1,0:T(8,128)S(1)} %add.290), channel_id=1, source_target_pairs={{0,2},{1,3},{2,0},{3,1},{4,6},{5,7},{6,4},{7,5},{8,10},{9,11},{10,... | collective-permute-start | bytes 2359304 | tf_op jit(solution)/shard_map/ppermute | solution.py:60
  181.2 3.6 collective-permute-start.15
  181.4 48.3 %collective-permute-start.20 = (f32[512,1024]{1,0:T(8,128)}, f32[512,1024]{1,0:T(8,128)}, u32[]{:S(2)}, u32[]{:S(2)}) collective-permute-start(f32[512,1024]{1,0:T(8,128)} %product_rows.14), channel_id=1, source_target_pairs={{0,8},{4,12},{8,0},{12,4},{16,24},{20,28},{24,16},{28,20},{1,9},{5... | collective-permute-start | bytes 6291464 | tf_op jit(solution)/shard_map/ppermute | solution.py:60
  183.3 49.8 %collective-permute-start.19 = (f32[512,1024]{1,0:T(8,128)}, f32[512,1024]{1,0:T(8,128)}, u32[]{:S(2)}, u32[]{:S(2)}) collective-permute-start(f32[512,1024]{1,0:T(8,128)} %product_rows.15), channel_id=1, source_target_pairs={{0,4},{4,0},{8,12},{12,8},{16,20},{20,16},{24,28},{28,24},{1,5},{5... | collective-permute-start | bytes 6291464 | tf_op jit(solution)/shard_map/ppermute | solution.py:60
  187.0 2.6 collective-permute-start.16
  187.0 20.3 %collective-permute-start.17 = (f32[192,1024]{1,0:T(8,128)}, f32[192,1024]{1,0:T(8,128)}, u32[]{:S(2)}, u32[]{:S(2)}) collective-permute-start(f32[192,1024]{1,0:T(8,128)} %add.297.mine_ref), channel_id=1, source_target_pairs={{0,2},{1,3},{2,0},{3,1},{4,6},{5,7},{6,4},{7,5},{8,10},{9,11},{10,... | collective-permute-start | bytes 2359304 | tf_op jit(solution)/shard_map/ppermute | solution.py:60
  210.4 26.0 %collective-permute-start.18 = (f32[192,1024]{1,0:T(8,128)}, f32[192,1024]{1,0:T(8,128)}, u32[]{:S(2)}, u32[]{:S(2)}) collective-permute-start(f32[192,1024]{1,0:T(8,128)} %add.298), channel_id=1, source_target_pairs={{0,2},{1,3},{2,0},{3,1},{4,6},{5,7},{6,4},{7,5},{8,10},{9,11},{10,... | collective-permute-start | bytes 2359304 | tf_op jit(solution)/shard_map/ppermute | solution.py:60
  238.9 7.3 %collective-permute-start.23 = (f32[192,1024]{1,0:T(8,128)}, f32[192,1024]{1,0:T(8,128)}, u32[]{:S(2)}, u32[]{:S(2)}) collective-permute-start(f32[192,1024]{1,0:T(8,128)} %add_add_fusion), channel_id=1, source_target_pairs={{0,1},{1,0},{2,3},{3,2},{4,5},{5,4},{6,7},{7,6},{8,9},{9,8},{10,11... | collective-permute-start | bytes 2359304 | tf_op jit(solution)/shard_map/ppermute | solution.py:60
  238.9 20.3 %collective-permute-start.24 = (f32[192,1024]{1,0:T(8,128)}, f32[192,1024]{1,0:T(8,128)}, u32[]{:S(2)}, u32[]{:S(2)}) collective-permute-start(f32[192,1024]{1,0:T(8,128)} %add.299.mine_ref), channel_id=1, source_target_pairs={{0,2},{1,3},{2,0},{3,1},{4,6},{5,7},{6,4},{7,5},{8,10},{9,11},{10,... | collective-permute-start | bytes 2359304 | tf_op jit(solution)/shard_map/ppermute | solution.py:60
  240.5 48.0 %collective-permute-start.28 = (f32[256,1024]{1,0:T(8,128)}, f32[256,1024]{1,0:T(8,128)}, u32[]{:S(2)}, u32[]{:S(2)}) collective-permute-start(f32[256,1024]{1,0:T(8,128)} %get-tuple-element.554), channel_id=1, source_target_pairs={{0,8},{4,12},{8,0},{12,4},{16,24},{20,28},{24,16},{28,20},{1,9},{5... | collective-permute-start | bytes 3145736 | tf_op jit(solution)/shard_map/ppermute | solution.py:60
  242.1 73.5 %collective-permute-start.31 = (f32[256,1024]{1,0:T(8,128)}, f32[256,1024]{1,0:T(8,128)}, u32[]{:S(2)}, u32[]{:S(2)}) collective-permute-start(f32[256,1024]{1,0:T(8,128)} %get-tuple-element.580), channel_id=1, source_target_pairs={{0,16},{4,20},{8,24},{12,28},{16,0},{20,4},{24,8},{28,12},{1,17},{... | collective-permute-start | bytes 3145736 | tf_op jit(solution)/shard_map/ppermute | solution.py:60
  244.7 73.3 %collective-permute-start.30 = (f32[512,1024]{1,0:T(8,128)}, f32[512,1024]{1,0:T(8,128)}, u32[]{:S(2)}, u32[]{:S(2)}) collective-permute-start(f32[512,1024]{1,0:T(8,128)} %product_rows.16), channel_id=1, source_target_pairs={{0,4},{4,0},{8,12},{12,8},{16,20},{20,16},{24,28},{28,24},{1,5},{5... | collective-permute-start | bytes 6291464 | tf_op jit(solution)/shard_map/ppermute | solution.py:60
  288.5 19.2 %collective-permute-start.27 = (f32[192,1024]{1,0:T(8,128)}, f32[192,1024]{1,0:T(8,128)}, u32[]{:S(2)}, u32[]{:S(2)}) collective-permute-start(f32[192,1024]{1,0:T(8,128)} %add.305.mine_ref), channel_id=1, source_target_pairs={{0,2},{1,3},{2,0},{3,1},{4,6},{5,7},{6,4},{7,5},{8,10},{9,11},{10,... | collective-permute-start | bytes 2359304 | tf_op jit(solution)/shard_map/ppermute | solution.py:60
  291.2 40.1 %collective-permute-start.36 = (f32[128,1024]{1,0:T(8,128)}, f32[128,1024]{1,0:T(8,128)}, u32[]{:S(2)}, u32[]{:S(2)}) collective-permute-start(f32[128,1024]{1,0:T(8,128)} %get-tuple-element.606), channel_id=1, source_target_pairs={{0,16},{4,20},{8,24},{12,28},{16,0},{20,4},{24,8},{28,12},{1,17},{... | collective-permute-start | bytes 1572872 | tf_op jit(solution)/shard_map/ppermute | solution.py:60
  292.0 63.9 %collective-permute-start.34 = (f32[512,1024]{1,0:T(8,128)}, f32[512,1024]{1,0:T(8,128)}, u32[]{:S(2)}, u32[]{:S(2)}) collective-permute-start(f32[512,1024]{1,0:T(8,128)} %product_rows.19), channel_id=1, source_target_pairs={{0,4},{4,0},{8,12},{12,8},{16,20},{20,16},{24,28},{28,24},{1,5},{5... | collective-permute-start | bytes 6291464 | tf_op jit(solution)/shard_map/ppermute | solution.py:60
  327.3 25.5 %collective-permute-start.35 = (f32[256,1024]{1,0:T(8,128)}, f32[256,1024]{1,0:T(8,128)}, u32[]{:S(2)}, u32[]{:S(2)}) collective-permute-start(f32[256,1024]{1,0:T(8,128)} %get-tuple-element.603), channel_id=1, source_target_pairs={{0,8},{4,12},{8,0},{12,4},{16,24},{20,28},{24,16},{28,20},{1,9},{5... | collective-permute-start | bytes 3145736 | tf_op jit(solution)/shard_map/ppermute | solution.py:60
  327.3 43.8 %collective-permute-start.38 = (f32[128,1024]{1,0:T(8,128)}, f32[128,1024]{1,0:T(8,128)}, u32[]{:S(2)}, u32[]{:S(2)}) collective-permute-start(f32[128,1024]{1,0:T(8,128)} %get-tuple-element.638), channel_id=1, source_target_pairs={{0,4},{4,0},{8,12},{12,8},{16,20},{20,16},{24,28},{28,24},{1,5},{5... | collective-permute-start | bytes 1572872 | tf_op jit(solution)/shard_map/ppermute | solution.py:60
  334.4 28.8 %collective-permute-start.33 = (f32[192,1024]{1,0:T(8,128)}, f32[192,1024]{1,0:T(8,128)}, u32[]{:S(2)}, u32[]{:S(2)}) collective-permute-start(f32[192,1024]{1,0:T(8,128)} %add.306.mine_ref), channel_id=1, source_target_pairs={{0,2},{1,3},{2,0},{3,1},{4,6},{5,7},{6,4},{7,5},{8,10},{9,11},{10,... | collective-permute-start | bytes 2359304 | tf_op jit(solution)/shard_map/ppermute | solution.py:60
  334.8 71.5 %collective-permute-start.41 = (f32[512,1024]{1,0:T(8,128)}, f32[512,1024]{1,0:T(8,128)}, u32[]{:S(2)}, u32[]{:S(2)}) collective-permute-start(f32[512,1024]{1,0:T(8,128)} %product_rows.21), channel_id=1, source_target_pairs={{0,4},{4,0},{8,12},{12,8},{16,20},{20,16},{24,28},{28,24},{1,5},{5... | collective-permute-start | bytes 6291464 | tf_op jit(solution)/shard_map/ppermute | solution.py:60
  360.1 42.5 %collective-permute-start.43 = (f32[256,1024]{1,0:T(8,128)}, f32[256,1024]{1,0:T(8,128)}, u32[]{:S(2)}, u32[]{:S(2)}) collective-permute-start(f32[256,1024]{1,0:T(8,128)} %get-tuple-element.686), channel_id=1, source_target_pairs={{0,8},{4,12},{8,0},{12,4},{16,24},{20,28},{24,16},{28,20},{1,9},{5... | collective-permute-start | bytes 3145736 | tf_op jit(solution)/shard_map/ppermute | solution.py:60
  360.4 44.5 %collective-permute-start.42 = (f32[128,1024]{1,0:T(8,128)}, f32[128,1024]{1,0:T(8,128)}, u32[]{:S(2)}, u32[]{:S(2)}) collective-permute-start(f32[128,1024]{1,0:T(8,128)} %get-tuple-element.684), channel_id=1, source_target_pairs={{0,16},{4,20},{8,24},{12,28},{16,0},{20,4},{24,8},{28,12},{1,17},{... | collective-permute-start | bytes 1572872 | tf_op jit(solution)/shard_map/ppermute | solution.py:60
  388.2 10.6 %collective-permute-start.39 = (f32[512,896]{1,0:T(8,128)}, f32[512,896]{1,0:T(8,128)}, u32[]{:S(2)}, u32[]{:S(2)}) collective-permute-start(f32[512,896]{1,0:T(8,128)} %get-tuple-element.671), channel_id=1, source_target_pairs={{0,1},{1,0},{2,3},{3,2},{4,5},{5,4},{6,7},{7,6},{8,9},{9,8},{10,11... | collective-permute-start | bytes 5505032 | tf_op jit(solution)/shard_map/ppermute | solution.py:60
  393.9 56.4 %collective-permute-start.47 = (f32[512,1024]{1,0:T(8,128)}, f32[512,1024]{1,0:T(8,128)}, u32[]{:S(2)}, u32[]{:S(2)}) collective-permute-start(f32[512,1024]{1,0:T(8,128)} %product_rows.23), channel_id=1, source_target_pairs={{0,4},{4,0},{8,12},{12,8},{16,20},{20,16},{24,28},{28,24},{1,5},{5... | collective-permute-start | bytes 6291464 | tf_op jit(solution)/shard_map/ppermute | solution.py:60
  409.8 2.9 collective-permute-start.44
  409.8 23.1 %collective-permute-start.40 = (f32[256,896]{1,0:T(8,128)}, f32[256,896]{1,0:T(8,128)}, u32[]{:S(2)}, u32[]{:S(2)}) collective-permute-start(f32[256,896]{1,0:T(8,128)} %get-tuple-element.677), channel_id=1, source_target_pairs={{0,2},{1,3},{2,0},{3,1},{4,6},{5,7},{6,4},{7,5},{8,10},{9,11},{10,... | collective-permute-start | bytes 2752520 | tf_op jit(solution)/shard_map/ppermute | solution.py:60
  410.7 36.2 %collective-permute-start.49 = (f32[128,1024]{1,0:T(8,128)}, f32[128,1024]{1,0:T(8,128)}, u32[]{:S(2)}, u32[]{:S(2)}) collective-permute-start(f32[128,1024]{1,0:T(8,128)} %get-tuple-element.727), channel_id=1, source_target_pairs={{0,16},{4,20},{8,24},{12,28},{16,0},{20,4},{24,8},{28,12},{1,17},{... | collective-permute-start | bytes 1572872 | tf_op jit(solution)/shard_map/ppermute | solution.py:60
  410.9 37.1 %collective-permute-start.48 = (f32[256,1024]{1,0:T(8,128)}, f32[256,1024]{1,0:T(8,128)}, u32[]{:S(2)}, u32[]{:S(2)}) collective-permute-start(f32[256,1024]{1,0:T(8,128)} %get-tuple-element.725), channel_id=1, source_target_pairs={{0,8},{4,12},{8,0},{12,4},{16,24},{20,28},{24,16},{28,20},{1,9},{5... | collective-permute-start | bytes 3145736 | tf_op jit(solution)/shard_map/ppermute | solution.py:60
  438.9 29.9 %collective-permute-start.54 = (f32[4,440,128]{2,1,0:T(8,128)}, f32[4,440,128]{2,1,0:T(8,128)}, u32[]{:S(2)}, u32[]{:S(2)}) collective-permute-start(f32[4,440,128]{2,1,0:T(8,128)} %bitcast.156), channel_id=1, source_target_pairs={{0,4},{4,0},{8,12},{12,8},{16,20},{20,16},{24,28},{28,24},{1,5},{5... | collective-permute-start | bytes 2703368 | tf_op jit(solution)/shard_map/ppermute | solution.py:60
  450.3 15.7 %collective-permute-start.46 = (f32[192,768]{1,0:T(8,128)}, f32[192,768]{1,0:T(8,128)}, u32[]{:S(2)}, u32[]{:S(2)}) collective-permute-start(f32[192,768]{1,0:T(8,128)} %add.313), channel_id=1, source_target_pairs={{0,2},{1,3},{2,0},{3,1},{4,6},{5,7},{6,4},{7,5},{8,10},{9,11},{10,... | collective-permute-start | bytes 1769480 | tf_op jit(solution)/shard_map/ppermute | solution.py:60
  454.4 25.6 %collective-permute-start.53 = (f32[128,1024]{1,0:T(8,128)}, f32[128,1024]{1,0:T(8,128)}, u32[]{:S(2)}, u32[]{:S(2)}) collective-permute-start(f32[128,1024]{1,0:T(8,128)} %get-tuple-element.754), channel_id=1, source_target_pairs={{0,16},{4,20},{8,24},{12,28},{16,0},{20,4},{24,8},{28,12},{1,17},{... | collective-permute-start | bytes 1572872 | tf_op jit(solution)/shard_map/ppermute | solution.py:60
  455.6 28.5 %collective-permute-start.52 = (f32[512,512]{1,0:T(8,128)}, f32[512,512]{1,0:T(8,128)}, u32[]{:S(2)}, u32[]{:S(2)}) collective-permute-start(f32[512,512]{1,0:T(8,128)} %product_rows.25), channel_id=1, source_target_pairs={{0,4},{4,0},{8,12},{12,8},{16,20},{20,16},{24,28},{28,24},{1,5},{5... | collective-permute-start | bytes 3145736 | tf_op jit(solution)/shard_map/ppermute | solution.py:60
  456.1 37.6 %collective-permute-start.51 = (f32[256,1024]{1,0:T(8,128)}, f32[256,1024]{1,0:T(8,128)}, u32[]{:S(2)}, u32[]{:S(2)}) collective-permute-start(f32[256,1024]{1,0:T(8,128)} %get-tuple-element.751), channel_id=1, source_target_pairs={{0,8},{4,12},{8,0},{12,4},{16,24},{20,28},{24,16},{28,20},{1,9},{5... | collective-permute-start | bytes 3145736 | tf_op jit(solution)/shard_map/ppermute | solution.py:60
  481.2 17.4 %collective-permute-start.50 = (f32[192,768]{1,0:T(8,128)}, f32[192,768]{1,0:T(8,128)}, u32[]{:S(2)}, u32[]{:S(2)}) collective-permute-start(f32[192,768]{1,0:T(8,128)} %add.315), channel_id=1, source_target_pairs={{0,1},{1,0},{2,3},{3,2},{4,5},{5,4},{6,7},{7,6},{8,9},{9,8},{10,11... | collective-permute-start | bytes 1769480 | tf_op jit(solution)/shard_map/ppermute | solution.py:60
  481.3 27.4 %collective-permute-start.55 = (f32[2,440,128]{2,1,0:T(8,128)}, f32[2,440,128]{2,1,0:T(8,128)}, u32[]{:S(2)}, u32[]{:S(2)}) collective-permute-start(f32[2,440,128]{2,1,0:T(8,128)} %dynamic-slice_bitcast_fusion), channel_id=1, source_target_pairs={{0,8},{4,12},{8,0},{12,4},{16,24},{20,28},{24,16},{28,20},{1,9},{5... | collective-permute-start | bytes 1351688 | tf_op jit(solution)/shard_map/ppermute | solution.py:60
  496.5 24.1 %collective-permute-start.58 = (f32[128,1024]{1,0:T(8,128)}, f32[128,1024]{1,0:T(8,128)}, u32[]{:S(2)}, u32[]{:S(2)}) collective-permute-start(f32[128,1024]{1,0:T(8,128)} %get-tuple-element.786), channel_id=1, source_target_pairs={{0,16},{4,20},{8,24},{12,28},{16,0},{20,4},{24,8},{28,12},{1,17},{... | collective-permute-start | bytes 1572872 | tf_op jit(solution)/shard_map/ppermute | solution.py:60
  496.5 31.6 %collective-permute-start.57 = (f32[256,512]{1,0:T(8,128)}, f32[256,512]{1,0:T(8,128)}, u32[]{:S(2)}, u32[]{:S(2)}) collective-permute-start(f32[256,512]{1,0:T(8,128)} %get-tuple-element.784), channel_id=1, source_target_pairs={{0,8},{4,12},{8,0},{12,4},{16,24},{20,28},{24,16},{28,20},{1,9},{5... | collective-permute-start | bytes 1572872 | tf_op jit(solution)/shard_map/ppermute | solution.py:60
  511.4 19.3 %collective-permute-start.56 = (f32[1,440,128]{2,1,0:T(8,128)}, f32[1,440,128]{2,1,0:T(8,128)}, u32[]{:S(2)}, u32[]{:S(2)}) collective-permute-start(f32[1,440,128]{2,1,0:T(8,128)} %constant_dynamic-slice_fusion), channel_id=1, source_target_pairs={{0,16},{4,20},{8,24},{12,28},{16,0},{20,4},{24,8},{28,12},{1,17},{... | collective-permute-start | bytes 675848 | tf_op jit(solution)/shard_map/ppermute | solution.py:60
  531.8 12.6 %collective-permute-start.59 = (f32[128,512]{1,0:T(8,128)}, f32[128,512]{1,0:T(8,128)}, u32[]{:S(2)}, u32[]{:S(2)}) collective-permute-start(f32[128,512]{1,0:T(8,128)} %get-tuple-element.799), channel_id=1, source_target_pairs={{0,16},{4,20},{8,24},{12,28},{16,0},{20,4},{24,8},{28,12},{1,17},{... | collective-permute-start | bytes 786440 | tf_op jit(solution)/shard_map/ppermute | solution.py:60
  546.4 8.8 %collective-permute-start.60 = (f32[192,128]{1,0:T(8,128)S(1)}, f32[192,128]{1,0:T(8,128)S(1)}, u32[]{:S(2)}, u32[]{:S(2)}) collective-permute-start(f32[192,128]{1,0:T(8,128)S(1)} %slice_bitcast_fusion.5), channel_id=1, source_target_pairs={{0,1},{1,0},{2,3},{3,2},{4,5},{5,4},{6,7},{7,6},{8,9},{9,8},{10,11... | collective-permute-start | bytes 294920 | tf_op jit(solution)/shard_map/ppermute | solution.py:60
  (201 other events, 1008.5 us)

commit v6 on v5

--- a/solution.py
+++ b/solution.py
@@ -138,6 +138,33 @@
         compiler_params=vmem_limit(16 * half * width),
         name="norm_rows",
     )(shards, own, other, gain[None], bias[None])
+
+
+def embed_columns(patch, embed, shards):
+    flat, width = patch.shape
+    var_count = embed.shape[0]
+    count = shards.shape[0]
+    shard = width // count
+    if shard % 128:
+        high, rest = two_part(embed)
+        return take_columns(jnp.concatenate([patch, high, rest], axis=0), shards, shard)
+
+    def kernel(shards_ref, patch_ref, embed_ref, out_ref):
+        for place in range(count):
+            column = pl.ds(pl.multiple_of(shards_ref[place] * shard, shard), shard)
+            target = slice(place * shard, (place + 1) * shard)
+            high, rest = two_part(embed_ref[:, column])
+            out_ref[:flat, target] = patch_ref[:, column]
+            out_ref[flat : flat + var_count, target] = high
+            out_ref[flat + var_count :, target] = rest
+
+    return pl.pallas_call(
+        kernel,
+        out_shape=jax.ShapeDtypeStruct((flat + 2 * var_count, width), BF),
+        in_specs=[pl.BlockSpec(memory_space=pltpu.SMEM)] + [pl.BlockSpec()] * 2,
+        compiler_params=vmem_limit(8 << 20),
+        name="embed_columns",
+    )(shards, patch, embed)
 
 
 def merge_rows(own, other, change, shards):
@@ -272,7 +299,7 @@
         ),
         scratch_shapes=[pltpu.VMEM((rows, width), BF)],
         cost_estimate=LONG,
-        compiler_params=vmem_limit(30 * rows * width),
+        compiler_params=vmem_limit(44 << 20),
         name="feed_forward",
     )(unit_own, unit_other, gains, biases, up_weight, up_bias, down_weight)
 
@@ -451,6 +478,26 @@
         compiler_params=vmem_limit(traffic + 2 * 4 * size * total * 4),
         name="product_rows",
     )(*operands)
+
+
+def add_rows(own, got):
+    rows, width = own.shape
+    size = rows // 2
+
+    def kernel(own_ref, got_ref, out_ref):
+        out_ref[...] = own_ref[...] + got_ref[...]
+
+    block = pl.BlockSpec((size, width), lambda j: (j, 0))
+    return pl.pallas_call(
+        kernel,
+        out_shape=jax.ShapeDtypeStruct((rows, width), F32),
+        grid=(rows // size,),
+        in_specs=[block, block],
+        out_specs=block,
+        cost_estimate=LONG,
+        compiler_params=vmem_limit(32 * size * width),
+        name="add_rows",
+    )(own, got)
 
 
 def add_split(keep, got):
@@ -814,14 +861,14 @@
         send = clock.one(send)
         got = exchange(send, "mp", self.mp, 0)
         clock.hold()
-        mine = clock.one(own() + clock.one(got))
+        mine = clock.one(add_rows(own(), clock.one(got)))
         last = bit_count(self.mp) - 1
         for bit in range(1, last):
             mine = clock.one(mine + exchange(mine, "mp", self.mp, bit))
         return mine, exchange(mine, "mp", self.mp, last)
 
     def begin_sum(self, own, send):
-        mine = own + exchange(send, "mp", self.mp, 0)
+        mine = add_rows(own, exchange(send, "mp", self.mp, 0))
         last = bit_count(self.mp) - 1
         for bit in range(1, last):
             mine = mine + exchange(mine, "mp", self.mp, bit)
@@ -1073,11 +1120,11 @@
             )
             if layer < top:
                 if layer == 0:
-                    embed_high, embed_rest = two_part(variable_embed)
-                    embed_all = jnp.concatenate([patch_flat, embed_high, embed_rest], axis=0)
-                    mine, embed_all = lax.optimization_barrier((mine, embed_all))
-                    embed_left = take_columns(embed_all, shards, shard)
-                    key_high, key_rest = two_part(key_rows)
+                    mine, embed_late, key_late = lax.optimization_barrier(
+                        (mine, variable_embed, key_rows)
+                    )
+                    embed_left = embed_columns(patch_flat, embed_late, shards)
+                    key_high, key_rest = two_part(key_late)
                     left_side = jnp.concatenate(
                         [
                             pool_value_weight,
@@ -1242,8 +1289,8 @@
             variable_embed,
             pool_key_weight,
         )
-        embed_all, embed_left = clock.both(embed_all, embed_left)
         value_low = value_grad.astype(BF)
+        query_late = clock.one(pool_query)
         merges["tail"] = Merge(
             links,
             [
@@ -1349,7 +1396,6 @@
             embed_grad = small[0, :size].reshape(sub, lane_blocks * 128)
             packed = small[0, size : size + packed_rows * 128]
             position = small[0, size + packed_rows * 128 :].reshape(row_count // 2, shard)
-        packed, position, _ = lax.optimization_barrier((packed, position, clock.cell))
         position = links.global_rows(position, links.other_rows(position))
         offset = 0
 
@@ -1375,7 +1421,7 @@
         thin_total = take(2 * layer_count + 1, local_width // dp)
         query_total = take(local_width)
 
-        query_low = pool_query.astype(BF)
+        query_low = query_late.astype(BF)
         query_rows = lax.dynamic_slice_in_dim(query_low, links.dp_index * shard, shard, 0)
         query_weight_grad = query_rows.astype(F32)[:, None] * query_total[None, :]
         key_weight_grad = (

time: 568 us -> 551 us (0.970)
  other arithmetic: 62.2 us -> 45.9 us
  Pallas kernels: 150 us -> 166 us
  local copies, waits for them, and re-layouts: 80.7 us -> 66.5 us
    add x9 -> x0, other arithmetic: 16.4 us -> none  [the longest x5 10.5 us: ordered_sum(): mine = clock.one(own() + clock.one(got))]
    pallas_call x0 -> x10, Pallas kernels: none -> 15.7 us  [the longest x9 14.8 us: add_rows(): pl.pallas_call(kernel, out_shape=jax.ShapeDtypeStruct((rows, width), F32)...]
    unnamed x398 -> x434, local copies, waits for them, and re-layouts: 49 us -> 40 us
  transfers between devices with their start and end apart: 61 -> 61, of which waited for: 38 -> 39; matrix products, arithmetic and copies ran while one was open for 14% -> 11% of each run, Pallas kernels for 19% -> 21%
where the time goes in v6:
time: 551 us; the launch traced here: 544 us
  waiting for transfers between devices  210 us (38%)
  Pallas kernels  166 us (30%)
  local copies, waits for them, and re-layouts  66.5 us (12%)
  starting transfers between devices  50.1 us (9%)
  other arithmetic  45.9 us (8%)
  between operations  5.66 us (1%)
    ppermute x61, waiting for transfers between devices, exchange(): return lax.ppermute(tensor, axis, [(i, i ^ 1 << bit) for i in range(size)])  210 us
    ppermute x61, starting transfers between devices, exchange(): return lax.ppermute(tensor, axis, [(i, i ^ 1 << bit) for i in range(size)])  50.1 us
    unnamed x434, local copies, waits for them, and re-layouts  40 us
    pallas_call x14, Pallas kernels, product_rows(): pl.pallas_call(kernel, out_shape=out_shape, grid=(count,), in_specs=in_sp...  37.5 us
    pallas_call x8, Pallas kernels, add_split(): pl.pallas_call(kernel, out_shape=[jax.ShapeDtypeStruct((half, width), F32...  19.2 us
    pallas_call x2, Pallas kernels, feed_forward(): pl.pallas_call(kernel, out_shape=(jax.ShapeDtypeStruct((rows, hidden), BF...  15.2 us
    pallas_call x9, Pallas kernels, add_rows(): pl.pallas_call(kernel, out_shape=jax.ShapeDtypeStruct((rows, width), F32)...  14.8 us
    pallas_call x2, Pallas kernels, feed_back(): pl.pallas_call(kernel, out_shape=(jax.ShapeDtypeStruct((rows, hidden), BF...  12.1 us
  transfers between devices with their start and end apart: 61, of which 39 were waited for; matrix products, arithmetic and copies ran while one was open for 11% of the time, Pallas kernels for 21%

profile of v6, /device:TPU:0, one launch (start us, length us, event | category | flops | bytes accessed | tf_op | source)
XLA Modules:
  0.0 543.8 jit_solution(17425396909810393064)
XLA Ops:
  2.6 10.2 %pool_front.1 = (bf16[384,768]{1,0:T(8,128)(2,1)}, f32[1,256]{1,0:T(1,128)}, f32[4,1024]{1,0:T(4,128)}, f32[4,768]{1,0:T(4,128)}, bf16[768,256]{1,0:T(8,128)(2,1...) custom-call(s32[1]{0:T(128)} %bitcast.core_ref, ...), custom_call_target="tpu_custom_call" | custom-call | flops 999999995904 | bytes 8 | tf_op jit(solution)/shard_map/pool_front/pallas_call | solution.py:765
  16.9 2.9 collective-permute-start.4
  27.1 2.6 collective-permute-start.3
  31.6 6.1 %collective-permute-done.4 = f32[192,1024]{1,0:T(8,128)S(1)} collective-permute-done((f32[192,1024]{1,0:T(8,128)S(1)}, f32[192,1024]{1,0:T(8,128)S(1)}, u32[]{:S(2)}, u32[]{:S(2)}) %collective-permute-start.4) | collective-permute-done | bytes 786464 | tf_op jit(solution)/shard_map/ppermute | solution.py:60
  42.7 3.9 attend_forward.2
  59.5 12.6 %collective-permute-done.7 = f32[192,1024]{1,0:T(8,128)} collective-permute-done((f32[192,1024]{1,0:T(8,128)}, f32[192,1024]{1,0:T(8,128)}, u32[]{:S(2)}, u32[]{:S(2)}) %collective-permute-start.7) | collective-permute-done | bytes 786464 | tf_op jit(solution)/shard_map/ppermute | solution.py:60
  77.9 7.5 %feed_forward.2 = (bf16[384,1024]{1,0:T(8,128)(2,1)}, f32[384,1024]{1,0:T(8,128)}, f32[192,1024]{1,0:T(8,128)}, f32[192,1024]{1,0:T(8,128)}) custom-call(f32[192,1024]{1,0:T(8,128)} %copy-done.7, f32[192,1024]{1,0:T(8,128)} %copy-done.35, f32[2,2,1024]{2,1,0:T(2,128)} %gain_ref.11, f32[2,2,1024]{2,1,0:T(2,128)} %bias_ref.3, bf16[2,1024,1024]{2,1,0:T(8,128)(2,1)} %up_ref.7, ...), custom_call_target="tpu_custom_call" | custom-call | flops 999999995904 | bytes 8 | tf_op jit(solution)/shard_map/feed_forward/pallas_call | solution.py:276
  102.0 9.5 %collective-permute-done.10 = f32[192,1024]{1,0:T(8,128)} collective-permute-done((f32[192,1024]{1,0:T(8,128)}, f32[192,1024]{1,0:T(8,128)}, u32[]{:S(2)}, u32[]{:S(2)}) %collective-permute-start.10) | collective-permute-done | bytes 786464 | tf_op jit(solution)/shard_map/ppermute | solution.py:60
  115.8 3.1 attend_forward.3
  124.4 16.8 %collective-permute-done.13 = f32[192,1024]{1,0:T(8,128)S(1)} collective-permute-done((f32[192,1024]{1,0:T(8,128)S(1)}, f32[192,1024]{1,0:T(8,128)S(1)}, u32[]{:S(2)}, u32[]{:S(2)}) %collective-permute-start.13) | collective-permute-done | bytes 786464 | tf_op jit(solution)/shard_map/ppermute | solution.py:60
  144.9 7.6 %feed_forward.3 = (bf16[384,1024]{1,0:T(8,128)(2,1)}, f32[384,1024]{1,0:T(8,128)}, f32[192,1024]{1,0:T(8,128)}, f32[192,1024]{1,0:T(8,128)}) custom-call(f32[192,1024]{1,0:T(8,128)} %copy-done.10, f32[192,1024]{1,0:T(8,128)} %collective-permute-done.14.other_ref, f32[2,2,1024]{2,1,0:T(2,128)} %gain_ref.11, f32[2,2,1024]{2,1,0:T(2,128)} %bias_ref.3, ...), custom_call_target="tpu_custom_call" | custom-call | flops 999999995904 | bytes 8 | tf_op jit(solution)/shard_map/feed_forward/pallas_call | solution.py:276
  158.5 6.0 %feed_back.2 = (bf16[384,1024]{1,0:T(8,128)(2,1)S(1)}, f32[1,1024]{1,0:T(1,128)S(1)}, f32[192,1024]{1,0:T(8,128)S(1)}, f32[192,1024]{1,0:T(8,128)}) custom-call(bf16[384,1024]{1,0:T(8,128)(2,1)S(1)} %copy-done.91, f32[384,1024]{1,0:T(8,128)S(1)} %copy-done.83, bf16[2,1024,1024]{2,1,0:T(8,128)(2,1)S(1)} %copy-done.65, bf16[2,1024,1024]{2,1,0:T(8,128)(2,1)S(1)} %copy-done.64), custom_call_target="tpu_custom_call" | custom-call | flops 999999995904 | bytes 8 | tf_op jit(solution)/shard_map/feed_back/pallas_call | solution.py:328
  179.2 15.5 %collective-permute-done.17.got_ref = f32[192,1024]{1,0:T(8,128)} collective-permute-done((f32[192,1024]{1,0:T(8,128)}, f32[192,1024]{1,0:T(8,128)}, u32[]{:S(2)}, u32[]{:S(2)}) %collective-permute-start.17) | collective-permute-done | bytes 786464 | tf_op jit(solution)/shard_map/ppermute | solution.py:60
  194.8 2.8 norm_back.4
  201.9 4.9 attend_back.2
  206.9 2.5 collective-permute-done.22.got_ref
  213.6 3.4 collective-permute-done.20.refs_2_
  216.9 3.3 product_rows.17
  220.3 3.3 product_rows.18
  223.6 2.5 add_add_fusion
  229.3 2.6 collective-permute-start.31
  236.4 10.0 %collective-permute-done.24.got_ref = f32[192,1024]{1,0:T(8,128)} collective-permute-done((f32[192,1024]{1,0:T(8,128)}, f32[192,1024]{1,0:T(8,128)}, u32[]{:S(2)}, u32[]{:S(2)}) %collective-permute-start.24) | collective-permute-done | bytes 786464 | tf_op jit(solution)/shard_map/ppermute | solution.py:60
  246.5 2.8 norm_back.5
  255.1 6.1 %feed_back.3 = (bf16[384,1024]{1,0:T(8,128)(2,1)S(1)}, f32[1,1024]{1,0:T(1,128)S(1)}, f32[192,1024]{1,0:T(8,128)S(1)}, f32[192,1024]{1,0:T(8,128)}) custom-call(bf16[384,1024]{1,0:T(8,128)(2,1)S(1)} %get-tuple-element.540.low_ref, f32[384,1024]{1,0:T(8,128)S(1)} %copy-done.82, bf16[2,1024,1024]{2,1,0:T(8,128)(2,1)S(1)} %copy-done.66, ...), custom_call_target="tpu_custom_call" | custom-call | flops 999999995904 | bytes 8 | tf_op jit(solution)/shard_map/feed_back/pallas_call | solution.py:328
  267.8 7.9 %collective-permute-done.28.got_ref = f32[256,1024]{1,0:T(8,128)} collective-permute-done((f32[256,1024]{1,0:T(8,128)}, f32[256,1024]{1,0:T(8,128)}, u32[]{:S(2)}, u32[]{:S(2)}) %collective-permute-start.28) | collective-permute-done | bytes 1048608 | tf_op jit(solution)/shard_map/ppermute | solution.py:60
  280.8 14.1 %collective-permute-done.27.got_ref = f32[192,1024]{1,0:T(8,128)} collective-permute-done((f32[192,1024]{1,0:T(8,128)}, f32[192,1024]{1,0:T(8,128)}, u32[]{:S(2)}, u32[]{:S(2)}) %collective-permute-start.27) | collective-permute-done | bytes 786464 | tf_op jit(solution)/shard_map/ppermute | solution.py:60
  295.0 2.8 norm_back.6
  306.1 3.4 product_rows.20
  309.6 4.9 attend_back.3
  324.3 16.5 %collective-permute-done.35.got_ref = f32[256,1024]{1,0:T(8,128)} collective-permute-done((f32[256,1024]{1,0:T(8,128)}, f32[256,1024]{1,0:T(8,128)}, u32[]{:S(2)}, u32[]{:S(2)}) %collective-permute-start.35) | collective-permute-done | bytes 1048608 | tf_op jit(solution)/shard_map/ppermute | solution.py:60
  343.1 3.5 product_rows.22
  347.8 2.8 collective-permute-start.42
  350.7 2.8 norm_back.7
  365.6 8.9 %pool_back.1 = (f32[816,256]{1,0:T(8,128)S(1)}, f32[4,768]{1,0:T(4,128)S(1)}, f32[4,48]{1,0:T(4,128)S(1)}, f32[192,768]{1,0:T(8,128)S(1)}, f32[192,768]{1,0:T(8,128)}) custom-call(bf16[384,1024]{1,0:T(8,128)(2,1)S(1)} %get-tuple-element.651.low_ref, bf16[256,1024]{1,0:T(8,128)(2,1)S(1)} %copy-done.71, bf16[768,256]{1,0:T(8,128)(2,1)S(1)} %copy-done.133, ...), custom_call_target="tpu_custom_call" | custom-call | flops 999999995904 | bytes 8 | tf_op jit(solution)/shard_map/pool_back/pallas_call | solution.py:832
  374.5 2.8 embed_terms.1
  388.5 3.9 add_split.11
  395.8 3.4 product_rows.24
  403.2 19.2 %collective-permute-done.40 = f32[256,896]{1,0:T(8,128)} collective-permute-done((f32[256,896]{1,0:T(8,128)}, f32[256,896]{1,0:T(8,128)}, u32[]{:S(2)}, u32[]{:S(2)}) %collective-permute-start.40) | collective-permute-done | bytes 917536 | tf_op jit(solution)/shard_map/ppermute | solution.py:60
  440.7 3.3 product_rows.26
  447.3 8.1 %collective-permute-done.46 = f32[192,768]{1,0:T(8,128)} collective-permute-done((f32[192,768]{1,0:T(8,128)}, f32[192,768]{1,0:T(8,128)}, u32[]{:S(2)}, u32[]{:S(2)}) %collective-permute-start.46) | collective-permute-done | bytes 589856 | tf_op jit(solution)/shard_map/ppermute | solution.py:60
  462.8 6.8 %collective-permute-done.53 = f32[128,1024]{1,0:T(8,128)} collective-permute-done((f32[128,1024]{1,0:T(8,128)}, f32[128,1024]{1,0:T(8,128)}, u32[]{:S(2)}, u32[]{:S(2)}) %collective-permute-start.53) | collective-permute-done | bytes 524320 | tf_op jit(solution)/shard_map/ppermute | solution.py:60
  470.8 2.8 collective-permute-done.52.refs_4_
  473.7 2.9 product_rows.27
  476.6 6.6 %collective-permute-done.51.got_ref = f32[256,1024]{1,0:T(8,128)} collective-permute-done((f32[256,1024]{1,0:T(8,128)}, f32[256,1024]{1,0:T(8,128)}, u32[]{:S(2)}, u32[]{:S(2)}) %collective-permute-start.51) | collective-permute-done | bytes 1048608 | tf_op jit(solution)/shard_map/ppermute | solution.py:60
  489.8 2.7 copy.79
  492.5 6.5 %collective-permute-done.55 = f32[2,440,128]{2,1,0:T(8,128)} collective-permute-done((f32[2,440,128]{2,1,0:T(8,128)}, f32[2,440,128]{2,1,0:T(8,128)}, u32[]{:S(2)}, u32[]{:S(2)}) %collective-permute-start.55) | collective-permute-done | bytes 450592 | tf_op jit(solution)/shard_map/ppermute | solution.py:60
  501.1 8.3 %collective-permute-done.58 = f32[128,1024]{1,0:T(8,128)} collective-permute-done((f32[128,1024]{1,0:T(8,128)}, f32[128,1024]{1,0:T(8,128)}, u32[]{:S(2)}, u32[]{:S(2)}) %collective-permute-start.58) | collective-permute-done | bytes 524320 | tf_op jit(solution)/shard_map/ppermute | solution.py:60
  510.5 7.2 %collective-permute-done.57.got_ref = f32[256,512]{1,0:T(8,128)} collective-permute-done((f32[256,512]{1,0:T(8,128)}, f32[256,512]{1,0:T(8,128)}, u32[]{:S(2)}, u32[]{:S(2)}) %collective-permute-start.57) | collective-permute-done | bytes 524320 | tf_op jit(solution)/shard_map/ppermute | solution.py:60
  (707 shorter events, 237.7 us)
Async XLA Ops:
  12.8 2.6 collective-permute-start
  16.9 20.8 %collective-permute-start.4 = (f32[192,1024]{1,0:T(8,128)S(1)}, f32[192,1024]{1,0:T(8,128)S(1)}, u32[]{:S(2)}, u32[]{:S(2)}) collective-permute-start(f32[192,1024]{1,0:T(8,128)S(1)} %add_rows.9), channel_id=1, source_target_pairs={{0,2},{1,3},{2,0},{3,1},{4,6},{5,7},{6,4},{7,5},{8,10},{9,11},{10,... | collective-permute-start | bytes 2359304 | tf_op jit(solution)/shard_map/ppermute | solution.py:60
  19.9 3.6 collective-permute-start.1
  23.5 3.6 collective-permute-start.2
  27.1 4.5 collective-permute-start.3
  52.1 19.9 %collective-permute-start.7 = (f32[192,1024]{1,0:T(8,128)}, f32[192,1024]{1,0:T(8,128)}, u32[]{:S(2)}, u32[]{:S(2)}) collective-permute-start(f32[192,1024]{1,0:T(8,128)} %add_rows.10), channel_id=1, source_target_pairs={{0,2},{1,3},{2,0},{3,1},{4,6},{5,7},{6,4},{7,5},{8,10},{9,11},{10,... | collective-permute-start | bytes 2359304 | tf_op jit(solution)/shard_map/ppermute | solution.py:60
  85.5 2.7 collective-permute-start.9
  91.5 20.0 %collective-permute-start.10 = (f32[192,1024]{1,0:T(8,128)}, f32[192,1024]{1,0:T(8,128)}, u32[]{:S(2)}, u32[]{:S(2)}) collective-permute-start(f32[192,1024]{1,0:T(8,128)} %add_rows.11), channel_id=1, source_target_pairs={{0,2},{1,3},{2,0},{3,1},{4,6},{5,7},{6,4},{7,5},{8,10},{9,11},{10,... | collective-permute-start | bytes 2359304 | tf_op jit(solution)/shard_map/ppermute | solution.py:60
  121.5 19.6 %collective-permute-start.13 = (f32[192,1024]{1,0:T(8,128)S(1)}, f32[192,1024]{1,0:T(8,128)S(1)}, u32[]{:S(2)}, u32[]{:S(2)}) collective-permute-start(f32[192,1024]{1,0:T(8,128)S(1)} %add_rows.12), channel_id=1, source_target_pairs={{0,2},{1,3},{2,0},{3,1},{4,6},{5,7},{6,4},{7,5},{8,10},{9,11},{10,... | collective-permute-start | bytes 2359304 | tf_op jit(solution)/shard_map/ppermute | solution.py:60
  168.5 3.5 collective-permute-start.15
  168.6 48.3 %collective-permute-start.20 = (f32[512,1024]{1,0:T(8,128)}, f32[512,1024]{1,0:T(8,128)}, u32[]{:S(2)}, u32[]{:S(2)}) collective-permute-start(f32[512,1024]{1,0:T(8,128)} %product_rows.14), channel_id=1, source_target_pairs={{0,8},{4,12},{8,0},{12,4},{16,24},{20,28},{24,16},{28,20},{1,9},{5... | collective-permute-start | bytes 6291464 | tf_op jit(solution)/shard_map/ppermute | solution.py:60
  170.5 49.8 %collective-permute-start.19 = (f32[512,1024]{1,0:T(8,128)}, f32[512,1024]{1,0:T(8,128)}, u32[]{:S(2)}, u32[]{:S(2)}) collective-permute-start(f32[512,1024]{1,0:T(8,128)} %product_rows.15), channel_id=1, source_target_pairs={{0,4},{4,0},{8,12},{12,8},{16,20},{20,16},{24,28},{28,24},{1,5},{5... | collective-permute-start | bytes 6291464 | tf_op jit(solution)/shard_map/ppermute | solution.py:60
  174.3 2.7 collective-permute-start.16
  174.4 20.3 %collective-permute-start.17 = (f32[192,1024]{1,0:T(8,128)}, f32[192,1024]{1,0:T(8,128)}, u32[]{:S(2)}, u32[]{:S(2)}) collective-permute-start(f32[192,1024]{1,0:T(8,128)} %add_rows.13.mine_ref), channel_id=1, source_target_pairs={{0,2},{1,3},{2,0},{3,1},{4,6},{5,7},{6,4},{7,5},{8,10},{9,11},{10,... | collective-permute-start | bytes 2359304 | tf_op jit(solution)/shard_map/ppermute | solution.py:60
  197.6 2.6 collective-permute-start.21
  197.6 26.0 %collective-permute-start.18 = (f32[192,1024]{1,0:T(8,128)}, f32[192,1024]{1,0:T(8,128)}, u32[]{:S(2)}, u32[]{:S(2)}) collective-permute-start(f32[192,1024]{1,0:T(8,128)} %add.262), channel_id=1, source_target_pairs={{0,2},{1,3},{2,0},{3,1},{4,6},{5,7},{6,4},{7,5},{8,10},{9,11},{10,... | collective-permute-start | bytes 2359304 | tf_op jit(solution)/shard_map/ppermute | solution.py:60
  226.1 7.4 %collective-permute-start.23 = (f32[192,1024]{1,0:T(8,128)}, f32[192,1024]{1,0:T(8,128)}, u32[]{:S(2)}, u32[]{:S(2)}) collective-permute-start(f32[192,1024]{1,0:T(8,128)} %add_add_fusion), channel_id=1, source_target_pairs={{0,1},{1,0},{2,3},{3,2},{4,5},{5,4},{6,7},{7,6},{8,9},{9,8},{10,11... | collective-permute-start | bytes 2359304 | tf_op jit(solution)/shard_map/ppermute | solution.py:60
  226.1 20.3 %collective-permute-start.24 = (f32[192,1024]{1,0:T(8,128)}, f32[192,1024]{1,0:T(8,128)}, u32[]{:S(2)}, u32[]{:S(2)}) collective-permute-start(f32[192,1024]{1,0:T(8,128)} %add_rows.14.mine_ref), channel_id=1, source_target_pairs={{0,2},{1,3},{2,0},{3,1},{4,6},{5,7},{6,4},{7,5},{8,10},{9,11},{10,... | collective-permute-start | bytes 2359304 | tf_op jit(solution)/shard_map/ppermute | solution.py:60
  227.8 48.0 %collective-permute-start.28 = (f32[256,1024]{1,0:T(8,128)}, f32[256,1024]{1,0:T(8,128)}, u32[]{:S(2)}, u32[]{:S(2)}) collective-permute-start(f32[256,1024]{1,0:T(8,128)} %get-tuple-element.554), channel_id=1, source_target_pairs={{0,8},{4,12},{8,0},{12,4},{16,24},{20,28},{24,16},{28,20},{1,9},{5... | collective-permute-start | bytes 3145736 | tf_op jit(solution)/shard_map/ppermute | solution.py:60
  229.3 73.4 %collective-permute-start.31 = (f32[256,1024]{1,0:T(8,128)}, f32[256,1024]{1,0:T(8,128)}, u32[]{:S(2)}, u32[]{:S(2)}) collective-permute-start(f32[256,1024]{1,0:T(8,128)} %get-tuple-element.580), channel_id=1, source_target_pairs={{0,16},{4,20},{8,24},{12,28},{16,0},{20,4},{24,8},{28,12},{1,17},{... | collective-permute-start | bytes 3145736 | tf_op jit(solution)/shard_map/ppermute | solution.py:60
  231.9 74.1 %collective-permute-start.30 = (f32[512,1024]{1,0:T(8,128)}, f32[512,1024]{1,0:T(8,128)}, u32[]{:S(2)}, u32[]{:S(2)}) collective-permute-start(f32[512,1024]{1,0:T(8,128)} %product_rows.16), channel_id=1, source_target_pairs={{0,4},{4,0},{8,12},{12,8},{16,20},{20,16},{24,28},{28,24},{1,5},{5... | collective-permute-start | bytes 6291464 | tf_op jit(solution)/shard_map/ppermute | solution.py:60
  275.7 19.2 %collective-permute-start.27 = (f32[192,1024]{1,0:T(8,128)}, f32[192,1024]{1,0:T(8,128)}, u32[]{:S(2)}, u32[]{:S(2)}) collective-permute-start(f32[192,1024]{1,0:T(8,128)} %add_rows.15.mine_ref), channel_id=1, source_target_pairs={{0,2},{1,3},{2,0},{3,1},{4,6},{5,7},{6,4},{7,5},{8,10},{9,11},{10,... | collective-permute-start | bytes 2359304 | tf_op jit(solution)/shard_map/ppermute | solution.py:60
  278.5 40.6 %collective-permute-start.36 = (f32[128,1024]{1,0:T(8,128)}, f32[128,1024]{1,0:T(8,128)}, u32[]{:S(2)}, u32[]{:S(2)}) collective-permute-start(f32[128,1024]{1,0:T(8,128)} %get-tuple-element.606), channel_id=1, source_target_pairs={{0,16},{4,20},{8,24},{12,28},{16,0},{20,4},{24,8},{28,12},{1,17},{... | collective-permute-start | bytes 1572872 | tf_op jit(solution)/shard_map/ppermute | solution.py:60
  279.3 63.8 %collective-permute-start.34 = (f32[512,1024]{1,0:T(8,128)}, f32[512,1024]{1,0:T(8,128)}, u32[]{:S(2)}, u32[]{:S(2)}) collective-permute-start(f32[512,1024]{1,0:T(8,128)} %product_rows.19), channel_id=1, source_target_pairs={{0,4},{4,0},{8,12},{12,8},{16,20},{20,16},{24,28},{28,24},{1,5},{5... | collective-permute-start | bytes 6291464 | tf_op jit(solution)/shard_map/ppermute | solution.py:60
  315.3 25.5 %collective-permute-start.35 = (f32[256,1024]{1,0:T(8,128)}, f32[256,1024]{1,0:T(8,128)}, u32[]{:S(2)}, u32[]{:S(2)}) collective-permute-start(f32[256,1024]{1,0:T(8,128)} %get-tuple-element.603), channel_id=1, source_target_pairs={{0,8},{4,12},{8,0},{12,4},{16,24},{20,28},{24,16},{28,20},{1,9},{5... | collective-permute-start | bytes 3145736 | tf_op jit(solution)/shard_map/ppermute | solution.py:60
  315.3 45.2 %collective-permute-start.38 = (f32[128,1024]{1,0:T(8,128)}, f32[128,1024]{1,0:T(8,128)}, u32[]{:S(2)}, u32[]{:S(2)}) collective-permute-start(f32[128,1024]{1,0:T(8,128)} %get-tuple-element.638), channel_id=1, source_target_pairs={{0,4},{4,0},{8,12},{12,8},{16,20},{20,16},{24,28},{28,24},{1,5},{5... | collective-permute-start | bytes 1572872 | tf_op jit(solution)/shard_map/ppermute | solution.py:60
  322.2 28.3 %collective-permute-start.33 = (f32[192,1024]{1,0:T(8,128)}, f32[192,1024]{1,0:T(8,128)}, u32[]{:S(2)}, u32[]{:S(2)}) collective-permute-start(f32[192,1024]{1,0:T(8,128)} %add_rows.16.mine_ref), channel_id=1, source_target_pairs={{0,2},{1,3},{2,0},{3,1},{4,6},{5,7},{6,4},{7,5},{8,10},{9,11},{10,... | collective-permute-start | bytes 2359304 | tf_op jit(solution)/shard_map/ppermute | solution.py:60
  322.6 73.2 %collective-permute-start.41 = (f32[512,1024]{1,0:T(8,128)}, f32[512,1024]{1,0:T(8,128)}, u32[]{:S(2)}, u32[]{:S(2)}) collective-permute-start(f32[512,1024]{1,0:T(8,128)} %product_rows.21), channel_id=1, source_target_pairs={{0,4},{4,0},{8,12},{12,8},{16,20},{20,16},{24,28},{28,24},{1,5},{5... | collective-permute-start | bytes 6291464 | tf_op jit(solution)/shard_map/ppermute | solution.py:60
  347.5 44.9 %collective-permute-start.43 = (f32[256,1024]{1,0:T(8,128)}, f32[256,1024]{1,0:T(8,128)}, u32[]{:S(2)}, u32[]{:S(2)}) collective-permute-start(f32[256,1024]{1,0:T(8,128)} %get-tuple-element.685), channel_id=1, source_target_pairs={{0,8},{4,12},{8,0},{12,4},{16,24},{20,28},{24,16},{28,20},{1,9},{5... | collective-permute-start | bytes 3145736 | tf_op jit(solution)/shard_map/ppermute | solution.py:60
  347.8 46.9 %collective-permute-start.42 = (f32[128,1024]{1,0:T(8,128)}, f32[128,1024]{1,0:T(8,128)}, u32[]{:S(2)}, u32[]{:S(2)}) collective-permute-start(f32[128,1024]{1,0:T(8,128)} %get-tuple-element.683), channel_id=1, source_target_pairs={{0,16},{4,20},{8,24},{12,28},{16,0},{20,4},{24,8},{28,12},{1,17},{... | collective-permute-start | bytes 1572872 | tf_op jit(solution)/shard_map/ppermute | solution.py:60
  377.3 11.2 %collective-permute-start.39 = (f32[512,896]{1,0:T(8,128)}, f32[512,896]{1,0:T(8,128)}, u32[]{:S(2)}, u32[]{:S(2)}) collective-permute-start(f32[512,896]{1,0:T(8,128)} %get-tuple-element.670), channel_id=1, source_target_pairs={{0,1},{1,0},{2,3},{3,2},{4,5},{5,4},{6,7},{7,6},{8,9},{9,8},{10,11... | collective-permute-start | bytes 5505032 | tf_op jit(solution)/shard_map/ppermute | solution.py:60
  383.1 56.7 %collective-permute-start.47 = (f32[512,1024]{1,0:T(8,128)}, f32[512,1024]{1,0:T(8,128)}, u32[]{:S(2)}, u32[]{:S(2)}) collective-permute-start(f32[512,1024]{1,0:T(8,128)} %product_rows.23), channel_id=1, source_target_pairs={{0,4},{4,0},{8,12},{12,8},{16,20},{20,16},{24,28},{28,24},{1,5},{5... | collective-permute-start | bytes 6291464 | tf_op jit(solution)/shard_map/ppermute | solution.py:60
  399.3 2.9 collective-permute-start.44
  399.4 23.1 %collective-permute-start.40 = (f32[256,896]{1,0:T(8,128)}, f32[256,896]{1,0:T(8,128)}, u32[]{:S(2)}, u32[]{:S(2)}) collective-permute-start(f32[256,896]{1,0:T(8,128)} %get-tuple-element.676), channel_id=1, source_target_pairs={{0,2},{1,3},{2,0},{3,1},{4,6},{5,7},{6,4},{7,5},{8,10},{9,11},{10,... | collective-permute-start | bytes 2752520 | tf_op jit(solution)/shard_map/ppermute | solution.py:60
  400.2 36.1 %collective-permute-start.49 = (f32[128,1024]{1,0:T(8,128)}, f32[128,1024]{1,0:T(8,128)}, u32[]{:S(2)}, u32[]{:S(2)}) collective-permute-start(f32[128,1024]{1,0:T(8,128)} %get-tuple-element.726), channel_id=1, source_target_pairs={{0,16},{4,20},{8,24},{12,28},{16,0},{20,4},{24,8},{28,12},{1,17},{... | collective-permute-start | bytes 1572872 | tf_op jit(solution)/shard_map/ppermute | solution.py:60
  400.4 37.0 %collective-permute-start.48 = (f32[256,1024]{1,0:T(8,128)}, f32[256,1024]{1,0:T(8,128)}, u32[]{:S(2)}, u32[]{:S(2)}) collective-permute-start(f32[256,1024]{1,0:T(8,128)} %get-tuple-element.724), channel_id=1, source_target_pairs={{0,8},{4,12},{8,0},{12,4},{16,24},{20,28},{24,16},{28,20},{1,9},{5... | collective-permute-start | bytes 3145736 | tf_op jit(solution)/shard_map/ppermute | solution.py:60
  428.5 29.1 %collective-permute-start.54 = (f32[4,440,128]{2,1,0:T(8,128)}, f32[4,440,128]{2,1,0:T(8,128)}, u32[]{:S(2)}, u32[]{:S(2)}) collective-permute-start(f32[4,440,128]{2,1,0:T(8,128)} %bitcast.157), channel_id=1, source_target_pairs={{0,4},{4,0},{8,12},{12,8},{16,20},{20,16},{24,28},{28,24},{1,5},{5... | collective-permute-start | bytes 2703368 | tf_op jit(solution)/shard_map/ppermute | solution.py:60
  439.8 15.7 %collective-permute-start.46 = (f32[192,768]{1,0:T(8,128)}, f32[192,768]{1,0:T(8,128)}, u32[]{:S(2)}, u32[]{:S(2)}) collective-permute-start(f32[192,768]{1,0:T(8,128)} %add_rows.17), channel_id=1, source_target_pairs={{0,2},{1,3},{2,0},{3,1},{4,6},{5,7},{6,4},{7,5},{8,10},{9,11},{10,... | collective-permute-start | bytes 1769480 | tf_op jit(solution)/shard_map/ppermute | solution.py:60
  444.0 25.6 %collective-permute-start.53 = (f32[128,1024]{1,0:T(8,128)}, f32[128,1024]{1,0:T(8,128)}, u32[]{:S(2)}, u32[]{:S(2)}) collective-permute-start(f32[128,1024]{1,0:T(8,128)} %get-tuple-element.753), channel_id=1, source_target_pairs={{0,16},{4,20},{8,24},{12,28},{16,0},{20,4},{24,8},{28,12},{1,17},{... | collective-permute-start | bytes 1572872 | tf_op jit(solution)/shard_map/ppermute | solution.py:60
  445.1 28.5 %collective-permute-start.52 = (f32[512,512]{1,0:T(8,128)}, f32[512,512]{1,0:T(8,128)}, u32[]{:S(2)}, u32[]{:S(2)}) collective-permute-start(f32[512,512]{1,0:T(8,128)} %product_rows.25), channel_id=1, source_target_pairs={{0,4},{4,0},{8,12},{12,8},{16,20},{20,16},{24,28},{28,24},{1,5},{5... | collective-permute-start | bytes 3145736 | tf_op jit(solution)/shard_map/ppermute | solution.py:60
  445.6 37.5 %collective-permute-start.51 = (f32[256,1024]{1,0:T(8,128)}, f32[256,1024]{1,0:T(8,128)}, u32[]{:S(2)}, u32[]{:S(2)}) collective-permute-start(f32[256,1024]{1,0:T(8,128)} %get-tuple-element.750), channel_id=1, source_target_pairs={{0,8},{4,12},{8,0},{12,4},{16,24},{20,28},{24,16},{28,20},{1,9},{5... | collective-permute-start | bytes 3145736 | tf_op jit(solution)/shard_map/ppermute | solution.py:60
  470.7 16.6 %collective-permute-start.50 = (f32[192,768]{1,0:T(8,128)}, f32[192,768]{1,0:T(8,128)}, u32[]{:S(2)}, u32[]{:S(2)}) collective-permute-start(f32[192,768]{1,0:T(8,128)} %add.275), channel_id=1, source_target_pairs={{0,1},{1,0},{2,3},{3,2},{4,5},{5,4},{6,7},{7,6},{8,9},{9,8},{10,11... | collective-permute-start | bytes 1769480 | tf_op jit(solution)/shard_map/ppermute | solution.py:60
  470.8 28.2 %collective-permute-start.55 = (f32[2,440,128]{2,1,0:T(8,128)}, f32[2,440,128]{2,1,0:T(8,128)}, u32[]{:S(2)}, u32[]{:S(2)}) collective-permute-start(f32[2,440,128]{2,1,0:T(8,128)} %dynamic-slice_bitcast_fusion), channel_id=1, source_target_pairs={{0,8},{4,12},{8,0},{12,4},{16,24},{20,28},{24,16},{28,20},{1,9},{5... | collective-permute-start | bytes 1351688 | tf_op jit(solution)/shard_map/ppermute | solution.py:60
  485.3 24.1 %collective-permute-start.58 = (f32[128,1024]{1,0:T(8,128)}, f32[128,1024]{1,0:T(8,128)}, u32[]{:S(2)}, u32[]{:S(2)}) collective-permute-start(f32[128,1024]{1,0:T(8,128)} %get-tuple-element.785), channel_id=1, source_target_pairs={{0,16},{4,20},{8,24},{12,28},{16,0},{20,4},{24,8},{28,12},{1,17},{... | collective-permute-start | bytes 1572872 | tf_op jit(solution)/shard_map/ppermute | solution.py:60
  485.3 32.4 %collective-permute-start.57 = (f32[256,512]{1,0:T(8,128)}, f32[256,512]{1,0:T(8,128)}, u32[]{:S(2)}, u32[]{:S(2)}) collective-permute-start(f32[256,512]{1,0:T(8,128)} %get-tuple-element.783), channel_id=1, source_target_pairs={{0,8},{4,12},{8,0},{12,4},{16,24},{20,28},{24,16},{28,20},{1,9},{5... | collective-permute-start | bytes 1572872 | tf_op jit(solution)/shard_map/ppermute | solution.py:60
  501.0 18.5 %collective-permute-start.56 = (f32[1,440,128]{2,1,0:T(8,128)}, f32[1,440,128]{2,1,0:T(8,128)}, u32[]{:S(2)}, u32[]{:S(2)}) collective-permute-start(f32[1,440,128]{2,1,0:T(8,128)} %constant_dynamic-slice_fusion), channel_id=1, source_target_pairs={{0,16},{4,20},{8,24},{12,28},{16,0},{20,4},{24,8},{28,12},{1,17},{... | collective-permute-start | bytes 675848 | tf_op jit(solution)/shard_map/ppermute | solution.py:60
  524.7 12.5 %collective-permute-start.60 = (f32[128,512]{1,0:T(8,128)}, f32[128,512]{1,0:T(8,128)}, u32[]{:S(2)}, u32[]{:S(2)}) collective-permute-start(f32[128,512]{1,0:T(8,128)} %get-tuple-element.800), channel_id=1, source_target_pairs={{0,16},{4,20},{8,24},{12,28},{16,0},{20,4},{24,8},{28,12},{1,17},{... | collective-permute-start | bytes 786440 | tf_op jit(solution)/shard_map/ppermute | solution.py:60
  525.6 9.0 %collective-permute-start.59 = (f32[192,128]{1,0:T(8,128)}, f32[192,128]{1,0:T(8,128)S(1)}, u32[]{:S(2)}, u32[]{:S(2)}) collective-permute-start(f32[192,128]{1,0:T(8,128)} %slice_bitcast_fusion.5), channel_id=1, source_target_pairs={{0,1},{1,0},{2,3},{3,2},{4,5},{5,4},{6,7},{7,6},{8,9},{9,8},{10,11... | collective-permute-start | bytes 294920 | tf_op jit(solution)/shard_map/ppermute | solution.py:60
  (219 other events, 2022.5 us)

commit v7 on v6

--- a/solution.py
+++ b/solution.py
@@ -11,8 +11,10 @@
 PLAN = {
     ("top", 0): [("down", 0)],
     ("pre", 0): [("up", 0)],
-    ("wait_one", 0): [("att", 0), ("down", 0), ("up", 0)],
-    ("wait_two", 1): [("down", 1), ("up", 0)],
+    ("core_one", 0): [("att", 0)],
+    ("wait_one", 0): [("down", 0), ("up", 0)],
+    ("core_two", 1): [("down", 1)],
+    ("wait_two", 1): [("up", 0)],
     ("mid", 1): [("down", 0), ("att", 0)],
     ("wait_one", 1): [("up", 0), ("up", 1), ("att", 0), ("down", 1)],
     ("end", 1): [("down", 0), ("att", 1)],
@@ -241,7 +243,7 @@
     )(mine, got, unit, inverse, gains, grad)
 
 
-def feed_forward(unit_own, unit_other, gains, biases, place, up_weight, up_bias, down_weight):
+def feed_forward(unit_own, unit_other, gains, biases, place, up_weight, up_bias, down_weight, shards):
     half, width = unit_own.shape
     rows = 2 * half
     layer, which = place
@@ -250,8 +252,11 @@
     spread_of = math.sqrt(2.0)
     peak = 1.0 / math.sqrt(2.0 * math.pi)
 
-    def kernel(own_ref, other_ref, gain_ref, bias_ref, up_ref, up_bias_ref, down_ref,
-               activation_out, slope_out, own_out, send_out, normed_ref):
+    count = shards.shape[0]
+    shard = width // count
+
+    def kernel(shards_ref, own_ref, other_ref, gain_ref, bias_ref, up_ref, up_bias_ref, down_ref,
+               activation_out, slope_out, own_out, send_out, ordered_out, normed_ref):
         step = pl.program_id(0)
 
         @pl.when(step == 0)
@@ -262,6 +267,10 @@
             normed_ref[half:] = (other_ref[...] * gain + bias).astype(BF)
             own_out[...] = jnp.zeros_like(own_out)
             send_out[...] = jnp.zeros_like(send_out)
+            if shard % 128:
+                ordered_out[...] = normed_ref[...]
+            else:
+                ordered_columns(normed_ref, ordered_out, shards_ref, count, shard)
 
         pre = matmul(normed_ref[...], up_ref[0]) + up_bias_ref[layer : layer + 1]
         below = 0.5 + 0.5 * lax.erf(pre / spread_of)
@@ -280,9 +289,11 @@
             jax.ShapeDtypeStruct((rows, hidden), F32),
             piece,
             piece,
+            jax.ShapeDtypeStruct((rows, width), BF),
         ),
         grid=(hidden // size,),
         in_specs=[
+            pl.BlockSpec(memory_space=pltpu.SMEM),
             whole,
             whole,
             pl.BlockSpec(gains.shape, lambda j: (0, 0, 0)),
@@ -296,12 +307,13 @@
             pl.BlockSpec((rows, size), lambda j: (0, j)),
             whole,
             whole,
+            pl.BlockSpec((rows, width), lambda j: (0, 0)),
         ),
         scratch_shapes=[pltpu.VMEM((rows, width), BF)],
         cost_estimate=LONG,
         compiler_params=vmem_limit(44 << 20),
         name="feed_forward",
-    )(unit_own, unit_other, gains, biases, up_weight, up_bias, down_weight)
+    )(shards, unit_own, unit_other, gains, biases, up_weight, up_bias, down_weight)
 
 
 def feed_back(low, slope, down_weight, up_weight, layer):
@@ -857,10 +869,13 @@
     def mp_bit(self, bit):
         return (self.mp_index >> bit) & 1
 
-    def ordered_sum(self, clock, own, send):
+    def ordered_sum(self, clock, own, send, fill=None):
         send = clock.one(send)
         got = exchange(send, "mp", self.mp, 0)
-        clock.hold()
+        if fill:
+            fill()
+        else:
+            clock.hold()
         mine = clock.one(add_rows(own(), clock.one(got)))
         last = bit_count(self.mp) - 1
         for bit in range(1, last):
@@ -1101,7 +1116,7 @@
             hidden = hidden + (mine + got) + output_bias[layer]
             unit_two, inverse_two = norm_parts(hidden)
             unit_other = links.other_rows(unit_two)
-            activation, slope, part_own, part_send = feed_forward(
+            activation, slope, part_own, part_send, normed_two = feed_forward(
                 unit_two,
                 unit_other,
                 norm_gain,
@@ -1110,14 +1125,12 @@
                 up_weight,
                 up_bias,
                 down_weight,
-            )
-            marker = activation
+                shards,
+            )
+            if shard % 128:
+                normed_two = take_columns(normed_two, shards, shard)
             if layer < top:
                 mine, got = links.begin_sum(part_own, part_send)
-                marker = mine
-            normed_two = norm_rows(
-                after(unit_two, marker), unit_other, norm_gain[layer, 1], norm_bias[layer, 1], shards
-            )
             if layer < top:
                 if layer == 0:
                     mine, embed_late, key_late = lax.optimization_barrier(
@@ -1181,6 +1194,9 @@
                 if name in merges and merges[name].open:
                     merges[name].advance(clock)
 
+        def fill(spot):
+            return (lambda: advance(spot)) if PLAN.get(spot) else None
+
         for layer in reversed(range(layer_count)):
             depth = top - layer
             (
@@ -1200,6 +1216,9 @@
                 links, [(down_left, activation)], bits if depth else bits_late
             )
             advance(("top", depth))
+            if layer == top:
+                last_send = clock.one(last_send)
+                last_other = exchange(last_send, "mp", mp, 0)
             pre_low, up_sums, part_own, part_send = feed_back(
                 clock.one(down_low), slope, down_weight, up_weight, layer
             )
@@ -1207,14 +1226,11 @@
             pre_low, part_send = clock.both(pre_low, part_send)
             merges["up", depth] = Merge(links, [(normed_two, pre_low)], bits)
             advance(("pre", depth))
-            mine, got = links.ordered_sum(clock, lambda: part_own, part_send)
+            mine, got = links.ordered_sum(clock, lambda: part_own, part_send, fill(("core_two", depth)))
             if not PLAN.get(("wait_two", depth)):
                 clock.hold()
             advance(("wait_two", depth))
             if layer == top:
-                last_send = clock.one(last_send)
-                last_other = exchange(last_send, "mp", mp, 0)
-                clock.hold()
                 last_mine = clock.one(last_own + clock.one(last_other))
             mine, got = clock.both(mine, got)
             if layer == top:
@@ -1241,10 +1257,10 @@
                 clock.one(out_low), qkv, totals, attention_weight[layer], output_weight[layer]
             )
             local_sums["qv", layer] = qv_sums
-            mine, got = links.ordered_sum(clock, lambda: part_own, part_send)
+            merges["att", depth] = Merge(links, [(out_left, mixed), (normed, grads)], bits)
+            mine, got = links.ordered_sum(clock, lambda: part_own, part_send, fill(("core_one", depth)))
             if not PLAN.get(("wait_one", depth)):
                 clock.hold()
-            merges["att", depth] = Merge(links, [(out_left, mixed), (normed, grads)], bits)
             advance(("wait_one", depth))
             if layer == top:
                 hidden = clock.one(hidden + (last_mine + clock.one(last_other)) + down_bias[top])
@@ -1308,9 +1324,6 @@
             embed_send, embed_own = add_split(embed_own, embed_got)
             embed_send = clock.one(embed_send)
             embed_got = exchange(embed_send, "mp", mp, bit)
-        advance("back")
-        lanes = embed_own.shape[1]
-
         names = []
         for layer in range(layer_count):
             names += [("gain", layer, 0), ("gain", layer, 1), ("bias", layer, 0), ("bias", layer, 1)]
@@ -1319,7 +1332,9 @@
         names += ["column", "lead"]
         own_sums = clock.one(jnp.stack([row_sums[name] for name in names]) * item_scale)
         other_sums = exchange(own_sums, "mp", mp, 0)
-        clock.hold()
+        advance("back")
+        lanes = embed_own.shape[1]
+
         full_sums = own_sums + clock.one(other_sums)
         local = jnp.stack([local_sums["up_bias", layer] for layer in range(layer_count)]) * item_scale
         thin = [local_sums["qv", layer] for layer in range(layer_count)]
@@ -1380,7 +1395,7 @@
         for kind in ("down", "up", "att"):
             parts = [merges[kind, top - layer].total for layer in range(layer_count)]
             finished[kind] = finish_layers(
-                kind, parts, clock.cell, layer_count, shard, local_width
+                kind, parts, clock.cell if kind == "att" else scale_cell, layer_count, shard, local_width
             )
         tail_total = merges["tail"].total
         small = merges["small"].total[0]

time: 551 us -> 543 us (0.985)
    unnamed x434 -> x400, local copies, waits for them, and re-layouts: 40 us -> 42.4 us
  transfers between devices with their start and end apart: 61 -> 61, of which waited for: 39 -> 37; matrix products, arithmetic and copies ran while one was open for 11% -> 11% of each run, Pallas kernels for 21% -> 21%
where the time goes in v7:
time: 543 us; the launch traced here: 536 us
  waiting for transfers between devices  212 us (39%)
  Pallas kernels  162 us (30%)
  local copies, waits for them, and re-layouts  64.8 us (12%)
  starting transfers between devices  50.9 us (9%)
  other arithmetic  40.6 us (7%)
  between operations  5.54 us (1%)
    ppermute x61, waiting for transfers between devices, exchange(): return lax.ppermute(tensor, axis, [(i, i ^ 1 << bit) for i in range(size)])  212 us
    ppermute x61, starting transfers between devices, exchange(): return lax.ppermute(tensor, axis, [(i, i ^ 1 << bit) for i in range(size)])  50.9 us
    unnamed x400, local copies, waits for them, and re-layouts  42.4 us
    pallas_call x14, Pallas kernels, product_rows(): pl.pallas_call(kernel, out_shape=out_shape, grid=(count,), in_specs=in_sp...  37.5 us
    pallas_call x8, Pallas kernels, add_split(): pl.pallas_call(kernel, out_shape=[jax.ShapeDtypeStruct((half, width), F32...  18.6 us
    pallas_call x2, Pallas kernels, feed_forward(): pl.pallas_call(kernel, out_shape=(jax.ShapeDtypeStruct((rows, hidden), BF...  16.7 us
    pallas_call x9, Pallas kernels, add_rows(): pl.pallas_call(kernel, out_shape=jax.ShapeDtypeStruct((rows, width), F32)...  12.8 us
    pallas_call x2, Pallas kernels, feed_back(): pl.pallas_call(kernel, out_shape=(jax.ShapeDtypeStruct((rows, hidden), BF...  12.1 us
  transfers between devices with their start and end apart: 61, of which 37 were waited for; matrix products, arithmetic and copies ran while one was open for 11% of the time, Pallas kernels for 21%

profile of v7, /device:TPU:0, one launch (start us, length us, event | category | flops | bytes accessed | tf_op | source)
XLA Modules:
  0.0 536.1 jit_solution(9244696999262708889)
XLA Ops:
  2.6 10.2 %pool_front.1 = (bf16[384,768]{1,0:T(8,128)(2,1)}, f32[1,256]{1,0:T(1,128)}, f32[4,1024]{1,0:T(4,128)}, f32[4,768]{1,0:T(4,128)}, bf16[768,256]{1,0:T(8,128)(2,1...) custom-call(s32[1]{0:T(128)} %bitcast.core_ref, ...), custom_call_target="tpu_custom_call" | custom-call | flops 999999995904 | bytes 8 | tf_op jit(solution)/shard_map/pool_front/pallas_call | solution.py:777
  17.0 2.9 collective-permute-start.4
  27.1 2.6 collective-permute-start.3
  31.6 6.1 %collective-permute-done.4 = f32[192,1024]{1,0:T(8,128)S(1)} collective-permute-done((f32[192,1024]{1,0:T(8,128)S(1)}, f32[192,1024]{1,0:T(8,128)S(1)}, u32[]{:S(2)}, u32[]{:S(2)}) %collective-permute-start.4) | collective-permute-done | bytes 786464 | tf_op jit(solution)/shard_map/ppermute | solution.py:62
  42.8 3.9 attend_forward.2
  60.0 12.6 %collective-permute-done.7 = f32[192,1024]{1,0:T(8,128)} collective-permute-done((f32[192,1024]{1,0:T(8,128)}, f32[192,1024]{1,0:T(8,128)}, u32[]{:S(2)}, u32[]{:S(2)}) %collective-permute-start.7) | collective-permute-done | bytes 786464 | tf_op jit(solution)/shard_map/ppermute | solution.py:62
  77.9 8.3 %feed_forward.2 = (bf16[384,1024]{1,0:T(8,128)(2,1)}, f32[384,1024]{1,0:T(8,128)}, f32[192,1024]{1,0:T(8,128)}, f32[192,1024]{1,0:T(8,128)}, bf16[384,1024]{1,0:T(8,128)(2,1)}) custom-call(s32[8]{0:T(128)} %copy-done.35, f32[192,1024]{1,0:T(8,128)} %copy-done.16, f32[192,1024]{1,0:T(8,128)} %copy-done.185, f32[2,2,1024]{2,1,0:T(2,128)} %gain_ref.11, ...), custom_call_target="tpu_custom_call" | custom-call | flops 999999995904 | bytes 8 | tf_op jit(solution)/shard_map/feed_forward/pallas_call | solution.py:285
  99.4 12.6 %collective-permute-done.10 = f32[192,1024]{1,0:T(8,128)} collective-permute-done((f32[192,1024]{1,0:T(8,128)S(1)}, f32[192,1024]{1,0:T(8,128)}, u32[]{:S(2)}, u32[]{:S(2)}) %collective-permute-start.10) | collective-permute-done | bytes 786464 | tf_op jit(solution)/shard_map/ppermute | solution.py:62
  116.2 3.1 attend_forward.3
  125.6 15.9 %collective-permute-done.13 = f32[192,1024]{1,0:T(8,128)S(1)} collective-permute-done((f32[192,1024]{1,0:T(8,128)S(1)}, f32[192,1024]{1,0:T(8,128)S(1)}, u32[]{:S(2)}, u32[]{:S(2)}) %collective-permute-start.13) | collective-permute-done | bytes 786464 | tf_op jit(solution)/shard_map/ppermute | solution.py:62
  145.7 8.4 %feed_forward.3 = (bf16[384,1024]{1,0:T(8,128)(2,1)}, f32[384,1024]{1,0:T(8,128)}, f32[192,1024]{1,0:T(8,128)}, f32[192,1024]{1,0:T(8,128)}, bf16[384,1024]{1,0:T(8,128)(2,1)}) custom-call(s32[8]{0:T(128)} %copy-done.35, f32[192,1024]{1,0:T(8,128)} %copy-done.18, f32[192,1024]{1,0:T(8,128)} %collective-permute-done.14.other_ref, f32[2,2,1024]{2,1,0:T(2,128)} %gain_ref.11, ...), custom_call_target="tpu_custom_call" | custom-call | flops 999999995904 | bytes 8 | tf_op jit(solution)/shard_map/feed_forward/pallas_call | solution.py:285
  160.0 6.0 %feed_back.2 = (bf16[384,1024]{1,0:T(8,128)(2,1)S(1)}, f32[1,1024]{1,0:T(1,128)S(1)}, f32[192,1024]{1,0:T(8,128)S(1)}, f32[192,1024]{1,0:T(8,128)}) custom-call(bf16[384,1024]{1,0:T(8,128)(2,1)S(1)} %copy-done.76, f32[384,1024]{1,0:T(8,128)S(1)} %copy-done.68, bf16[2,1024,1024]{2,1,0:T(8,128)(2,1)S(1)} %copy-done.45, bf16[2,1024,1024]{2,1,0:T(8,128)(2,1)S(1)} %copy-done.44), custom_call_target="tpu_custom_call" | custom-call | flops 999999995904 | bytes 8 | tf_op jit(solution)/shard_map/feed_back/pallas_call | solution.py:340
  179.1 14.6 %collective-permute-done.17.got_ref = f32[192,1024]{1,0:T(8,128)} collective-permute-done((f32[192,1024]{1,0:T(8,128)}, f32[192,1024]{1,0:T(8,128)}, u32[]{:S(2)}, u32[]{:S(2)}) %collective-permute-start.17) | collective-permute-done | bytes 786464 | tf_op jit(solution)/shard_map/ppermute | solution.py:62
  193.8 2.8 norm_back.4
  200.8 4.9 attend_back.2
  211.1 5.5 %collective-permute-done.20.refs_2_ = f32[512,1024]{1,0:T(8,128)} collective-permute-done((f32[512,1024]{1,0:T(8,128)}, f32[512,1024]{1,0:T(8,128)}, u32[]{:S(2)}, u32[]{:S(2)}) %collective-permute-start.20) | collective-permute-done | bytes 2097184 | tf_op jit(solution)/shard_map/ppermute | solution.py:62
  216.6 3.3 product_rows.17
  220.0 3.3 product_rows.18
  229.0 2.6 collective-permute-start.31
  234.6 11.5 %collective-permute-done.24.got_ref = f32[192,1024]{1,0:T(8,128)} collective-permute-done((f32[192,1024]{1,0:T(8,128)}, f32[192,1024]{1,0:T(8,128)}, u32[]{:S(2)}, u32[]{:S(2)}) %collective-permute-start.24) | collective-permute-done | bytes 786464 | tf_op jit(solution)/shard_map/ppermute | solution.py:62
  246.2 2.8 norm_back.5
  254.8 6.0 %feed_back.3 = (bf16[384,1024]{1,0:T(8,128)(2,1)S(1)}, f32[1,1024]{1,0:T(1,128)S(1)}, f32[192,1024]{1,0:T(8,128)S(1)}, f32[192,1024]{1,0:T(8,128)}) custom-call(bf16[384,1024]{1,0:T(8,128)(2,1)S(1)} %get-tuple-element.540.low_ref, f32[384,1024]{1,0:T(8,128)S(1)} %copy-done.67, bf16[2,1024,1024]{2,1,0:T(8,128)(2,1)S(1)} %copy-done.46, ...), custom_call_target="tpu_custom_call" | custom-call | flops 999999995904 | bytes 8 | tf_op jit(solution)/shard_map/feed_back/pallas_call | solution.py:340
  266.6 8.8 %collective-permute-done.28.got_ref = f32[256,1024]{1,0:T(8,128)} collective-permute-done((f32[256,1024]{1,0:T(8,128)}, f32[256,1024]{1,0:T(8,128)}, u32[]{:S(2)}, u32[]{:S(2)}) %collective-permute-start.28) | collective-permute-done | bytes 1048608 | tf_op jit(solution)/shard_map/ppermute | solution.py:62
  279.0 15.6 %collective-permute-done.27.got_ref = f32[192,1024]{1,0:T(8,128)} collective-permute-done((f32[192,1024]{1,0:T(8,128)}, f32[192,1024]{1,0:T(8,128)}, u32[]{:S(2)}, u32[]{:S(2)}) %collective-permute-start.27) | collective-permute-done | bytes 786464 | tf_op jit(solution)/shard_map/ppermute | solution.py:62
  294.7 2.8 norm_back.6
  305.0 3.4 product_rows.20
  308.5 4.9 attend_back.3
  323.2 16.5 %collective-permute-done.35.got_ref = f32[256,1024]{1,0:T(8,128)} collective-permute-done((f32[256,1024]{1,0:T(8,128)}, f32[256,1024]{1,0:T(8,128)}, u32[]{:S(2)}, u32[]{:S(2)}) %collective-permute-start.35) | collective-permute-done | bytes 1048608 | tf_op jit(solution)/shard_map/ppermute | solution.py:62
  342.0 3.5 product_rows.22
  346.7 2.8 collective-permute-start.43
  349.6 2.8 norm_back.7
  364.5 8.9 %pool_back.1 = (f32[816,256]{1,0:T(8,128)S(1)}, f32[4,768]{1,0:T(4,128)S(1)}, f32[4,48]{1,0:T(4,128)S(1)}, f32[192,768]{1,0:T(8,128)S(1)}, f32[192,768]{1,0:T(8,128)}) custom-call(bf16[384,1024]{1,0:T(8,128)(2,1)S(1)} %get-tuple-element.651.low_ref, bf16[256,1024]{1,0:T(8,128)(2,1)S(1)} %copy-done.53, bf16[768,256]{1,0:T(8,128)(2,1)S(1)} %copy-done.120, ...), custom_call_target="tpu_custom_call" | custom-call | flops 999999995904 | bytes 8 | tf_op jit(solution)/shard_map/pool_back/pallas_call | solution.py:844
  373.4 2.8 embed_terms.1
  386.6 3.8 add_split.11
  394.6 3.4 product_rows.24
  404.2 12.8 %collective-permute-done.40 = f32[256,896]{1,0:T(8,128)} collective-permute-done((f32[256,896]{1,0:T(8,128)}, f32[256,896]{1,0:T(8,128)}, u32[]{:S(2)}, u32[]{:S(2)}) %collective-permute-start.40) | collective-permute-done | bytes 917536 | tf_op jit(solution)/shard_map/ppermute | solution.py:62
  419.5 2.5 constant_dynamic-slice_fusion.1
  431.9 3.9 collective-permute-done.48.got_ref
  439.6 3.3 product_rows.26
  447.6 5.1 collective-permute-done.46
  458.6 9.6 %collective-permute-done.53 = f32[128,1024]{1,0:T(8,128)} collective-permute-done((f32[128,1024]{1,0:T(8,128)}, f32[128,1024]{1,0:T(8,128)}, u32[]{:S(2)}, u32[]{:S(2)}) %collective-permute-start.53) | collective-permute-done | bytes 524320 | tf_op jit(solution)/shard_map/ppermute | solution.py:62
  471.7 2.9 product_rows.27
  474.5 7.6 %collective-permute-done.51.got_ref = f32[256,1024]{1,0:T(8,128)} collective-permute-done((f32[256,1024]{1,0:T(8,128)}, f32[256,1024]{1,0:T(8,128)}, u32[]{:S(2)}, u32[]{:S(2)}) %collective-permute-start.51) | collective-permute-done | bytes 1048608 | tf_op jit(solution)/shard_map/ppermute | solution.py:62
  488.8 2.7 copy.79
  491.4 6.4 %collective-permute-done.55 = f32[2,440,128]{2,1,0:T(8,128)} collective-permute-done((f32[2,440,128]{2,1,0:T(8,128)}, f32[2,440,128]{2,1,0:T(8,128)}, u32[]{:S(2)}, u32[]{:S(2)}) %collective-permute-start.55) | collective-permute-done | bytes 450592 | tf_op jit(solution)/shard_map/ppermute | solution.py:62
  499.8 8.3 %collective-permute-done.58 = f32[128,1024]{1,0:T(8,128)} collective-permute-done((f32[128,1024]{1,0:T(8,128)}, f32[128,1024]{1,0:T(8,128)}, u32[]{:S(2)}, u32[]{:S(2)}) %collective-permute-start.58) | collective-permute-done | bytes 524320 | tf_op jit(solution)/shard_map/ppermute | solution.py:62
  509.2 7.4 %collective-permute-done.57.got_ref = f32[256,512]{1,0:T(8,128)} collective-permute-done((f32[256,512]{1,0:T(8,128)}, f32[256,512]{1,0:T(8,128)}, u32[]{:S(2)}, u32[]{:S(2)}) %collective-permute-start.57) | collective-permute-done | bytes 524320 | tf_op jit(solution)/shard_map/ppermute | solution.py:62
  527.1 5.8 %collective-permute-done.60 = f32[128,512]{1,0:T(8,128)S(1)} collective-permute-done((f32[128,512]{1,0:T(8,128)S(1)}, f32[128,512]{1,0:T(8,128)S(1)}, u32[]{:S(2)}, u32[]{:S(2)}) %collective-permute-start.60) | collective-permute-done | bytes 262176 | tf_op jit(solution)/shard_map/ppermute | solution.py:62
  (667 shorter events, 222.2 us)
Async XLA Ops:
  12.8 2.6 collective-permute-start
  17.0 20.8 %collective-permute-start.4 = (f32[192,1024]{1,0:T(8,128)S(1)}, f32[192,1024]{1,0:T(8,128)S(1)}, u32[]{:S(2)}, u32[]{:S(2)}) collective-permute-start(f32[192,1024]{1,0:T(8,128)S(1)} %add_rows.9), channel_id=1, source_target_pairs={{0,2},{1,3},{2,0},{3,1},{4,6},{5,7},{6,4},{7,5},{8,10},{9,11},{10,... | collective-permute-start | bytes 2359304 | tf_op jit(solution)/shard_map/ppermute | solution.py:62
  19.9 3.6 collective-permute-start.1
  23.5 3.6 collective-permute-start.2
  27.1 4.5 collective-permute-start.3
  52.7 19.9 %collective-permute-start.7 = (f32[192,1024]{1,0:T(8,128)}, f32[192,1024]{1,0:T(8,128)}, u32[]{:S(2)}, u32[]{:S(2)}) collective-permute-start(f32[192,1024]{1,0:T(8,128)} %add_rows.10), channel_id=1, source_target_pairs={{0,2},{1,3},{2,0},{3,1},{4,6},{5,7},{6,4},{7,5},{8,10},{9,11},{10,... | collective-permute-start | bytes 2359304 | tf_op jit(solution)/shard_map/ppermute | solution.py:62
  92.3 19.8 %collective-permute-start.10 = (f32[192,1024]{1,0:T(8,128)S(1)}, f32[192,1024]{1,0:T(8,128)}, u32[]{:S(2)}, u32[]{:S(2)}) collective-permute-start(f32[192,1024]{1,0:T(8,128)S(1)} %add_rows.11), channel_id=1, source_target_pairs={{0,2},{1,3},{2,0},{3,1},{4,6},{5,7},{6,4},{7,5},{8,10},{9,11},{10,... | collective-permute-start | bytes 2359304 | tf_op jit(solution)/shard_map/ppermute | solution.py:62
  121.9 19.6 %collective-permute-start.13 = (f32[192,1024]{1,0:T(8,128)S(1)}, f32[192,1024]{1,0:T(8,128)S(1)}, u32[]{:S(2)}, u32[]{:S(2)}) collective-permute-start(f32[192,1024]{1,0:T(8,128)S(1)} %add_rows.12), channel_id=1, source_target_pairs={{0,2},{1,3},{2,0},{3,1},{4,6},{5,7},{6,4},{7,5},{8,10},{9,11},{10,... | collective-permute-start | bytes 2359304 | tf_op jit(solution)/shard_map/ppermute | solution.py:62
  168.1 3.9 collective-permute-start.16
  168.2 7.6 %collective-permute-start.15 = (f32[192,1024]{1,0:T(8,128)}, f32[192,1024]{1,0:T(8,128)}, u32[]{:S(2)}, u32[]{:S(2)}) collective-permute-start(f32[192,1024]{1,0:T(8,128)} %get-tuple-element.451), channel_id=1, source_target_pairs={{0,1},{1,0},{2,3},{3,2},{4,5},{5,4},{6,7},{7,6},{8,9},{9,8},{10,11... | collective-permute-start | bytes 2359304 | tf_op jit(solution)/shard_map/ppermute | solution.py:62
  168.6 48.1 %collective-permute-start.20 = (f32[512,1024]{1,0:T(8,128)}, f32[512,1024]{1,0:T(8,128)}, u32[]{:S(2)}, u32[]{:S(2)}) collective-permute-start(f32[512,1024]{1,0:T(8,128)} %product_rows.14), channel_id=1, source_target_pairs={{0,8},{4,12},{8,0},{12,4},{16,24},{20,28},{24,16},{28,20},{1,9},{5... | collective-permute-start | bytes 6291464 | tf_op jit(solution)/shard_map/ppermute | solution.py:62
  170.4 49.6 %collective-permute-start.19 = (f32[512,1024]{1,0:T(8,128)}, f32[512,1024]{1,0:T(8,128)}, u32[]{:S(2)}, u32[]{:S(2)}) collective-permute-start(f32[512,1024]{1,0:T(8,128)} %product_rows.15), channel_id=1, source_target_pairs={{0,4},{4,0},{8,12},{12,8},{16,20},{20,16},{24,28},{28,24},{1,5},{5... | collective-permute-start | bytes 6291464 | tf_op jit(solution)/shard_map/ppermute | solution.py:62
  174.2 19.4 %collective-permute-start.17 = (f32[192,1024]{1,0:T(8,128)}, f32[192,1024]{1,0:T(8,128)}, u32[]{:S(2)}, u32[]{:S(2)}) collective-permute-start(f32[192,1024]{1,0:T(8,128)} %add_rows.13.mine_ref), channel_id=1, source_target_pairs={{0,2},{1,3},{2,0},{3,1},{4,6},{5,7},{6,4},{7,5},{8,10},{9,11},{10,... | collective-permute-start | bytes 2359304 | tf_op jit(solution)/shard_map/ppermute | solution.py:62
  196.6 26.7 %collective-permute-start.18 = (f32[192,1024]{1,0:T(8,128)}, f32[192,1024]{1,0:T(8,128)}, u32[]{:S(2)}, u32[]{:S(2)}) collective-permute-start(f32[192,1024]{1,0:T(8,128)} %add.262), channel_id=1, source_target_pairs={{0,2},{1,3},{2,0},{3,1},{4,6},{5,7},{6,4},{7,5},{8,10},{9,11},{10,... | collective-permute-start | bytes 2359304 | tf_op jit(solution)/shard_map/ppermute | solution.py:62
  205.7 3.4 collective-permute-start.22
  208.0 97.0 %collective-permute-start.30 = (f32[512,1024]{1,0:T(8,128)}, f32[512,1024]{1,0:T(8,128)}, u32[]{:S(2)}, u32[]{:S(2)}) collective-permute-start(f32[512,1024]{1,0:T(8,128)} %product_rows.16), channel_id=1, source_target_pairs={{0,4},{4,0},{8,12},{12,8},{16,20},{20,16},{24,28},{28,24},{1,5},{5... | collective-permute-start | bytes 6291464 | tf_op jit(solution)/shard_map/ppermute | solution.py:62
  225.8 5.8 %collective-permute-start.23 = (f32[192,1024]{1,0:T(8,128)}, f32[192,1024]{1,0:T(8,128)}, u32[]{:S(2)}, u32[]{:S(2)}) collective-permute-start(f32[192,1024]{1,0:T(8,128)} %add_add_fusion), channel_id=1, source_target_pairs={{0,1},{1,0},{2,3},{3,2},{4,5},{5,4},{6,7},{7,6},{8,9},{9,8},{10,11... | collective-permute-start | bytes 2359304 | tf_op jit(solution)/shard_map/ppermute | solution.py:62
  225.8 20.3 %collective-permute-start.24 = (f32[192,1024]{1,0:T(8,128)}, f32[192,1024]{1,0:T(8,128)}, u32[]{:S(2)}, u32[]{:S(2)}) collective-permute-start(f32[192,1024]{1,0:T(8,128)} %add_rows.14.mine_ref), channel_id=1, source_target_pairs={{0,2},{1,3},{2,0},{3,1},{4,6},{5,7},{6,4},{7,5},{8,10},{9,11},{10,... | collective-permute-start | bytes 2359304 | tf_op jit(solution)/shard_map/ppermute | solution.py:62
  227.5 48.0 %collective-permute-start.28 = (f32[256,1024]{1,0:T(8,128)}, f32[256,1024]{1,0:T(8,128)}, u32[]{:S(2)}, u32[]{:S(2)}) collective-permute-start(f32[256,1024]{1,0:T(8,128)} %get-tuple-element.559), channel_id=1, source_target_pairs={{0,8},{4,12},{8,0},{12,4},{16,24},{20,28},{24,16},{28,20},{1,9},{5... | collective-permute-start | bytes 3145736 | tf_op jit(solution)/shard_map/ppermute | solution.py:62
  229.0 73.4 %collective-permute-start.31 = (f32[256,1024]{1,0:T(8,128)}, f32[256,1024]{1,0:T(8,128)}, u32[]{:S(2)}, u32[]{:S(2)}) collective-permute-start(f32[256,1024]{1,0:T(8,128)} %get-tuple-element.580), channel_id=1, source_target_pairs={{0,16},{4,20},{8,24},{12,28},{16,0},{20,4},{24,8},{28,12},{1,17},{... | collective-permute-start | bytes 3145736 | tf_op jit(solution)/shard_map/ppermute | solution.py:62
  260.8 3.9 collective-permute-start.26
  263.0 79.0 %collective-permute-start.34 = (f32[512,1024]{1,0:T(8,128)}, f32[512,1024]{1,0:T(8,128)}, u32[]{:S(2)}, u32[]{:S(2)}) collective-permute-start(f32[512,1024]{1,0:T(8,128)} %product_rows.19), channel_id=1, source_target_pairs={{0,4},{4,0},{8,12},{12,8},{16,20},{20,16},{24,28},{28,24},{1,5},{5... | collective-permute-start | bytes 6291464 | tf_op jit(solution)/shard_map/ppermute | solution.py:62
  275.4 19.2 %collective-permute-start.27 = (f32[192,1024]{1,0:T(8,128)}, f32[192,1024]{1,0:T(8,128)}, u32[]{:S(2)}, u32[]{:S(2)}) collective-permute-start(f32[192,1024]{1,0:T(8,128)} %add_rows.15.mine_ref), channel_id=1, source_target_pairs={{0,2},{1,3},{2,0},{3,1},{4,6},{5,7},{6,4},{7,5},{8,10},{9,11},{10,... | collective-permute-start | bytes 2359304 | tf_op jit(solution)/shard_map/ppermute | solution.py:62
  278.2 39.8 %collective-permute-start.36 = (f32[128,1024]{1,0:T(8,128)}, f32[128,1024]{1,0:T(8,128)}, u32[]{:S(2)}, u32[]{:S(2)}) collective-permute-start(f32[128,1024]{1,0:T(8,128)} %get-tuple-element.606), channel_id=1, source_target_pairs={{0,16},{4,20},{8,24},{12,28},{16,0},{20,4},{24,8},{28,12},{1,17},{... | collective-permute-start | bytes 1572872 | tf_op jit(solution)/shard_map/ppermute | solution.py:62
  314.2 25.5 %collective-permute-start.35 = (f32[256,1024]{1,0:T(8,128)}, f32[256,1024]{1,0:T(8,128)}, u32[]{:S(2)}, u32[]{:S(2)}) collective-permute-start(f32[256,1024]{1,0:T(8,128)} %get-tuple-element.603), channel_id=1, source_target_pairs={{0,8},{4,12},{8,0},{12,4},{16,24},{20,28},{24,16},{28,20},{1,9},{5... | collective-permute-start | bytes 3145736 | tf_op jit(solution)/shard_map/ppermute | solution.py:62
  314.2 45.2 %collective-permute-start.38 = (f32[128,1024]{1,0:T(8,128)}, f32[128,1024]{1,0:T(8,128)}, u32[]{:S(2)}, u32[]{:S(2)}) collective-permute-start(f32[128,1024]{1,0:T(8,128)} %get-tuple-element.638), channel_id=1, source_target_pairs={{0,4},{4,0},{8,12},{12,8},{16,20},{20,16},{24,28},{28,24},{1,5},{5... | collective-permute-start | bytes 1572872 | tf_op jit(solution)/shard_map/ppermute | solution.py:62
  321.1 28.4 %collective-permute-start.33 = (f32[192,1024]{1,0:T(8,128)}, f32[192,1024]{1,0:T(8,128)}, u32[]{:S(2)}, u32[]{:S(2)}) collective-permute-start(f32[192,1024]{1,0:T(8,128)} %add_rows.16.mine_ref), channel_id=1, source_target_pairs={{0,2},{1,3},{2,0},{3,1},{4,6},{5,7},{6,4},{7,5},{8,10},{9,11},{10,... | collective-permute-start | bytes 2359304 | tf_op jit(solution)/shard_map/ppermute | solution.py:62
  321.5 72.4 %collective-permute-start.42 = (f32[512,1024]{1,0:T(8,128)}, f32[512,1024]{1,0:T(8,128)}, u32[]{:S(2)}, u32[]{:S(2)}) collective-permute-start(f32[512,1024]{1,0:T(8,128)} %product_rows.21), channel_id=1, source_target_pairs={{0,4},{4,0},{8,12},{12,8},{16,20},{20,16},{24,28},{28,24},{1,5},{5... | collective-permute-start | bytes 6291464 | tf_op jit(solution)/shard_map/ppermute | solution.py:62
  346.4 44.0 %collective-permute-start.44 = (f32[256,1024]{1,0:T(8,128)}, f32[256,1024]{1,0:T(8,128)}, u32[]{:S(2)}, u32[]{:S(2)}) collective-permute-start(f32[256,1024]{1,0:T(8,128)} %get-tuple-element.687), channel_id=1, source_target_pairs={{0,8},{4,12},{8,0},{12,4},{16,24},{20,28},{24,16},{28,20},{1,9},{5... | collective-permute-start | bytes 3145736 | tf_op jit(solution)/shard_map/ppermute | solution.py:62
  346.7 46.0 %collective-permute-start.43 = (f32[128,1024]{1,0:T(8,128)}, f32[128,1024]{1,0:T(8,128)}, u32[]{:S(2)}, u32[]{:S(2)}) collective-permute-start(f32[128,1024]{1,0:T(8,128)} %get-tuple-element.685), channel_id=1, source_target_pairs={{0,16},{4,20},{8,24},{12,28},{16,0},{20,4},{24,8},{28,12},{1,17},{... | collective-permute-start | bytes 1572872 | tf_op jit(solution)/shard_map/ppermute | solution.py:62
  376.2 10.4 %collective-permute-start.39 = (f32[512,896]{1,0:T(8,128)}, f32[512,896]{1,0:T(8,128)}, u32[]{:S(2)}, u32[]{:S(2)}) collective-permute-start(f32[512,896]{1,0:T(8,128)} %get-tuple-element.670), channel_id=1, source_target_pairs={{0,1},{1,0},{2,3},{3,2},{4,5},{5,4},{6,7},{7,6},{8,9},{9,8},{10,11... | collective-permute-start | bytes 5505032 | tf_op jit(solution)/shard_map/ppermute | solution.py:62
  381.9 56.2 %collective-permute-start.47 = (f32[512,1024]{1,0:T(8,128)}, f32[512,1024]{1,0:T(8,128)}, u32[]{:S(2)}, u32[]{:S(2)}) collective-permute-start(f32[512,1024]{1,0:T(8,128)} %product_rows.23), channel_id=1, source_target_pairs={{0,4},{4,0},{8,12},{12,8},{16,20},{20,16},{24,28},{28,24},{1,5},{5... | collective-permute-start | bytes 6291464 | tf_op jit(solution)/shard_map/ppermute | solution.py:62
  393.9 7.0 %collective-permute-start.41 = (f32[14,1024]{1,0:T(8,128)}, f32[14,1024]{1,0:T(8,128)}, u32[]{:S(2)}, u32[]{:S(2)}) collective-permute-start(f32[14,1024]{1,0:T(8,128)} %broadcast_multiply_fusion.1), channel_id=1, source_target_pairs={{0,1},{1,0},{2,3},{3,2},{4,5},{5,4},{6,7},{7,6},{8,9},{9,8},{10,11... | collective-permute-start | bytes 172040 | tf_op jit(solution)/shard_map/ppermute | solution.py:62
  394.0 23.1 %collective-permute-start.40 = (f32[256,896]{1,0:T(8,128)}, f32[256,896]{1,0:T(8,128)}, u32[]{:S(2)}, u32[]{:S(2)}) collective-permute-start(f32[256,896]{1,0:T(8,128)} %get-tuple-element.676), channel_id=1, source_target_pairs={{0,2},{1,3},{2,0},{3,1},{4,6},{5,7},{6,4},{7,5},{8,10},{9,11},{10,... | collective-permute-start | bytes 2752520 | tf_op jit(solution)/shard_map/ppermute | solution.py:62
  399.0 31.8 %collective-permute-start.49 = (f32[128,1024]{1,0:T(8,128)}, f32[128,1024]{1,0:T(8,128)}, u32[]{:S(2)}, u32[]{:S(2)}) collective-permute-start(f32[128,1024]{1,0:T(8,128)} %get-tuple-element.726), channel_id=1, source_target_pairs={{0,16},{4,20},{8,24},{12,28},{16,0},{20,4},{24,8},{28,12},{1,17},{... | collective-permute-start | bytes 1572872 | tf_op jit(solution)/shard_map/ppermute | solution.py:62
  399.2 36.6 %collective-permute-start.48 = (f32[256,1024]{1,0:T(8,128)}, f32[256,1024]{1,0:T(8,128)}, u32[]{:S(2)}, u32[]{:S(2)}) collective-permute-start(f32[256,1024]{1,0:T(8,128)} %get-tuple-element.724), channel_id=1, source_target_pairs={{0,8},{4,12},{8,0},{12,4},{16,24},{20,28},{24,16},{28,20},{1,9},{5... | collective-permute-start | bytes 3145736 | tf_op jit(solution)/shard_map/ppermute | solution.py:62
  423.1 31.8 %collective-permute-start.54 = (f32[4,440,128]{2,1,0:T(8,128)}, f32[4,440,128]{2,1,0:T(8,128)}, u32[]{:S(2)}, u32[]{:S(2)}) collective-permute-start(f32[4,440,128]{2,1,0:T(8,128)} %bitcast.149), channel_id=1, source_target_pairs={{0,4},{4,0},{8,12},{12,8},{16,20},{20,16},{24,28},{28,24},{1,5},{5... | collective-permute-start | bytes 2703368 | tf_op jit(solution)/shard_map/ppermute | solution.py:62
  438.1 14.7 %collective-permute-start.46 = (f32[192,768]{1,0:T(8,128)}, f32[192,768]{1,0:T(8,128)}, u32[]{:S(2)}, u32[]{:S(2)}) collective-permute-start(f32[192,768]{1,0:T(8,128)} %add_rows.17), channel_id=1, source_target_pairs={{0,2},{1,3},{2,0},{3,1},{4,6},{5,7},{6,4},{7,5},{8,10},{9,11},{10,... | collective-permute-start | bytes 1769480 | tf_op jit(solution)/shard_map/ppermute | solution.py:62
  442.9 25.2 %collective-permute-start.53 = (f32[128,1024]{1,0:T(8,128)}, f32[128,1024]{1,0:T(8,128)}, u32[]{:S(2)}, u32[]{:S(2)}) collective-permute-start(f32[128,1024]{1,0:T(8,128)} %get-tuple-element.753), channel_id=1, source_target_pairs={{0,16},{4,20},{8,24},{12,28},{16,0},{20,4},{24,8},{28,12},{1,17},{... | collective-permute-start | bytes 1572872 | tf_op jit(solution)/shard_map/ppermute | solution.py:62
  444.1 27.5 %collective-permute-start.52 = (f32[512,512]{1,0:T(8,128)}, f32[512,512]{1,0:T(8,128)}, u32[]{:S(2)}, u32[]{:S(2)}) collective-permute-start(f32[512,512]{1,0:T(8,128)} %product_rows.25), channel_id=1, source_target_pairs={{0,4},{4,0},{8,12},{12,8},{16,20},{20,16},{24,28},{28,24},{1,5},{5... | collective-permute-start | bytes 3145736 | tf_op jit(solution)/shard_map/ppermute | solution.py:62
  444.6 37.5 %collective-permute-start.51 = (f32[256,1024]{1,0:T(8,128)}, f32[256,1024]{1,0:T(8,128)}, u32[]{:S(2)}, u32[]{:S(2)}) collective-permute-start(f32[256,1024]{1,0:T(8,128)} %get-tuple-element.750), channel_id=1, source_target_pairs={{0,8},{4,12},{8,0},{12,4},{16,24},{20,28},{24,16},{28,20},{1,9},{5... | collective-permute-start | bytes 3145736 | tf_op jit(solution)/shard_map/ppermute | solution.py:62
  469.3 17.0 %collective-permute-start.50 = (f32[192,768]{1,0:T(8,128)}, f32[192,768]{1,0:T(8,128)}, u32[]{:S(2)}, u32[]{:S(2)}) collective-permute-start(f32[192,768]{1,0:T(8,128)} %add.275), channel_id=1, source_target_pairs={{0,1},{1,0},{2,3},{3,2},{4,5},{5,4},{6,7},{7,6},{8,9},{9,8},{10,11... | collective-permute-start | bytes 1769480 | tf_op jit(solution)/shard_map/ppermute | solution.py:62
  469.4 28.5 %collective-permute-start.55 = (f32[2,440,128]{2,1,0:T(8,128)}, f32[2,440,128]{2,1,0:T(8,128)}, u32[]{:S(2)}, u32[]{:S(2)}) collective-permute-start(f32[2,440,128]{2,1,0:T(8,128)} %dynamic-slice_bitcast_fusion), channel_id=1, source_target_pairs={{0,8},{4,12},{8,0},{12,4},{16,24},{20,28},{24,16},{28,20},{1,9},{5... | collective-permute-start | bytes 1351688 | tf_op jit(solution)/shard_map/ppermute | solution.py:62
  484.2 23.9 %collective-permute-start.58 = (f32[128,1024]{1,0:T(8,128)}, f32[128,1024]{1,0:T(8,128)}, u32[]{:S(2)}, u32[]{:S(2)}) collective-permute-start(f32[128,1024]{1,0:T(8,128)} %get-tuple-element.785), channel_id=1, source_target_pairs={{0,16},{4,20},{8,24},{12,28},{16,0},{20,4},{24,8},{28,12},{1,17},{... | collective-permute-start | bytes 1572872 | tf_op jit(solution)/shard_map/ppermute | solution.py:62
  484.2 32.3 %collective-permute-start.57 = (f32[256,512]{1,0:T(8,128)}, f32[256,512]{1,0:T(8,128)}, u32[]{:S(2)}, u32[]{:S(2)}) collective-permute-start(f32[256,512]{1,0:T(8,128)} %get-tuple-element.783), channel_id=1, source_target_pairs={{0,8},{4,12},{8,0},{12,4},{16,24},{20,28},{24,16},{28,20},{1,9},{5... | collective-permute-start | bytes 1572872 | tf_op jit(solution)/shard_map/ppermute | solution.py:62
  499.8 17.9 %collective-permute-start.56 = (f32[1,440,128]{2,1,0:T(8,128)}, f32[1,440,128]{2,1,0:T(8,128)}, u32[]{:S(2)}, u32[]{:S(2)}) collective-permute-start(f32[1,440,128]{2,1,0:T(8,128)} %constant_dynamic-slice_fusion), channel_id=1, source_target_pairs={{0,16},{4,20},{8,24},{12,28},{16,0},{20,4},{24,8},{28,12},{1,17},{... | collective-permute-start | bytes 675848 | tf_op jit(solution)/shard_map/ppermute | solution.py:62
  521.1 11.7 %collective-permute-start.60 = (f32[128,512]{1,0:T(8,128)S(1)}, f32[128,512]{1,0:T(8,128)S(1)}, u32[]{:S(2)}, u32[]{:S(2)}) collective-permute-start(f32[128,512]{1,0:T(8,128)S(1)} %get-tuple-element.800), channel_id=1, source_target_pairs={{0,16},{4,20},{8,24},{12,28},{16,0},{20,4},{24,8},{28,12},{1,17},{... | collective-permute-start | bytes 786440 | tf_op jit(solution)/shard_map/ppermute | solution.py:62
  522.0 4.4 collective-permute-start.59
  (202 other events, 1049.1 us)

commit v8 on v7

--- a/solution.py
+++ b/solution.py
@@ -9,8 +9,7 @@
 
 HEAD_DIM = 64
 PLAN = {
-    ("top", 0): [("down", 0)],
-    ("pre", 0): [("up", 0)],
+    ("pre", 0): [("up", 0), ("down", 0)],
     ("core_one", 0): [("att", 0)],
     ("wait_one", 0): [("down", 0), ("up", 0)],
     ("core_two", 1): [("down", 1)],
@@ -243,7 +242,7 @@
     )(mine, got, unit, inverse, gains, grad)
 
 
-def feed_forward(unit_own, unit_other, gains, biases, place, up_weight, up_bias, down_weight, shards):
+def feed_forward(unit_own, unit_other, gains, biases, place, up_weight, up_bias, down_weight, shards, with_down):
     half, width = unit_own.shape
     rows = 2 * half
     layer, which = place
@@ -256,7 +255,9 @@
     shard = width // count
 
     def kernel(shards_ref, own_ref, other_ref, gain_ref, bias_ref, up_ref, up_bias_ref, down_ref,
-               activation_out, slope_out, own_out, send_out, ordered_out, normed_ref):
+               activation_out, slope_out, *refs):
+        *parts, ordered_out, normed_ref = refs
+        own_out, send_out = parts if with_down else (None, None)
         step = pl.program_id(0)
 
         @pl.when(step == 0)
@@ -265,8 +266,9 @@
             bias = bias_ref[layer, which : which + 1]
             normed_ref[:half] = (own_ref[...] * gain + bias).astype(BF)
             normed_ref[half:] = (other_ref[...] * gain + bias).astype(BF)
-            own_out[...] = jnp.zeros_like(own_out)
-            send_out[...] = jnp.zeros_like(send_out)
+            if with_down:
+                own_out[...] = jnp.zeros_like(own_out)
+                send_out[...] = jnp.zeros_like(send_out)
             if shard % 128:
                 ordered_out[...] = normed_ref[...]
             else:
@@ -277,8 +279,9 @@
         slope_out[...] = below + pre * (jnp.exp(-0.5 * pre * pre) * peak)
         activation = (pre * below).astype(BF)
         activation_out[...] = activation
-        send_out[...] += matmul(activation[half:], down_ref[0])
-        own_out[...] += matmul(activation[:half], down_ref[0])
+        if with_down:
+            send_out[...] += matmul(activation[half:], down_ref[0])
+            own_out[...] += matmul(activation[:half], down_ref[0])
 
     piece = jax.ShapeDtypeStruct((half, width), F32)
     whole = pl.BlockSpec((half, width), lambda j: (0, 0))
@@ -287,8 +290,7 @@
         out_shape=(
             jax.ShapeDtypeStruct((rows, hidden), BF),
             jax.ShapeDtypeStruct((rows, hidden), F32),
-            piece,
-            piece,
+            *([piece, piece] if with_down else []),
             jax.ShapeDtypeStruct((rows, width), BF),
         ),
         grid=(hidden // size,),
@@ -305,8 +307,7 @@
         out_specs=(
             pl.BlockSpec((rows, size), lambda j: (0, j)),
             pl.BlockSpec((rows, size), lambda j: (0, j)),
-            whole,
-            whole,
+            *([whole, whole] if with_down else []),
             pl.BlockSpec((rows, width), lambda j: (0, 0)),
         ),
         scratch_shapes=[pltpu.VMEM((rows, width), BF)],
@@ -316,7 +317,7 @@
     )(shards, unit_own, unit_other, gains, biases, up_weight, up_bias, down_weight)
 
 
-def feed_back(low, slope, down_weight, up_weight, layer):
+def feed_back(low, slope, down_weight, up_weight, layer, stream):
     rows, width = low.shape
     half = rows // 2
     hidden = slope.shape[1]
@@ -359,7 +360,7 @@
             whole,
         ),
         cost_estimate=LONG,
-        compiler_params=vmem_limit(26 * rows * width),
+        compiler_params=vmem_limit((44 << 20) if stream else 26 * rows * width),
         name="feed_back",
     )(low, slope, down_weight, up_weight)
 
@@ -1116,7 +1117,7 @@
             hidden = hidden + (mine + got) + output_bias[layer]
             unit_two, inverse_two = norm_parts(hidden)
             unit_other = links.other_rows(unit_two)
-            activation, slope, part_own, part_send, normed_two = feed_forward(
+            activation, slope, *parts, normed_two = feed_forward(
                 unit_two,
                 unit_other,
                 norm_gain,
@@ -1126,11 +1127,12 @@
                 up_bias,
                 down_weight,
                 shards,
+                layer < top,
             )
             if shard % 128:
                 normed_two = take_columns(normed_two, shards, shard)
             if layer < top:
-                mine, got = links.begin_sum(part_own, part_send)
+                mine, got = links.begin_sum(*parts)
             if layer < top:
                 if layer == 0:
                     mine, embed_late, key_late = lax.optimization_barrier(
@@ -1179,7 +1181,7 @@
                 )
             )
 
-        last_own, last_send = part_own, part_send
+        activation_top = activation
         row_sums = {}
         local_sums = {}
         merges = {}
@@ -1216,11 +1218,8 @@
                 links, [(down_left, activation)], bits if depth else bits_late
             )
             advance(("top", depth))
-            if layer == top:
-                last_send = clock.one(last_send)
-                last_other = exchange(last_send, "mp", mp, 0)
             pre_low, up_sums, part_own, part_send = feed_back(
-                clock.one(down_low), slope, down_weight, up_weight, layer
+                clock.one(down_low), slope, down_weight, up_weight, layer, layer == top
             )
             local_sums["up_bias", layer] = up_sums[0]
             pre_low, part_send = clock.both(pre_low, part_send)
@@ -1231,6 +1230,13 @@
                 clock.hold()
             advance(("wait_two", depth))
             if layer == top:
+                half = row_count // 2
+                activation_top = clock.one(activation_top)
+                last_send = clock.one(matmul(activation_top[half:], down_weight[top]))
+                last_other = exchange(last_send, "mp", mp, 0)
+                last_own = matmul(activation_top[:half], down_weight[top])
+                last_own = clock.one(last_own)
+                clock.hold()
                 last_mine = clock.one(last_own + clock.one(last_other))
             mine, got = clock.both(mine, got)
             if layer == top:

time: 543 us -> 539 us (level)
    unnamed x400 -> x390, local copies, waits for them, and re-layouts: 42.4 us -> 41.5 us
where the time goes in v8:
time: 539 us; the launch traced here: 532 us
  waiting for transfers between devices  208 us (39%)
  Pallas kernels  161 us (30%)
  local copies, waits for them, and re-layouts  63.8 us (12%)
  starting transfers between devices  50.1 us (9%)
  other arithmetic  40.6 us (8%)
  between operations  5.52 us (1%)
    ppermute x61, waiting for transfers between devices, exchange(): return lax.ppermute(tensor, axis, [(i, i ^ 1 << bit) for i in range(size)])  208 us
    ppermute x61, starting transfers between devices, exchange(): return lax.ppermute(tensor, axis, [(i, i ^ 1 << bit) for i in range(size)])  50.1 us
    unnamed x390, local copies, waits for them, and re-layouts  41.5 us
    pallas_call x14, Pallas kernels, product_rows(): pl.pallas_call(kernel, out_shape=out_shape, grid=(count,), in_specs=in_sp...  37.5 us
    pallas_call x8, Pallas kernels, add_split(): pl.pallas_call(kernel, out_shape=[jax.ShapeDtypeStruct((half, width), F32...  18.4 us
    pallas_call x2, Pallas kernels, feed_forward(): pl.pallas_call(kernel, out_shape=(jax.ShapeDtypeStruct((rows, hidden), BF...  14.4 us
    pallas_call x2, Pallas kernels, feed_back(): pl.pallas_call(kernel, out_shape=(jax.ShapeDtypeStruct((rows, hidden), BF...  13.8 us
    pallas_call x9, Pallas kernels, add_rows(): pl.pallas_call(kernel, out_shape=jax.ShapeDtypeStruct((rows, width), F32)...  12.9 us
  transfers between devices with their start and end apart: 61, of which 37 were waited for; matrix products, arithmetic and copies ran while one was open for 11% of the time, Pallas kernels for 21%

profile of v8, /device:TPU:0, one launch (start us, length us, event | category | flops | bytes accessed | tf_op | source)
XLA Modules:
  0.0 532.2 jit_solution(2437284655167881298)
XLA Ops:
  2.6 10.2 %pool_front.1 = (bf16[384,768]{1,0:T(8,128)(2,1)}, f32[1,256]{1,0:T(1,128)}, f32[4,1024]{1,0:T(4,128)}, f32[4,768]{1,0:T(4,128)}, bf16[768,256]{1,0:T(8,128)(2,1...) custom-call(s32[1]{0:T(128)} %bitcast.core_ref, ...), custom_call_target="tpu_custom_call" | custom-call | flops 999999995904 | bytes 8 | tf_op jit(solution)/shard_map/pool_front/pallas_call | solution.py:778
  17.0 2.9 collective-permute-start.4
  27.1 2.6 collective-permute-start.3
  31.6 6.1 %collective-permute-done.4 = f32[192,1024]{1,0:T(8,128)S(1)} collective-permute-done((f32[192,1024]{1,0:T(8,128)S(1)}, f32[192,1024]{1,0:T(8,128)S(1)}, u32[]{:S(2)}, u32[]{:S(2)}) %collective-permute-start.4) | collective-permute-done | bytes 786464 | tf_op jit(solution)/shard_map/ppermute | solution.py:61
  42.8 3.9 attend_forward.2
  60.0 12.6 %collective-permute-done.7 = f32[192,1024]{1,0:T(8,128)} collective-permute-done((f32[192,1024]{1,0:T(8,128)}, f32[192,1024]{1,0:T(8,128)}, u32[]{:S(2)}, u32[]{:S(2)}) %collective-permute-start.7) | collective-permute-done | bytes 786464 | tf_op jit(solution)/shard_map/ppermute | solution.py:61
  77.9 8.3 %feed_forward.2 = (bf16[384,1024]{1,0:T(8,128)(2,1)}, f32[384,1024]{1,0:T(8,128)}, f32[192,1024]{1,0:T(8,128)}, f32[192,1024]{1,0:T(8,128)}, bf16[384,1024]{1,0:T(8,128)(2,1)}) custom-call(s32[8]{0:T(128)} %copy-done.35, f32[192,1024]{1,0:T(8,128)} %copy-done.16, f32[192,1024]{1,0:T(8,128)} %copy-done.180, f32[2,2,1024]{2,1,0:T(2,128)} %gain_ref.11, ...), custom_call_target="tpu_custom_call" | custom-call | flops 999999995904 | bytes 8 | tf_op jit(solution)/shard_map/feed_forward/pallas_call | solution.py:288
  99.4 12.6 %collective-permute-done.10 = f32[192,1024]{1,0:T(8,128)} collective-permute-done((f32[192,1024]{1,0:T(8,128)S(1)}, f32[192,1024]{1,0:T(8,128)}, u32[]{:S(2)}, u32[]{:S(2)}) %collective-permute-start.10) | collective-permute-done | bytes 786464 | tf_op jit(solution)/shard_map/ppermute | solution.py:61
  116.2 3.1 attend_forward.3
  125.6 15.9 %collective-permute-done.13 = f32[192,1024]{1,0:T(8,128)S(1)} collective-permute-done((f32[192,1024]{1,0:T(8,128)S(1)}, f32[192,1024]{1,0:T(8,128)S(1)}, u32[]{:S(2)}, u32[]{:S(2)}) %collective-permute-start.13) | collective-permute-done | bytes 786464 | tf_op jit(solution)/shard_map/ppermute | solution.py:61
  145.7 6.1 %feed_forward.3 = (bf16[384,1024]{1,0:T(8,128)(2,1)}, f32[384,1024]{1,0:T(8,128)}, bf16[384,1024]{1,0:T(8,128)(2,1)}) custom-call(s32[8]{0:T(128)} %copy-done.35, f32[192,1024]{1,0:T(8,128)} %copy-done.18, f32[192,1024]{1,0:T(8,128)} %collective-permute-done.14.other_ref, f32[2,2,1024]{2,1,0:T(2,128)} %gain_ref.11, f32[2,2,1024]{2,1,0:T(2,128)} %bias_ref.3, ...), custom_call_target="tpu_custom_call" | custom-call | flops 999999995904 | bytes 8 | tf_op jit(solution)/shard_map/feed_forward/pallas_call | solution.py:288
  151.8 7.7 %feed_back.2 = (bf16[384,1024]{1,0:T(8,128)(2,1)}, f32[1,1024]{1,0:T(1,128)}, f32[192,1024]{1,0:T(8,128)}, f32[192,1024]{1,0:T(8,128)}) custom-call(bf16[384,1024]{1,0:T(8,128)(2,1)} %copy-done.76, f32[384,1024]{1,0:T(8,128)} %get-tuple-element.449.slope_ref, bf16[2,1024,1024]{2,1,0:T(8,128)(2,1)} %down_ref.7, bf16[2,1024,1024]{2,1,0:T(8,128)(2,1)} %up_ref.7), custom_call_target="tpu_custom_call" | custom-call | flops 999999995904 | bytes 8 | tf_op jit(solution)/shard_map/feed_back/pallas_call | solution.py:341
  180.3 15.5 %collective-permute-done.17.got_ref = f32[192,1024]{1,0:T(8,128)} collective-permute-done((f32[192,1024]{1,0:T(8,128)}, f32[192,1024]{1,0:T(8,128)}, u32[]{:S(2)}, u32[]{:S(2)}) %collective-permute-start.17) | collective-permute-done | bytes 786464 | tf_op jit(solution)/shard_map/ppermute | solution.py:61
  196.0 2.8 norm_back.4
  203.0 4.9 attend_back.2
  213.2 3.3 product_rows.17
  216.5 3.3 product_rows.18
  219.8 2.5 add_add_fusion
  225.4 2.6 collective-permute-start.31
  231.0 11.6 %collective-permute-done.24.got_ref = f32[192,1024]{1,0:T(8,128)} collective-permute-done((f32[192,1024]{1,0:T(8,128)}, f32[192,1024]{1,0:T(8,128)}, u32[]{:S(2)}, u32[]{:S(2)}) %collective-permute-start.24) | collective-permute-done | bytes 786464 | tf_op jit(solution)/shard_map/ppermute | solution.py:61
  242.7 2.8 norm_back.5
  252.2 6.1 %feed_back.3 = (bf16[384,1024]{1,0:T(8,128)(2,1)S(1)}, f32[1,1024]{1,0:T(1,128)S(1)}, f32[192,1024]{1,0:T(8,128)S(1)}, f32[192,1024]{1,0:T(8,128)}) custom-call(bf16[384,1024]{1,0:T(8,128)(2,1)S(1)} %get-tuple-element.544.low_ref, f32[384,1024]{1,0:T(8,128)S(1)} %copy-done.69, bf16[2,1024,1024]{2,1,0:T(8,128)(2,1)S(1)} %copy-done.46, ...), custom_call_target="tpu_custom_call" | custom-call | flops 999999995904 | bytes 8 | tf_op jit(solution)/shard_map/feed_back/pallas_call | solution.py:341
  264.0 7.8 %collective-permute-done.28.got_ref = f32[256,1024]{1,0:T(8,128)} collective-permute-done((f32[256,1024]{1,0:T(8,128)}, f32[256,1024]{1,0:T(8,128)}, u32[]{:S(2)}, u32[]{:S(2)}) %collective-permute-start.28) | collective-permute-done | bytes 1048608 | tf_op jit(solution)/shard_map/ppermute | solution.py:61
  275.4 15.6 %collective-permute-done.27.got_ref = f32[192,1024]{1,0:T(8,128)} collective-permute-done((f32[192,1024]{1,0:T(8,128)}, f32[192,1024]{1,0:T(8,128)}, u32[]{:S(2)}, u32[]{:S(2)}) %collective-permute-start.27) | collective-permute-done | bytes 786464 | tf_op jit(solution)/shard_map/ppermute | solution.py:61
  291.0 2.8 norm_back.6
  301.3 3.4 product_rows.20
  304.8 4.9 attend_back.3
  319.6 16.5 %collective-permute-done.35.got_ref = f32[256,1024]{1,0:T(8,128)} collective-permute-done((f32[256,1024]{1,0:T(8,128)}, f32[256,1024]{1,0:T(8,128)}, u32[]{:S(2)}, u32[]{:S(2)}) %collective-permute-start.35) | collective-permute-done | bytes 1048608 | tf_op jit(solution)/shard_map/ppermute | solution.py:61
  338.1 3.5 product_rows.22
  342.9 2.8 collective-permute-start.43
  345.7 2.8 norm_back.7
  360.6 8.9 %pool_back.1 = (f32[816,256]{1,0:T(8,128)S(1)}, f32[4,768]{1,0:T(4,128)S(1)}, f32[4,48]{1,0:T(4,128)S(1)}, f32[192,768]{1,0:T(8,128)S(1)}, f32[192,768]{1,0:T(8,128)}) custom-call(bf16[384,1024]{1,0:T(8,128)(2,1)S(1)} %get-tuple-element.655.low_ref, bf16[256,1024]{1,0:T(8,128)(2,1)S(1)} %copy-done.53, bf16[768,256]{1,0:T(8,128)(2,1)S(1)} %copy-done.114, ...), custom_call_target="tpu_custom_call" | custom-call | flops 999999995904 | bytes 8 | tf_op jit(solution)/shard_map/pool_back/pallas_call | solution.py:845
  369.5 2.8 embed_terms.1
  382.8 3.8 add_split.11
  390.7 3.4 product_rows.24
  400.3 12.8 %collective-permute-done.40 = f32[256,896]{1,0:T(8,128)} collective-permute-done((f32[256,896]{1,0:T(8,128)}, f32[256,896]{1,0:T(8,128)}, u32[]{:S(2)}, u32[]{:S(2)}) %collective-permute-start.40) | collective-permute-done | bytes 917536 | tf_op jit(solution)/shard_map/ppermute | solution.py:61
  415.6 2.6 constant_dynamic-slice_fusion.1
  428.0 3.9 collective-permute-done.48.got_ref
  435.7 3.3 product_rows.26
  443.7 5.2 collective-permute-done.46
  454.6 9.6 %collective-permute-done.53 = f32[128,1024]{1,0:T(8,128)} collective-permute-done((f32[128,1024]{1,0:T(8,128)}, f32[128,1024]{1,0:T(8,128)}, u32[]{:S(2)}, u32[]{:S(2)}) %collective-permute-start.53) | collective-permute-done | bytes 524320 | tf_op jit(solution)/shard_map/ppermute | solution.py:61
  467.8 2.9 product_rows.27
  470.6 7.5 %collective-permute-done.51.got_ref = f32[256,1024]{1,0:T(8,128)} collective-permute-done((f32[256,1024]{1,0:T(8,128)}, f32[256,1024]{1,0:T(8,128)}, u32[]{:S(2)}, u32[]{:S(2)}) %collective-permute-start.51) | collective-permute-done | bytes 1048608 | tf_op jit(solution)/shard_map/ppermute | solution.py:61
  484.8 2.7 copy.79
  487.5 6.5 %collective-permute-done.55 = f32[2,440,128]{2,1,0:T(8,128)} collective-permute-done((f32[2,440,128]{2,1,0:T(8,128)}, f32[2,440,128]{2,1,0:T(8,128)}, u32[]{:S(2)}, u32[]{:S(2)}) %collective-permute-start.55) | collective-permute-done | bytes 450592 | tf_op jit(solution)/shard_map/ppermute | solution.py:61
  495.9 8.3 %collective-permute-done.58 = f32[128,1024]{1,0:T(8,128)} collective-permute-done((f32[128,1024]{1,0:T(8,128)}, f32[128,1024]{1,0:T(8,128)}, u32[]{:S(2)}, u32[]{:S(2)}) %collective-permute-start.58) | collective-permute-done | bytes 524320 | tf_op jit(solution)/shard_map/ppermute | solution.py:61
  505.2 7.4 %collective-permute-done.57.got_ref = f32[256,512]{1,0:T(8,128)} collective-permute-done((f32[256,512]{1,0:T(8,128)}, f32[256,512]{1,0:T(8,128)}, u32[]{:S(2)}, u32[]{:S(2)}) %collective-permute-start.57) | collective-permute-done | bytes 524320 | tf_op jit(solution)/shard_map/ppermute | solution.py:61
  523.2 5.8 %collective-permute-done.60 = f32[128,512]{1,0:T(8,128)S(1)} collective-permute-done((f32[128,512]{1,0:T(8,128)S(1)}, f32[128,512]{1,0:T(8,128)S(1)}, u32[]{:S(2)}, u32[]{:S(2)}) %collective-permute-start.60) | collective-permute-done | bytes 262176 | tf_op jit(solution)/shard_map/ppermute | solution.py:61
  (660 shorter events, 222.1 us)
Async XLA Ops:
  12.8 2.6 collective-permute-start
  17.0 20.8 %collective-permute-start.4 = (f32[192,1024]{1,0:T(8,128)S(1)}, f32[192,1024]{1,0:T(8,128)S(1)}, u32[]{:S(2)}, u32[]{:S(2)}) collective-permute-start(f32[192,1024]{1,0:T(8,128)S(1)} %add_rows.9), channel_id=1, source_target_pairs={{0,2},{1,3},{2,0},{3,1},{4,6},{5,7},{6,4},{7,5},{8,10},{9,11},{10,... | collective-permute-start | bytes 2359304 | tf_op jit(solution)/shard_map/ppermute | solution.py:61
  19.9 3.6 collective-permute-start.1
  23.5 3.6 collective-permute-start.2
  27.1 4.5 collective-permute-start.3
  48.0 2.6 collective-permute-start.6
  52.7 19.9 %collective-permute-start.7 = (f32[192,1024]{1,0:T(8,128)}, f32[192,1024]{1,0:T(8,128)}, u32[]{:S(2)}, u32[]{:S(2)}) collective-permute-start(f32[192,1024]{1,0:T(8,128)} %add_rows.10), channel_id=1, source_target_pairs={{0,2},{1,3},{2,0},{3,1},{4,6},{5,7},{6,4},{7,5},{8,10},{9,11},{10,... | collective-permute-start | bytes 2359304 | tf_op jit(solution)/shard_map/ppermute | solution.py:61
  92.3 19.8 %collective-permute-start.10 = (f32[192,1024]{1,0:T(8,128)S(1)}, f32[192,1024]{1,0:T(8,128)}, u32[]{:S(2)}, u32[]{:S(2)}) collective-permute-start(f32[192,1024]{1,0:T(8,128)S(1)} %add_rows.11), channel_id=1, source_target_pairs={{0,2},{1,3},{2,0},{3,1},{4,6},{5,7},{6,4},{7,5},{8,10},{9,11},{10,... | collective-permute-start | bytes 2359304 | tf_op jit(solution)/shard_map/ppermute | solution.py:61
  121.9 19.7 %collective-permute-start.13 = (f32[192,1024]{1,0:T(8,128)S(1)}, f32[192,1024]{1,0:T(8,128)S(1)}, u32[]{:S(2)}, u32[]{:S(2)}) collective-permute-start(f32[192,1024]{1,0:T(8,128)S(1)} %add_rows.12), channel_id=1, source_target_pairs={{0,2},{1,3},{2,0},{3,1},{4,6},{5,7},{6,4},{7,5},{8,10},{9,11},{10,... | collective-permute-start | bytes 2359304 | tf_op jit(solution)/shard_map/ppermute | solution.py:61
  164.6 3.5 collective-permute-start.15
  164.7 48.4 %collective-permute-start.20 = (f32[512,1024]{1,0:T(8,128)}, f32[512,1024]{1,0:T(8,128)}, u32[]{:S(2)}, u32[]{:S(2)}) collective-permute-start(f32[512,1024]{1,0:T(8,128)} %product_rows.15), channel_id=1, source_target_pairs={{0,8},{4,12},{8,0},{12,4},{16,24},{20,28},{24,16},{28,20},{1,9},{5... | collective-permute-start | bytes 6291464 | tf_op jit(solution)/shard_map/ppermute | solution.py:61
  166.6 49.9 %collective-permute-start.19 = (f32[512,1024]{1,0:T(8,128)}, f32[512,1024]{1,0:T(8,128)}, u32[]{:S(2)}, u32[]{:S(2)}) collective-permute-start(f32[512,1024]{1,0:T(8,128)} %product_rows.14), channel_id=1, source_target_pairs={{0,4},{4,0},{8,12},{12,8},{16,20},{20,16},{24,28},{28,24},{1,5},{5... | collective-permute-start | bytes 6291464 | tf_op jit(solution)/shard_map/ppermute | solution.py:61
  175.6 20.3 %collective-permute-start.17 = (f32[192,1024]{1,0:T(8,128)}, f32[192,1024]{1,0:T(8,128)}, u32[]{:S(2)}, u32[]{:S(2)}) collective-permute-start(f32[192,1024]{1,0:T(8,128)} %add_rows.13.mine_ref), channel_id=1, source_target_pairs={{0,2},{1,3},{2,0},{3,1},{4,6},{5,7},{6,4},{7,5},{8,10},{9,11},{10,... | collective-permute-start | bytes 2359304 | tf_op jit(solution)/shard_map/ppermute | solution.py:61
  198.8 21.0 %collective-permute-start.18 = (f32[192,1024]{1,0:T(8,128)}, f32[192,1024]{1,0:T(8,128)}, u32[]{:S(2)}, u32[]{:S(2)}) collective-permute-start(f32[192,1024]{1,0:T(8,128)} %add.262), channel_id=1, source_target_pairs={{0,2},{1,3},{2,0},{3,1},{4,6},{5,7},{6,4},{7,5},{8,10},{9,11},{10,... | collective-permute-start | bytes 2359304 | tf_op jit(solution)/shard_map/ppermute | solution.py:61
  207.9 3.2 collective-permute-start.22
  210.2 91.0 %collective-permute-start.30 = (f32[512,1024]{1,0:T(8,128)}, f32[512,1024]{1,0:T(8,128)}, u32[]{:S(2)}, u32[]{:S(2)}) collective-permute-start(f32[512,1024]{1,0:T(8,128)} %product_rows.16), channel_id=1, source_target_pairs={{0,4},{4,0},{8,12},{12,8},{16,20},{20,16},{24,28},{28,24},{1,5},{5... | collective-permute-start | bytes 6291464 | tf_op jit(solution)/shard_map/ppermute | solution.py:61
  222.3 5.7 %collective-permute-start.23 = (f32[192,1024]{1,0:T(8,128)}, f32[192,1024]{1,0:T(8,128)}, u32[]{:S(2)}, u32[]{:S(2)}) collective-permute-start(f32[192,1024]{1,0:T(8,128)} %add_add_fusion), channel_id=1, source_target_pairs={{0,1},{1,0},{2,3},{3,2},{4,5},{5,4},{6,7},{7,6},{8,9},{9,8},{10,11... | collective-permute-start | bytes 2359304 | tf_op jit(solution)/shard_map/ppermute | solution.py:61
  222.4 20.2 %collective-permute-start.24 = (f32[192,1024]{1,0:T(8,128)}, f32[192,1024]{1,0:T(8,128)}, u32[]{:S(2)}, u32[]{:S(2)}) collective-permute-start(f32[192,1024]{1,0:T(8,128)} %add_rows.14.mine_ref), channel_id=1, source_target_pairs={{0,2},{1,3},{2,0},{3,1},{4,6},{5,7},{6,4},{7,5},{8,10},{9,11},{10,... | collective-permute-start | bytes 2359304 | tf_op jit(solution)/shard_map/ppermute | solution.py:61
  223.8 47.9 %collective-permute-start.28 = (f32[256,1024]{1,0:T(8,128)}, f32[256,1024]{1,0:T(8,128)}, u32[]{:S(2)}, u32[]{:S(2)}) collective-permute-start(f32[256,1024]{1,0:T(8,128)} %get-tuple-element.563), channel_id=1, source_target_pairs={{0,8},{4,12},{8,0},{12,4},{16,24},{20,28},{24,16},{28,20},{1,9},{5... | collective-permute-start | bytes 3145736 | tf_op jit(solution)/shard_map/ppermute | solution.py:61
  225.4 73.4 %collective-permute-start.31 = (f32[256,1024]{1,0:T(8,128)}, f32[256,1024]{1,0:T(8,128)}, u32[]{:S(2)}, u32[]{:S(2)}) collective-permute-start(f32[256,1024]{1,0:T(8,128)} %get-tuple-element.584), channel_id=1, source_target_pairs={{0,16},{4,20},{8,24},{12,28},{16,0},{20,4},{24,8},{28,12},{1,17},{... | collective-permute-start | bytes 3145736 | tf_op jit(solution)/shard_map/ppermute | solution.py:61
  258.3 3.8 collective-permute-start.26
  260.5 77.6 %collective-permute-start.34 = (f32[512,1024]{1,0:T(8,128)}, f32[512,1024]{1,0:T(8,128)}, u32[]{:S(2)}, u32[]{:S(2)}) collective-permute-start(f32[512,1024]{1,0:T(8,128)} %product_rows.19), channel_id=1, source_target_pairs={{0,4},{4,0},{8,12},{12,8},{16,20},{20,16},{24,28},{28,24},{1,5},{5... | collective-permute-start | bytes 6291464 | tf_op jit(solution)/shard_map/ppermute | solution.py:61
  271.8 19.1 %collective-permute-start.27 = (f32[192,1024]{1,0:T(8,128)}, f32[192,1024]{1,0:T(8,128)}, u32[]{:S(2)}, u32[]{:S(2)}) collective-permute-start(f32[192,1024]{1,0:T(8,128)} %add_rows.15.mine_ref), channel_id=1, source_target_pairs={{0,2},{1,3},{2,0},{3,1},{4,6},{5,7},{6,4},{7,5},{8,10},{9,11},{10,... | collective-permute-start | bytes 2359304 | tf_op jit(solution)/shard_map/ppermute | solution.py:61
  274.7 39.6 %collective-permute-start.36 = (f32[128,1024]{1,0:T(8,128)}, f32[128,1024]{1,0:T(8,128)}, u32[]{:S(2)}, u32[]{:S(2)}) collective-permute-start(f32[128,1024]{1,0:T(8,128)} %get-tuple-element.610), channel_id=1, source_target_pairs={{0,16},{4,20},{8,24},{12,28},{16,0},{20,4},{24,8},{28,12},{1,17},{... | collective-permute-start | bytes 1572872 | tf_op jit(solution)/shard_map/ppermute | solution.py:61
  310.5 25.5 %collective-permute-start.35 = (f32[256,1024]{1,0:T(8,128)}, f32[256,1024]{1,0:T(8,128)}, u32[]{:S(2)}, u32[]{:S(2)}) collective-permute-start(f32[256,1024]{1,0:T(8,128)} %get-tuple-element.607), channel_id=1, source_target_pairs={{0,8},{4,12},{8,0},{12,4},{16,24},{20,28},{24,16},{28,20},{1,9},{5... | collective-permute-start | bytes 3145736 | tf_op jit(solution)/shard_map/ppermute | solution.py:61
  310.5 45.0 %collective-permute-start.38 = (f32[128,1024]{1,0:T(8,128)}, f32[128,1024]{1,0:T(8,128)}, u32[]{:S(2)}, u32[]{:S(2)}) collective-permute-start(f32[128,1024]{1,0:T(8,128)} %get-tuple-element.642), channel_id=1, source_target_pairs={{0,4},{4,0},{8,12},{12,8},{16,20},{20,16},{24,28},{28,24},{1,5},{5... | collective-permute-start | bytes 1572872 | tf_op jit(solution)/shard_map/ppermute | solution.py:61
  317.5 28.1 %collective-permute-start.33 = (f32[192,1024]{1,0:T(8,128)}, f32[192,1024]{1,0:T(8,128)}, u32[]{:S(2)}, u32[]{:S(2)}) collective-permute-start(f32[192,1024]{1,0:T(8,128)} %add_rows.16.mine_ref), channel_id=1, source_target_pairs={{0,2},{1,3},{2,0},{3,1},{4,6},{5,7},{6,4},{7,5},{8,10},{9,11},{10,... | collective-permute-start | bytes 2359304 | tf_op jit(solution)/shard_map/ppermute | solution.py:61
  317.9 72.1 %collective-permute-start.42 = (f32[512,1024]{1,0:T(8,128)}, f32[512,1024]{1,0:T(8,128)}, u32[]{:S(2)}, u32[]{:S(2)}) collective-permute-start(f32[512,1024]{1,0:T(8,128)} %product_rows.21), channel_id=1, source_target_pairs={{0,4},{4,0},{8,12},{12,8},{16,20},{20,16},{24,28},{28,24},{1,5},{5... | collective-permute-start | bytes 6291464 | tf_op jit(solution)/shard_map/ppermute | solution.py:61
  342.6 44.0 %collective-permute-start.44 = (f32[256,1024]{1,0:T(8,128)}, f32[256,1024]{1,0:T(8,128)}, u32[]{:S(2)}, u32[]{:S(2)}) collective-permute-start(f32[256,1024]{1,0:T(8,128)} %get-tuple-element.691), channel_id=1, source_target_pairs={{0,8},{4,12},{8,0},{12,4},{16,24},{20,28},{24,16},{28,20},{1,9},{5... | collective-permute-start | bytes 3145736 | tf_op jit(solution)/shard_map/ppermute | solution.py:61
  342.9 46.0 %collective-permute-start.43 = (f32[128,1024]{1,0:T(8,128)}, f32[128,1024]{1,0:T(8,128)}, u32[]{:S(2)}, u32[]{:S(2)}) collective-permute-start(f32[128,1024]{1,0:T(8,128)} %get-tuple-element.689), channel_id=1, source_target_pairs={{0,16},{4,20},{8,24},{12,28},{16,0},{20,4},{24,8},{28,12},{1,17},{... | collective-permute-start | bytes 1572872 | tf_op jit(solution)/shard_map/ppermute | solution.py:61
  372.3 10.5 %collective-permute-start.39 = (f32[512,896]{1,0:T(8,128)}, f32[512,896]{1,0:T(8,128)}, u32[]{:S(2)}, u32[]{:S(2)}) collective-permute-start(f32[512,896]{1,0:T(8,128)} %get-tuple-element.674), channel_id=1, source_target_pairs={{0,1},{1,0},{2,3},{3,2},{4,5},{5,4},{6,7},{7,6},{8,9},{9,8},{10,11... | collective-permute-start | bytes 5505032 | tf_op jit(solution)/shard_map/ppermute | solution.py:61
  378.0 56.2 %collective-permute-start.47 = (f32[512,1024]{1,0:T(8,128)}, f32[512,1024]{1,0:T(8,128)}, u32[]{:S(2)}, u32[]{:S(2)}) collective-permute-start(f32[512,1024]{1,0:T(8,128)} %product_rows.23), channel_id=1, source_target_pairs={{0,4},{4,0},{8,12},{12,8},{16,20},{20,16},{24,28},{28,24},{1,5},{5... | collective-permute-start | bytes 6291464 | tf_op jit(solution)/shard_map/ppermute | solution.py:61
  390.0 7.0 %collective-permute-start.41 = (f32[14,1024]{1,0:T(8,128)}, f32[14,1024]{1,0:T(8,128)}, u32[]{:S(2)}, u32[]{:S(2)}) collective-permute-start(f32[14,1024]{1,0:T(8,128)} %broadcast_multiply_fusion.1), channel_id=1, source_target_pairs={{0,1},{1,0},{2,3},{3,2},{4,5},{5,4},{6,7},{7,6},{8,9},{9,8},{10,11... | collective-permute-start | bytes 172040 | tf_op jit(solution)/shard_map/ppermute | solution.py:61
  390.1 23.1 %collective-permute-start.40 = (f32[256,896]{1,0:T(8,128)}, f32[256,896]{1,0:T(8,128)}, u32[]{:S(2)}, u32[]{:S(2)}) collective-permute-start(f32[256,896]{1,0:T(8,128)} %get-tuple-element.680), channel_id=1, source_target_pairs={{0,2},{1,3},{2,0},{3,1},{4,6},{5,7},{6,4},{7,5},{8,10},{9,11},{10,... | collective-permute-start | bytes 2752520 | tf_op jit(solution)/shard_map/ppermute | solution.py:61
  395.1 31.8 %collective-permute-start.49 = (f32[128,1024]{1,0:T(8,128)}, f32[128,1024]{1,0:T(8,128)}, u32[]{:S(2)}, u32[]{:S(2)}) collective-permute-start(f32[128,1024]{1,0:T(8,128)} %get-tuple-element.730), channel_id=1, source_target_pairs={{0,16},{4,20},{8,24},{12,28},{16,0},{20,4},{24,8},{28,12},{1,17},{... | collective-permute-start | bytes 1572872 | tf_op jit(solution)/shard_map/ppermute | solution.py:61
  395.3 36.6 %collective-permute-start.48 = (f32[256,1024]{1,0:T(8,128)}, f32[256,1024]{1,0:T(8,128)}, u32[]{:S(2)}, u32[]{:S(2)}) collective-permute-start(f32[256,1024]{1,0:T(8,128)} %get-tuple-element.728), channel_id=1, source_target_pairs={{0,8},{4,12},{8,0},{12,4},{16,24},{20,28},{24,16},{28,20},{1,9},{5... | collective-permute-start | bytes 3145736 | tf_op jit(solution)/shard_map/ppermute | solution.py:61
  419.2 31.9 %collective-permute-start.54 = (f32[4,440,128]{2,1,0:T(8,128)}, f32[4,440,128]{2,1,0:T(8,128)}, u32[]{:S(2)}, u32[]{:S(2)}) collective-permute-start(f32[4,440,128]{2,1,0:T(8,128)} %bitcast.154), channel_id=1, source_target_pairs={{0,4},{4,0},{8,12},{12,8},{16,20},{20,16},{24,28},{28,24},{1,5},{5... | collective-permute-start | bytes 2703368 | tf_op jit(solution)/shard_map/ppermute | solution.py:61
  434.2 14.7 %collective-permute-start.46 = (f32[192,768]{1,0:T(8,128)}, f32[192,768]{1,0:T(8,128)}, u32[]{:S(2)}, u32[]{:S(2)}) collective-permute-start(f32[192,768]{1,0:T(8,128)} %add_rows.17), channel_id=1, source_target_pairs={{0,2},{1,3},{2,0},{3,1},{4,6},{5,7},{6,4},{7,5},{8,10},{9,11},{10,... | collective-permute-start | bytes 1769480 | tf_op jit(solution)/shard_map/ppermute | solution.py:61
  439.0 25.3 %collective-permute-start.53 = (f32[128,1024]{1,0:T(8,128)}, f32[128,1024]{1,0:T(8,128)}, u32[]{:S(2)}, u32[]{:S(2)}) collective-permute-start(f32[128,1024]{1,0:T(8,128)} %get-tuple-element.757), channel_id=1, source_target_pairs={{0,16},{4,20},{8,24},{12,28},{16,0},{20,4},{24,8},{28,12},{1,17},{... | collective-permute-start | bytes 1572872 | tf_op jit(solution)/shard_map/ppermute | solution.py:61
  440.2 27.5 %collective-permute-start.52 = (f32[512,512]{1,0:T(8,128)}, f32[512,512]{1,0:T(8,128)}, u32[]{:S(2)}, u32[]{:S(2)}) collective-permute-start(f32[512,512]{1,0:T(8,128)} %product_rows.25), channel_id=1, source_target_pairs={{0,4},{4,0},{8,12},{12,8},{16,20},{20,16},{24,28},{28,24},{1,5},{5... | collective-permute-start | bytes 3145736 | tf_op jit(solution)/shard_map/ppermute | solution.py:61
  440.7 37.5 %collective-permute-start.51 = (f32[256,1024]{1,0:T(8,128)}, f32[256,1024]{1,0:T(8,128)}, u32[]{:S(2)}, u32[]{:S(2)}) collective-permute-start(f32[256,1024]{1,0:T(8,128)} %get-tuple-element.754), channel_id=1, source_target_pairs={{0,8},{4,12},{8,0},{12,4},{16,24},{20,28},{24,16},{28,20},{1,9},{5... | collective-permute-start | bytes 3145736 | tf_op jit(solution)/shard_map/ppermute | solution.py:61
  465.4 17.0 %collective-permute-start.50 = (f32[192,768]{1,0:T(8,128)}, f32[192,768]{1,0:T(8,128)}, u32[]{:S(2)}, u32[]{:S(2)}) collective-permute-start(f32[192,768]{1,0:T(8,128)} %add.275), channel_id=1, source_target_pairs={{0,1},{1,0},{2,3},{3,2},{4,5},{5,4},{6,7},{7,6},{8,9},{9,8},{10,11... | collective-permute-start | bytes 1769480 | tf_op jit(solution)/shard_map/ppermute | solution.py:61
  465.5 28.5 %collective-permute-start.55 = (f32[2,440,128]{2,1,0:T(8,128)}, f32[2,440,128]{2,1,0:T(8,128)}, u32[]{:S(2)}, u32[]{:S(2)}) collective-permute-start(f32[2,440,128]{2,1,0:T(8,128)} %dynamic-slice_bitcast_fusion), channel_id=1, source_target_pairs={{0,8},{4,12},{8,0},{12,4},{16,24},{20,28},{24,16},{28,20},{1,9},{5... | collective-permute-start | bytes 1351688 | tf_op jit(solution)/shard_map/ppermute | solution.py:61
  480.2 23.9 %collective-permute-start.58 = (f32[128,1024]{1,0:T(8,128)}, f32[128,1024]{1,0:T(8,128)}, u32[]{:S(2)}, u32[]{:S(2)}) collective-permute-start(f32[128,1024]{1,0:T(8,128)} %get-tuple-element.789), channel_id=1, source_target_pairs={{0,16},{4,20},{8,24},{12,28},{16,0},{20,4},{24,8},{28,12},{1,17},{... | collective-permute-start | bytes 1572872 | tf_op jit(solution)/shard_map/ppermute | solution.py:61
  480.3 32.3 %collective-permute-start.57 = (f32[256,512]{1,0:T(8,128)}, f32[256,512]{1,0:T(8,128)}, u32[]{:S(2)}, u32[]{:S(2)}) collective-permute-start(f32[256,512]{1,0:T(8,128)} %get-tuple-element.787), channel_id=1, source_target_pairs={{0,8},{4,12},{8,0},{12,4},{16,24},{20,28},{24,16},{28,20},{1,9},{5... | collective-permute-start | bytes 1572872 | tf_op jit(solution)/shard_map/ppermute | solution.py:61
  495.9 17.9 %collective-permute-start.56 = (f32[1,440,128]{2,1,0:T(8,128)}, f32[1,440,128]{2,1,0:T(8,128)}, u32[]{:S(2)}, u32[]{:S(2)}) collective-permute-start(f32[1,440,128]{2,1,0:T(8,128)} %constant_dynamic-slice_fusion), channel_id=1, source_target_pairs={{0,16},{4,20},{8,24},{12,28},{16,0},{20,4},{24,8},{28,12},{1,17},{... | collective-permute-start | bytes 675848 | tf_op jit(solution)/shard_map/ppermute | solution.py:61
  517.2 11.8 %collective-permute-start.60 = (f32[128,512]{1,0:T(8,128)S(1)}, f32[128,512]{1,0:T(8,128)S(1)}, u32[]{:S(2)}, u32[]{:S(2)}) collective-permute-start(f32[128,512]{1,0:T(8,128)S(1)} %get-tuple-element.804), channel_id=1, source_target_pairs={{0,16},{4,20},{8,24},{12,28},{16,0},{20,4},{24,8},{28,12},{1,17},{... | collective-permute-start | bytes 786440 | tf_op jit(solution)/shard_map/ppermute | solution.py:61
  518.1 4.4 collective-permute-start.59
  (197 other events, 1017.4 us)

commit v9 on v8

--- a/solution.py
+++ b/solution.py
@@ -745,8 +745,8 @@
         theirs = pl.multiple_of(half - core_ref[0] * half, 8)
         low_out[:half] = turned_ref[pl.ds(mine, half)].astype(BF)
         low_out[half:] = turned_ref[pl.ds(theirs, half)].astype(BF)
-        for copy in copies[3:]:
-            copy.wait()
+        copies[3].wait()
+        copies[4].wait()
         key_high, key_rest = two_part(key_out[...])
         embed_high, embed_rest = two_part(embed_ref[...])
         score_out[...] = matmul_nt(key_high, patch_ref[...]) + matmul_nt(key_rest, patch_ref[...])
@@ -755,6 +755,7 @@
             + matmul_nt(key_rest, embed_high)
             + matmul_nt(key_high, embed_rest)
         )
+        copies[5].wait()
         flat_out[...] = matmul(patch_ref[...], value_weight_ref[...]).astype(BF)
         value_var = matmul(embed_high, value_weight_ref[...]) + matmul(embed_rest, value_weight_ref[...])
         var_out[...] = (value_var + bias_ref[...]).astype(BF)
@@ -771,6 +772,7 @@
             low = probs.astype(BF)
             mixed = (matmul(low, segment) * pix).astype(BF)
             pooled_out[:, one] = (matmul(mixed, flat_out[:, one]) + matmul(low, var_out[:, one])).astype(BF)
+        copies[6].wait()
         send_out[...] = matmul(pooled_out[half:], out_weight_ref[...])
         own_out[...] = matmul(pooled_out[:half], out_weight_ref[...])
 

time: 539 us -> 540 us (level)
  no operation moved by 1% of the time
where the time goes in v9:
time: 540 us; the launch traced here: 533 us
  waiting for transfers between devices  208 us (39%)
  Pallas kernels  162 us (30%)
  local copies, waits for them, and re-layouts  63.8 us (12%)
  starting transfers between devices  50.2 us (9%)
  other arithmetic  40.6 us (8%)
  between operations  5.52 us (1%)
    ppermute x61, waiting for transfers between devices, exchange(): return lax.ppermute(tensor, axis, [(i, i ^ 1 << bit) for i in range(size)])  208 us
    ppermute x61, starting transfers between devices, exchange(): return lax.ppermute(tensor, axis, [(i, i ^ 1 << bit) for i in range(size)])  50.2 us
    unnamed x390, local copies, waits for them, and re-layouts  41.5 us
    pallas_call x14, Pallas kernels, product_rows(): pl.pallas_call(kernel, out_shape=out_shape, grid=(count,), in_specs=in_sp...  37.5 us
    pallas_call x8, Pallas kernels, add_split(): pl.pallas_call(kernel, out_shape=[jax.ShapeDtypeStruct((half, width), F32...  18.4 us
    pallas_call x2, Pallas kernels, feed_forward(): pl.pallas_call(kernel, out_shape=(jax.ShapeDtypeStruct((rows, hidden), BF...  14.4 us
    pallas_call x2, Pallas kernels, feed_back(): pl.pallas_call(kernel, out_shape=(jax.ShapeDtypeStruct((rows, hidden), BF...  13.8 us
    pallas_call x9, Pallas kernels, add_rows(): pl.pallas_call(kernel, out_shape=jax.ShapeDtypeStruct((rows, width), F32)...  12.9 us
  transfers between devices with their start and end apart: 61, of which 37 were waited for; matrix products, arithmetic and copies ran while one was open for 11% of the time, Pallas kernels for 21%

profile of v9, /device:TPU:0, one launch (start us, length us, event | category | flops | bytes accessed | tf_op | source)
XLA Modules:
  0.0 532.9 jit_solution(14353938481659377915)
XLA Ops:
  2.6 10.8 %pool_front.1 = (bf16[384,768]{1,0:T(8,128)(2,1)}, f32[1,256]{1,0:T(1,128)}, f32[4,1024]{1,0:T(4,128)}, f32[4,768]{1,0:T(4,128)}, bf16[768,256]{1,0:T(8,128)(2,1...) custom-call(s32[1]{0:T(128)} %bitcast.core_ref, ...), custom_call_target="tpu_custom_call" | custom-call | flops 999999995904 | bytes 8 | tf_op jit(solution)/shard_map/pool_front/pallas_call | solution.py:780
  17.6 2.9 collective-permute-start.4
  27.7 2.6 collective-permute-start.3
  32.2 6.1 %collective-permute-done.4 = f32[192,1024]{1,0:T(8,128)S(1)} collective-permute-done((f32[192,1024]{1,0:T(8,128)S(1)}, f32[192,1024]{1,0:T(8,128)S(1)}, u32[]{:S(2)}, u32[]{:S(2)}) %collective-permute-start.4) | collective-permute-done | bytes 786464 | tf_op jit(solution)/shard_map/ppermute | solution.py:61
  43.4 3.9 attend_forward.2
  60.6 12.6 %collective-permute-done.7 = f32[192,1024]{1,0:T(8,128)} collective-permute-done((f32[192,1024]{1,0:T(8,128)}, f32[192,1024]{1,0:T(8,128)}, u32[]{:S(2)}, u32[]{:S(2)}) %collective-permute-start.7) | collective-permute-done | bytes 786464 | tf_op jit(solution)/shard_map/ppermute | solution.py:61
  78.5 8.3 %feed_forward.2 = (bf16[384,1024]{1,0:T(8,128)(2,1)}, f32[384,1024]{1,0:T(8,128)}, f32[192,1024]{1,0:T(8,128)}, f32[192,1024]{1,0:T(8,128)}, bf16[384,1024]{1,0:T(8,128)(2,1)}) custom-call(s32[8]{0:T(128)} %copy-done.35, f32[192,1024]{1,0:T(8,128)} %copy-done.16, f32[192,1024]{1,0:T(8,128)} %copy-done.180, f32[2,2,1024]{2,1,0:T(2,128)} %gain_ref.11, ...), custom_call_target="tpu_custom_call" | custom-call | flops 999999995904 | bytes 8 | tf_op jit(solution)/shard_map/feed_forward/pallas_call | solution.py:288
  100.1 12.6 %collective-permute-done.10 = f32[192,1024]{1,0:T(8,128)} collective-permute-done((f32[192,1024]{1,0:T(8,128)S(1)}, f32[192,1024]{1,0:T(8,128)}, u32[]{:S(2)}, u32[]{:S(2)}) %collective-permute-start.10) | collective-permute-done | bytes 786464 | tf_op jit(solution)/shard_map/ppermute | solution.py:61
  116.8 3.1 attend_forward.3
  126.2 16.0 %collective-permute-done.13 = f32[192,1024]{1,0:T(8,128)S(1)} collective-permute-done((f32[192,1024]{1,0:T(8,128)S(1)}, f32[192,1024]{1,0:T(8,128)S(1)}, u32[]{:S(2)}, u32[]{:S(2)}) %collective-permute-start.13) | collective-permute-done | bytes 786464 | tf_op jit(solution)/shard_map/ppermute | solution.py:61
  146.3 6.1 %feed_forward.3 = (bf16[384,1024]{1,0:T(8,128)(2,1)}, f32[384,1024]{1,0:T(8,128)}, bf16[384,1024]{1,0:T(8,128)(2,1)}) custom-call(s32[8]{0:T(128)} %copy-done.35, f32[192,1024]{1,0:T(8,128)} %copy-done.18, f32[192,1024]{1,0:T(8,128)} %collective-permute-done.14.other_ref, f32[2,2,1024]{2,1,0:T(2,128)} %gain_ref.11, f32[2,2,1024]{2,1,0:T(2,128)} %bias_ref.3, ...), custom_call_target="tpu_custom_call" | custom-call | flops 999999995904 | bytes 8 | tf_op jit(solution)/shard_map/feed_forward/pallas_call | solution.py:288
  152.4 7.7 %feed_back.2 = (bf16[384,1024]{1,0:T(8,128)(2,1)}, f32[1,1024]{1,0:T(1,128)}, f32[192,1024]{1,0:T(8,128)}, f32[192,1024]{1,0:T(8,128)}) custom-call(bf16[384,1024]{1,0:T(8,128)(2,1)} %copy-done.76, f32[384,1024]{1,0:T(8,128)} %get-tuple-element.449.slope_ref, bf16[2,1024,1024]{2,1,0:T(8,128)(2,1)} %down_ref.7, bf16[2,1024,1024]{2,1,0:T(8,128)(2,1)} %up_ref.7), custom_call_target="tpu_custom_call" | custom-call | flops 999999995904 | bytes 8 | tf_op jit(solution)/shard_map/feed_back/pallas_call | solution.py:341
  181.0 15.5 %collective-permute-done.17.got_ref = f32[192,1024]{1,0:T(8,128)} collective-permute-done((f32[192,1024]{1,0:T(8,128)}, f32[192,1024]{1,0:T(8,128)}, u32[]{:S(2)}, u32[]{:S(2)}) %collective-permute-start.17) | collective-permute-done | bytes 786464 | tf_op jit(solution)/shard_map/ppermute | solution.py:61
  196.6 2.8 norm_back.4
  203.6 4.9 attend_back.2
  213.8 3.3 product_rows.17
  217.1 3.3 product_rows.18
  220.4 2.5 add_add_fusion
  226.0 2.6 collective-permute-start.31
  231.6 11.6 %collective-permute-done.24.got_ref = f32[192,1024]{1,0:T(8,128)} collective-permute-done((f32[192,1024]{1,0:T(8,128)}, f32[192,1024]{1,0:T(8,128)}, u32[]{:S(2)}, u32[]{:S(2)}) %collective-permute-start.24) | collective-permute-done | bytes 786464 | tf_op jit(solution)/shard_map/ppermute | solution.py:61
  243.3 2.8 norm_back.5
  252.8 6.1 %feed_back.3 = (bf16[384,1024]{1,0:T(8,128)(2,1)S(1)}, f32[1,1024]{1,0:T(1,128)S(1)}, f32[192,1024]{1,0:T(8,128)S(1)}, f32[192,1024]{1,0:T(8,128)}) custom-call(bf16[384,1024]{1,0:T(8,128)(2,1)S(1)} %get-tuple-element.544.low_ref, f32[384,1024]{1,0:T(8,128)S(1)} %copy-done.69, bf16[2,1024,1024]{2,1,0:T(8,128)(2,1)S(1)} %copy-done.46, ...), custom_call_target="tpu_custom_call" | custom-call | flops 999999995904 | bytes 8 | tf_op jit(solution)/shard_map/feed_back/pallas_call | solution.py:341
  264.6 7.8 %collective-permute-done.28.got_ref = f32[256,1024]{1,0:T(8,128)} collective-permute-done((f32[256,1024]{1,0:T(8,128)}, f32[256,1024]{1,0:T(8,128)}, u32[]{:S(2)}, u32[]{:S(2)}) %collective-permute-start.28) | collective-permute-done | bytes 1048608 | tf_op jit(solution)/shard_map/ppermute | solution.py:61
  276.0 15.5 %collective-permute-done.27.got_ref = f32[192,1024]{1,0:T(8,128)} collective-permute-done((f32[192,1024]{1,0:T(8,128)}, f32[192,1024]{1,0:T(8,128)}, u32[]{:S(2)}, u32[]{:S(2)}) %collective-permute-start.27) | collective-permute-done | bytes 786464 | tf_op jit(solution)/shard_map/ppermute | solution.py:61
  291.6 2.8 norm_back.6
  301.9 3.4 product_rows.20
  305.4 4.9 attend_back.3
  320.2 16.4 %collective-permute-done.35.got_ref = f32[256,1024]{1,0:T(8,128)} collective-permute-done((f32[256,1024]{1,0:T(8,128)}, f32[256,1024]{1,0:T(8,128)}, u32[]{:S(2)}, u32[]{:S(2)}) %collective-permute-start.35) | collective-permute-done | bytes 1048608 | tf_op jit(solution)/shard_map/ppermute | solution.py:61
  338.7 3.5 product_rows.22
  343.5 2.8 collective-permute-start.43
  346.4 2.8 norm_back.7
  361.2 8.9 %pool_back.1 = (f32[816,256]{1,0:T(8,128)S(1)}, f32[4,768]{1,0:T(4,128)S(1)}, f32[4,48]{1,0:T(4,128)S(1)}, f32[192,768]{1,0:T(8,128)S(1)}, f32[192,768]{1,0:T(8,128)}) custom-call(bf16[384,1024]{1,0:T(8,128)(2,1)S(1)} %get-tuple-element.655.low_ref, bf16[256,1024]{1,0:T(8,128)(2,1)S(1)} %copy-done.53, bf16[768,256]{1,0:T(8,128)(2,1)S(1)} %copy-done.114, ...), custom_call_target="tpu_custom_call" | custom-call | flops 999999995904 | bytes 8 | tf_op jit(solution)/shard_map/pool_back/pallas_call | solution.py:847
  370.1 2.8 embed_terms.1
  383.4 3.8 add_split.11
  391.3 3.4 product_rows.24
  401.0 12.8 %collective-permute-done.40 = f32[256,896]{1,0:T(8,128)} collective-permute-done((f32[256,896]{1,0:T(8,128)}, f32[256,896]{1,0:T(8,128)}, u32[]{:S(2)}, u32[]{:S(2)}) %collective-permute-start.40) | collective-permute-done | bytes 917536 | tf_op jit(solution)/shard_map/ppermute | solution.py:61
  416.2 2.6 constant_dynamic-slice_fusion.1
  428.6 3.9 collective-permute-done.48.got_ref
  436.3 3.3 product_rows.26
  444.3 5.1 collective-permute-done.46
  455.2 9.6 %collective-permute-done.53 = f32[128,1024]{1,0:T(8,128)} collective-permute-done((f32[128,1024]{1,0:T(8,128)}, f32[128,1024]{1,0:T(8,128)}, u32[]{:S(2)}, u32[]{:S(2)}) %collective-permute-start.53) | collective-permute-done | bytes 524320 | tf_op jit(solution)/shard_map/ppermute | solution.py:61
  468.4 2.9 product_rows.27
  471.3 7.5 %collective-permute-done.51.got_ref = f32[256,1024]{1,0:T(8,128)} collective-permute-done((f32[256,1024]{1,0:T(8,128)}, f32[256,1024]{1,0:T(8,128)}, u32[]{:S(2)}, u32[]{:S(2)}) %collective-permute-start.51) | collective-permute-done | bytes 1048608 | tf_op jit(solution)/shard_map/ppermute | solution.py:61
  485.5 2.7 copy.79
  488.1 6.4 %collective-permute-done.55 = f32[2,440,128]{2,1,0:T(8,128)} collective-permute-done((f32[2,440,128]{2,1,0:T(8,128)}, f32[2,440,128]{2,1,0:T(8,128)}, u32[]{:S(2)}, u32[]{:S(2)}) %collective-permute-start.55) | collective-permute-done | bytes 450592 | tf_op jit(solution)/shard_map/ppermute | solution.py:61
  496.5 8.3 %collective-permute-done.58 = f32[128,1024]{1,0:T(8,128)} collective-permute-done((f32[128,1024]{1,0:T(8,128)}, f32[128,1024]{1,0:T(8,128)}, u32[]{:S(2)}, u32[]{:S(2)}) %collective-permute-start.58) | collective-permute-done | bytes 524320 | tf_op jit(solution)/shard_map/ppermute | solution.py:61
  505.9 7.4 %collective-permute-done.57.got_ref = f32[256,512]{1,0:T(8,128)} collective-permute-done((f32[256,512]{1,0:T(8,128)}, f32[256,512]{1,0:T(8,128)}, u32[]{:S(2)}, u32[]{:S(2)}) %collective-permute-start.57) | collective-permute-done | bytes 524320 | tf_op jit(solution)/shard_map/ppermute | solution.py:61
  523.8 5.8 %collective-permute-done.60 = f32[128,512]{1,0:T(8,128)S(1)} collective-permute-done((f32[128,512]{1,0:T(8,128)S(1)}, f32[128,512]{1,0:T(8,128)S(1)}, u32[]{:S(2)}, u32[]{:S(2)}) %collective-permute-start.60) | collective-permute-done | bytes 262176 | tf_op jit(solution)/shard_map/ppermute | solution.py:61
  (660 shorter events, 222.2 us)
Async XLA Ops:
  13.4 2.6 collective-permute-start
  17.6 20.8 %collective-permute-start.4 = (f32[192,1024]{1,0:T(8,128)S(1)}, f32[192,1024]{1,0:T(8,128)S(1)}, u32[]{:S(2)}, u32[]{:S(2)}) collective-permute-start(f32[192,1024]{1,0:T(8,128)S(1)} %add_rows.9), channel_id=1, source_target_pairs={{0,2},{1,3},{2,0},{3,1},{4,6},{5,7},{6,4},{7,5},{8,10},{9,11},{10,... | collective-permute-start | bytes 2359304 | tf_op jit(solution)/shard_map/ppermute | solution.py:61
  20.5 3.6 collective-permute-start.1
  24.1 3.6 collective-permute-start.2
  27.7 4.5 collective-permute-start.3
  48.7 2.6 collective-permute-start.6
  53.4 19.9 %collective-permute-start.7 = (f32[192,1024]{1,0:T(8,128)}, f32[192,1024]{1,0:T(8,128)}, u32[]{:S(2)}, u32[]{:S(2)}) collective-permute-start(f32[192,1024]{1,0:T(8,128)} %add_rows.10), channel_id=1, source_target_pairs={{0,2},{1,3},{2,0},{3,1},{4,6},{5,7},{6,4},{7,5},{8,10},{9,11},{10,... | collective-permute-start | bytes 2359304 | tf_op jit(solution)/shard_map/ppermute | solution.py:61
  92.9 19.8 %collective-permute-start.10 = (f32[192,1024]{1,0:T(8,128)S(1)}, f32[192,1024]{1,0:T(8,128)}, u32[]{:S(2)}, u32[]{:S(2)}) collective-permute-start(f32[192,1024]{1,0:T(8,128)S(1)} %add_rows.11), channel_id=1, source_target_pairs={{0,2},{1,3},{2,0},{3,1},{4,6},{5,7},{6,4},{7,5},{8,10},{9,11},{10,... | collective-permute-start | bytes 2359304 | tf_op jit(solution)/shard_map/ppermute | solution.py:61
  122.5 19.6 %collective-permute-start.13 = (f32[192,1024]{1,0:T(8,128)S(1)}, f32[192,1024]{1,0:T(8,128)S(1)}, u32[]{:S(2)}, u32[]{:S(2)}) collective-permute-start(f32[192,1024]{1,0:T(8,128)S(1)} %add_rows.12), channel_id=1, source_target_pairs={{0,2},{1,3},{2,0},{3,1},{4,6},{5,7},{6,4},{7,5},{8,10},{9,11},{10,... | collective-permute-start | bytes 2359304 | tf_op jit(solution)/shard_map/ppermute | solution.py:61
  165.2 3.5 collective-permute-start.15
  165.4 48.4 %collective-permute-start.20 = (f32[512,1024]{1,0:T(8,128)}, f32[512,1024]{1,0:T(8,128)}, u32[]{:S(2)}, u32[]{:S(2)}) collective-permute-start(f32[512,1024]{1,0:T(8,128)} %product_rows.15), channel_id=1, source_target_pairs={{0,8},{4,12},{8,0},{12,4},{16,24},{20,28},{24,16},{28,20},{1,9},{5... | collective-permute-start | bytes 6291464 | tf_op jit(solution)/shard_map/ppermute | solution.py:61
  167.2 49.9 %collective-permute-start.19 = (f32[512,1024]{1,0:T(8,128)}, f32[512,1024]{1,0:T(8,128)}, u32[]{:S(2)}, u32[]{:S(2)}) collective-permute-start(f32[512,1024]{1,0:T(8,128)} %product_rows.14), channel_id=1, source_target_pairs={{0,4},{4,0},{8,12},{12,8},{16,20},{20,16},{24,28},{28,24},{1,5},{5... | collective-permute-start | bytes 6291464 | tf_op jit(solution)/shard_map/ppermute | solution.py:61
  176.2 20.3 %collective-permute-start.17 = (f32[192,1024]{1,0:T(8,128)}, f32[192,1024]{1,0:T(8,128)}, u32[]{:S(2)}, u32[]{:S(2)}) collective-permute-start(f32[192,1024]{1,0:T(8,128)} %add_rows.13.mine_ref), channel_id=1, source_target_pairs={{0,2},{1,3},{2,0},{3,1},{4,6},{5,7},{6,4},{7,5},{8,10},{9,11},{10,... | collective-permute-start | bytes 2359304 | tf_op jit(solution)/shard_map/ppermute | solution.py:61
  199.4 21.0 %collective-permute-start.18 = (f32[192,1024]{1,0:T(8,128)}, f32[192,1024]{1,0:T(8,128)}, u32[]{:S(2)}, u32[]{:S(2)}) collective-permute-start(f32[192,1024]{1,0:T(8,128)} %add.262), channel_id=1, source_target_pairs={{0,2},{1,3},{2,0},{3,1},{4,6},{5,7},{6,4},{7,5},{8,10},{9,11},{10,... | collective-permute-start | bytes 2359304 | tf_op jit(solution)/shard_map/ppermute | solution.py:61
  208.5 3.2 collective-permute-start.22
  210.8 91.0 %collective-permute-start.30 = (f32[512,1024]{1,0:T(8,128)}, f32[512,1024]{1,0:T(8,128)}, u32[]{:S(2)}, u32[]{:S(2)}) collective-permute-start(f32[512,1024]{1,0:T(8,128)} %product_rows.16), channel_id=1, source_target_pairs={{0,4},{4,0},{8,12},{12,8},{16,20},{20,16},{24,28},{28,24},{1,5},{5... | collective-permute-start | bytes 6291464 | tf_op jit(solution)/shard_map/ppermute | solution.py:61
  222.9 5.7 %collective-permute-start.23 = (f32[192,1024]{1,0:T(8,128)}, f32[192,1024]{1,0:T(8,128)}, u32[]{:S(2)}, u32[]{:S(2)}) collective-permute-start(f32[192,1024]{1,0:T(8,128)} %add_add_fusion), channel_id=1, source_target_pairs={{0,1},{1,0},{2,3},{3,2},{4,5},{5,4},{6,7},{7,6},{8,9},{9,8},{10,11... | collective-permute-start | bytes 2359304 | tf_op jit(solution)/shard_map/ppermute | solution.py:61
  223.0 20.2 %collective-permute-start.24 = (f32[192,1024]{1,0:T(8,128)}, f32[192,1024]{1,0:T(8,128)}, u32[]{:S(2)}, u32[]{:S(2)}) collective-permute-start(f32[192,1024]{1,0:T(8,128)} %add_rows.14.mine_ref), channel_id=1, source_target_pairs={{0,2},{1,3},{2,0},{3,1},{4,6},{5,7},{6,4},{7,5},{8,10},{9,11},{10,... | collective-permute-start | bytes 2359304 | tf_op jit(solution)/shard_map/ppermute | solution.py:61
  224.5 47.9 %collective-permute-start.28 = (f32[256,1024]{1,0:T(8,128)}, f32[256,1024]{1,0:T(8,128)}, u32[]{:S(2)}, u32[]{:S(2)}) collective-permute-start(f32[256,1024]{1,0:T(8,128)} %get-tuple-element.563), channel_id=1, source_target_pairs={{0,8},{4,12},{8,0},{12,4},{16,24},{20,28},{24,16},{28,20},{1,9},{5... | collective-permute-start | bytes 3145736 | tf_op jit(solution)/shard_map/ppermute | solution.py:61
  226.0 73.4 %collective-permute-start.31 = (f32[256,1024]{1,0:T(8,128)}, f32[256,1024]{1,0:T(8,128)}, u32[]{:S(2)}, u32[]{:S(2)}) collective-permute-start(f32[256,1024]{1,0:T(8,128)} %get-tuple-element.584), channel_id=1, source_target_pairs={{0,16},{4,20},{8,24},{12,28},{16,0},{20,4},{24,8},{28,12},{1,17},{... | collective-permute-start | bytes 3145736 | tf_op jit(solution)/shard_map/ppermute | solution.py:61
  258.9 3.8 collective-permute-start.26
  261.1 77.6 %collective-permute-start.34 = (f32[512,1024]{1,0:T(8,128)}, f32[512,1024]{1,0:T(8,128)}, u32[]{:S(2)}, u32[]{:S(2)}) collective-permute-start(f32[512,1024]{1,0:T(8,128)} %product_rows.19), channel_id=1, source_target_pairs={{0,4},{4,0},{8,12},{12,8},{16,20},{20,16},{24,28},{28,24},{1,5},{5... | collective-permute-start | bytes 6291464 | tf_op jit(solution)/shard_map/ppermute | solution.py:61
  272.4 19.1 %collective-permute-start.27 = (f32[192,1024]{1,0:T(8,128)}, f32[192,1024]{1,0:T(8,128)}, u32[]{:S(2)}, u32[]{:S(2)}) collective-permute-start(f32[192,1024]{1,0:T(8,128)} %add_rows.15.mine_ref), channel_id=1, source_target_pairs={{0,2},{1,3},{2,0},{3,1},{4,6},{5,7},{6,4},{7,5},{8,10},{9,11},{10,... | collective-permute-start | bytes 2359304 | tf_op jit(solution)/shard_map/ppermute | solution.py:61
  275.3 39.6 %collective-permute-start.36 = (f32[128,1024]{1,0:T(8,128)}, f32[128,1024]{1,0:T(8,128)}, u32[]{:S(2)}, u32[]{:S(2)}) collective-permute-start(f32[128,1024]{1,0:T(8,128)} %get-tuple-element.610), channel_id=1, source_target_pairs={{0,16},{4,20},{8,24},{12,28},{16,0},{20,4},{24,8},{28,12},{1,17},{... | collective-permute-start | bytes 1572872 | tf_op jit(solution)/shard_map/ppermute | solution.py:61
  311.1 25.5 %collective-permute-start.35 = (f32[256,1024]{1,0:T(8,128)}, f32[256,1024]{1,0:T(8,128)}, u32[]{:S(2)}, u32[]{:S(2)}) collective-permute-start(f32[256,1024]{1,0:T(8,128)} %get-tuple-element.607), channel_id=1, source_target_pairs={{0,8},{4,12},{8,0},{12,4},{16,24},{20,28},{24,16},{28,20},{1,9},{5... | collective-permute-start | bytes 3145736 | tf_op jit(solution)/shard_map/ppermute | solution.py:61
  311.1 45.0 %collective-permute-start.38 = (f32[128,1024]{1,0:T(8,128)}, f32[128,1024]{1,0:T(8,128)}, u32[]{:S(2)}, u32[]{:S(2)}) collective-permute-start(f32[128,1024]{1,0:T(8,128)} %get-tuple-element.642), channel_id=1, source_target_pairs={{0,4},{4,0},{8,12},{12,8},{16,20},{20,16},{24,28},{28,24},{1,5},{5... | collective-permute-start | bytes 1572872 | tf_op jit(solution)/shard_map/ppermute | solution.py:61
  318.1 28.2 %collective-permute-start.33 = (f32[192,1024]{1,0:T(8,128)}, f32[192,1024]{1,0:T(8,128)}, u32[]{:S(2)}, u32[]{:S(2)}) collective-permute-start(f32[192,1024]{1,0:T(8,128)} %add_rows.16.mine_ref), channel_id=1, source_target_pairs={{0,2},{1,3},{2,0},{3,1},{4,6},{5,7},{6,4},{7,5},{8,10},{9,11},{10,... | collective-permute-start | bytes 2359304 | tf_op jit(solution)/shard_map/ppermute | solution.py:61
  318.5 72.1 %collective-permute-start.42 = (f32[512,1024]{1,0:T(8,128)}, f32[512,1024]{1,0:T(8,128)}, u32[]{:S(2)}, u32[]{:S(2)}) collective-permute-start(f32[512,1024]{1,0:T(8,128)} %product_rows.21), channel_id=1, source_target_pairs={{0,4},{4,0},{8,12},{12,8},{16,20},{20,16},{24,28},{28,24},{1,5},{5... | collective-permute-start | bytes 6291464 | tf_op jit(solution)/shard_map/ppermute | solution.py:61
  343.2 44.0 %collective-permute-start.44 = (f32[256,1024]{1,0:T(8,128)}, f32[256,1024]{1,0:T(8,128)}, u32[]{:S(2)}, u32[]{:S(2)}) collective-permute-start(f32[256,1024]{1,0:T(8,128)} %get-tuple-element.691), channel_id=1, source_target_pairs={{0,8},{4,12},{8,0},{12,4},{16,24},{20,28},{24,16},{28,20},{1,9},{5... | collective-permute-start | bytes 3145736 | tf_op jit(solution)/shard_map/ppermute | solution.py:61
  343.5 46.0 %collective-permute-start.43 = (f32[128,1024]{1,0:T(8,128)}, f32[128,1024]{1,0:T(8,128)}, u32[]{:S(2)}, u32[]{:S(2)}) collective-permute-start(f32[128,1024]{1,0:T(8,128)} %get-tuple-element.689), channel_id=1, source_target_pairs={{0,16},{4,20},{8,24},{12,28},{16,0},{20,4},{24,8},{28,12},{1,17},{... | collective-permute-start | bytes 1572872 | tf_op jit(solution)/shard_map/ppermute | solution.py:61
  372.9 10.4 %collective-permute-start.39 = (f32[512,896]{1,0:T(8,128)}, f32[512,896]{1,0:T(8,128)}, u32[]{:S(2)}, u32[]{:S(2)}) collective-permute-start(f32[512,896]{1,0:T(8,128)} %get-tuple-element.674), channel_id=1, source_target_pairs={{0,1},{1,0},{2,3},{3,2},{4,5},{5,4},{6,7},{7,6},{8,9},{9,8},{10,11... | collective-permute-start | bytes 5505032 | tf_op jit(solution)/shard_map/ppermute | solution.py:61
  378.7 56.1 %collective-permute-start.47 = (f32[512,1024]{1,0:T(8,128)}, f32[512,1024]{1,0:T(8,128)}, u32[]{:S(2)}, u32[]{:S(2)}) collective-permute-start(f32[512,1024]{1,0:T(8,128)} %product_rows.23), channel_id=1, source_target_pairs={{0,4},{4,0},{8,12},{12,8},{16,20},{20,16},{24,28},{28,24},{1,5},{5... | collective-permute-start | bytes 6291464 | tf_op jit(solution)/shard_map/ppermute | solution.py:61
  390.6 7.1 %collective-permute-start.41 = (f32[14,1024]{1,0:T(8,128)}, f32[14,1024]{1,0:T(8,128)}, u32[]{:S(2)}, u32[]{:S(2)}) collective-permute-start(f32[14,1024]{1,0:T(8,128)} %broadcast_multiply_fusion.1), channel_id=1, source_target_pairs={{0,1},{1,0},{2,3},{3,2},{4,5},{5,4},{6,7},{7,6},{8,9},{9,8},{10,11... | collective-permute-start | bytes 172040 | tf_op jit(solution)/shard_map/ppermute | solution.py:61
  390.7 23.1 %collective-permute-start.40 = (f32[256,896]{1,0:T(8,128)}, f32[256,896]{1,0:T(8,128)}, u32[]{:S(2)}, u32[]{:S(2)}) collective-permute-start(f32[256,896]{1,0:T(8,128)} %get-tuple-element.680), channel_id=1, source_target_pairs={{0,2},{1,3},{2,0},{3,1},{4,6},{5,7},{6,4},{7,5},{8,10},{9,11},{10,... | collective-permute-start | bytes 2752520 | tf_op jit(solution)/shard_map/ppermute | solution.py:61
  395.7 31.8 %collective-permute-start.49 = (f32[128,1024]{1,0:T(8,128)}, f32[128,1024]{1,0:T(8,128)}, u32[]{:S(2)}, u32[]{:S(2)}) collective-permute-start(f32[128,1024]{1,0:T(8,128)} %get-tuple-element.730), channel_id=1, source_target_pairs={{0,16},{4,20},{8,24},{12,28},{16,0},{20,4},{24,8},{28,12},{1,17},{... | collective-permute-start | bytes 1572872 | tf_op jit(solution)/shard_map/ppermute | solution.py:61
  395.9 36.6 %collective-permute-start.48 = (f32[256,1024]{1,0:T(8,128)}, f32[256,1024]{1,0:T(8,128)}, u32[]{:S(2)}, u32[]{:S(2)}) collective-permute-start(f32[256,1024]{1,0:T(8,128)} %get-tuple-element.728), channel_id=1, source_target_pairs={{0,8},{4,12},{8,0},{12,4},{16,24},{20,28},{24,16},{28,20},{1,9},{5... | collective-permute-start | bytes 3145736 | tf_op jit(solution)/shard_map/ppermute | solution.py:61
  419.8 31.8 %collective-permute-start.54 = (f32[4,440,128]{2,1,0:T(8,128)}, f32[4,440,128]{2,1,0:T(8,128)}, u32[]{:S(2)}, u32[]{:S(2)}) collective-permute-start(f32[4,440,128]{2,1,0:T(8,128)} %bitcast.154), channel_id=1, source_target_pairs={{0,4},{4,0},{8,12},{12,8},{16,20},{20,16},{24,28},{28,24},{1,5},{5... | collective-permute-start | bytes 2703368 | tf_op jit(solution)/shard_map/ppermute | solution.py:61
  434.8 14.7 %collective-permute-start.46 = (f32[192,768]{1,0:T(8,128)}, f32[192,768]{1,0:T(8,128)}, u32[]{:S(2)}, u32[]{:S(2)}) collective-permute-start(f32[192,768]{1,0:T(8,128)} %add_rows.17), channel_id=1, source_target_pairs={{0,2},{1,3},{2,0},{3,1},{4,6},{5,7},{6,4},{7,5},{8,10},{9,11},{10,... | collective-permute-start | bytes 1769480 | tf_op jit(solution)/shard_map/ppermute | solution.py:61
  439.6 25.2 %collective-permute-start.53 = (f32[128,1024]{1,0:T(8,128)}, f32[128,1024]{1,0:T(8,128)}, u32[]{:S(2)}, u32[]{:S(2)}) collective-permute-start(f32[128,1024]{1,0:T(8,128)} %get-tuple-element.757), channel_id=1, source_target_pairs={{0,16},{4,20},{8,24},{12,28},{16,0},{20,4},{24,8},{28,12},{1,17},{... | collective-permute-start | bytes 1572872 | tf_op jit(solution)/shard_map/ppermute | solution.py:61
  440.9 27.6 %collective-permute-start.52 = (f32[512,512]{1,0:T(8,128)}, f32[512,512]{1,0:T(8,128)}, u32[]{:S(2)}, u32[]{:S(2)}) collective-permute-start(f32[512,512]{1,0:T(8,128)} %product_rows.25), channel_id=1, source_target_pairs={{0,4},{4,0},{8,12},{12,8},{16,20},{20,16},{24,28},{28,24},{1,5},{5... | collective-permute-start | bytes 3145736 | tf_op jit(solution)/shard_map/ppermute | solution.py:61
  441.3 37.5 %collective-permute-start.51 = (f32[256,1024]{1,0:T(8,128)}, f32[256,1024]{1,0:T(8,128)}, u32[]{:S(2)}, u32[]{:S(2)}) collective-permute-start(f32[256,1024]{1,0:T(8,128)} %get-tuple-element.754), channel_id=1, source_target_pairs={{0,8},{4,12},{8,0},{12,4},{16,24},{20,28},{24,16},{28,20},{1,9},{5... | collective-permute-start | bytes 3145736 | tf_op jit(solution)/shard_map/ppermute | solution.py:61
  466.0 17.0 %collective-permute-start.50 = (f32[192,768]{1,0:T(8,128)}, f32[192,768]{1,0:T(8,128)}, u32[]{:S(2)}, u32[]{:S(2)}) collective-permute-start(f32[192,768]{1,0:T(8,128)} %add.275), channel_id=1, source_target_pairs={{0,1},{1,0},{2,3},{3,2},{4,5},{5,4},{6,7},{7,6},{8,9},{9,8},{10,11... | collective-permute-start | bytes 1769480 | tf_op jit(solution)/shard_map/ppermute | solution.py:61
  466.1 28.5 %collective-permute-start.55 = (f32[2,440,128]{2,1,0:T(8,128)}, f32[2,440,128]{2,1,0:T(8,128)}, u32[]{:S(2)}, u32[]{:S(2)}) collective-permute-start(f32[2,440,128]{2,1,0:T(8,128)} %dynamic-slice_bitcast_fusion), channel_id=1, source_target_pairs={{0,8},{4,12},{8,0},{12,4},{16,24},{20,28},{24,16},{28,20},{1,9},{5... | collective-permute-start | bytes 1351688 | tf_op jit(solution)/shard_map/ppermute | solution.py:61
  480.9 23.9 %collective-permute-start.58 = (f32[128,1024]{1,0:T(8,128)}, f32[128,1024]{1,0:T(8,128)}, u32[]{:S(2)}, u32[]{:S(2)}) collective-permute-start(f32[128,1024]{1,0:T(8,128)} %get-tuple-element.789), channel_id=1, source_target_pairs={{0,16},{4,20},{8,24},{12,28},{16,0},{20,4},{24,8},{28,12},{1,17},{... | collective-permute-start | bytes 1572872 | tf_op jit(solution)/shard_map/ppermute | solution.py:61
  480.9 32.3 %collective-permute-start.57 = (f32[256,512]{1,0:T(8,128)}, f32[256,512]{1,0:T(8,128)}, u32[]{:S(2)}, u32[]{:S(2)}) collective-permute-start(f32[256,512]{1,0:T(8,128)} %get-tuple-element.787), channel_id=1, source_target_pairs={{0,8},{4,12},{8,0},{12,4},{16,24},{20,28},{24,16},{28,20},{1,9},{5... | collective-permute-start | bytes 1572872 | tf_op jit(solution)/shard_map/ppermute | solution.py:61
  496.5 17.9 %collective-permute-start.56 = (f32[1,440,128]{2,1,0:T(8,128)}, f32[1,440,128]{2,1,0:T(8,128)}, u32[]{:S(2)}, u32[]{:S(2)}) collective-permute-start(f32[1,440,128]{2,1,0:T(8,128)} %constant_dynamic-slice_fusion), channel_id=1, source_target_pairs={{0,16},{4,20},{8,24},{12,28},{16,0},{20,4},{24,8},{28,12},{1,17},{... | collective-permute-start | bytes 675848 | tf_op jit(solution)/shard_map/ppermute | solution.py:61
  517.8 11.8 %collective-permute-start.60 = (f32[128,512]{1,0:T(8,128)S(1)}, f32[128,512]{1,0:T(8,128)S(1)}, u32[]{:S(2)}, u32[]{:S(2)}) collective-permute-start(f32[128,512]{1,0:T(8,128)S(1)} %get-tuple-element.804), channel_id=1, source_target_pairs={{0,16},{4,20},{8,24},{12,28},{16,0},{20,4},{24,8},{28,12},{1,17},{... | collective-permute-start | bytes 786440 | tf_op jit(solution)/shard_map/ppermute | solution.py:61
  518.7 4.4 collective-permute-start.59
  (197 other events, 1017.4 us)
